TPU v7x, 128 devices: a whole 4x4x4 slice. The times are simulated.
128 devices in a mesh: dp: 4 (over y), row: 4 (over z_hi, core), col: 8 (over x, z_lo).
Axes of the slice: x: 4, y: 4, z: 4 (z_hi: 2, z_lo: 2; z = z_hi * 2 + z_lo), core: 2. Of those that a mesh axis runs over, the one named last changes fastest.
Arguments:
- latent: bfloat16 [4, 64, 64, 2240], P('dp', 'row', 'col'), may hold values from -40 to 40
- query_weight: bfloat16 [2240, 1120], replicated, may hold values from -0.125 to 0.125
- key_weight: bfloat16 [2240, 1120], replicated, may hold values from -0.125 to 0.125
- value_weight: bfloat16 [2240, 1120], replicated, may hold values from -0.125 to 0.125
- upstream_grad: bfloat16 [4, 64, 64, 1120], P('dp', 'row', 'col'), may hold values from -6 to 6
Outputs:
- latent_grad: bfloat16 [4, 64, 64, 2240], P('dp', 'row', 'col')
- query_weight_grad: float32 [2240, 1120], P(('row', 'col'), 'dp')
- key_weight_grad: float32 [2240, 1120], P(('row', 'col'), 'dp')
- value_weight_grad: float32 [2240, 1120], P(('row', 'col'), 'dp')
All inputs are finite; a program needn't handle non-finite values.
Results may differ from a plain program's by a relative error of at most 0.039.
Values sent between devices are 32-bit elements; how exact they have to be, the bound alone decides.
No kernel may reach another device: no remote copies, remote signals or barrier semaphores. Data moves between devices by JAX's collectives and lax.ppermute only.
A program may use at most 192 MiB of HBM per device.

v0:
```python
import math

import jax
import jax.numpy as jnp
from jax import lax
from jax.sharding import PartitionSpec as P

D = 2240
HD = 112
HEADS = 10


EPSILON = 1e-15
HIGHEST_PRECISION = lax.Precision.HIGHEST


def project(token_rows, weight):
    return jnp.dot(token_rows, weight, preferred_element_type=jnp.float32).astype(jnp.bfloat16)


def back_project(gradient, weight):
    return lax.dot_general(
        gradient, weight, (((1,), (1,)), ((), ())), preferred_element_type=jnp.float32
    )


def body(latent, query_weight, key_weight, value_weight, upstream_grad):
    grid_devices = lax.axis_size("row") * lax.axis_size("col")
    replicas = lax.axis_size("dp")
    token_rows = latent.reshape(-1, D)
    local_count = token_rows.shape[0]
    image_tokens = local_count * grid_devices
    loss_scale = 4.0 * math.sqrt(image_tokens)
    normalizer = 1.0 / math.sqrt(image_tokens * replicas)
    head_width = HEADS * HD
    key_rows = project(token_rows, key_weight)
    value_rows = project(token_rows, value_weight)
    relu_key = jax.nn.relu(key_rows).reshape(-1, HEADS, HD)
    value_heads = value_rows.reshape(-1, HEADS, HD)
    local_state = jnp.einsum(
        "thj,thm->hjm", relu_key, value_heads, preferred_element_type=jnp.float32
    )
    local_total = jnp.sum(relu_key, axis=0, dtype=jnp.float32)
    key_state, key_total = lax.psum((local_state, local_total), ("row", "col"))
    query_rows = project(token_rows, query_weight)
    query_heads = query_rows.reshape(-1, HEADS, HD)
    relu_query = jax.nn.relu(query_heads)
    denominator = (
        jnp.einsum(
            "thj,hj->th",
            relu_query,
            key_total,
            precision=HIGHEST_PRECISION,
            preferred_element_type=jnp.float32,
        )
        + EPSILON
    )
    attended = (
        jnp.einsum(
            "thj,hjm->thm",
            relu_query,
            key_state,
            precision=HIGHEST_PRECISION,
            preferred_element_type=jnp.float32,
        )
        / denominator[:, :, None]
    )
    cotangent = upstream_grad.reshape(-1, HEADS, HD).astype(jnp.float32) * loss_scale
    grad_numer = cotangent / denominator[:, :, None]
    grad_denom = -jnp.sum(cotangent * attended, axis=2) / denominator
    grad_numer_low = grad_numer.astype(jnp.bfloat16)
    local_state_grad = jnp.einsum(
        "thj,thm->hjm", relu_query, grad_numer_low, preferred_element_type=jnp.float32
    )
    local_total_grad = jnp.einsum(
        "thj,th->hj",
        relu_query,
        grad_denom,
        precision=HIGHEST_PRECISION,
        preferred_element_type=jnp.float32,
    )
    state_grad, total_grad = lax.psum((local_state_grad, local_total_grad), ("row", "col"))
    grad_relu_query = (
        jnp.einsum(
            "thm,hjm->thj",
            grad_numer_low,
            key_state,
            precision=HIGHEST_PRECISION,
            preferred_element_type=jnp.float32,
        )
        + grad_denom[:, :, None] * key_total[None]
    )
    grad_query = (
        jnp.where(query_heads > 0, grad_relu_query, 0.0)
        .reshape(-1, head_width)
        .astype(jnp.bfloat16)
    )
    grad_value = (
        jnp.einsum(
            "thj,hjm->thm",
            relu_key,
            state_grad,
            precision=HIGHEST_PRECISION,
            preferred_element_type=jnp.float32,
        )
        .reshape(-1, head_width)
        .astype(jnp.bfloat16)
    )
    grad_relu_key = (
        jnp.einsum(
            "thm,hjm->thj",
            value_heads,
            state_grad,
            precision=HIGHEST_PRECISION,
            preferred_element_type=jnp.float32,
        )
        + total_grad[None]
    )
    grad_key = (
        jnp.where(key_rows.reshape(-1, HEADS, HD) > 0, grad_relu_key, 0.0)
        .reshape(-1, head_width)
        .astype(jnp.bfloat16)
    )
    summed = back_project(grad_query, query_weight) + back_project(grad_key, key_weight)
    summed = summed + back_project(grad_value, value_weight)
    latent_grad = summed.astype(jnp.bfloat16).reshape(latent.shape)
    stacked = jnp.stack([grad_query, grad_key, grad_value], axis=1).reshape(
        local_count, 3, replicas, head_width // replicas
    )
    stacked = jnp.transpose(stacked, (0, 2, 1, 3)).reshape(local_count, 3 * head_width)
    row_block = lax.psum_scatter(
        lax.dot_general(
            token_rows, stacked, (((0,), (0,)), ((), ())), preferred_element_type=jnp.float32
        )
        * normalizer,
        ("row", "col"),
        scatter_dimension=0,
        tiled=True,
    )
    weight_block = lax.psum_scatter(row_block, "dp", scatter_dimension=1, tiled=True)
    weight_block = weight_block.reshape(weight_block.shape[0], 3, head_width // replicas)
    return (latent_grad, weight_block[:, 0], weight_block[:, 1], weight_block[:, 2])


def solution(mesh):
    return jax.shard_map(
        body,
        mesh=mesh,
        in_specs=(P("dp", "row", "col", None), P(), P(), P(), P("dp", "row", "col", None)),
        out_specs=(
            P("dp", "row", "col", None),
            P(("row", "col"), "dp"),
            P(("row", "col"), "dp"),
            P(("row", "col"), "dp"),
        ),
        check_vma=False,
    )
```

profile of v0, /device:TPU:8, one launch (start us, length us, event | category | flops | bytes accessed | tf_op | source)
XLA Modules:
  0.0 546.2 jit_solution(5383486594765757244)
XLA Ops:
  7.2 1.0 copy-done
  8.2 4.7 broadcast_compare_fusion.1
  13.0 4.6 broadcast_maximum_fusion.1
  17.6 2.2 convolution_convert_fusion
  19.9 0.6 mul.36
  20.5 0.3 copy.27
  20.8 0.2 convert_reduce_fusion
  21.1 69.4 %psum.29 = f32[10,112]{1,0:T(8,128)S(1)} all-reduce(f32[10,112]{1,0:T(8,128)S(1)} %reduce_sum.21), channel_id=1, replica_groups=mesh['dp'=4,'row'=4,'col'=8] {'row','col'}, use_global_device_ids=true, to_apply=%region_2.3 | all-reduce | flops 1120 | bytes 8960 | tf_op jit(solution)/shard_map/psum | solution.py:44
  90.4 0.3 fusion.17
  90.8 1.1 fusion.21
  91.9 1.2 fusion.19
  93.2 101.6 %all-reduce.8.cloned.1.call-done = (f32[10,112,112]{2,1,0:T(8,128)}, f32[10,112,112]{2,1,0:T(8,128)}) async-done(((f32[10,112,112]{2,1,0:T(8,128)}, f32[10,112,112]{2,1,0:T(8,128)}), (f32[10,112,112]{2,1,0:T(8,128)}, f32[10,112,112]{2,1,0:T(8,128)})) %all-reduce.8.cloned.1.call-update) | async-done | bytes 1003536 | tf_op jit(solution)/shard_map/psum | solution.py:44
  194.9 1.8 fusion.9
  196.7 1.6 fusion.8
  198.2 0.5 fusion.15
  198.8 67.3 %psum.31 = f32[10,112]{1,0:T(8,128)S(1)} all-reduce(f32[10,112]{1,0:T(8,128)S(1)} %bitcast.132), channel_id=1, replica_groups=mesh['dp'=4,'row'=4,'col'=8] {'row','col'}, use_global_device_ids=true, to_apply=%region_5.6 | all-reduce | flops 1120 | bytes 8960 | tf_op jit(solution)/shard_map/psum | solution.py:82
  266.1 0.6 convolution_convert_fusion.3
  266.8 0.5 fusion.7
  267.4 12.2 %multiply_bitcast_fusion = f32[2240,3360]{0,1:T(8,128)} fusion(bf16[128,3360]{0,1:T(8,128)(2,1)S(1)} %bitcast.110, bf16[1,16,8,2240]{3,2,1,0:T(8,128)(2,1)S(1)} %copy-done), kind=kOutput, calls=%fused_computation | convolution fusion | flops 1934284800 | bytes 31539200 | tf_op jit(solution)/shard_map/dot_general | solution.py:132
  279.6 0.6 copy-done.5
  280.2 0.6 dynamic-slice
  281.4 225.2 %all-reduce.6.cloned.1.call-done = f32[2240,3360]{0,1:T(8,128)} async-done(((f32[2240,3360]{0,1:T(8,128)}), f32[2240,3360]{0,1:T(8,128)}) %all-reduce.6.cloned.1.call-update) | async-done | bytes 30105616
  506.6 3.7 constant_dynamic-slice_fusion
  510.3 4.1 fusion.22
  514.5 4.1 convolution_add_fusion.1
  518.6 1.6 fusion
  520.2 1.1 copy.31
  521.3 15.0 %reduce-scatter.5.cloned.1.call-done = f32[70,840]{0,1:T(8,128)} async-done(((f32[70,3360]{0,1:T(8,128)}), f32[70,840]{0,1:T(8,128)}) %reduce-scatter.5.cloned.1.call-update) | async-done | bytes 235216
  536.2 1.1 fusion.20
  537.3 0.8 copy.46
  538.1 0.8 copy.47
  538.9 0.8 copy.48
  (29 shorter events, 0.6 us)
Async XLA Ops:
  7.2 1.1 copy-start
  7.2 187.7 %all-reduce.8.cloned.1.call-start = ((), (), s32[]{:S(2)}) async-start(), calls=%async_computation.3 | async-start | bytes 2293760 | tf_op jit(solution)/shard_map/psum | solution.py:44
  8.2 9.4 %copy-start.2 = (bf16[2240,1120]{1,0:T(8,128)(2,1)S(1)}, bf16[2240,1120]{1,0:T(8,128)(2,1)}, u32[]{:S(2)}) copy-start(bf16[2240,1120]{1,0:T(8,128)(2,1)} %param.8) | copy-start | bytes 15052804
  13.0 6.9 %copy-start.4 = (bf16[1,16,8,1120]{3,2,1,0:T(8,128)(2,1)S(1)}, bf16[1,16,8,1120]{3,2,1,0:T(8,128)(2,1)}, u32[]{:S(2)}) copy-start(bf16[1,16,8,1120]{3,2,1,0:T(8,128)(2,1)} %param.9) | copy-start | bytes 860164
  93.1 413.5 %all-reduce.6.cloned.1.call-start = ((), (), s32[]{:S(2)}) async-start(), calls=%async_computation.1 | async-start | bytes 61931520
  194.9 71.3 %copy-start.3 = (f32[10,112,112]{2,1,0:T(8,128)S(1)}, f32[10,112,112]{2,1,0:T(8,128)}, u32[]{:S(2)}) copy-start(f32[10,112,112]{2,1,0:T(8,128)} %get-tuple-element.9) | copy-start | bytes 1505284
  279.5 0.7 copy-start.5
  279.6 256.7 %reduce-scatter.5.cloned.1.call-start = ((), (), s32[]{:S(2)}) async-start(), calls=%async_computation.2 | async-start | bytes 2150400
  510.3 8.3 %slice-start = ((s8[5160960]{0:T(1024)(128)(4,1)}), s8[4194304]{0:T(1024)(128)(4,1)S(1)}, s32[]{:S(2)}) async-start(s8[5160960]{0:T(1024)(128)(4,1)} %bitcast.108), calls=%async_computation.4 | async-start | bytes 8388608
  514.5 4.2 slice-start.1
  518.6 21.0 %copy-start.1 = (bf16[1,16,8,2240]{3,2,1,0:T(8,128)(2,1)S(1)}, bf16[1,16,8,2240]{3,2,1,0:T(8,128)(2,1)}, u32[]{:S(2)}) copy-start(bf16[1,16,8,2240]{3,2,1,0:T(8,128)(2,1)} %param.5) | copy-start | bytes 1720324
Sparse Core Ops, SparseCore 0:
  93.2 101.5 all-reduce.7
  279.7 226.8 all-reduce.5
  510.4 25.7 reduce-scatter.4
where the time goes:
time: 549 us; the launch traced here: 546 us
  waiting for transfers between devices  342 us (62%)
  blocking collectives  137 us (25%)
  matrix products  41.2 us (8%)
  between operations  14.6 us (3%)
  local copies, waits for them, and re-layouts  11.3 us (2%)
    unnamed x5, waiting for transfers between devices  240 us
    psum x1, waiting for transfers between devices, body(): key_state, key_total = lax.psum((local_state, local_total), ('row', 'col'))  102 us
    psum x1, blocking collectives, body(): key_state, key_total = lax.psum((local_state, local_total), ('row', 'col'))  69.4 us
    psum x1, blocking collectives, body(): lax.psum((local_state_grad, local_total_grad), ('row', 'col'))  67.3 us
    dot_general x1, matrix products, body(): lax.dot_general(token_rows, stacked, (((0,), (0,)), ((), ())), preferred_...  12.2 us
    dot_general x3, matrix products, project(): jnp.dot(token_rows, weight, preferred_element_type=jnp.float32)  11.6 us
  transfers between devices with their start and end apart: 3, of which 3 were waited for; matrix products, arithmetic and copies ran while one was open for 2% of the time, Pallas kernels for 0%

commit v1 on v0

v1 whole, which is shorter than its diff:
```python
import math

import jax
import jax.numpy as jnp
from jax import lax
from jax.sharding import Mesh, PartitionSpec as P

D = 2240
HD = 112
HEADS = 10
HW = HEADS * HD

EPSILON = 1e-15
HIGHEST = lax.Precision.HIGHEST
IMAGE = ("zh", "core", "x", "zl")
PLANE = ("zh", "x", "zl")


def project(token_rows, weight):
    return jnp.dot(token_rows, weight, preferred_element_type=jnp.float32).astype(jnp.bfloat16)


def back_project(gradient, weight):
    return lax.dot_general(
        gradient, weight, (((1,), (1,)), ((), ())), preferred_element_type=jnp.float32
    )


def exchange(blocks, axes):
    return lax.all_to_all(blocks, axes, 0, 0, tiled=True)


def einsum_high(spec, left, right):
    return jnp.einsum(
        spec, left, right, precision=HIGHEST, preferred_element_type=jnp.float32
    )


def gather_columns(gradient, replicas, scale):
    count = gradient.shape[0]
    blocks = gradient.astype(jnp.float32).reshape(count, replicas, HW // replicas)
    blocks = exchange(jnp.transpose(blocks, (1, 0, 2)), "dp")
    return (blocks.reshape(replicas * count, HW // replicas) * scale).astype(jnp.bfloat16)


def scatter_rows(partial, zh, plane):
    cols = partial.shape[1]
    cores = 2
    blocks = partial.reshape(zh, cores, plane // zh, D // (plane * cores), cols)
    core = lax.axis_index("core")
    own = lax.dynamic_index_in_dim(blocks, core, 1, keepdims=False)
    other = lax.dynamic_index_in_dim(blocks, 1 - core, 1, keepdims=False)
    own = own + lax.ppermute(other, "core", [(0, 1), (1, 0)])
    own = exchange(own.reshape(plane, D // (plane * cores), cols), PLANE)
    return jnp.sum(own, axis=0)


def body(latent, query_weight, key_weight, value_weight, upstream_grad):
    zh = lax.axis_size("zh")
    plane = zh * lax.axis_size("x") * lax.axis_size("zl")
    tiles = plane * lax.axis_size("core")
    replicas = lax.axis_size("dp")
    tokens = latent.reshape(-1, D)
    count = tokens.shape[0]
    image_tokens = count * tiles
    loss_scale = 4.0 * math.sqrt(image_tokens)
    normalizer = 1.0 / math.sqrt(image_tokens * replicas)
    part = HW // tiles

    all_tokens = exchange(
        jnp.broadcast_to(tokens.astype(jnp.float32)[None], (replicas, count, D)), "dp"
    )
    all_tokens = (all_tokens.reshape(replicas * count, D) * 0.5).astype(jnp.bfloat16)

    key_rows = project(tokens, key_weight)
    value_rows = project(tokens, value_weight)
    relu_key = jax.nn.relu(key_rows).reshape(-1, HEADS, HD)
    value_heads = value_rows.reshape(-1, HEADS, HD)
    local_state = jnp.einsum(
        "thj,thm->hjm", relu_key, value_heads, preferred_element_type=jnp.float32
    )
    local_total = jnp.sum(relu_key, axis=0, dtype=jnp.float32)
    sent = jnp.concatenate(
        [
            local_state.reshape(tiles, part, HD),
            jnp.broadcast_to(local_total[None], (tiles, HEADS, HD)),
        ],
        axis=1,
    )
    got = exchange(sent, IMAGE)
    sums = jnp.sum(got, axis=0)
    state_part = sums[:part]
    key_total = sums[part:]

    query_heads = project(tokens, query_weight).reshape(-1, HEADS, HD)
    relu_query = jax.nn.relu(query_heads)
    denominator = einsum_high("thj,hj->th", relu_query, key_total) + EPSILON
    cotangent = upstream_grad.reshape(-1, HEADS, HD).astype(jnp.float32) * loss_scale
    grad_numer = cotangent / denominator[:, :, None]
    grad_numer_low = grad_numer.astype(jnp.bfloat16)
    local_state_grad = jnp.einsum(
        "thj,thm->hjm", relu_query, grad_numer_low, preferred_element_type=jnp.float32
    )
    sent = jnp.concatenate(
        [
            jnp.broadcast_to(state_part[None], (tiles, part, HD)),
            local_state_grad.reshape(tiles, part, HD),
        ],
        axis=1,
    )
    got = exchange(sent, IMAGE)
    key_state = got[:, :part].reshape(HEADS, HD, HD)
    state_grad_part = jnp.sum(got[:, part:], axis=0)

    attended = einsum_high("thj,hjm->thm", relu_query, key_state) / denominator[:, :, None]
    grad_denom = -jnp.sum(cotangent * attended, axis=2) / denominator
    local_total_grad = einsum_high("thj,th->hj", relu_query, grad_denom)
    sent = jnp.concatenate(
        [
            jnp.broadcast_to(state_grad_part[None], (tiles, part, HD)),
            jnp.broadcast_to(local_total_grad[None], (tiles, HEADS, HD)),
        ],
        axis=1,
    )
    got = exchange(sent, IMAGE)
    state_grad = got[:, :part].reshape(HEADS, HD, HD)
    total_grad = jnp.sum(got[:, part:], axis=0)

    grad_relu_query = (
        einsum_high("thm,hjm->thj", grad_numer_low, key_state)
        + grad_denom[:, :, None] * key_total[None]
    )
    grad_query = jnp.where(query_heads > 0, grad_relu_query, 0.0)
    grad_query = grad_query.reshape(-1, HW).astype(jnp.bfloat16)
    query_columns = gather_columns(grad_query, replicas, 2.0 * normalizer)

    grad_value = einsum_high("thj,hjm->thm", relu_key, state_grad)
    grad_value = grad_value.reshape(-1, HW).astype(jnp.bfloat16)
    grad_relu_key = einsum_high("thm,hjm->thj", value_heads, state_grad) + total_grad[None]
    grad_key = jnp.where(key_rows.reshape(-1, HEADS, HD) > 0, grad_relu_key, 0.0)
    grad_key = grad_key.reshape(-1, HW).astype(jnp.bfloat16)
    key_columns = gather_columns(grad_key, replicas, 2.0 * normalizer)
    value_columns = gather_columns(grad_value, replicas, 2.0 * normalizer)

    summed = back_project(grad_query, query_weight) + back_project(grad_key, key_weight)
    summed = summed + back_project(grad_value, value_weight)
    latent_grad = summed.astype(jnp.bfloat16).reshape(latent.shape)

    def weight_grad(columns):
        partial = lax.dot_general(
            all_tokens, columns, (((0,), (0,)), ((), ())), preferred_element_type=jnp.float32
        )
        return scatter_rows(partial, zh, plane)

    return (
        latent_grad,
        weight_grad(query_columns),
        weight_grad(key_columns),
        weight_grad(value_columns),
    )


def solution(mesh):
    devices = mesh.devices
    cores = 2
    zl = 2
    dp, row, col = devices.shape
    fine = Mesh(
        devices.reshape(dp, row // cores, cores, col // zl, zl),
        ("dp", "zh", "core", "x", "zl"),
    )
    grid = P("dp", ("zh", "core"), ("x", "zl"), None)
    weight_out = P(("zh", "core", "x", "zl"), "dp")
    return jax.shard_map(
        body,
        mesh=fine,
        in_specs=(grid, P(), P(), P(), grid),
        out_specs=(grid, weight_out, weight_out, weight_out),
        check_vma=False,
    )
```

time: 549 us -> 298 us (0.54)
  waiting for transfers between devices: 342 us -> 127 us
  blocking collectives: 137 us -> 23 us
  starting transfers between devices: 0.12 us -> 50.6 us
  other arithmetic: 0.43 us -> 23.5 us
  local copies, waits for them, and re-layouts: 11.3 us -> 34 us
  between operations: 14.6 us -> 1.09 us
    unnamed x5 -> x0, waiting for transfers between devices: 240 us -> none
    psum x2 -> x0, blocking collectives: 137 us -> none  [the longest x1 69.4 us: body(): key_state, key_total = lax.psum((local_state, local_total), ('row', 'col'))]
    all_to_all x0 -> x9, waiting for transfers between devices: none -> 127 us  [exchange(): return lax.all_to_all(blocks, axes, 0, 0, tiled=True)]
    psum x1 -> x0, waiting for transfers between devices: 102 us -> none  [body(): key_state, key_total = lax.psum((local_state, local_total), ('row', 'col'))]
    all_to_all x0 -> x9, starting transfers between devices: none -> 50 us  [exchange(): return lax.all_to_all(blocks, axes, 0, 0, tiled=True)]
    all_to_all x0 -> x1, blocking collectives: none -> 23 us  [exchange(): return lax.all_to_all(blocks, axes, 0, 0, tiled=True)]
    dynamic_slice x0 -> x5, local copies, waits for them, and re-layouts: none -> 9.34 us  [the longest x3 6.16 us: scatter_rows(): other = lax.dynamic_index_in_dim(blocks, 1 - core, 1, keepdims=False)]
    unnamed x21 -> x22, local copies, waits for them, and re-layouts: 8.18 us -> 0.13 us
  transfers between devices with their start and end apart: 3 -> 12, of which waited for: 3 -> 8; matrix products, arithmetic and copies ran while one was open for 2% -> 25% of each run, Pallas kernels for 0% -> 0%
where the time goes in v1:
time: 298 us; the launch traced here: 296 us
  waiting for transfers between devices  127 us (43%)
  starting transfers between devices  50.6 us (17%)
  matrix products  36.9 us (12%)
  local copies, waits for them, and re-layouts  34 us (11%)
  other arithmetic  23.5 us (8%)
  blocking collectives  23 us (8%)
    all_to_all x9, waiting for transfers between devices, exchange(): return lax.all_to_all(blocks, axes, 0, 0, tiled=True)  127 us
    all_to_all x9, starting transfers between devices, exchange(): return lax.all_to_all(blocks, axes, 0, 0, tiled=True)  50 us
    all_to_all x1, blocking collectives, exchange(): return lax.all_to_all(blocks, axes, 0, 0, tiled=True)  23 us
    dot_general x3, matrix products, project(): jnp.dot(token_rows, weight, preferred_element_type=jnp.float32)  14.9 us
    dot_general x3, matrix products, back_project(): lax.dot_general(gradient, weight, (((1,), (1,)), ((), ())), preferred_ele...  10.7 us
    dynamic_slice x3, local copies, waits for them, and re-layouts, scatter_rows(): other = lax.dynamic_index_in_dim(blocks, 1 - core, 1, keepdims=False)  6.16 us
  transfers between devices with their start and end apart: 12, of which 8 were waited for; matrix products, arithmetic and copies ran while one was open for 25% of the time, Pallas kernels for 0%

profile of v1, /device:TPU:8, one launch (start us, length us, event | category | flops | bytes accessed | tf_op | source)
XLA Modules:
  0.0 296.3 jit_solution(6153336771265712744)
XLA Ops:
  0.6 5.0 %convert_reduce_fusion = (f32[1120]{0:T(1024)S(1)}, bf16[128,1120]{0,1:T(8,128)(2,1)S(1)}) fusion(bf16[2240,1120]{1,0:T(8,128)(2,1)} %param.7, bf16[1,16,8,2240]{3,2,1,0:T(8,128)(2,1)} %param.5), kind=kOutput, calls=%fused_computation.41 | convolution fusion | flops 642825088 | bytes 5882240 | tf_op jit(solution)/shard_map/dot_general | solution.py:20
  5.7 4.6 %convolution_convert_fusion = bf16[128,1120]{0,1:T(8,128)(2,1)S(1)} fusion(bf16[2240,1120]{1,0:T(8,128)(2,1)} %param.8, bf16[1,16,8,2240]{3,2,1,0:T(8,128)(2,1)S(1)} %copy-done), kind=kOutput, calls=%fused_computation.4 | convolution fusion | flops 642396160 | bytes 5877760 | tf_op jit(solution)/shard_map/dot_general | solution.py:20
  11.7 8.2 %all-to-all-start = ((f32[32,45,112]{2,1,0:T(8,128)}), f32[32,45,112]{2,1,0:T(8,128)S(1)}, u32[]{:S(2)}, u32[]{:S(2)}) async-start(f32[32,45,112]{2,1,0:T(8,128)} %pad_maximum_fusion.1), calls=%async_computation | async-start | bytes 1572864 | tf_op jit(solution)/shard_map/all_to_all | solution.py:30
  21.7 5.4 %broadcast_compare_fusion.1 = (pred[128,1120]{0,1:T(8,128)(4,1)}, bf16[128,1120]{0,1:T(8,128)(2,1)}) fusion(bf16[2240,1120]{1,0:T(8,128)(2,1)} %param.6, bf16[1,16,8,2240]{3,2,1,0:T(8,128)(2,1)S(1)} %copy-done), kind=kOutput, calls=%fused_computation.52 | convolution fusion | flops 642539520 | bytes 6021120 | tf_op jit(solution)/shard_map/dot_general | solution.py:20
  30.8 3.6 %all-to-all-done = f32[32,45,112]{2,1,0:T(8,128)S(1)} async-done(((f32[32,45,112]{2,1,0:T(8,128)}), f32[32,45,112]{2,1,0:T(8,128)S(1)}, u32[]{:S(2)}, u32[]{:S(2)}) %all-to-all-start) | async-done | bytes 645152 | tf_op jit(solution)/shard_map/all_to_all | solution.py:30
  36.5 23.0 %all_to_all.50 = f32[32,70,112]{2,1,0:T(8,128)S(1)} all-to-all(f32[32,70,112]{2,1,0:T(8,128)S(1)} %pad_maximum_fusion), channel_id=1, replica_groups=mesh['dp'=4,'zh'=2,'core'=2,'x'=4,'zl'=2] {'zh','core','x','zl'}, dimensions={0} | all-to-all | bytes 2007040 | tf_op jit(solution)/shard_map/all_to_all | solution.py:30
  63.9 3.9 %all-to-all-start.2 = ((f32[32,45,112]{2,1,0:T(8,128)}), f32[32,45,112]{2,1,0:T(8,128)S(1)}, u32[]{:S(2)}, u32[]{:S(2)}) async-start(f32[32,45,112]{2,1,0:T(8,128)} %pad_maximum_fusion.2), calls=%async_computation.2 | async-start | bytes 1572864 | tf_op jit(solution)/shard_map/all_to_all | solution.py:30
  70.3 12.0 %all-to-all-done.2 = f32[32,45,112]{2,1,0:T(8,128)S(1)} async-done(((f32[32,45,112]{2,1,0:T(8,128)}), f32[32,45,112]{2,1,0:T(8,128)S(1)}, u32[]{:S(2)}, u32[]{:S(2)}) %all-to-all-start.2) | async-done | bytes 645152 | tf_op jit(solution)/shard_map/all_to_all | solution.py:30
  82.4 4.9 %all-to-all-start.4 = ((f32[4,128,280]{1,2,0:T(8,128)}), f32[4,128,280]{1,2,0:T(8,128)}, u32[]{:S(2)}, u32[]{:S(2)}) async-start(f32[4,128,280]{1,2,0:T(8,128)} %convert_bitcast_fusion.2), calls=%async_computation.4 | async-start | bytes 1146880 | tf_op jit(solution)/shard_map/all_to_all | solution.py:30
  88.9 6.3 %all-to-all-done.4 = f32[4,128,280]{1,2,0:T(8,128)} async-done(((f32[4,128,280]{1,2,0:T(8,128)}), f32[4,128,280]{1,2,0:T(8,128)}, u32[]{:S(2)}, u32[]{:S(2)}) %all-to-all-start.4) | async-done | bytes 573472 | tf_op jit(solution)/shard_map/all_to_all | solution.py:30
  95.2 5.5 %all-to-all-start.8 = ((f32[4,128,280]{1,2,0:T(8,128)}), f32[4,128,280]{1,2,0:T(8,128)}, u32[]{:S(2)}, u32[]{:S(2)}) async-start(f32[4,128,280]{1,2,0:T(8,128)} %convert_bitcast_fusion), calls=%async_computation.8 | async-start | bytes 1146880 | tf_op jit(solution)/shard_map/all_to_all | solution.py:30
  101.7 6.0 %all-to-all-done.8 = f32[4,128,280]{1,2,0:T(8,128)} async-done(((f32[4,128,280]{1,2,0:T(8,128)}), f32[4,128,280]{1,2,0:T(8,128)}, u32[]{:S(2)}, u32[]{:S(2)}) %all-to-all-start.8) | async-done | bytes 573472 | tf_op jit(solution)/shard_map/all_to_all | solution.py:30
  107.7 3.5 %broadcast_in_dim.22 = f32[4,128,2240]{1,2,0:T(8,128)} broadcast(bf16[128,2240]{0,1:T(8,128)(2,1)} %copy.60), dimensions={1,2} | broadcast | bytes 5160960 | tf_op jit(solution)/shard_map/broadcast_in_dim | solution.py:71
  111.1 6.4 %all-to-all-start.3 = ((f32[4,128,2240]{1,2,0:T(8,128)}), f32[4,128,2240]{1,2,0:T(8,128)}, u32[]{:S(2)}, u32[]{:S(2)}) async-start(f32[4,128,2240]{1,2,0:T(8,128)} %broadcast_in_dim.22), calls=%async_computation.3 | async-start | bytes 9175040 | tf_op jit(solution)/shard_map/all_to_all | solution.py:30
  121.7 44.3 %all-to-all-done.3 = f32[4,128,2240]{1,2,0:T(8,128)} async-done(((f32[4,128,2240]{1,2,0:T(8,128)}), f32[4,128,2240]{1,2,0:T(8,128)}, u32[]{:S(2)}, u32[]{:S(2)}) %all-to-all-start.3) | async-done | bytes 4587552 | tf_op jit(solution)/shard_map/all_to_all | solution.py:30
  166.0 4.9 %all-to-all-start.6 = ((f32[4,128,280]{1,2,0:T(8,128)}), f32[4,128,280]{1,2,0:T(8,128)S(1)}, u32[]{:S(2)}, u32[]{:S(2)}) async-start(f32[4,128,280]{1,2,0:T(8,128)} %convert_bitcast_fusion.1), calls=%async_computation.6 | async-start | bytes 1146880 | tf_op jit(solution)/shard_map/all_to_all | solution.py:30
  170.9 4.1 %multiply_convert_fusion = bf16[4,128,2240]{1,2,0:T(8,128)(2,1)} fusion(f32[4,128,2240]{1,2,0:T(8,128)} %all-to-all-done.3), kind=kLoop, calls=%fused_computation | loop fusion | flops 2293760 | bytes 6881280 | tf_op jit(solution)/shard_map/convert_element_type | solution.py:73
  175.0 2.8 copy.61
  177.8 2.5 copy.62
  180.3 2.6 dot_general.70
  198.0 8.9 %all-to-all-start.5 = ((f32[16,70,280]{2,1,0:T(8,128)}), f32[16,70,280]{2,1,0:T(8,128)}, u32[]{:S(2)}, u32[]{:S(2)}) async-start(f32[16,70,280]{2,1,0:T(8,128)} %copy.67), calls=%async_computation.5 | async-start | bytes 3538944 | tf_op jit(solution)/shard_map/all_to_all | solution.py:30
  207.0 3.0 %copy.107 = f32[2,1,8,70,280]{4,2,3,1,0:T(8,128)} copy(f32[2,1,8,70,280]{4,3,2,1,0:T(8,128)} %get-tuple-element.9) | data formatting | bytes 2508800 | tf_op jit(solution)/shard_map/jit(dynamic_index_in_dim)/dynamic_slice | solution.py:52
  213.7 21.0 %all-to-all-done.5 = f32[16,70,280]{2,1,0:T(8,128)} async-done(((f32[16,70,280]{2,1,0:T(8,128)}), f32[16,70,280]{2,1,0:T(8,128)}, u32[]{:S(2)}, u32[]{:S(2)}) %all-to-all-start.5) | async-done | bytes 1254432 | tf_op jit(solution)/shard_map/all_to_all | solution.py:30
  234.7 3.7 %all-to-all-start.7 = ((f32[16,70,280]{2,1,0:T(8,128)}), f32[16,70,280]{2,1,0:T(8,128)S(1)}, u32[]{:S(2)}, u32[]{:S(2)}) async-start(f32[16,70,280]{2,1,0:T(8,128)} %copy.72), calls=%async_computation.7 | async-start | bytes 3538944 | tf_op jit(solution)/shard_map/all_to_all | solution.py:30
  242.0 23.1 %all-to-all-done.7 = f32[16,70,280]{2,1,0:T(8,128)S(1)} async-done(((f32[16,70,280]{2,1,0:T(8,128)}), f32[16,70,280]{2,1,0:T(8,128)S(1)}, u32[]{:S(2)}, u32[]{:S(2)}) %all-to-all-start.7) | async-done | bytes 1254432 | tf_op jit(solution)/shard_map/all_to_all | solution.py:30
  265.1 3.7 %all-to-all-start.9 = ((f32[16,70,280]{2,1,0:T(8,128)}), f32[16,70,280]{2,1,0:T(8,128)S(1)}, u32[]{:S(2)}, u32[]{:S(2)}) async-start(f32[16,70,280]{2,1,0:T(8,128)} %copy.77), calls=%async_computation.9 | async-start | bytes 3538944 | tf_op jit(solution)/shard_map/all_to_all | solution.py:30
  268.9 4.2 %fusion.27 = f32[128,2240]{0,1:T(8,128)S(1)} fusion(bf16[2240,1120]{1,0:T(8,128)(2,1)} %param.6, bf16[128,1120]{0,1:T(8,128)(2,1)} %bitcast.158), kind=kOutput, calls=%fused_computation.74 | convolution fusion | flops 642252800 | bytes 6451200 | tf_op jit(solution)/shard_map/dot_general | solution.py:24
  273.1 4.1 %convolution_add_fusion.1 = f32[128,2240]{0,1:T(8,128)S(1)} fusion(f32[128,2240]{0,1:T(8,128)S(1)} %fusion.27, bf16[2240,1120]{1,0:T(8,128)(2,1)} %param.7, bf16[128,1120]{0,1:T(8,128)(2,1)S(1)} %bitcast.150), kind=kOutput, calls=%fused_computation.2 | convolution fusion | flops 642539520 | bytes 7598080 | tf_op jit(solution)/shard_map/dot_general | solution.py:24
  277.2 2.4 fusion
  279.6 2.1 copy.59
  281.7 2.2 reduce_sum.77
  284.7 10.8 %all-to-all-done.9 = f32[16,70,280]{2,1,0:T(8,128)S(1)} async-done(((f32[16,70,280]{2,1,0:T(8,128)}), f32[16,70,280]{2,1,0:T(8,128)S(1)}, u32[]{:S(2)}, u32[]{:S(2)}) %all-to-all-start.9) | async-done | bytes 1254432 | tf_op jit(solution)/shard_map/all_to_all | solution.py:30
  (93 shorter events, 46.5 us)
Async XLA Ops:
  0.6 5.1 %copy-start = (bf16[1,16,8,2240]{3,2,1,0:T(8,128)(2,1)S(1)}, bf16[1,16,8,2240]{3,2,1,0:T(8,128)(2,1)}, u32[]{:S(2)}) copy-start(bf16[1,16,8,2240]{3,2,1,0:T(8,128)(2,1)} %param.5) | copy-start | bytes 1720324
  11.7 22.7 %all-to-all-start = ((f32[32,45,112]{2,1,0:T(8,128)}), f32[32,45,112]{2,1,0:T(8,128)S(1)}, u32[]{:S(2)}, u32[]{:S(2)}) async-start(f32[32,45,112]{2,1,0:T(8,128)} %pad_maximum_fusion.1), calls=%async_computation | async-start | bytes 1572864 | tf_op jit(solution)/shard_map/all_to_all | solution.py:30
  59.5 1.1 copy-start.7
  62.9 4.9 %copy-start.8 = (pred[128,1120]{0,1:T(8,128)(4,1)S(1)}, pred[128,1120]{0,1:T(8,128)(4,1)}, u32[]{:S(2)}) copy-start(pred[128,1120]{0,1:T(8,128)(4,1)} %get-tuple-element.18) | copy-start | bytes 430084
  63.9 18.4 %all-to-all-start.2 = ((f32[32,45,112]{2,1,0:T(8,128)}), f32[32,45,112]{2,1,0:T(8,128)S(1)}, u32[]{:S(2)}, u32[]{:S(2)}) async-start(f32[32,45,112]{2,1,0:T(8,128)} %pad_maximum_fusion.2), calls=%async_computation.2 | async-start | bytes 1572864 | tf_op jit(solution)/shard_map/all_to_all | solution.py:30
  69.4 17.8 %copy-start.6 = (bf16[128,10,112]{0,2,1:T(8,128)(2,1)}, bf16[128,10,112]{0,2,1:T(8,128)(2,1)S(1)}, u32[]{:S(2)}) copy-start(bf16[128,10,112]{0,2,1:T(8,128)(2,1)S(1)} %fusion.8) | copy-start | bytes 860164
  82.4 12.9 %all-to-all-start.4 = ((f32[4,128,280]{1,2,0:T(8,128)}), f32[4,128,280]{1,2,0:T(8,128)}, u32[]{:S(2)}, u32[]{:S(2)}) async-start(f32[4,128,280]{1,2,0:T(8,128)} %convert_bitcast_fusion.2), calls=%async_computation.4 | async-start | bytes 1146880 | tf_op jit(solution)/shard_map/all_to_all | solution.py:30
  88.0 23.1 %copy-start.2 = (bf16[10,112,128]{2,1,0:T(8,128)(2,1)}, bf16[10,112,128]{2,1,0:T(8,128)(2,1)S(1)}, u32[]{:S(2)}) copy-start(bf16[10,112,128]{2,1,0:T(8,128)(2,1)S(1)} %convolution_convert_fusion.3) | copy-start | bytes 860164
  95.2 12.5 %all-to-all-start.8 = ((f32[4,128,280]{1,2,0:T(8,128)}), f32[4,128,280]{1,2,0:T(8,128)}, u32[]{:S(2)}, u32[]{:S(2)}) async-start(f32[4,128,280]{1,2,0:T(8,128)} %convert_bitcast_fusion), calls=%async_computation.8 | async-start | bytes 1146880 | tf_op jit(solution)/shard_map/all_to_all | solution.py:30
  111.1 54.8 %all-to-all-start.3 = ((f32[4,128,2240]{1,2,0:T(8,128)}), f32[4,128,2240]{1,2,0:T(8,128)}, u32[]{:S(2)}, u32[]{:S(2)}) async-start(f32[4,128,2240]{1,2,0:T(8,128)} %broadcast_in_dim.22), calls=%async_computation.3 | async-start | bytes 9175040 | tf_op jit(solution)/shard_map/all_to_all | solution.py:30
  119.5 46.5 %copy-start.4 = (bf16[128,10,112]{0,2,1:T(8,128)(2,1)}, bf16[128,10,112]{0,2,1:T(8,128)(2,1)S(1)}, u32[]{:S(2)}) copy-start(bf16[128,10,112]{0,2,1:T(8,128)(2,1)S(1)} %fusion.7) | copy-start | bytes 860164
  166.0 21.5 %all-to-all-start.6 = ((f32[4,128,280]{1,2,0:T(8,128)}), f32[4,128,280]{1,2,0:T(8,128)S(1)}, u32[]{:S(2)}, u32[]{:S(2)}) async-start(f32[4,128,280]{1,2,0:T(8,128)} %convert_bitcast_fusion.1), calls=%async_computation.6 | async-start | bytes 1146880 | tf_op jit(solution)/shard_map/all_to_all | solution.py:30
  187.4 7.0 %collective-permute-start = (f32[2,8,70,280]{3,1,2,0:T(8,128)}, f32[2,8,70,280]{3,1,2,0:T(8,128)}, u32[]{:S(2)}, u32[]{:S(2)}) collective-permute-start(f32[2,8,70,280]{3,1,2,0:T(8,128)} %bitcast.139), channel_id=1, source_target_pairs={{0,8},{8,0},{1,9},{9,1},{2,10},{10,2},{3,11},{11,3},{4,12},{12,4},... | collective-permute-start | bytes 3763208 | tf_op jit(solution)/shard_map/ppermute | solution.py:53
  192.4 2.1 copy-start.1
  193.9 16.1 %collective-permute-start.1 = (f32[2,8,70,280]{3,1,2,0:T(8,128)}, f32[2,8,70,280]{3,1,2,0:T(8,128)}, u32[]{:S(2)}, u32[]{:S(2)}) collective-permute-start(f32[2,8,70,280]{3,1,2,0:T(8,128)} %bitcast.138), channel_id=1, source_target_pairs={{0,8},{8,0},{1,9},{9,1},{2,10},{10,2},{3,11},{11,3},{4,12},{12,4},... | collective-permute-start | bytes 3763208 | tf_op jit(solution)/shard_map/ppermute | solution.py:53
  198.0 36.7 %all-to-all-start.5 = ((f32[16,70,280]{2,1,0:T(8,128)}), f32[16,70,280]{2,1,0:T(8,128)}, u32[]{:S(2)}, u32[]{:S(2)}) async-start(f32[16,70,280]{2,1,0:T(8,128)} %copy.67), calls=%async_computation.5 | async-start | bytes 3538944 | tf_op jit(solution)/shard_map/all_to_all | solution.py:30
  210.0 28.5 %collective-permute-start.2 = (f32[2,8,70,280]{3,1,2,0:T(8,128)}, f32[2,8,70,280]{3,1,2,0:T(8,128)}, u32[]{:S(2)}, u32[]{:S(2)}) collective-permute-start(f32[2,8,70,280]{3,1,2,0:T(8,128)} %bitcast.137), channel_id=1, source_target_pairs={{0,8},{8,0},{1,9},{9,1},{2,10},{10,2},{3,11},{11,3},{4,12},{12,4},... | collective-permute-start | bytes 3763208 | tf_op jit(solution)/shard_map/ppermute | solution.py:53
  234.7 30.4 %all-to-all-start.7 = ((f32[16,70,280]{2,1,0:T(8,128)}), f32[16,70,280]{2,1,0:T(8,128)S(1)}, u32[]{:S(2)}, u32[]{:S(2)}) async-start(f32[16,70,280]{2,1,0:T(8,128)} %copy.72), calls=%async_computation.7 | async-start | bytes 3538944 | tf_op jit(solution)/shard_map/all_to_all | solution.py:30
  265.1 30.4 %all-to-all-start.9 = ((f32[16,70,280]{2,1,0:T(8,128)}), f32[16,70,280]{2,1,0:T(8,128)S(1)}, u32[]{:S(2)}, u32[]{:S(2)}) async-start(f32[16,70,280]{2,1,0:T(8,128)} %copy.77), calls=%async_computation.9 | async-start | bytes 3538944 | tf_op jit(solution)/shard_map/all_to_all | solution.py:30
  268.8 4.2 %copy-start.5 = (bf16[128,10,112]{0,2,1:T(8,128)(2,1)S(1)}, bf16[128,10,112]{0,2,1:T(8,128)(2,1)}, u32[]{:S(2)}) copy-start(bf16[128,10,112]{0,2,1:T(8,128)(2,1)} %copy-done.4) | copy-start | bytes 860164
  268.8 8.4 %slice-start = ((s8[5160960]{0:T(1024)(128)(4,1)}), s8[4194304]{0:T(1024)(128)(4,1)S(1)}, s32[]{:S(2)}) async-start(s8[5160960]{0:T(1024)(128)(4,1)} %bitcast.141), calls=%async_computation.10 | async-start | bytes 8388608
  273.0 4.2 %slice-start.1 = ((s8[5160960]{0:T(1024)(128)(4,1)}), s8[966656]{0:T(1024)(128)(4,1)S(1)}, s32[]{:S(2)}) async-start(s8[5160960]{0:T(1024)(128)(4,1)} %bitcast.141), calls=%async_computation.11 | async-start | bytes 1933312
  273.1 4.2 %copy-start.3 = (bf16[10,112,128]{2,1,0:T(8,128)(2,1)S(1)}, bf16[10,112,128]{2,1,0:T(8,128)(2,1)}, u32[]{:S(2)}) copy-start(bf16[10,112,128]{2,1,0:T(8,128)(2,1)} %copy-done.2) | copy-start | bytes 860164

commit v2 on v1

v2 whole, which is shorter than its diff:
```python
import math

import jax
import jax.numpy as jnp
from jax import lax
from jax.experimental import pallas as pl
from jax.experimental.pallas import tpu as pltpu
from jax.sharding import Mesh, PartitionSpec as P

D = 2240
HD = 112
HEADS = 10
HW = HEADS * HD
TILES = 32
PART = HW // TILES
PLANE_SIZE = 16
CORES = 2
ROWS = D // TILES
PADDED_ROWS = 72
REPLICAS = 4
COLS = HW // REPLICAS
TOKENS = 128

EPSILON = 1e-15
IMAGE = ("zh", "core", "x", "zl")
PLANE = ("zh", "x", "zl")
CHUNKS = [(start, min(384, D - start)) for start in range(0, D, 384)]

F32 = jnp.float32
BF16 = jnp.bfloat16
IN_VMEM = pl.BlockSpec(memory_space=pltpu.VMEM)
IN_SMEM = pl.BlockSpec(memory_space=pltpu.SMEM)
IN_HBM = pl.BlockSpec(memory_space=pltpu.HBM)


def shaped(shape, dtype=F32):
    return jax.ShapeDtypeStruct(shape, dtype)


def call(kernel, name, outs, in_specs, scratch=(), vmem=12):
    return pl.pallas_call(
        kernel,
        name=name,
        out_shape=outs,
        in_specs=in_specs,
        out_specs=[IN_VMEM] * len(outs),
        scratch_shapes=list(scratch),
        compiler_params=pltpu.CompilerParams(vmem_limit_bytes=vmem * 1024 * 1024),
    )


def dot(left, right, left_dim, right_dim):
    return lax.dot_general(
        left, right, (((left_dim,), (right_dim,)), ((), ())), preferred_element_type=F32
    )


def split_dot(left, right, left_dim, right_dim):
    high = right.astype(BF16)
    low = (right - high.astype(F32)).astype(BF16)
    return dot(left, high, left_dim, right_dim) + dot(left, low, left_dim, right_dim)


def relu(values):
    return jnp.maximum(values, jnp.zeros_like(values))


def weight_copies(weight, buffer, semaphores, first):
    copies = []
    for index, (start, size) in enumerate(CHUNKS):
        copies.append(
            pltpu.make_async_copy(
                weight.at[pl.ds(start, size)],
                buffer.at[pl.ds(start, size)],
                semaphores.at[first + index],
            )
        )
    return copies


def project(tokens, buffer, copies):
    total = None
    for (start, size), copy in zip(CHUNKS, copies):
        copy.wait()
        term = dot(tokens[:, start : start + size], buffer[start : start + size, :], 1, 0)
        total = term if total is None else total + term
    return total.astype(BF16)


def store_parts(sent, at, state):
    for tile in range(TILES):
        sent[tile, at : at + PART, :] = state[tile * PART : (tile + 1) * PART, :]


def load_parts(state, got):
    for tile in range(TILES):
        state[tile * PART : (tile + 1) * PART, :] = got[tile, :PART, :]


def head(ref, index):
    return ref[index * HD : (index + 1) * HD, :]


def key_value_kernel(
    tokens, key_weight, value_weight, key, value, sent, key_buffer, value_buffer, state, total, semaphores
):
    value_copies = weight_copies(value_weight, value_buffer, semaphores, 0)
    key_copies = weight_copies(key_weight, key_buffer, semaphores, len(CHUNKS))
    for copy in value_copies + key_copies:
        copy.start()
    rows = tokens[...]
    value_rows = project(rows, value_buffer, value_copies)
    key_rows = project(rows, key_buffer, key_copies)
    for index in range(HEADS):
        part = slice(index * HD, (index + 1) * HD)
        key_head = key_rows[:, part]
        value_head = value_rows[:, part]
        key[index] = key_head
        value[index] = value_head
        positive = relu(key_head)
        state[index * HD : (index + 1) * HD, :] = dot(positive, value_head, 0, 0)
        total[index : index + 1, :] = jnp.sum(positive.astype(F32), axis=0, keepdims=True)
    store_parts(sent, 0, state)
    totals = total[...]
    for tile in range(TILES):
        sent[tile, PART : PART + HEADS, :] = totals


def query_kernel(tokens, weight, query):
    query_rows = dot(tokens[...], weight[...], 1, 0).astype(BF16)
    for index in range(HEADS):
        query[index] = query_rows[:, index * HD : (index + 1) * HD]


def inverse_denominator(positive, total):
    return 1.0 / (jnp.sum(positive * total, axis=1, keepdims=True) + EPSILON)


def numerator_kernel(loss_scale, got, query, upstream, sent, numer, total, state):
    sums = got[0]
    for tile in range(1, TILES):
        sums = sums + got[tile]
    state_part = sums[:PART]
    totals = sums[PART : PART + HEADS]
    total[...] = totals
    for index in range(HEADS):
        part = slice(index * HD, (index + 1) * HD)
        positive = relu(query[index])
        inverse = inverse_denominator(positive.astype(F32), totals[index : index + 1])
        cotangent = upstream[:, part].astype(F32) * loss_scale
        numer_low = (cotangent * inverse).astype(BF16)
        numer[index] = numer_low
        state[index * HD : (index + 1) * HD, :] = dot(positive, numer_low, 0, 0)
    for tile in range(TILES):
        sent[tile, :PART, :] = state_part
    store_parts(sent, PART, state)


def total_grad_kernel(loss_scale, got, query, upstream, total, sent, grad_denom, state, totals):
    load_parts(state, got)
    for index in range(HEADS):
        part = slice(index * HD, (index + 1) * HD)
        positive = relu(query[index])
        wide = positive.astype(F32)
        inverse = inverse_denominator(wide, total[index : index + 1, :])
        cotangent = upstream[:, part].astype(F32) * loss_scale
        product = split_dot(positive, head(state, index), 1, 0)
        grad = -(jnp.sum(cotangent * product, axis=1, keepdims=True) * inverse) * inverse
        grad_denom[:, index : index + 1] = grad
        totals[index : index + 1, :] = jnp.sum(wide * grad, axis=0, keepdims=True)
    part_sum = got[0, PART:, :]
    for tile in range(1, TILES):
        part_sum = part_sum + got[tile, PART:, :]
    values = totals[...]
    for tile in range(TILES):
        sent[tile, :PART, :] = part_sum
        sent[tile, PART : PART + HEADS, :] = values


def place_columns(place, blocks, outs, at):
    for slot, out in enumerate(outs):
        out[:, at : at + COLS] = blocks[lax.rem(place[0] + slot, REPLICAS)]


def split_columns(flat, blocks):
    for block in range(REPLICAS):
        blocks[block] = flat[:, block * COLS : (block + 1) * COLS]


def query_grad_kernel(
    place, got, query, numer, total, grad_denom, grad, own, first, second, third, state, flat, blocks
):
    load_parts(state, got)
    for index in range(HEADS):
        part = slice(index * HD, (index + 1) * HD)
        values = split_dot(numer[index], head(state, index), 1, 1)
        values = values + grad_denom[:, index : index + 1] * total[index : index + 1, :]
        values = jnp.where(query[index].astype(F32) > 0, values, 0.0).astype(BF16)
        grad[:, part] = values
        flat[:, part] = values.astype(F32)
    split_columns(flat, blocks)
    place_columns(place, blocks, (own, first, second, third), 0)


def key_value_grad_kernel(
    place, got, key, value, grad_key, grad_value, own, first, second, third, state, flat_key, flat_value, blocks
):
    load_parts(state, got)
    totals = got[0, PART : PART + HEADS, :]
    for tile in range(1, TILES):
        totals = totals + got[tile, PART : PART + HEADS, :]
    for index in range(HEADS):
        part = slice(index * HD, (index + 1) * HD)
        key_head = key[index]
        positive = relu(key_head)
        state_head = head(state, index)
        values = split_dot(positive, state_head, 1, 0).astype(BF16)
        grad_value[:, part] = values
        flat_value[:, part] = values.astype(F32)
        values = split_dot(value[index], state_head, 1, 1) + totals[index : index + 1]
        values = jnp.where(key_head.astype(F32) > 0, values, 0.0).astype(BF16)
        grad_key[:, part] = values
        flat_key[:, part] = values.astype(F32)
    outs = (own, first, second, third)
    split_columns(flat_key, blocks)
    place_columns(place, blocks, outs, 0)
    split_columns(flat_value, blocks)
    place_columns(place, blocks, outs, COLS)


def turn_kernel(tokens, out):
    for start in range(0, D, 128):
        size = min(128, D - start)
        out[start : start + size, :] = tokens[:, start : start + size].astype(F32).T


def join_kernel(own, first, second, third, out):
    for slot, turned in enumerate((own, first, second, third)):
        out[:, slot * TOKENS : (slot + 1) * TOKENS] = turned[...].astype(BF16)


def weight_grad_kernel(normalizer, core, tokens, own, first, second, third, kept, sent, columns):
    for slot, block in enumerate((own, first, second, third)):
        columns[slot * TOKENS : (slot + 1) * TOKENS, :] = block[...].astype(BF16)
    right = columns[...]
    span = PLANE_SIZE // CORES
    for out, which in ((sent, 1 - core[0]), (kept, core[0])):
        for half in range(CORES):
            start = pl.multiple_of((half * CORES + which) * (span * ROWS), 16)
            product = dot(tokens[pl.ds(start, span * ROWS), :], right, 1, 0) * normalizer
            for index in range(span):
                out[half * span + index, :ROWS, :] = product[index * ROWS : (index + 1) * ROWS]


def exchange(blocks, axes):
    return lax.all_to_all(blocks, axes, 0, 0, tiled=True)


def shift(values, by):
    return lax.ppermute(values, "dp", [(i, (i + by) % REPLICAS) for i in range(REPLICAS)])


def back_project(gradient, weight):
    return dot(gradient, weight, 1, 1)


def body(latent, query_weight, key_weight, value_weight, upstream_grad):
    image_tokens = TOKENS * TILES
    loss_scale = 4.0 * math.sqrt(image_tokens)
    normalizer = 1.0 / math.sqrt(image_tokens * REPLICAS)
    tokens = latent.reshape(TOKENS, D)
    upstream = upstream_grad.reshape(TOKENS, HW)
    place = lax.axis_index("dp").reshape(1)
    core = lax.axis_index("core").reshape(1)
    heads = shaped((HEADS, TOKENS, HD), BF16)
    flat = shaped((TOKENS, HW), BF16)
    state = pltpu.VMEM((HW, HD), F32)
    totals = pltpu.VMEM((HEADS, HD), F32)
    weight = pltpu.VMEM((D, HW), BF16)
    wide = pltpu.VMEM((TOKENS, HW), F32)
    blocks = pltpu.VMEM((REPLICAS, TOKENS, COLS), F32)

    key, value, sent = call(
        key_value_kernel,
        "key_value",
        [heads, heads, shaped((TILES, PART + HEADS, HD))],
        [IN_VMEM, IN_HBM, IN_HBM],
        [weight, weight, state, totals, pltpu.SemaphoreType.DMA((2 * len(CHUNKS),))],
        vmem=20,
    )(tokens, key_weight, value_weight)
    sent, later_tokens = lax.optimization_barrier((sent, tokens))
    (turned,) = call(turn_kernel, "turn", [shaped((D, TOKENS))], [IN_VMEM])(later_tokens)
    turned = [turned] + [shift(turned, s) for s in (1, 2, 3)]
    got = exchange(sent, IMAGE)
    (query,) = call(
        query_kernel,
        "query",
        [heads],
        [IN_VMEM, IN_VMEM],
    )(tokens, query_weight)
    sent, numer, total = call(
        lambda *refs: numerator_kernel(loss_scale, *refs),
        "numerator",
        [shaped((TILES, 2 * PART, HD)), heads, shaped((HEADS, HD))],
        [IN_VMEM] * 3,
        [state],
    )(got, query, upstream)
    got_state = exchange(sent, IMAGE)
    sent, grad_denom = call(
        lambda *refs: total_grad_kernel(loss_scale, *refs),
        "total_grad",
        [shaped((TILES, PART + HEADS, HD)), shaped((TOKENS, HEADS))],
        [IN_VMEM] * 4,
        [state, totals],
    )(got_state, query, upstream, total)
    sent, turned[1], turned[3] = lax.optimization_barrier((sent, turned[1], turned[3]))
    got = exchange(sent, IMAGE)

    block = shaped((TOKENS, COLS))
    grad_query, *query_columns = call(
        query_grad_kernel,
        "query_grad",
        [flat, block, block, block, block],
        [IN_SMEM] + [IN_VMEM] * 5,
        [state, wide, blocks],
    )(place, got_state, query, numer, total, grad_denom)
    query_columns = [query_columns[0]] + [shift(query_columns[s], s) for s in (1, 2, 3)]
    (all_tokens,) = call(
        join_kernel, "join", [shaped((D, REPLICAS * TOKENS), BF16)], [IN_VMEM] * 4
    )(*turned)
    got, all_tokens, query_columns = lax.optimization_barrier((got, all_tokens, query_columns))

    block = shaped((TOKENS, 2 * COLS))
    grad_key, grad_value, *key_value_columns = call(
        key_value_grad_kernel,
        "key_value_grad",
        [flat, flat, block, block, block, block],
        [IN_SMEM] + [IN_VMEM] * 3,
        [state, wide, wide, blocks],
    )(place, got, key, value)
    key_value_columns = [key_value_columns[0]] + [
        shift(key_value_columns[s], s) for s in (1, 2, 3)
    ]

    def weight_grad(columns):
        width = columns[0].shape[1]
        half = shaped((PLANE_SIZE, PADDED_ROWS, width))
        kept, given = call(
            lambda *refs: weight_grad_kernel(normalizer, *refs),
            "weight_grad",
            [half, half],
            [IN_SMEM] + [IN_VMEM] * 5,
            [pltpu.VMEM((REPLICAS * TOKENS, width), BF16)],
            vmem=24,
        )(core, all_tokens, *columns)
        kept = kept + lax.ppermute(given, "core", [(0, 1), (1, 0)])
        return jnp.sum(exchange(kept, PLANE), axis=0)[:ROWS]

    query_out = weight_grad(query_columns)
    key_value_out = weight_grad(key_value_columns)

    summed = back_project(grad_query, query_weight) + back_project(grad_key, key_weight)
    summed = summed + back_project(grad_value, value_weight)
    latent_grad = summed.astype(BF16).reshape(latent.shape)
    return latent_grad, query_out, key_value_out[:, :COLS], key_value_out[:, COLS:]


def solution(mesh):
    devices = mesh.devices
    fine = Mesh(
        devices.reshape(REPLICAS, 2, CORES, 4, 2), ("dp", "zh", "core", "x", "zl")
    )
    grid = P("dp", ("zh", "core"), ("x", "zl"), None)
    weight_out = P(("zh", "core", "x", "zl"), "dp")
    return jax.shard_map(
        body,
        mesh=fine,
        in_specs=(grid, P(), P(), P(), grid),
        out_specs=(grid, weight_out, weight_out, weight_out),
        check_vma=False,
    )
```

time: 298 us -> 227 us (0.76)
  waiting for transfers between devices: 127 us -> 99.6 us
  matrix products: 36.9 us -> 10.7 us
  Pallas kernels: 0 us -> 24.5 us
  blocking collectives: 23 us -> 0 us
  other arithmetic: 23.5 us -> 7.6 us
  local copies, waits for them, and re-layouts: 34 us -> 23.2 us
  starting transfers between devices: 50.6 us -> 57.8 us
    all_to_all x9 -> x5, waiting for transfers between devices: 127 us -> 74.7 us  [exchange(): return lax.all_to_all(blocks, axes, 0, 0, tiled=True)]
    ppermute x3 -> x11, starting transfers between devices: 0.58 us -> 29.8 us  [the longest x9 29.2 us: shift(): lax.ppermute(values, 'dp', [(i, (i + by) % REPLICAS) for i in range(REPLI...]
    dot_general x17 -> x3, matrix products: 36.9 us -> 10.7 us  [dot(): lax.dot_general(left, right, (((left_dim,), (right_dim,)), ((), ())), pre...]
    ppermute x3 -> x11, waiting for transfers between devices: 0.01 us -> 24.9 us  [the longest x9 19 us: shift(): lax.ppermute(values, 'dp', [(i, (i + by) % REPLICAS) for i in range(REPLI...]
    pallas_call x0 -> x10, Pallas kernels: none -> 24.5 us  [the longest x1 7.97 us: body(): call(key_value_kernel, 'key_value', [heads, heads, shaped((TILES, PART +...]
    all_to_all x1 -> x0, blocking collectives: 23 us -> none  [exchange(): return lax.all_to_all(blocks, axes, 0, 0, tiled=True)]
    all_to_all x9 -> x5, starting transfers between devices: 50 us -> 28 us  [exchange(): return lax.all_to_all(blocks, axes, 0, 0, tiled=True)]
    unnamed x22 -> x60, local copies, waits for them, and re-layouts: 0.13 us -> 20.4 us
  transfers between devices with their start and end apart: 12 -> 16, of which waited for: 8 -> 11; matrix products, arithmetic and copies ran while one was open for 25% -> 9% of each run, Pallas kernels for 0% -> 4%
where the time goes in v2:
time: 227 us; the launch traced here: 224 us
  waiting for transfers between devices  99.6 us (44%)
  starting transfers between devices  57.8 us (25%)
  Pallas kernels  24.5 us (11%)
  local copies, waits for them, and re-layouts  23.2 us (10%)
  matrix products  10.7 us (5%)
  other arithmetic  7.6 us (3%)
    all_to_all x5, waiting for transfers between devices, exchange(): return lax.all_to_all(blocks, axes, 0, 0, tiled=True)  74.7 us
    ppermute x9, starting transfers between devices, shift(): lax.ppermute(values, 'dp', [(i, (i + by) % REPLICAS) for i in range(REPLI...  29.2 us
    all_to_all x5, starting transfers between devices, exchange(): return lax.all_to_all(blocks, axes, 0, 0, tiled=True)  28 us
    unnamed x60, local copies, waits for them, and re-layouts  20.4 us
    ppermute x9, waiting for transfers between devices, shift(): lax.ppermute(values, 'dp', [(i, (i + by) % REPLICAS) for i in range(REPLI...  19 us
    dot_general x3, matrix products, dot(): lax.dot_general(left, right, (((left_dim,), (right_dim,)), ((), ())), pre...  10.7 us
    pallas_call x1, Pallas kernels, body(): call(key_value_kernel, 'key_value', [heads, heads, shaped((TILES, PART +...  7.97 us
    ppermute x2, waiting for transfers between devices, weight_grad(): kept = kept + lax.ppermute(given, 'core', [(0, 1), (1, 0)])  5.92 us
  transfers between devices with their start and end apart: 16, of which 11 were waited for; matrix products, arithmetic and copies ran while one was open for 9% of the time, Pallas kernels for 4%

profile of v2, /device:TPU:8, one launch (start us, length us, event | category | flops | bytes accessed | tf_op | source)
XLA Modules:
  0.0 224.3 jit_solution(2317395954603055242)
XLA Ops:
  0.6 2.5 %copy-done.1 = bf16[2240,1120]{1,0:T(8,128)(2,1)S(1)} copy-done((bf16[2240,1120]{1,0:T(8,128)(2,1)S(1)}, bf16[2240,1120]{1,0:T(8,128)(2,1)}, u32[]{:S(2)}) %copy-start.1) | copy-done | bytes 5017624
  3.1 2.5 %copy-done.2 = bf16[2240,1120]{1,0:T(8,128)(2,1)S(1)} copy-done((bf16[2240,1120]{1,0:T(8,128)(2,1)S(1)}, bf16[2240,1120]{1,0:T(8,128)(2,1)}, u32[]{:S(2)}) %copy-start.2) | copy-done | bytes 5017624
  6.6 8.0 %key_value.1 = (bf16[10,128,112]{2,1,0:T(8,128)(2,1)S(1)}, bf16[10,128,112]{2,1,0:T(8,128)(2,1)S(1)}, f32[32,45,112]{2,1,0:T(8,128)}) custom-call(bf16[128,2240]{1,0:T(8,128)(2,1)S(1)} %bitcast.14, bf16[2240,1120]{1,0:T(8,128)(2,1)S(1)} %copy-done.2, bf16[2240,1120]{1,0:T(8,128)(2,1)S(1)} %copy-done.1), custom_call_target="tpu_custom_call" | custom-call | tf_op jit(solution)/shard_map/key_value/pallas_call | solution.py:283
  16.1 8.3 %all-to-all-start = ((f32[32,45,112]{2,1,0:T(8,128)}), f32[32,45,112]{2,1,0:T(8,128)S(1)}, u32[]{:S(2)}, u32[]{:S(2)}) async-start(f32[32,45,112]{2,1,0:T(8,128)} %get-tuple-element.39), calls=%async_computation | async-start | bytes 1572864 | tf_op jit(solution)/shard_map/all_to_all | solution.py:256
  26.7 2.5 %copy-done = bf16[2240,1120]{1,0:T(8,128)(2,1)S(1)} copy-done((bf16[2240,1120]{1,0:T(8,128)(2,1)S(1)}, bf16[2240,1120]{1,0:T(8,128)(2,1)}, u32[]{:S(2)}) %copy-start) | copy-done | bytes 5017624
  30.2 8.7 %all-to-all-done.refs_0_ = f32[32,45,112]{2,1,0:T(8,128)S(1)} async-done(((f32[32,45,112]{2,1,0:T(8,128)}), f32[32,45,112]{2,1,0:T(8,128)S(1)}, u32[]{:S(2)}, u32[]{:S(2)}) %all-to-all-start) | async-done | bytes 645152 | tf_op jit(solution)/shard_map/all_to_all | solution.py:256
  41.3 4.2 %all-to-all-start.1 = ((f32[32,70,112]{2,1,0:T(8,128)}), f32[32,70,112]{2,1,0:T(8,128)S(1)}, u32[]{:S(2)}, u32[]{:S(2)}) async-start(f32[32,70,112]{2,1,0:T(8,128)} %copy-done.7), calls=%async_computation.1 | async-start | bytes 2359296 | tf_op jit(solution)/shard_map/all_to_all | solution.py:256
  45.5 2.4 %collective-permute-start.2 = (f32[2240,128]{1,0:T(8,128)S(1)}, f32[2240,128]{1,0:T(8,128)}, u32[]{:S(2)}, u32[]{:S(2)}) collective-permute-start(f32[2240,128]{1,0:T(8,128)S(1)} %turn.1.own), channel_id=1, source_target_pairs={{0,64},{32,96},{64,0},{96,32},{1,65},{33,97},{65,1},{97,33},{2,66}... | collective-permute-start | bytes 3440648 | tf_op jit(solution)/shard_map/ppermute | solution.py:260
  47.9 16.4 %all-to-all-done.1.refs_0_.got = f32[32,70,112]{2,1,0:T(8,128)S(1)} async-done(((f32[32,70,112]{2,1,0:T(8,128)}), f32[32,70,112]{2,1,0:T(8,128)S(1)}, u32[]{:S(2)}, u32[]{:S(2)}) %all-to-all-start.1) | async-done | bytes 1003552 | tf_op jit(solution)/shard_map/all_to_all | solution.py:256
  64.3 1.7 total_grad.1
  66.9 4.6 %all-to-all-start.2 = ((f32[32,45,112]{2,1,0:T(8,128)}), f32[32,45,112]{2,1,0:T(8,128)}, u32[]{:S(2)}, u32[]{:S(2)}) async-start(f32[32,45,112]{2,1,0:T(8,128)} %copy-done.9), calls=%async_computation.2 | async-start | bytes 1572864 | tf_op jit(solution)/shard_map/all_to_all | solution.py:256
  75.4 17.6 %collective-permute-start.4 = (f32[128,280]{1,0:T(8,128)S(1)}, f32[128,280]{1,0:T(8,128)S(1)}, u32[]{:S(2)}, u32[]{:S(2)}) collective-permute-start(f32[128,280]{1,0:T(8,128)S(1)} %get-tuple-element.52), channel_id=1, source_target_pairs={{0,64},{32,96},{64,0},{96,32},{1,65},{33,97},{65,1},{97,33},{2,66}... | collective-permute-start | bytes 430088 | tf_op jit(solution)/shard_map/ppermute | solution.py:260
  93.0 2.3 %join.1.refs_1_ = bf16[2240,512]{1,0:T(8,128)(2,1)S(1)} custom-call(f32[2240,128]{1,0:T(8,128)S(1)} %turn.1.own, f32[2240,128]{1,0:T(8,128)} %collective-permute-done.first, f32[2240,128]{1,0:T(8,128)} %collective-permute-done.2.second, f32[2240,128]{1,0:T(8,128)} %collective-permute-done.1.third), custom_call_target="tpu_custom_call" | custom-call | tf_op jit(solution)/shard_map/join/pallas_call | solution.py:328
  99.4 2.8 %collective-permute-done.5.refs_5_ = f32[128,280]{1,0:T(8,128)S(1)} collective-permute-done((f32[128,280]{1,0:T(8,128)S(1)}, f32[128,280]{1,0:T(8,128)S(1)}, u32[]{:S(2)}, u32[]{:S(2)}) %collective-permute-start.5) | collective-permute-done | bytes 143392 | tf_op jit(solution)/shard_map/ppermute | solution.py:260
  104.8 3.5 %key_value_grad.1 = (bf16[128,1120]{1,0:T(8,128)(2,1)S(1)}, bf16[128,1120]{1,0:T(8,128)(2,1)S(1)}, f32[128,560]{1,0:T(8,128)S(1)}, f32[128,560]{1,0:T(8,128)}, f32[128,560]{1,0:T(8,128)}, /*index=5*/f32[128,560]{1,0:T(8,128)}) custom-call(s32[1]{0:T(128)} %bitcast.place, f32[32,45,112]{2,1,0:T(8,128)} %all-to-all-done.2.got, ...), custom_call_target="tpu_custom_call" | custom-call | tf_op jit(solution)/shard_map/key_value_grad/pallas_call | solution.py:334
  110.4 4.0 %collective-permute-start.8 = (f32[128,560]{1,0:T(8,128)}, f32[128,560]{1,0:T(8,128)S(1)}, u32[]{:S(2)}, u32[]{:S(2)}) collective-permute-start(f32[128,560]{1,0:T(8,128)} %get-tuple-element.68), channel_id=1, source_target_pairs={{0,64},{32,96},{64,0},{96,32},{1,65},{33,97},{65,1},{97,33},{2,66}... | collective-permute-start | bytes 860168 | tf_op jit(solution)/shard_map/ppermute | solution.py:260
  115.3 5.7 %collective-permute-done.7.refs_3_ = f32[128,560]{1,0:T(8,128)S(1)} collective-permute-done((f32[128,560]{1,0:T(8,128)}, f32[128,560]{1,0:T(8,128)S(1)}, u32[]{:S(2)}, u32[]{:S(2)}) %collective-permute-start.7) | collective-permute-done | bytes 286752 | tf_op jit(solution)/shard_map/ppermute | solution.py:260
  121.1 2.2 collective-permute-done.8.refs_4_
  123.2 5.6 %collective-permute-done.9.refs_5_ = f32[128,560]{1,0:T(8,128)} collective-permute-done((f32[128,560]{1,0:T(8,128)}, f32[128,560]{1,0:T(8,128)}, u32[]{:S(2)}, u32[]{:S(2)}) %collective-permute-start.9) | collective-permute-done | bytes 286752 | tf_op jit(solution)/shard_map/ppermute | solution.py:260
  128.8 4.2 %weight_grad.3 = (f32[16,72,560]{2,1,0:T(8,128)S(1)}, f32[16,72,560]{2,1,0:T(8,128)}) custom-call(s32[1]{0:T(128)} %bitcast.4.refs_0_, bf16[2240,512]{1,0:T(8,128)(2,1)S(1)} %join.1.refs_1_, f32[128,560]{1,0:T(8,128)S(1)} %get-tuple-element.66.refs_2_, f32[128,560]{1,0:T(8,128)S(1)} %collective-permute-done.7.refs_3_, ...), custom_call_target="tpu_custom_call" | custom-call | tf_op jit(solution)/shard_map/weight_grad/pallas_call | solution.py:348
  133.0 1.6 copy-done.5
  136.6 5.9 %collective-permute-done.6 = f32[16,72,280]{2,1,0:T(8,128)S(1)} collective-permute-done((f32[16,72,280]{2,1,0:T(8,128)S(1)}, f32[16,72,280]{2,1,0:T(8,128)S(1)}, u32[]{:S(2)}, u32[]{:S(2)}) %collective-permute-start.6) | collective-permute-done | bytes 1290272 | tf_op jit(solution)/shard_map/ppermute | solution.py:356
  144.0 7.2 %all-to-all-start.3 = ((f32[16,72,280]{2,1,0:T(8,128)}), f32[16,72,280]{2,1,0:T(8,128)}, u32[]{:S(2)}, u32[]{:S(2)}) async-start(f32[16,72,280]{2,1,0:T(8,128)} %add.14), calls=%async_computation.3 | async-start | bytes 3538944 | tf_op jit(solution)/shard_map/all_to_all | solution.py:256
  151.2 3.7 %add.15 = f32[16,72,560]{2,1,0:T(8,128)} add(f32[16,72,560]{2,1,0:T(8,128)S(1)} %copy-done.6, f32[16,72,560]{2,1,0:T(8,128)} %collective-permute-done.10) | non-fusion elementwise | flops 645120 | bytes 7741440 | tf_op jit(solution)/shard_map/add | solution.py:356
  154.9 23.8 %all-to-all-done.3 = f32[16,72,280]{2,1,0:T(8,128)} async-done(((f32[16,72,280]{2,1,0:T(8,128)}), f32[16,72,280]{2,1,0:T(8,128)}, u32[]{:S(2)}, u32[]{:S(2)}) %all-to-all-start.3) | async-done | bytes 1290272 | tf_op jit(solution)/shard_map/all_to_all | solution.py:256
  178.8 3.7 %all-to-all-start.4 = ((f32[16,72,560]{2,1,0:T(8,128)}), f32[16,72,560]{2,1,0:T(8,128)S(1)}, u32[]{:S(2)}, u32[]{:S(2)}) async-start(f32[16,72,560]{2,1,0:T(8,128)} %add.15), calls=%async_computation.4 | async-start | bytes 5898240 | tf_op jit(solution)/shard_map/all_to_all | solution.py:256
  182.6 4.2 %fusion.2 = f32[128,2240]{0,1:T(8,128)S(1)} fusion(bf16[128,1120]{1,0:T(8,128)(2,1)S(1)} %copy-done.11, bf16[2240,1120]{1,0:T(8,128)(2,1)} %weight.1), kind=kOutput, calls=%fused_computation.4 | convolution fusion | flops 642252800 | bytes 6451200 | tf_op jit(solution)/shard_map/dot_general | solution.py:53
  186.8 4.1 %convolution_add_fusion.1 = f32[128,2240]{0,1:T(8,128)S(1)} fusion(f32[128,2240]{0,1:T(8,128)S(1)} %fusion.2, bf16[128,1120]{1,0:T(8,128)(2,1)S(1)} %copy-done.15, bf16[2240,1120]{1,0:T(8,128)(2,1)} %key_weight.1), kind=kOutput, calls=%fused_computation.1 | convolution fusion | flops 642539520 | bytes 7598080 | tf_op jit(solution)/shard_map/dot_general | solution.py:53
  190.9 2.4 %fusion = bf16[128,2240]{0,1:T(8,128)(2,1)} fusion(f32[128,2240]{0,1:T(8,128)S(1)} %convolution_add_fusion.1, bf16[128,1120]{1,0:T(8,128)(2,1)S(1)} %copy-done.13, bf16[2240,1120]{1,0:T(8,128)(2,1)S(1)} %bitcast.13), kind=kOutput, calls=%fused_computation.2 | convolution fusion | flops 642826240 | bytes 7024640 | tf_op jit(solution)/shard_map/dot_general | solution.py:53
  193.3 2.1 copy.10
  195.4 2.2 reduce_sum.18
  197.6 25.7 %all-to-all-done.4 = f32[16,72,560]{2,1,0:T(8,128)S(1)} async-done(((f32[16,72,560]{2,1,0:T(8,128)}), f32[16,72,560]{2,1,0:T(8,128)S(1)}, u32[]{:S(2)}, u32[]{:S(2)}) %all-to-all-start.4) | async-done | bytes 2580512 | tf_op jit(solution)/shard_map/all_to_all | solution.py:256
  (80 shorter events, 27.2 us)
Async XLA Ops:
  0.6 2.5 %copy-start.1 = (bf16[2240,1120]{1,0:T(8,128)(2,1)S(1)}, bf16[2240,1120]{1,0:T(8,128)(2,1)}, u32[]{:S(2)}) copy-start(bf16[2240,1120]{1,0:T(8,128)(2,1)} %value_weight.1) | copy-start | bytes 15052804
  3.1 2.5 %copy-start.2 = (bf16[2240,1120]{1,0:T(8,128)(2,1)S(1)}, bf16[2240,1120]{1,0:T(8,128)(2,1)}, u32[]{:S(2)}) copy-start(bf16[2240,1120]{1,0:T(8,128)(2,1)} %key_weight.1) | copy-start | bytes 15052804
  16.1 8.3 %copy-start.4 = (bf16[1,16,8,2240]{3,2,1,0:T(8,128)(2,1)S(1)}, bf16[1,16,8,2240]{3,2,1,0:T(8,128)(2,1)}, u32[]{:S(2)}) copy-start(bf16[1,16,8,2240]{3,2,1,0:T(8,128)(2,1)} %param.5) | copy-start | bytes 1720324
  16.1 22.8 %all-to-all-start = ((f32[32,45,112]{2,1,0:T(8,128)}), f32[32,45,112]{2,1,0:T(8,128)S(1)}, u32[]{:S(2)}, u32[]{:S(2)}) async-start(f32[32,45,112]{2,1,0:T(8,128)} %get-tuple-element.39), calls=%async_computation | async-start | bytes 1572864 | tf_op jit(solution)/shard_map/all_to_all | solution.py:256
  24.4 14.5 %copy-start.8 = (bf16[1,16,8,1120]{3,2,1,0:T(8,128)(2,1)S(1)}, bf16[1,16,8,1120]{3,2,1,0:T(8,128)(2,1)}, u32[]{:S(2)}) copy-start(bf16[1,16,8,1120]{3,2,1,0:T(8,128)(2,1)} %param.9) | copy-start | bytes 860164
  24.6 42.3 %collective-permute-start.1 = (f32[2240,128]{1,0:T(8,128)S(1)}, f32[2240,128]{1,0:T(8,128)}, u32[]{:S(2)}, u32[]{:S(2)}) collective-permute-start(f32[2240,128]{1,0:T(8,128)S(1)} %turn.1.own), channel_id=1, source_target_pairs={{0,96},{32,0},{64,32},{96,64},{1,97},{33,1},{65,33},{97,65},{2,98}... | collective-permute-start | bytes 3440648 | tf_op jit(solution)/shard_map/ppermute | solution.py:260
  25.2 41.7 %collective-permute-start = (f32[2240,128]{1,0:T(8,128)S(1)}, f32[2240,128]{1,0:T(8,128)}, u32[]{:S(2)}, u32[]{:S(2)}) collective-permute-start(f32[2240,128]{1,0:T(8,128)S(1)} %turn.1.own), channel_id=1, source_target_pairs={{0,32},{32,64},{64,96},{96,0},{1,33},{33,65},{65,97},{97,1},{2,34}... | collective-permute-start | bytes 3440648 | tf_op jit(solution)/shard_map/ppermute | solution.py:260
  26.7 2.5 %copy-start = (bf16[2240,1120]{1,0:T(8,128)(2,1)S(1)}, bf16[2240,1120]{1,0:T(8,128)(2,1)}, u32[]{:S(2)}) copy-start(bf16[2240,1120]{1,0:T(8,128)(2,1)} %weight.1) | copy-start | bytes 15052804
  41.3 23.0 %all-to-all-start.1 = ((f32[32,70,112]{2,1,0:T(8,128)}), f32[32,70,112]{2,1,0:T(8,128)S(1)}, u32[]{:S(2)}, u32[]{:S(2)}) async-start(f32[32,70,112]{2,1,0:T(8,128)} %copy-done.7), calls=%async_computation.1 | async-start | bytes 2359296 | tf_op jit(solution)/shard_map/all_to_all | solution.py:256
  45.5 47.5 %collective-permute-start.2 = (f32[2240,128]{1,0:T(8,128)S(1)}, f32[2240,128]{1,0:T(8,128)}, u32[]{:S(2)}, u32[]{:S(2)}) collective-permute-start(f32[2240,128]{1,0:T(8,128)S(1)} %turn.1.own), channel_id=1, source_target_pairs={{0,64},{32,96},{64,0},{96,32},{1,65},{33,97},{65,1},{97,33},{2,66}... | collective-permute-start | bytes 3440648 | tf_op jit(solution)/shard_map/ppermute | solution.py:260
  66.9 36.0 %all-to-all-start.2 = ((f32[32,45,112]{2,1,0:T(8,128)}), f32[32,45,112]{2,1,0:T(8,128)}, u32[]{:S(2)}, u32[]{:S(2)}) async-start(f32[32,45,112]{2,1,0:T(8,128)} %copy-done.9), calls=%async_computation.2 | async-start | bytes 1572864 | tf_op jit(solution)/shard_map/all_to_all | solution.py:256
  73.8 22.8 %collective-permute-start.3 = (f32[128,280]{1,0:T(8,128)S(1)}, f32[128,280]{1,0:T(8,128)S(1)}, u32[]{:S(2)}, u32[]{:S(2)}) collective-permute-start(f32[128,280]{1,0:T(8,128)S(1)} %get-tuple-element.51), channel_id=1, source_target_pairs={{0,32},{32,64},{64,96},{96,0},{1,33},{33,65},{65,97},{97,1},{2,34}... | collective-permute-start | bytes 430088 | tf_op jit(solution)/shard_map/ppermute | solution.py:260
  75.4 23.3 %collective-permute-start.4 = (f32[128,280]{1,0:T(8,128)S(1)}, f32[128,280]{1,0:T(8,128)S(1)}, u32[]{:S(2)}, u32[]{:S(2)}) collective-permute-start(f32[128,280]{1,0:T(8,128)S(1)} %get-tuple-element.52), channel_id=1, source_target_pairs={{0,64},{32,96},{64,0},{96,32},{1,65},{33,97},{65,1},{97,33},{2,66}... | collective-permute-start | bytes 430088 | tf_op jit(solution)/shard_map/ppermute | solution.py:260
  93.0 9.2 %collective-permute-start.5 = (f32[128,280]{1,0:T(8,128)S(1)}, f32[128,280]{1,0:T(8,128)S(1)}, u32[]{:S(2)}, u32[]{:S(2)}) collective-permute-start(f32[128,280]{1,0:T(8,128)S(1)} %get-tuple-element.53), channel_id=1, source_target_pairs={{0,96},{32,0},{64,32},{96,64},{1,97},{33,1},{65,33},{97,65},{2,98}... | collective-permute-start | bytes 430088 | tf_op jit(solution)/shard_map/ppermute | solution.py:260
  109.8 11.3 %collective-permute-start.7 = (f32[128,560]{1,0:T(8,128)}, f32[128,560]{1,0:T(8,128)S(1)}, u32[]{:S(2)}, u32[]{:S(2)}) collective-permute-start(f32[128,560]{1,0:T(8,128)} %get-tuple-element.67), channel_id=1, source_target_pairs={{0,32},{32,64},{64,96},{96,0},{1,33},{33,65},{65,97},{97,1},{2,34}... | collective-permute-start | bytes 860168 | tf_op jit(solution)/shard_map/ppermute | solution.py:260
  110.4 12.9 %collective-permute-start.8 = (f32[128,560]{1,0:T(8,128)}, f32[128,560]{1,0:T(8,128)S(1)}, u32[]{:S(2)}, u32[]{:S(2)}) collective-permute-start(f32[128,560]{1,0:T(8,128)} %get-tuple-element.68), channel_id=1, source_target_pairs={{0,64},{32,96},{64,0},{96,32},{1,65},{33,97},{65,1},{97,33},{2,66}... | collective-permute-start | bytes 860168 | tf_op jit(solution)/shard_map/ppermute | solution.py:260
  114.3 14.4 %collective-permute-start.9 = (f32[128,560]{1,0:T(8,128)}, f32[128,560]{1,0:T(8,128)}, u32[]{:S(2)}, u32[]{:S(2)}) collective-permute-start(f32[128,560]{1,0:T(8,128)} %get-tuple-element.69), channel_id=1, source_target_pairs={{0,96},{32,0},{64,32},{96,64},{1,97},{33,1},{65,33},{97,65},{2,98}... | collective-permute-start | bytes 860168 | tf_op jit(solution)/shard_map/ppermute | solution.py:260
  128.8 5.9 %copy-start.21 = (f32[128,280]{1,0:T(8,128)S(1)}, f32[128,280]{1,0:T(8,128)}, u32[]{:S(2)}) copy-start(f32[128,280]{1,0:T(8,128)} %copy-done.20) | copy-start | bytes 430084
  128.8 5.9 %copy-start.23 = (f32[128,280]{1,0:T(8,128)S(1)}, f32[128,280]{1,0:T(8,128)}, u32[]{:S(2)}) copy-start(f32[128,280]{1,0:T(8,128)} %copy-done.22) | copy-start | bytes 430084
  128.8 5.9 %copy-start.25 = (f32[128,280]{1,0:T(8,128)S(1)}, f32[128,280]{1,0:T(8,128)}, u32[]{:S(2)}) copy-start(f32[128,280]{1,0:T(8,128)} %copy-done.24) | copy-start | bytes 430084
  128.8 5.9 %copy-start.27 = (f32[128,280]{1,0:T(8,128)S(1)}, f32[128,280]{1,0:T(8,128)}, u32[]{:S(2)}) copy-start(f32[128,280]{1,0:T(8,128)} %copy-done.26) | copy-start | bytes 430084
  133.0 1.7 copy-start.5
  134.6 16.6 %collective-permute-start.10 = (f32[16,72,560]{2,1,0:T(8,128)}, f32[16,72,560]{2,1,0:T(8,128)}, u32[]{:S(2)}, u32[]{:S(2)}) collective-permute-start(f32[16,72,560]{2,1,0:T(8,128)} %get-tuple-element.71), channel_id=1, source_target_pairs={{0,8},{8,0},{1,9},{9,1},{2,10},{10,2},{3,11},{11,3},{4,12},{12,4},... | collective-permute-start | bytes 7741448 | tf_op jit(solution)/shard_map/ppermute | solution.py:356
  136.0 6.5 %collective-permute-start.6 = (f32[16,72,280]{2,1,0:T(8,128)S(1)}, f32[16,72,280]{2,1,0:T(8,128)S(1)}, u32[]{:S(2)}, u32[]{:S(2)}) collective-permute-start(f32[16,72,280]{2,1,0:T(8,128)S(1)} %get-tuple-element.65), channel_id=1, source_target_pairs={{0,8},{8,0},{1,9},{9,1},{2,10},{10,2},{3,11},{11,3},{4,12},{12,4},... | collective-permute-start | bytes 3870728 | tf_op jit(solution)/shard_map/ppermute | solution.py:356
  144.0 7.2 %copy-start.6 = (f32[16,72,560]{2,1,0:T(8,128)S(1)}, f32[16,72,560]{2,1,0:T(8,128)}, u32[]{:S(2)}) copy-start(f32[16,72,560]{2,1,0:T(8,128)} %copy-done.5) | copy-start | bytes 7741444
  144.0 34.7 %all-to-all-start.3 = ((f32[16,72,280]{2,1,0:T(8,128)}), f32[16,72,280]{2,1,0:T(8,128)}, u32[]{:S(2)}, u32[]{:S(2)}) async-start(f32[16,72,280]{2,1,0:T(8,128)} %add.14), calls=%async_computation.3 | async-start | bytes 3538944 | tf_op jit(solution)/shard_map/all_to_all | solution.py:256
  154.9 27.6 %copy-start.11 = (bf16[128,1120]{1,0:T(8,128)(2,1)S(1)}, bf16[128,1120]{1,0:T(8,128)(2,1)}, u32[]{:S(2)}) copy-start(bf16[128,1120]{1,0:T(8,128)(2,1)} %copy-done.10) | copy-start | bytes 860164
  178.8 44.6 %all-to-all-start.4 = ((f32[16,72,560]{2,1,0:T(8,128)}), f32[16,72,560]{2,1,0:T(8,128)S(1)}, u32[]{:S(2)}, u32[]{:S(2)}) async-start(f32[16,72,560]{2,1,0:T(8,128)} %add.15), calls=%async_computation.4 | async-start | bytes 5898240 | tf_op jit(solution)/shard_map/all_to_all | solution.py:256
  182.5 4.2 %copy-start.15 = (bf16[128,1120]{1,0:T(8,128)(2,1)S(1)}, bf16[128,1120]{1,0:T(8,128)(2,1)}, u32[]{:S(2)}) copy-start(bf16[128,1120]{1,0:T(8,128)(2,1)} %copy-done.14) | copy-start | bytes 860164
  182.5 8.3 %slice-start = ((s8[5160960]{0:T(1024)(128)(4,1)}), s8[4194304]{0:T(1024)(128)(4,1)S(1)}, s32[]{:S(2)}) async-start(s8[5160960]{0:T(1024)(128)(4,1)} %bitcast.12), calls=%async_computation.5 | async-start | bytes 8388608
  186.7 4.1 %slice-start.1 = ((s8[5160960]{0:T(1024)(128)(4,1)}), s8[966656]{0:T(1024)(128)(4,1)S(1)}, s32[]{:S(2)}) async-start(s8[5160960]{0:T(1024)(128)(4,1)} %bitcast.12), calls=%async_computation.6 | async-start | bytes 1933312
  186.8 4.1 %copy-start.13 = (bf16[128,1120]{1,0:T(8,128)(2,1)S(1)}, bf16[128,1120]{1,0:T(8,128)(2,1)}, u32[]{:S(2)}) copy-start(bf16[128,1120]{1,0:T(8,128)(2,1)} %copy-done.12) | copy-start | bytes 860164
  (14 other events, 11.3 us)

commit v3 on v2

--- a/solution.py
+++ b/solution.py
@@ -17,7 +17,9 @@
 CORES = 2
 ROWS = D // TILES
 PADDED_ROWS = 72
+SPLIT = 40
 REPLICAS = 4
+RING = 4
 COLS = HW // REPLICAS
 TOKENS = 128
 
@@ -252,12 +254,53 @@
                 out[half * span + index, :ROWS, :] = product[index * ROWS : (index + 1) * ROWS]
 
 
+def first_stage_kernel(spot, kept, got, *outs):
+    for slot in range(RING):
+        across = lax.rem(spot[0] + slot, RING)
+        along = lax.rem(spot[1] + slot, RING)
+        for other in range(RING):
+            at = (other // 2) * (2 * RING) + across * 2 + other % 2
+            outs[slot][other] = kept[at, :SPLIT, :] + got[at, :SPLIT, :]
+            at = (along // 2) * (2 * RING) + other * 2 + lax.rem(along, 2)
+            outs[RING + slot][other] = kept[at, SPLIT:, :] + got[at, SPLIT:, :]
+
+
+def second_stage_kernel(spot, *refs):
+    uppers, lowers, outs = refs[:RING], refs[RING : 2 * RING], refs[2 * RING :]
+    for slot in range(RING):
+        along = lax.rem(spot[1] + slot, RING)
+        outs[slot][...] = sum_at(uppers, along)
+        across = lax.rem(spot[0] + slot, RING)
+        outs[RING + slot][...] = sum_at(lowers, across)
+
+
+def sum_at(refs, at):
+    return (refs[0][at] + refs[1][at]) + (refs[2][at] + refs[3][at])
+
+
+def last_kernel(query, *refs):
+    uppers, lowers = refs[:RING], refs[RING : 2 * RING]
+    query_out, key_out, value_out = refs[2 * RING :]
+    total = query[0]
+    for index in range(1, PLANE_SIZE):
+        total = total + query[index]
+    query_out[...] = total[:ROWS]
+    for refs, rows, size in ((uppers, 0, SPLIT), (lowers, SPLIT, ROWS - SPLIT)):
+        total = (refs[0][...] + refs[1][...]) + (refs[2][...] + refs[3][...])
+        key_out[rows : rows + size, :] = total[:size, :COLS]
+        value_out[rows : rows + size, :] = total[:size, COLS:]
+
+
 def exchange(blocks, axes):
     return lax.all_to_all(blocks, axes, 0, 0, tiled=True)
 
 
-def shift(values, by):
-    return lax.ppermute(values, "dp", [(i, (i + by) % REPLICAS) for i in range(REPLICAS)])
+def shift(values, by, axis):
+    return lax.ppermute(values, axis, [(i, (i + by) % RING) for i in range(RING)])
+
+
+def shifted(slots, axis):
+    return [slots[0]] + [shift(slots[s], s, axis) for s in range(1, RING)]
 
 
 def back_project(gradient, weight):
@@ -272,6 +315,7 @@
     upstream = upstream_grad.reshape(TOKENS, HW)
     place = lax.axis_index("dp").reshape(1)
     core = lax.axis_index("core").reshape(1)
+    spot = jnp.stack([lax.axis_index("x"), lax.axis_index(("zh", "zl"))])
     heads = shaped((HEADS, TOKENS, HD), BF16)
     flat = shaped((TOKENS, HW), BF16)
     state = pltpu.VMEM((HW, HD), F32)
@@ -280,6 +324,9 @@
     wide = pltpu.VMEM((TOKENS, HW), F32)
     blocks = pltpu.VMEM((REPLICAS, TOKENS, COLS), F32)
 
+    (turned,) = call(turn_kernel, "turn", [shaped((D, TOKENS))], [IN_VMEM])(tokens)
+    turned = [turned] + [shift(turned, s, "dp") for s in (1, 3, 2)]
+
     key, value, sent = call(
         key_value_kernel,
         "key_value",
@@ -287,10 +334,11 @@
         [IN_VMEM, IN_HBM, IN_HBM],
         [weight, weight, state, totals, pltpu.SemaphoreType.DMA((2 * len(CHUNKS),))],
         vmem=20,
-    )(tokens, key_weight, value_weight)
-    sent, later_tokens = lax.optimization_barrier((sent, tokens))
-    (turned,) = call(turn_kernel, "turn", [shaped((D, TOKENS))], [IN_VMEM])(later_tokens)
-    turned = [turned] + [shift(turned, s) for s in (1, 2, 3)]
+    )(
+        tokens,
+        pltpu.with_memory_space_constraint(key_weight, pltpu.HBM),
+        pltpu.with_memory_space_constraint(value_weight, pltpu.HBM),
+    )
     got = exchange(sent, IMAGE)
     (query,) = call(
         query_kernel,
@@ -313,7 +361,7 @@
         [IN_VMEM] * 4,
         [state, totals],
     )(got_state, query, upstream, total)
-    sent, turned[1], turned[3] = lax.optimization_barrier((sent, turned[1], turned[3]))
+    sent, turned[1], turned[2] = lax.optimization_barrier((sent, turned[1], turned[2]))
     got = exchange(sent, IMAGE)
 
     block = shaped((TOKENS, COLS))
@@ -324,10 +372,10 @@
         [IN_SMEM] + [IN_VMEM] * 5,
         [state, wide, blocks],
     )(place, got_state, query, numer, total, grad_denom)
-    query_columns = [query_columns[0]] + [shift(query_columns[s], s) for s in (1, 2, 3)]
+    query_columns = shifted(query_columns, "dp")
     (all_tokens,) = call(
         join_kernel, "join", [shaped((D, REPLICAS * TOKENS), BF16)], [IN_VMEM] * 4
-    )(*turned)
+    )(turned[0], turned[1], turned[3], turned[2])
     got, all_tokens, query_columns = lax.optimization_barrier((got, all_tokens, query_columns))
 
     block = shaped((TOKENS, 2 * COLS))
@@ -338,11 +386,9 @@
         [IN_SMEM] + [IN_VMEM] * 3,
         [state, wide, wide, blocks],
     )(place, got, key, value)
-    key_value_columns = [key_value_columns[0]] + [
-        shift(key_value_columns[s], s) for s in (1, 2, 3)
-    ]
-
-    def weight_grad(columns):
+    key_value_columns = shifted(key_value_columns, "dp")
+
+    def partial_sum(columns):
         width = columns[0].shape[1]
         half = shaped((PLANE_SIZE, PADDED_ROWS, width))
         kept, given = call(
@@ -353,16 +399,42 @@
             [pltpu.VMEM((REPLICAS * TOKENS, width), BF16)],
             vmem=24,
         )(core, all_tokens, *columns)
-        kept = kept + lax.ppermute(given, "core", [(0, 1), (1, 0)])
-        return jnp.sum(exchange(kept, PLANE), axis=0)[:ROWS]
-
-    query_out = weight_grad(query_columns)
-    key_value_out = weight_grad(key_value_columns)
+        return kept, lax.ppermute(given, "core", [(0, 1), (1, 0)])
+
+    kept, got = partial_sum(query_columns)
+    query_part, key_value_columns = lax.optimization_barrier((kept + got, key_value_columns))
+    query_out = exchange(query_part, PLANE)
+
+    kept, got = partial_sum(key_value_columns)
+    upper = shaped((RING, SPLIT, 2 * COLS))
+    lower = shaped((RING, PADDED_ROWS - SPLIT, 2 * COLS))
+    slots = call(
+        first_stage_kernel,
+        "first_stage",
+        [upper] * RING + [lower] * RING,
+        [IN_SMEM, IN_VMEM, IN_VMEM],
+        vmem=24,
+    )(spot, kept, got)
+    slots = shifted(slots[:RING], "x") + shifted(slots[RING:], ("zh", "zl"))
+    slots, query_out = lax.optimization_barrier((slots, query_out))
+    upper = shaped((SPLIT, 2 * COLS))
+    lower = shaped((PADDED_ROWS - SPLIT, 2 * COLS))
+    slots = call(
+        second_stage_kernel,
+        "second_stage",
+        [upper] * RING + [lower] * RING,
+        [IN_SMEM] + [IN_VMEM] * (2 * RING),
+    )(spot, *slots)
+    slots = shifted(slots[:RING], ("zh", "zl")) + shifted(slots[RING:], "x")
+    block = shaped((ROWS, COLS))
+    query_out, key_out, value_out = call(
+        last_kernel, "last", [block] * 3, [IN_VMEM] * (1 + 2 * RING)
+    )(query_out, *slots)
 
     summed = back_project(grad_query, query_weight) + back_project(grad_key, key_weight)
     summed = summed + back_project(grad_value, value_weight)
     latent_grad = summed.astype(BF16).reshape(latent.shape)
-    return latent_grad, query_out, key_value_out[:, :COLS], key_value_out[:, COLS:]
+    return latent_grad, query_out, key_out, value_out
 
 
 def solution(mesh):

time: 227 us -> 205 us (0.903)
  waiting for transfers between devices: 99.6 us -> 63.9 us
  starting transfers between devices: 57.8 us -> 76.9 us
  other arithmetic: 7.6 us -> 1.46 us
  Pallas kernels: 24.5 us -> 30.2 us
  local copies, waits for them, and re-layouts: 23.2 us -> 18.6 us
    all_to_all x5 -> x4, waiting for transfers between devices: 74.7 us -> 25.1 us  [exchange(): return lax.all_to_all(blocks, axes, 0, 0, tiled=True)]
    ppermute x11 -> x23, starting transfers between devices: 29.8 us -> 52.9 us  [the longest x21 52.7 us: shift(): lax.ppermute(values, axis, [(i, (i + by) % RING) for i in range(RING)])]
    ppermute x11 -> x23, waiting for transfers between devices: 24.9 us -> 38.8 us  [the longest x21 38.8 us: shift(): lax.ppermute(values, axis, [(i, (i + by) % RING) for i in range(RING)])]
    pallas_call x3 -> x6, Pallas kernels: 5.79 us -> 12.6 us  [the longest x2 5.98 us: partial_sum(): call(lambda *refs: weight_grad_kernel(normalizer, *refs), 'weight_grad',...]
    all_to_all x5 -> x4, starting transfers between devices: 28 us -> 24.1 us  [exchange(): return lax.all_to_all(blocks, axes, 0, 0, tiled=True)]
    add x2 -> x1, other arithmetic: 5.21 us -> 1.39 us  [body(): kept + got]
    unnamed x60 -> x52, local copies, waits for them, and re-layouts: 20.4 us -> 17.6 us
    reduce_sum x2 -> x0, other arithmetic: 2.38 us -> none  [weight_grad(): return jnp.sum(exchange(kept, PLANE), axis=0)[:ROWS]]
  transfers between devices with their start and end apart: 16 -> 27, of which waited for: 11 -> 13; matrix products, arithmetic and copies ran while one was open for 9% -> 7% of each run, Pallas kernels for 4% -> 7%
where the time goes in v3:
time: 205 us; the launch traced here: 203 us
  starting transfers between devices  76.9 us (38%)
  waiting for transfers between devices  63.9 us (31%)
  Pallas kernels  30.2 us (15%)
  local copies, waits for them, and re-layouts  18.6 us (9%)
  matrix products  11 us (5%)
    ppermute x21, starting transfers between devices, shift(): lax.ppermute(values, axis, [(i, (i + by) % RING) for i in range(RING)])  52.7 us
    ppermute x21, waiting for transfers between devices, shift(): lax.ppermute(values, axis, [(i, (i + by) % RING) for i in range(RING)])  38.8 us
    all_to_all x4, waiting for transfers between devices, exchange(): return lax.all_to_all(blocks, axes, 0, 0, tiled=True)  25.1 us
    all_to_all x4, starting transfers between devices, exchange(): return lax.all_to_all(blocks, axes, 0, 0, tiled=True)  24.1 us
    unnamed x52, local copies, waits for them, and re-layouts  17.6 us
    dot_general x3, matrix products, dot(): lax.dot_general(left, right, (((left_dim,), (right_dim,)), ((), ())), pre...  11 us
    pallas_call x1, Pallas kernels, body(): call(key_value_kernel, 'key_value', [heads, heads, shaped((TILES, PART +...  6.9 us
    pallas_call x2, Pallas kernels, partial_sum(): call(lambda *refs: weight_grad_kernel(normalizer, *refs), 'weight_grad',...  5.98 us
  transfers between devices with their start and end apart: 27, of which 13 were waited for; matrix products, arithmetic and copies ran while one was open for 7% of the time, Pallas kernels for 7%

profile of v3, /device:TPU:8, one launch (start us, length us, event | category | flops | bytes accessed | tf_op | source)
XLA Modules:
  0.0 203.1 jit_solution(11863932035700698618)
XLA Ops:
  1.7 6.9 %key_value.1 = (bf16[10,128,112]{2,1,0:T(8,128)(2,1)S(1)}, bf16[10,128,112]{2,1,0:T(8,128)(2,1)S(1)}, f32[32,45,112]{2,1,0:T(8,128)}) custom-call(bf16[128,2240]{1,0:T(8,128)(2,1)S(1)} %bitcast.13, bf16[2240,1120]{1,0:T(8,128)(2,1)} %key_weight.1, bf16[2240,1120]{1,0:T(8,128)(2,1)} %value_weight.1), custom_call_target="tpu_custom_call" | custom-call | tf_op jit(solution)/shard_map/key_value/pallas_call | solution.py:330
  10.1 8.3 %all-to-all-start = ((f32[32,45,112]{2,1,0:T(8,128)}), f32[32,45,112]{2,1,0:T(8,128)S(1)}, u32[]{:S(2)}, u32[]{:S(2)}) async-start(f32[32,45,112]{2,1,0:T(8,128)} %get-tuple-element.69), calls=%async_computation | async-start | bytes 1572864 | tf_op jit(solution)/shard_map/all_to_all | solution.py:295
  20.7 2.5 %copy-done = bf16[2240,1120]{1,0:T(8,128)(2,1)S(1)} copy-done((bf16[2240,1120]{1,0:T(8,128)(2,1)S(1)}, bf16[2240,1120]{1,0:T(8,128)(2,1)}, u32[]{:S(2)}) %copy-start) | copy-done | bytes 5017624
  24.2 8.7 %all-to-all-done.refs_0_ = f32[32,45,112]{2,1,0:T(8,128)S(1)} async-done(((f32[32,45,112]{2,1,0:T(8,128)}), f32[32,45,112]{2,1,0:T(8,128)S(1)}, u32[]{:S(2)}, u32[]{:S(2)}) %all-to-all-start) | async-done | bytes 645152 | tf_op jit(solution)/shard_map/all_to_all | solution.py:295
  35.3 4.2 %all-to-all-start.1 = ((f32[32,70,112]{2,1,0:T(8,128)}), f32[32,70,112]{2,1,0:T(8,128)S(1)}, u32[]{:S(2)}, u32[]{:S(2)}) async-start(f32[32,70,112]{2,1,0:T(8,128)} %copy-done.5), calls=%async_computation.1 | async-start | bytes 2359296 | tf_op jit(solution)/shard_map/all_to_all | solution.py:295
  39.5 2.4 %collective-permute-start.2 = (f32[2240,128]{1,0:T(8,128)S(1)}, f32[2240,128]{1,0:T(8,128)}, u32[]{:S(2)}, u32[]{:S(2)}) collective-permute-start(f32[2240,128]{1,0:T(8,128)S(1)} %turn.1.own), channel_id=1, source_target_pairs={{0,64},{32,96},{64,0},{96,32},{1,65},{33,97},{65,1},{97,33},{2,66}... | collective-permute-start | bytes 3440648 | tf_op jit(solution)/shard_map/ppermute | solution.py:299
  41.9 16.4 %all-to-all-done.1.refs_0_.got = f32[32,70,112]{2,1,0:T(8,128)S(1)} async-done(((f32[32,70,112]{2,1,0:T(8,128)}), f32[32,70,112]{2,1,0:T(8,128)S(1)}, u32[]{:S(2)}, u32[]{:S(2)}) %all-to-all-start.1) | async-done | bytes 1003552 | tf_op jit(solution)/shard_map/all_to_all | solution.py:295
  60.8 4.6 %all-to-all-start.2 = ((f32[32,45,112]{2,1,0:T(8,128)}), f32[32,45,112]{2,1,0:T(8,128)}, u32[]{:S(2)}, u32[]{:S(2)}) async-start(f32[32,45,112]{2,1,0:T(8,128)} %copy-done.7), calls=%async_computation.2 | async-start | bytes 1572864 | tf_op jit(solution)/shard_map/all_to_all | solution.py:295
  70.2 17.7 %collective-permute-start.4 = (f32[128,280]{1,0:T(8,128)}, f32[128,280]{1,0:T(8,128)}, u32[]{:S(2)}, u32[]{:S(2)}) collective-permute-start(f32[128,280]{1,0:T(8,128)} %get-tuple-element.81), channel_id=1, source_target_pairs={{0,64},{32,96},{64,0},{96,32},{1,65},{33,97},{65,1},{97,33},{2,66}... | collective-permute-start | bytes 430088 | tf_op jit(solution)/shard_map/ppermute | solution.py:299
  87.8 2.3 %join.1.refs_1_ = bf16[2240,512]{1,0:T(8,128)(2,1)S(1)} custom-call(f32[2240,128]{1,0:T(8,128)S(1)} %turn.1.own, f32[2240,128]{1,0:T(8,128)} %collective-permute-done.first, f32[2240,128]{1,0:T(8,128)} %collective-permute-done.2.second, f32[2240,128]{1,0:T(8,128)} %collective-permute-done.1.third), custom_call_target="tpu_custom_call" | custom-call | tf_op jit(solution)/shard_map/join/pallas_call | solution.py:376
  91.8 2.2 %collective-permute-done.4.refs_4_ = f32[128,280]{1,0:T(8,128)} collective-permute-done((f32[128,280]{1,0:T(8,128)}, f32[128,280]{1,0:T(8,128)}, u32[]{:S(2)}, u32[]{:S(2)}) %collective-permute-start.4) | collective-permute-done | bytes 143392 | tf_op jit(solution)/shard_map/ppermute | solution.py:299
  93.9 3.4 %collective-permute-done.5.refs_5_ = f32[128,280]{1,0:T(8,128)} collective-permute-done((f32[128,280]{1,0:T(8,128)}, f32[128,280]{1,0:T(8,128)}, u32[]{:S(2)}, u32[]{:S(2)}) %collective-permute-start.5) | collective-permute-done | bytes 143392 | tf_op jit(solution)/shard_map/ppermute | solution.py:299
  98.3 2.5 %weight_grad.2 = (f32[16,72,280]{2,1,0:T(8,128)S(1)}, f32[16,72,280]{2,1,0:T(8,128)S(1)}) custom-call(s32[1]{0:T(128)} %bitcast.6.refs_0_, bf16[2240,512]{1,0:T(8,128)(2,1)S(1)} %join.1.refs_1_, f32[128,280]{1,0:T(8,128)S(1)} %copy-done.23, f32[128,280]{1,0:T(8,128)} %collective-permute-done.3.refs_3_, f32[128,280]{1,0:T(8,128)} %collective-permute-done.4.refs_4_, ...), custom_call_target="tpu_custom_call" | custom-call | tf_op jit(solution)/shard_map/weight_grad/pallas_call | solution.py:394
  100.9 2.7 %key_value_grad.1 = (bf16[128,1120]{1,0:T(8,128)(2,1)S(1)}, bf16[128,1120]{1,0:T(8,128)(2,1)S(1)}, f32[128,560]{1,0:T(8,128)S(1)}, f32[128,560]{1,0:T(8,128)S(1)...) custom-call(s32[1]{0:T(128)} %bitcast.place, f32[32,45,112]{2,1,0:T(8,128)} %all-to-all-done.2.got, ...), custom_call_target="tpu_custom_call" | custom-call | tf_op jit(solution)/shard_map/key_value_grad/pallas_call | solution.py:382
  105.6 3.3 %collective-permute-start.8 = (f32[128,560]{1,0:T(8,128)S(1)}, f32[128,560]{1,0:T(8,128)S(1)}, u32[]{:S(2)}, u32[]{:S(2)}) collective-permute-start(f32[128,560]{1,0:T(8,128)S(1)} %get-tuple-element.97), channel_id=1, source_target_pairs={{0,64},{32,96},{64,0},{96,32},{1,65},{33,97},{65,1},{97,33},{2,66}... | collective-permute-start | bytes 860168 | tf_op jit(solution)/shard_map/ppermute | solution.py:299
  112.0 3.5 %collective-permute-done.7.refs_3_ = f32[128,560]{1,0:T(8,128)S(1)} collective-permute-done((f32[128,560]{1,0:T(8,128)S(1)}, f32[128,560]{1,0:T(8,128)S(1)}, u32[]{:S(2)}, u32[]{:S(2)}) %collective-permute-start.7) | collective-permute-done | bytes 286752 | tf_op jit(solution)/shard_map/ppermute | solution.py:299
  115.5 2.2 %collective-permute-done.8.refs_4_ = f32[128,560]{1,0:T(8,128)S(1)} collective-permute-done((f32[128,560]{1,0:T(8,128)S(1)}, f32[128,560]{1,0:T(8,128)S(1)}, u32[]{:S(2)}, u32[]{:S(2)}) %collective-permute-start.8) | collective-permute-done | bytes 286752 | tf_op jit(solution)/shard_map/ppermute | solution.py:299
  117.7 6.2 %collective-permute-done.9.refs_5_ = f32[128,560]{1,0:T(8,128)S(1)} collective-permute-done((f32[128,560]{1,0:T(8,128)S(1)}, f32[128,560]{1,0:T(8,128)S(1)}, u32[]{:S(2)}, u32[]{:S(2)}) %collective-permute-start.9) | collective-permute-done | bytes 286752 | tf_op jit(solution)/shard_map/ppermute | solution.py:299
  124.0 3.5 %weight_grad.3 = (f32[16,72,560]{2,1,0:T(8,128)S(1)}, f32[16,72,560]{2,1,0:T(8,128)}) custom-call(s32[1]{0:T(128)} %bitcast.6.refs_0_, bf16[2240,512]{1,0:T(8,128)(2,1)S(1)} %join.1.refs_1_, f32[128,560]{1,0:T(8,128)S(1)} %get-tuple-element.99.refs_2_, f32[128,560]{1,0:T(8,128)S(1)} %collective-permute-done.7.refs_3_, ...), custom_call_target="tpu_custom_call" | custom-call | tf_op jit(solution)/shard_map/weight_grad/pallas_call | solution.py:394
  129.1 7.0 %all-to-all-start.3 = ((f32[16,72,280]{2,1,0:T(8,128)}), f32[16,72,280]{2,1,0:T(8,128)S(1)}, u32[]{:S(2)}, u32[]{:S(2)}) async-start(f32[16,72,280]{2,1,0:T(8,128)} %add.15), calls=%async_computation.3 | async-start | bytes 3538944 | tf_op jit(solution)/shard_map/all_to_all | solution.py:295
  138.0 3.3 %first_stage.1 = (f32[4,40,560]{2,1,0:T(8,128)S(1)}, f32[4,40,560]{2,1,0:T(8,128)}, f32[4,40,560]{2,1,0:T(8,128)}, f32[4,40,560]{2,1,0:T(8,128)}, f32[4,32,560]{...) custom-call(s32[2]{0:T(128)S(1)} %pad_add_fusion.spot, ...), custom_call_target="tpu_custom_call" | custom-call | tf_op jit(solution)/shard_map/first_stage/pallas_call | solution.py:411
  144.0 2.7 %collective-permute-start.15 = (f32[4,32,560]{2,1,0:T(8,128)}, f32[4,32,560]{2,1,0:T(8,128)}, u32[]{:S(2)}, u32[]{:S(2)}) collective-permute-start(f32[4,32,560]{2,1,0:T(8,128)} %get-tuple-element.111), channel_id=1, source_target_pairs={{0,16},{1,17},{16,0},{17,1},{2,18},{3,19},{18,2},{19,3},{4,20},{5,... | collective-permute-start | bytes 860168 | tf_op jit(solution)/shard_map/ppermute | solution.py:299
  149.6 2.7 %collective-permute-start.12 = (f32[4,40,560]{2,1,0:T(8,128)}, f32[4,40,560]{2,1,0:T(8,128)S(1)}, u32[]{:S(2)}, u32[]{:S(2)}) collective-permute-start(f32[4,40,560]{2,1,0:T(8,128)} %get-tuple-element.107), channel_id=1, source_target_pairs={{0,4},{2,6},{4,0},{6,2},{1,5},{3,7},{5,1},{7,3},{8,12},{10,14},{12... | collective-permute-start | bytes 1075208 | tf_op jit(solution)/shard_map/ppermute | solution.py:299
  152.3 14.3 %collective-permute-done.14.refs_5_ = f32[4,32,560]{2,1,0:T(8,128)S(1)} collective-permute-done((f32[4,32,560]{2,1,0:T(8,128)S(1)}, f32[4,32,560]{2,1,0:T(8,128)S(1)}, u32[]{:S(2)}, u32[]{:S(2)}) %collective-permute-start.14) | collective-permute-done | bytes 286752 | tf_op jit(solution)/shard_map/ppermute | solution.py:299
  167.3 2.7 %collective-permute-start.13 = (f32[4,40,560]{2,1,0:T(8,128)}, f32[4,40,560]{2,1,0:T(8,128)}, u32[]{:S(2)}, u32[]{:S(2)}) collective-permute-start(f32[4,40,560]{2,1,0:T(8,128)} %get-tuple-element.108), channel_id=1, source_target_pairs={{0,6},{2,0},{4,2},{6,4},{1,7},{3,1},{5,3},{7,5},{8,14},{10,8},{12,... | collective-permute-start | bytes 1075208 | tf_op jit(solution)/shard_map/ppermute | solution.py:299
  170.0 5.0 %fusion.1 = f32[128,2240]{0,1:T(8,128)} fusion(bf16[128,1120]{1,0:T(8,128)(2,1)S(1)} %copy-done.11, bf16[2240,1120]{1,0:T(8,128)(2,1)} %weight.1), kind=kOutput, calls=%fused_computation.4 | convolution fusion | flops 642252800 | bytes 6451200 | tf_op jit(solution)/shard_map/dot_general | solution.py:55
  175.1 3.9 %collective-permute-done.12.refs_2_ = f32[4,40,560]{2,1,0:T(8,128)S(1)} collective-permute-done((f32[4,40,560]{2,1,0:T(8,128)}, f32[4,40,560]{2,1,0:T(8,128)S(1)}, u32[]{:S(2)}, u32[]{:S(2)}) %collective-permute-start.12) | collective-permute-done | bytes 358432 | tf_op jit(solution)/shard_map/ppermute | solution.py:299
  181.2 2.2 %second_stage.1 = (f32[40,560]{1,0:T(8,128)S(1)}, f32[40,560]{1,0:T(8,128)}, f32[40,560]{1,0:T(8,128)}, f32[40,560]{1,0:T(8,128)}, f32[32,560]{1,0:T(8,128)S(1)}...) custom-call(s32[2]{0:T(128)S(1)} %pad_add_fusion.spot, ...), custom_call_target="tpu_custom_call" | custom-call | tf_op jit(solution)/shard_map/second_stage/pallas_call | solution.py:422
  184.1 4.4 %convolution_add_fusion.1 = f32[128,2240]{0,1:T(8,128)S(1)} fusion(f32[128,2240]{0,1:T(8,128)} %fusion.1, bf16[128,1120]{1,0:T(8,128)(2,1)S(1)} %copy-done.13, bf16[2240,1120]{1,0:T(8,128)(2,1)} %key_weight.1), kind=kOutput, calls=%fused_computation.1 | convolution fusion | flops 642539520 | bytes 7598080 | tf_op jit(solution)/shard_map/dot_general | solution.py:55
  188.5 4.1 %collective-permute-start.21 = (f32[32,560]{1,0:T(8,128)}, f32[32,560]{1,0:T(8,128)S(1)}, u32[]{:S(2)}, u32[]{:S(2)}) collective-permute-start(f32[32,560]{1,0:T(8,128)} %get-tuple-element.129), channel_id=1, source_target_pairs={{0,4},{2,6},{4,0},{6,2},{1,5},{3,7},{5,1},{7,3},{8,12},{10,14},{12... | collective-permute-start | bytes 215048 | tf_op jit(solution)/shard_map/ppermute | solution.py:299
  194.2 2.0 collective-permute-start.18
  196.2 2.3 %collective-permute-start.19 = (f32[40,560]{1,0:T(8,128)}, f32[40,560]{1,0:T(8,128)S(1)}, u32[]{:S(2)}, u32[]{:S(2)}) collective-permute-start(f32[40,560]{1,0:T(8,128)} %get-tuple-element.126), channel_id=1, source_target_pairs={{0,17},{1,0},{16,1},{17,16},{2,19},{3,2},{18,3},{19,18},{4,21},{5,... | collective-permute-start | bytes 268808 | tf_op jit(solution)/shard_map/ppermute | solution.py:299
  (94 shorter events, 42.2 us)
Async XLA Ops:
  10.1 22.8 %all-to-all-start = ((f32[32,45,112]{2,1,0:T(8,128)}), f32[32,45,112]{2,1,0:T(8,128)S(1)}, u32[]{:S(2)}, u32[]{:S(2)}) async-start(f32[32,45,112]{2,1,0:T(8,128)} %get-tuple-element.69), calls=%async_computation | async-start | bytes 1572864 | tf_op jit(solution)/shard_map/all_to_all | solution.py:295
  18.4 14.5 %copy-start.6 = (bf16[1,16,8,1120]{3,2,1,0:T(8,128)(2,1)S(1)}, bf16[1,16,8,1120]{3,2,1,0:T(8,128)(2,1)}, u32[]{:S(2)}) copy-start(bf16[1,16,8,1120]{3,2,1,0:T(8,128)(2,1)} %param.9) | copy-start | bytes 860164
  18.6 42.2 %collective-permute-start.1 = (f32[2240,128]{1,0:T(8,128)S(1)}, f32[2240,128]{1,0:T(8,128)}, u32[]{:S(2)}, u32[]{:S(2)}) collective-permute-start(f32[2240,128]{1,0:T(8,128)S(1)} %turn.1.own), channel_id=1, source_target_pairs={{0,96},{32,0},{64,32},{96,64},{1,97},{33,1},{65,33},{97,65},{2,98}... | collective-permute-start | bytes 3440648 | tf_op jit(solution)/shard_map/ppermute | solution.py:299
  19.2 41.7 %collective-permute-start = (f32[2240,128]{1,0:T(8,128)S(1)}, f32[2240,128]{1,0:T(8,128)}, u32[]{:S(2)}, u32[]{:S(2)}) collective-permute-start(f32[2240,128]{1,0:T(8,128)S(1)} %turn.1.own), channel_id=1, source_target_pairs={{0,32},{32,64},{64,96},{96,0},{1,33},{33,65},{65,97},{97,1},{2,34}... | collective-permute-start | bytes 3440648 | tf_op jit(solution)/shard_map/ppermute | solution.py:299
  35.3 23.0 %all-to-all-start.1 = ((f32[32,70,112]{2,1,0:T(8,128)}), f32[32,70,112]{2,1,0:T(8,128)S(1)}, u32[]{:S(2)}, u32[]{:S(2)}) async-start(f32[32,70,112]{2,1,0:T(8,128)} %copy-done.5), calls=%async_computation.1 | async-start | bytes 2359296 | tf_op jit(solution)/shard_map/all_to_all | solution.py:295
  39.5 48.4 %collective-permute-start.2 = (f32[2240,128]{1,0:T(8,128)S(1)}, f32[2240,128]{1,0:T(8,128)}, u32[]{:S(2)}, u32[]{:S(2)}) collective-permute-start(f32[2240,128]{1,0:T(8,128)S(1)} %turn.1.own), channel_id=1, source_target_pairs={{0,64},{32,96},{64,0},{96,32},{1,65},{33,97},{65,1},{97,33},{2,66}... | collective-permute-start | bytes 3440648 | tf_op jit(solution)/shard_map/ppermute | solution.py:299
  60.8 36.5 %all-to-all-start.2 = ((f32[32,45,112]{2,1,0:T(8,128)}), f32[32,45,112]{2,1,0:T(8,128)}, u32[]{:S(2)}, u32[]{:S(2)}) async-start(f32[32,45,112]{2,1,0:T(8,128)} %copy-done.7), calls=%async_computation.2 | async-start | bytes 1572864 | tf_op jit(solution)/shard_map/all_to_all | solution.py:295
  68.6 23.2 %collective-permute-start.3 = (f32[128,280]{1,0:T(8,128)}, f32[128,280]{1,0:T(8,128)}, u32[]{:S(2)}, u32[]{:S(2)}) collective-permute-start(f32[128,280]{1,0:T(8,128)} %get-tuple-element.80), channel_id=1, source_target_pairs={{0,32},{32,64},{64,96},{96,0},{1,33},{33,65},{65,97},{97,1},{2,34}... | collective-permute-start | bytes 430088 | tf_op jit(solution)/shard_map/ppermute | solution.py:299
  70.2 23.7 %collective-permute-start.4 = (f32[128,280]{1,0:T(8,128)}, f32[128,280]{1,0:T(8,128)}, u32[]{:S(2)}, u32[]{:S(2)}) collective-permute-start(f32[128,280]{1,0:T(8,128)} %get-tuple-element.81), channel_id=1, source_target_pairs={{0,64},{32,96},{64,0},{96,32},{1,65},{33,97},{65,1},{97,33},{2,66}... | collective-permute-start | bytes 430088 | tf_op jit(solution)/shard_map/ppermute | solution.py:299
  87.8 9.5 %collective-permute-start.5 = (f32[128,280]{1,0:T(8,128)}, f32[128,280]{1,0:T(8,128)}, u32[]{:S(2)}, u32[]{:S(2)}) collective-permute-start(f32[128,280]{1,0:T(8,128)} %get-tuple-element.82), channel_id=1, source_target_pairs={{0,96},{32,0},{64,32},{96,64},{1,97},{33,1},{65,33},{97,65},{2,98}... | collective-permute-start | bytes 430088 | tf_op jit(solution)/shard_map/ppermute | solution.py:299
  100.8 9.8 %collective-permute-start.6 = (f32[16,72,280]{2,1,0:T(8,128)S(1)}, f32[16,72,280]{2,1,0:T(8,128)S(1)}, u32[]{:S(2)}, u32[]{:S(2)}) collective-permute-start(f32[16,72,280]{2,1,0:T(8,128)S(1)} %get-tuple-element.94), channel_id=1, source_target_pairs={{0,8},{8,0},{1,9},{9,1},{2,10},{10,2},{3,11},{11,3},{4,12},{12,4},... | collective-permute-start | bytes 3870728 | tf_op jit(solution)/shard_map/ppermute | solution.py:402
  105.0 10.5 %collective-permute-start.7 = (f32[128,560]{1,0:T(8,128)S(1)}, f32[128,560]{1,0:T(8,128)S(1)}, u32[]{:S(2)}, u32[]{:S(2)}) collective-permute-start(f32[128,560]{1,0:T(8,128)S(1)} %get-tuple-element.96), channel_id=1, source_target_pairs={{0,32},{32,64},{64,96},{96,0},{1,33},{33,65},{65,97},{97,1},{2,34}... | collective-permute-start | bytes 860168 | tf_op jit(solution)/shard_map/ppermute | solution.py:299
  105.6 12.1 %collective-permute-start.8 = (f32[128,560]{1,0:T(8,128)S(1)}, f32[128,560]{1,0:T(8,128)S(1)}, u32[]{:S(2)}, u32[]{:S(2)}) collective-permute-start(f32[128,560]{1,0:T(8,128)S(1)} %get-tuple-element.97), channel_id=1, source_target_pairs={{0,64},{32,96},{64,0},{96,32},{1,65},{33,97},{65,1},{97,33},{2,66}... | collective-permute-start | bytes 860168 | tf_op jit(solution)/shard_map/ppermute | solution.py:299
  108.9 15.1 %collective-permute-start.9 = (f32[128,560]{1,0:T(8,128)S(1)}, f32[128,560]{1,0:T(8,128)S(1)}, u32[]{:S(2)}, u32[]{:S(2)}) collective-permute-start(f32[128,560]{1,0:T(8,128)S(1)} %get-tuple-element.98), channel_id=1, source_target_pairs={{0,96},{32,0},{64,32},{96,64},{1,97},{33,1},{65,33},{97,65},{2,98}... | collective-permute-start | bytes 860168 | tf_op jit(solution)/shard_map/ppermute | solution.py:299
  129.1 7.1 %collective-permute-start.10 = (f32[16,72,560]{2,1,0:T(8,128)}, f32[16,72,560]{2,1,0:T(8,128)}, u32[]{:S(2)}, u32[]{:S(2)}) collective-permute-start(f32[16,72,560]{2,1,0:T(8,128)} %get-tuple-element.104), channel_id=1, source_target_pairs={{0,8},{8,0},{1,9},{9,1},{2,10},{10,2},{3,11},{11,3},{4,12},{12,4},... | collective-permute-start | bytes 7741448 | tf_op jit(solution)/shard_map/ppermute | solution.py:402
  129.1 45.9 %all-to-all-start.3 = ((f32[16,72,280]{2,1,0:T(8,128)}), f32[16,72,280]{2,1,0:T(8,128)S(1)}, u32[]{:S(2)}, u32[]{:S(2)}) async-start(f32[16,72,280]{2,1,0:T(8,128)} %add.15), calls=%async_computation.3 | async-start | bytes 3538944 | tf_op jit(solution)/shard_map/all_to_all | solution.py:295
  138.0 32.0 %copy-start.11 = (bf16[128,1120]{1,0:T(8,128)(2,1)S(1)}, bf16[128,1120]{1,0:T(8,128)(2,1)}, u32[]{:S(2)}) copy-start(bf16[128,1120]{1,0:T(8,128)(2,1)} %copy-done.10) | copy-start | bytes 860164
  142.1 24.5 %collective-permute-start.14 = (f32[4,32,560]{2,1,0:T(8,128)S(1)}, f32[4,32,560]{2,1,0:T(8,128)S(1)}, u32[]{:S(2)}, u32[]{:S(2)}) collective-permute-start(f32[4,32,560]{2,1,0:T(8,128)S(1)} %get-tuple-element.110), channel_id=1, source_target_pairs={{0,1},{1,16},{16,17},{17,0},{2,3},{3,18},{18,19},{19,2},{4,5},{5,2... | collective-permute-start | bytes 860168 | tf_op jit(solution)/shard_map/ppermute | solution.py:299
  144.0 31.0 %collective-permute-start.15 = (f32[4,32,560]{2,1,0:T(8,128)}, f32[4,32,560]{2,1,0:T(8,128)}, u32[]{:S(2)}, u32[]{:S(2)}) collective-permute-start(f32[4,32,560]{2,1,0:T(8,128)} %get-tuple-element.111), channel_id=1, source_target_pairs={{0,16},{1,17},{16,0},{17,1},{2,18},{3,19},{18,2},{19,3},{4,20},{5,... | collective-permute-start | bytes 860168 | tf_op jit(solution)/shard_map/ppermute | solution.py:299
  146.7 28.3 %collective-permute-start.16 = (f32[4,32,560]{2,1,0:T(8,128)}, f32[4,32,560]{2,1,0:T(8,128)}, u32[]{:S(2)}, u32[]{:S(2)}) collective-permute-start(f32[4,32,560]{2,1,0:T(8,128)} %get-tuple-element.112), channel_id=1, source_target_pairs={{0,17},{1,0},{16,1},{17,16},{2,19},{3,2},{18,3},{19,18},{4,21},{5,... | collective-permute-start | bytes 860168 | tf_op jit(solution)/shard_map/ppermute | solution.py:299
  148.2 26.9 %collective-permute-start.11 = (f32[4,40,560]{2,1,0:T(8,128)}, f32[4,40,560]{2,1,0:T(8,128)S(1)}, u32[]{:S(2)}, u32[]{:S(2)}) collective-permute-start(f32[4,40,560]{2,1,0:T(8,128)} %get-tuple-element.106), channel_id=1, source_target_pairs={{0,2},{2,4},{4,6},{6,0},{1,3},{3,5},{5,7},{7,1},{8,10},{10,12},{12... | collective-permute-start | bytes 1075208 | tf_op jit(solution)/shard_map/ppermute | solution.py:299
  149.6 29.4 %collective-permute-start.12 = (f32[4,40,560]{2,1,0:T(8,128)}, f32[4,40,560]{2,1,0:T(8,128)S(1)}, u32[]{:S(2)}, u32[]{:S(2)}) collective-permute-start(f32[4,40,560]{2,1,0:T(8,128)} %get-tuple-element.107), channel_id=1, source_target_pairs={{0,4},{2,6},{4,0},{6,2},{1,5},{3,7},{5,1},{7,3},{8,12},{10,14},{12... | collective-permute-start | bytes 1075208 | tf_op jit(solution)/shard_map/ppermute | solution.py:299
  167.3 11.9 %collective-permute-start.13 = (f32[4,40,560]{2,1,0:T(8,128)}, f32[4,40,560]{2,1,0:T(8,128)}, u32[]{:S(2)}, u32[]{:S(2)}) collective-permute-start(f32[4,40,560]{2,1,0:T(8,128)} %get-tuple-element.108), channel_id=1, source_target_pairs={{0,6},{2,0},{4,2},{6,4},{1,7},{3,1},{5,3},{7,5},{8,14},{10,8},{12,... | collective-permute-start | bytes 1075208 | tf_op jit(solution)/shard_map/ppermute | solution.py:299
  181.2 17.2 %slice-start = ((s8[5160960]{0:T(1024)(128)(4,1)}), s8[4194304]{0:T(1024)(128)(4,1)S(1)}, s32[]{:S(2)}) async-start(s8[5160960]{0:T(1024)(128)(4,1)} %bitcast.18), calls=%async_computation.4 | async-start | bytes 8388608
  183.4 12.7 %collective-permute-start.20 = (f32[32,560]{1,0:T(8,128)S(1)}, f32[32,560]{1,0:T(8,128)S(1)}, u32[]{:S(2)}, u32[]{:S(2)}) collective-permute-start(f32[32,560]{1,0:T(8,128)S(1)} %get-tuple-element.128), channel_id=1, source_target_pairs={{0,2},{2,4},{4,6},{6,0},{1,3},{3,5},{5,7},{7,1},{8,10},{10,12},{12... | collective-permute-start | bytes 215048 | tf_op jit(solution)/shard_map/ppermute | solution.py:299
  184.1 14.4 %copy-start.9 = (bf16[128,1120]{1,0:T(8,128)(2,1)S(1)}, bf16[128,1120]{1,0:T(8,128)(2,1)}, u32[]{:S(2)}) copy-start(bf16[128,1120]{1,0:T(8,128)(2,1)} %copy-done.8) | copy-start | bytes 860164
  184.1 14.4 %slice-start.1 = ((s8[5160960]{0:T(1024)(128)(4,1)}), s8[966656]{0:T(1024)(128)(4,1)S(1)}, s32[]{:S(2)}) async-start(s8[5160960]{0:T(1024)(128)(4,1)} %bitcast.18), calls=%async_computation.5 | async-start | bytes 1933312
  188.5 12.6 %collective-permute-start.21 = (f32[32,560]{1,0:T(8,128)}, f32[32,560]{1,0:T(8,128)S(1)}, u32[]{:S(2)}, u32[]{:S(2)}) collective-permute-start(f32[32,560]{1,0:T(8,128)} %get-tuple-element.129), channel_id=1, source_target_pairs={{0,4},{2,6},{4,0},{6,2},{1,5},{3,7},{5,1},{7,3},{8,12},{10,14},{12... | collective-permute-start | bytes 215048 | tf_op jit(solution)/shard_map/ppermute | solution.py:299
  192.7 8.5 %collective-permute-start.22 = (f32[32,560]{1,0:T(8,128)}, f32[32,560]{1,0:T(8,128)S(1)}, u32[]{:S(2)}, u32[]{:S(2)}) collective-permute-start(f32[32,560]{1,0:T(8,128)} %get-tuple-element.130), channel_id=1, source_target_pairs={{0,6},{2,0},{4,2},{6,4},{1,7},{3,1},{5,3},{7,5},{8,14},{10,8},{12,... | collective-permute-start | bytes 215048 | tf_op jit(solution)/shard_map/ppermute | solution.py:299
  194.2 7.3 %collective-permute-start.17 = (f32[40,560]{1,0:T(8,128)}, f32[40,560]{1,0:T(8,128)S(1)}, u32[]{:S(2)}, u32[]{:S(2)}) collective-permute-start(f32[40,560]{1,0:T(8,128)} %get-tuple-element.124), channel_id=1, source_target_pairs={{0,1},{1,16},{16,17},{17,0},{2,3},{3,18},{18,19},{19,2},{4,5},{5,2... | collective-permute-start | bytes 268808 | tf_op jit(solution)/shard_map/ppermute | solution.py:299
  194.2 7.3 %collective-permute-start.18 = (f32[40,560]{1,0:T(8,128)}, f32[40,560]{1,0:T(8,128)S(1)}, u32[]{:S(2)}, u32[]{:S(2)}) collective-permute-start(f32[40,560]{1,0:T(8,128)} %get-tuple-element.125), channel_id=1, source_target_pairs={{0,16},{1,17},{16,0},{17,1},{2,18},{3,19},{18,2},{19,3},{4,20},{5,... | collective-permute-start | bytes 268808 | tf_op jit(solution)/shard_map/ppermute | solution.py:299
  196.2 6.1 %collective-permute-start.19 = (f32[40,560]{1,0:T(8,128)}, f32[40,560]{1,0:T(8,128)S(1)}, u32[]{:S(2)}, u32[]{:S(2)}) collective-permute-start(f32[40,560]{1,0:T(8,128)} %get-tuple-element.126), channel_id=1, source_target_pairs={{0,17},{1,0},{16,1},{17,16},{2,19},{3,2},{18,3},{19,18},{4,21},{5,... | collective-permute-start | bytes 268808 | tf_op jit(solution)/shard_map/ppermute | solution.py:299
  (21 other events, 56.3 us)

commit v4 on v3

--- a/solution.py
+++ b/solution.py
@@ -21,6 +21,9 @@
 REPLICAS = 4
 RING = 4
 COLS = HW // REPLICAS
+EARLY = 256
+LATE = COLS - EARLY
+WIDE = 2 * COLS + LATE
 TOKENS = 128
 
 EPSILON = 1e-15
@@ -30,25 +33,37 @@
 
 F32 = jnp.float32
 BF16 = jnp.bfloat16
-IN_VMEM = pl.BlockSpec(memory_space=pltpu.VMEM)
+BLOCK = pl.BlockSpec()
 IN_SMEM = pl.BlockSpec(memory_space=pltpu.SMEM)
 IN_HBM = pl.BlockSpec(memory_space=pltpu.HBM)
 
 
 def shaped(shape, dtype=F32):
-    return jax.ShapeDtypeStruct(shape, dtype)
-
-
-def call(kernel, name, outs, in_specs, scratch=(), vmem=12):
-    return pl.pallas_call(
+    return pltpu.HBM(shape, dtype)
+
+
+def call(kernel, name, outs, in_specs, scratch=(), vmem=12, arrived=()):
+    run = pl.pallas_call(
         kernel,
         name=name,
+        grid=(1,),
         out_shape=outs,
         in_specs=in_specs,
-        out_specs=[IN_VMEM] * len(outs),
+        out_specs=[BLOCK] * len(outs),
         scratch_shapes=list(scratch),
         compiler_params=pltpu.CompilerParams(vmem_limit_bytes=vmem * 1024 * 1024),
     )
+
+    def with_placed(*operands):
+        placed = [
+            operand
+            if spec is IN_SMEM or index in arrived
+            else pltpu.with_memory_space_constraint(operand, pltpu.HBM)
+            for index, (operand, spec) in enumerate(zip(operands, in_specs))
+        ]
+        return run(*placed)
+
+    return with_placed
 
 
 def dot(left, right, left_dim, right_dim):
@@ -179,9 +194,10 @@
         sent[tile, PART : PART + HEADS, :] = values
 
 
-def place_columns(place, blocks, outs, at):
+def place_columns(place, blocks, outs, at, first=0, last=COLS):
     for slot, out in enumerate(outs):
-        out[:, at : at + COLS] = blocks[lax.rem(place[0] + slot, REPLICAS)]
+        block = blocks[lax.rem(place[0] + slot, REPLICAS)]
+        out[:, at : at + last - first] = block[:, first:last]
 
 
 def split_columns(flat, blocks):
@@ -190,7 +206,7 @@
 
 
 def query_grad_kernel(
-    place, got, query, numer, total, grad_denom, grad, own, first, second, third, state, flat, blocks
+    place, got, query, numer, total, grad_denom, grad, own, first, second, third, late, state, flat, blocks
 ):
     load_parts(state, got)
     for index in range(HEADS):
@@ -201,11 +217,13 @@
         grad[:, part] = values
         flat[:, part] = values.astype(F32)
     split_columns(flat, blocks)
-    place_columns(place, blocks, (own, first, second, third), 0)
+    place_columns(place, blocks, (own, first, second, third), 0, 0, EARLY)
+    for slot in range(REPLICAS):
+        late[slot] = blocks[lax.rem(place[0] + slot, REPLICAS)][:, EARLY:]
 
 
 def key_value_grad_kernel(
-    place, got, key, value, grad_key, grad_value, own, first, second, third, state, flat_key, flat_value, blocks
+    place, got, key, value, late, grad_key, grad_value, own, first, second, third, state, flat_key, flat_value, blocks
 ):
     load_parts(state, got)
     totals = got[0, PART : PART + HEADS, :]
@@ -228,17 +246,27 @@
     place_columns(place, blocks, outs, 0)
     split_columns(flat_value, blocks)
     place_columns(place, blocks, outs, COLS)
-
-
-def turn_kernel(tokens, out):
+    for slot, out in enumerate(outs):
+        out[:, 2 * COLS :] = late[slot]
+
+
+def turn_kernel(tokens, top, bottom):
     for start in range(0, D, 128):
-        size = min(128, D - start)
-        out[start : start + size, :] = tokens[:, start : start + size].astype(F32).T
-
-
-def join_kernel(own, first, second, third, out):
-    for slot, turned in enumerate((own, first, second, third)):
-        out[:, slot * TOKENS : (slot + 1) * TOKENS] = turned[...].astype(BF16)
+        turned = tokens[:, start : min(start + 128, D)].astype(F32).T
+        cut = min(max(D // 2 - start, 0), turned.shape[0])
+        if cut > 0:
+            top[start : start + cut, :] = turned[:cut]
+        if cut < turned.shape[0]:
+            at = start + cut - D // 2
+            bottom[at : at + turned.shape[0] - cut, :] = turned[cut:]
+
+
+def join_kernel(*refs):
+    out = refs[-1]
+    for index, half in enumerate(refs[:-1]):
+        slot, rows = index // 2, index % 2 * (D // 2)
+        at = slice(slot * TOKENS, (slot + 1) * TOKENS)
+        out[rows : rows + D // 2, at] = half[...].astype(BF16)
 
 
 def weight_grad_kernel(normalizer, core, tokens, own, first, second, third, kept, sent, columns):
@@ -257,21 +285,21 @@
 def first_stage_kernel(spot, kept, got, *outs):
     for slot in range(RING):
         across = lax.rem(spot[0] + slot, RING)
-        along = lax.rem(spot[1] + slot, RING)
         for other in range(RING):
             at = (other // 2) * (2 * RING) + across * 2 + other % 2
             outs[slot][other] = kept[at, :SPLIT, :] + got[at, :SPLIT, :]
-            at = (along // 2) * (2 * RING) + other * 2 + lax.rem(along, 2)
-            outs[RING + slot][other] = kept[at, SPLIT:, :] + got[at, SPLIT:, :]
+            at = (slot // 2) * (2 * RING) + other * 2 + slot % 2
+            outs[RING][slot, other] = kept[at, SPLIT:, :] + got[at, SPLIT:, :]
 
 
 def second_stage_kernel(spot, *refs):
-    uppers, lowers, outs = refs[:RING], refs[RING : 2 * RING], refs[2 * RING :]
+    uppers, lowers, outs = refs[:RING], refs[RING], refs[RING + 1 :]
     for slot in range(RING):
-        along = lax.rem(spot[1] + slot, RING)
-        outs[slot][...] = sum_at(uppers, along)
+        outs[RING][slot] = sum_at(uppers, slot)
         across = lax.rem(spot[0] + slot, RING)
-        outs[RING + slot][...] = sum_at(lowers, across)
+        outs[slot][...] = (lowers[0, across] + lowers[1, across]) + (
+            lowers[2, across] + lowers[3, across]
+        )
 
 
 def sum_at(refs, at):
@@ -279,16 +307,17 @@
 
 
 def last_kernel(query, *refs):
-    uppers, lowers = refs[:RING], refs[RING : 2 * RING]
-    query_out, key_out, value_out = refs[2 * RING :]
+    lowers, uppers, query_out, key_out, value_out = refs[:RING], *refs[RING:]
     total = query[0]
     for index in range(1, PLANE_SIZE):
         total = total + query[index]
-    query_out[...] = total[:ROWS]
-    for refs, rows, size in ((uppers, 0, SPLIT), (lowers, SPLIT, ROWS - SPLIT)):
-        total = (refs[0][...] + refs[1][...]) + (refs[2][...] + refs[3][...])
+    query_out[:, :EARLY] = total[:ROWS]
+    upper = (uppers[0] + uppers[1]) + (uppers[2] + uppers[3])
+    lower = (lowers[0][...] + lowers[1][...]) + (lowers[2][...] + lowers[3][...])
+    for total, rows, size in ((upper, 0, SPLIT), (lower, SPLIT, ROWS - SPLIT)):
         key_out[rows : rows + size, :] = total[:size, :COLS]
-        value_out[rows : rows + size, :] = total[:size, COLS:]
+        value_out[rows : rows + size, :] = total[:size, COLS : 2 * COLS]
+        query_out[rows : rows + size, EARLY:] = total[:size, 2 * COLS :]
 
 
 def exchange(blocks, axes):
@@ -301,6 +330,10 @@
 
 def shifted(slots, axis):
     return [slots[0]] + [shift(slots[s], s, axis) for s in range(1, RING)]
+
+
+def swap_cores(values):
+    return lax.ppermute(values, "core", [(0, 1), (1, 0)])
 
 
 def back_project(gradient, weight):
@@ -324,112 +357,125 @@
     wide = pltpu.VMEM((TOKENS, HW), F32)
     blocks = pltpu.VMEM((REPLICAS, TOKENS, COLS), F32)
 
-    (turned,) = call(turn_kernel, "turn", [shaped((D, TOKENS))], [IN_VMEM])(tokens)
-    turned = [turned] + [shift(turned, s, "dp") for s in (1, 3, 2)]
-
     key, value, sent = call(
         key_value_kernel,
         "key_value",
         [heads, heads, shaped((TILES, PART + HEADS, HD))],
-        [IN_VMEM, IN_HBM, IN_HBM],
+        [BLOCK, IN_HBM, IN_HBM],
         [weight, weight, state, totals, pltpu.SemaphoreType.DMA((2 * len(CHUNKS),))],
         vmem=20,
-    )(
-        tokens,
-        pltpu.with_memory_space_constraint(key_weight, pltpu.HBM),
-        pltpu.with_memory_space_constraint(value_weight, pltpu.HBM),
-    )
+    )(tokens, key_weight, value_weight)
+    sent, later_tokens = lax.optimization_barrier((sent, tokens))
+    half = shaped((D // 2, TOKENS))
+    top, bottom = call(turn_kernel, "turn", [half, half], [BLOCK])(later_tokens)
+    left_top = shift(top, 1, "dp")
+    right_bottom = shift(bottom, 3, "dp")
     got = exchange(sent, IMAGE)
     (query,) = call(
         query_kernel,
         "query",
         [heads],
-        [IN_VMEM, IN_VMEM],
+        [BLOCK, BLOCK],
     )(tokens, query_weight)
     sent, numer, total = call(
         lambda *refs: numerator_kernel(loss_scale, *refs),
         "numerator",
         [shaped((TILES, 2 * PART, HD)), heads, shaped((HEADS, HD))],
-        [IN_VMEM] * 3,
+        [BLOCK] * 3,
         [state],
+        arrived=(0,),
     )(got, query, upstream)
+    sent, left_top, right_bottom, later_top, later_bottom = lax.optimization_barrier(
+        (sent, left_top, right_bottom, top, bottom)
+    )
+    far_top = shift(left_top, 1, "dp")
+    far_bottom = shift(right_bottom, 3, "dp")
+    left_bottom = shift(later_bottom, 1, "dp")
+    right_top = shift(later_top, 3, "dp")
     got_state = exchange(sent, IMAGE)
     sent, grad_denom = call(
         lambda *refs: total_grad_kernel(loss_scale, *refs),
         "total_grad",
         [shaped((TILES, PART + HEADS, HD)), shaped((TOKENS, HEADS))],
-        [IN_VMEM] * 4,
+        [BLOCK] * 4,
         [state, totals],
+        arrived=(0,),
     )(got_state, query, upstream, total)
-    sent, turned[1], turned[2] = lax.optimization_barrier((sent, turned[1], turned[2]))
+    sent, far_top, far_bottom, left_bottom, right_top = lax.optimization_barrier(
+        (sent, far_top, far_bottom, left_bottom, right_top)
+    )
     got = exchange(sent, IMAGE)
 
-    block = shaped((TOKENS, COLS))
-    grad_query, *query_columns = call(
+    block = shaped((TOKENS, EARLY))
+    grad_query, *query_columns, late = call(
         query_grad_kernel,
         "query_grad",
-        [flat, block, block, block, block],
-        [IN_SMEM] + [IN_VMEM] * 5,
+        [flat, block, block, block, block, shaped((REPLICAS, TOKENS, LATE))],
+        [IN_SMEM] + [BLOCK] * 5,
         [state, wide, blocks],
+        arrived=(1,),
     )(place, got_state, query, numer, total, grad_denom)
     query_columns = shifted(query_columns, "dp")
     (all_tokens,) = call(
-        join_kernel, "join", [shaped((D, REPLICAS * TOKENS), BF16)], [IN_VMEM] * 4
-    )(turned[0], turned[1], turned[3], turned[2])
-    got, all_tokens, query_columns = lax.optimization_barrier((got, all_tokens, query_columns))
-
-    block = shaped((TOKENS, 2 * COLS))
+        join_kernel, "join", [shaped((D, REPLICAS * TOKENS), BF16)], [BLOCK] * 8, arrived=(2, 3, 4, 5, 6, 7)
+    )(top, bottom, left_top, left_bottom, far_top, far_bottom, right_top, right_bottom)
+    def partial_products(columns):
+        width = columns[0].shape[1]
+        half = shaped((PLANE_SIZE, PADDED_ROWS, width))
+        return call(
+            lambda *refs: weight_grad_kernel(normalizer, *refs),
+            "weight_grad",
+            [half, half],
+            [IN_SMEM] + [BLOCK] * 5,
+            [pltpu.VMEM((REPLICAS * TOKENS, width), BF16)],
+            vmem=24,
+            arrived=(3, 4, 5),
+        )(core, all_tokens, *columns)
+
+    query_kept, query_given = partial_products(query_columns)
+    got, query_kept, query_given = lax.optimization_barrier((got, query_kept, query_given))
+
+    block = shaped((TOKENS, WIDE))
     grad_key, grad_value, *key_value_columns = call(
         key_value_grad_kernel,
         "key_value_grad",
         [flat, flat, block, block, block, block],
-        [IN_SMEM] + [IN_VMEM] * 3,
+        [IN_SMEM] + [BLOCK] * 4,
         [state, wide, wide, blocks],
-    )(place, got, key, value)
+        arrived=(1,),
+    )(place, got, key, value, late)
+    key_value_columns, query_given = lax.optimization_barrier((key_value_columns, query_given))
     key_value_columns = shifted(key_value_columns, "dp")
 
-    def partial_sum(columns):
-        width = columns[0].shape[1]
-        half = shaped((PLANE_SIZE, PADDED_ROWS, width))
-        kept, given = call(
-            lambda *refs: weight_grad_kernel(normalizer, *refs),
-            "weight_grad",
-            [half, half],
-            [IN_SMEM] + [IN_VMEM] * 5,
-            [pltpu.VMEM((REPLICAS * TOKENS, width), BF16)],
-            vmem=24,
-        )(core, all_tokens, *columns)
-        return kept, lax.ppermute(given, "core", [(0, 1), (1, 0)])
-
-    kept, got = partial_sum(query_columns)
-    query_part, key_value_columns = lax.optimization_barrier((kept + got, key_value_columns))
-    query_out = exchange(query_part, PLANE)
-
-    kept, got = partial_sum(key_value_columns)
-    upper = shaped((RING, SPLIT, 2 * COLS))
-    lower = shaped((RING, PADDED_ROWS - SPLIT, 2 * COLS))
-    slots = call(
+    query_out = exchange(query_kept + swap_cores(query_given), PLANE)
+    query_out, key_value_columns = lax.optimization_barrier((query_out, key_value_columns))
+
+    kept, given = partial_products(key_value_columns)
+    got = swap_cores(given)
+    rest = PADDED_ROWS - SPLIT
+    *uppers, lowers = call(
         first_stage_kernel,
         "first_stage",
-        [upper] * RING + [lower] * RING,
-        [IN_SMEM, IN_VMEM, IN_VMEM],
+        [shaped((RING, SPLIT, WIDE))] * RING + [shaped((RING, RING, rest, WIDE))],
+        [IN_SMEM, BLOCK, BLOCK],
         vmem=24,
+        arrived=(2,),
     )(spot, kept, got)
-    slots = shifted(slots[:RING], "x") + shifted(slots[RING:], ("zh", "zl"))
-    slots, query_out = lax.optimization_barrier((slots, query_out))
-    upper = shaped((SPLIT, 2 * COLS))
-    lower = shaped((PADDED_ROWS - SPLIT, 2 * COLS))
-    slots = call(
+    lowers = exchange(lowers, ("zh", "zl"))
+    uppers = shifted(uppers, "x")
+    *lowers, uppers = call(
         second_stage_kernel,
         "second_stage",
-        [upper] * RING + [lower] * RING,
-        [IN_SMEM] + [IN_VMEM] * (2 * RING),
-    )(spot, *slots)
-    slots = shifted(slots[:RING], ("zh", "zl")) + shifted(slots[RING:], "x")
+        [shaped((rest, WIDE))] * RING + [shaped((RING, SPLIT, WIDE))],
+        [IN_SMEM] + [BLOCK] * (RING + 1),
+        arrived=(2, 3, 4, 5),
+    )(spot, *uppers, lowers)
+    uppers = exchange(uppers, ("zh", "zl"))
+    lowers = shifted(lowers, "x")
     block = shaped((ROWS, COLS))
     query_out, key_out, value_out = call(
-        last_kernel, "last", [block] * 3, [IN_VMEM] * (1 + 2 * RING)
-    )(query_out, *slots)
+        last_kernel, "last", [block] * 3, [BLOCK] * (RING + 2), arrived=(0, 2, 3, 4, 5)
+    )(query_out, *lowers, uppers)
 
     summed = back_project(grad_query, query_weight) + back_project(grad_key, key_weight)
     summed = summed + back_project(grad_value, value_weight)

time: 205 us -> 199 us (0.971)
  Pallas kernels: 30.2 us -> 49.2 us
  local copies, waits for them, and re-layouts: 18.6 us -> 4.75 us
  starting transfers between devices: 76.9 us -> 64 us
  waiting for transfers between devices: 63.9 us -> 66.8 us
    ppermute x21 -> x18, starting transfers between devices: 52.7 us -> 26.1 us  [shift(): lax.ppermute(values, axis, [(i, (i + by) % RING) for i in range(RING)])]
    pallas_call x13, Pallas kernels: 30.2 us -> 49.2 us  [with_placed(): return run(*placed)]
    unnamed x52 -> x30, local copies, waits for them, and re-layouts: 17.6 us -> 3.69 us
    all_to_all x4 -> x6, starting transfers between devices: 24.1 us -> 38 us  [exchange(): return lax.all_to_all(blocks, axes, 0, 0, tiled=True)]
    ppermute x2, waiting for transfers between devices: 0.01 us -> 8.7 us  [swap_cores(): return lax.ppermute(values, 'core', [(0, 1), (1, 0)])]
    all_to_all x4 -> x6, waiting for transfers between devices: 25.1 us -> 21.7 us  [exchange(): return lax.all_to_all(blocks, axes, 0, 0, tiled=True)]
    ppermute x21 -> x18, waiting for transfers between devices: 38.8 us -> 36.3 us  [shift(): lax.ppermute(values, axis, [(i, (i + by) % RING) for i in range(RING)])]
  transfers between devices with their start and end apart: 27 -> 26, of which waited for: 13 -> 15; matrix products, arithmetic and copies ran while one was open for 7% -> 6% of each run, Pallas kernels for 7% -> 12%
where the time goes in v4:
time: 199 us; the launch traced here: 198 us
  waiting for transfers between devices  66.8 us (34%)
  starting transfers between devices  64 us (32%)
  Pallas kernels  49.2 us (25%)
  matrix products  11.2 us (6%)
  local copies, waits for them, and re-layouts  4.75 us (2%)
    pallas_call x13, Pallas kernels, with_placed(): return run(*placed)  49.2 us
    all_to_all x6, starting transfers between devices, exchange(): return lax.all_to_all(blocks, axes, 0, 0, tiled=True)  38 us
    ppermute x18, waiting for transfers between devices, shift(): lax.ppermute(values, axis, [(i, (i + by) % RING) for i in range(RING)])  36.3 us
    ppermute x18, starting transfers between devices, shift(): lax.ppermute(values, axis, [(i, (i + by) % RING) for i in range(RING)])  26.1 us
    all_to_all x6, waiting for transfers between devices, exchange(): return lax.all_to_all(blocks, axes, 0, 0, tiled=True)  21.7 us
    dot_general x3, matrix products, dot(): lax.dot_general(left, right, (((left_dim,), (right_dim,)), ((), ())), pre...  11.2 us
    ppermute x2, waiting for transfers between devices, swap_cores(): return lax.ppermute(values, 'core', [(0, 1), (1, 0)])  8.7 us
  transfers between devices with their start and end apart: 26, of which 15 were waited for; matrix products, arithmetic and copies ran while one was open for 6% of the time, Pallas kernels for 12%

profile of v4, /device:TPU:8, one launch (start us, length us, event | category | flops | bytes accessed | tf_op | source)
XLA Modules:
  0.0 198.0 jit_solution(9716090672350586970)
XLA Ops:
  0.6 8.1 %key_value.1 = (bf16[10,128,112]{2,1,0:T(8,128)(2,1)}, bf16[10,128,112]{2,1,0:T(8,128)(2,1)}, f32[32,45,112]{2,1,0:T(8,128)}) custom-call(bf16[128,2240]{1,0:T(8,128)(2,1)} %bitcast.15, bf16[2240,1120]{1,0:T(8,128)(2,1)} %key_weight.1, bf16[2240,1120]{1,0:T(8,128)(2,1)} %value_weight.1), custom_call_target="tpu_custom_call" | custom-call | tf_op jit(solution)/shard_map/key_value/pallas_call | solution.py:64
  8.8 8.2 %all-to-all-start = ((f32[32,45,112]{2,1,0:T(8,128)}), f32[32,45,112]{2,1,0:T(8,128)S(1)}, u32[]{:S(2)}, u32[]{:S(2)}) async-start(f32[32,45,112]{2,1,0:T(8,128)} %get-tuple-element.69), calls=%async_computation | async-start | bytes 1572864 | tf_op jit(solution)/shard_map/all_to_all | solution.py:324
  21.2 4.4 %query.1.refs_1_ = bf16[10,128,112]{2,1,0:T(8,128)(2,1)} custom-call(bf16[128,2240]{1,0:T(8,128)(2,1)} %bitcast.17, bf16[2240,1120]{1,0:T(8,128)(2,1)} %weight.1), custom_call_target="tpu_custom_call" | custom-call | tf_op jit(solution)/shard_map/query/pallas_call | solution.py:64
  25.6 5.8 %all-to-all-done.refs_0_ = f32[32,45,112]{2,1,0:T(8,128)S(1)} async-done(((f32[32,45,112]{2,1,0:T(8,128)}), f32[32,45,112]{2,1,0:T(8,128)S(1)}, u32[]{:S(2)}, u32[]{:S(2)}) %all-to-all-start) | async-done | bytes 645152 | tf_op jit(solution)/shard_map/all_to_all | solution.py:324
  31.5 3.5 %numerator.1 = (f32[32,70,112]{2,1,0:T(8,128)}, bf16[10,128,112]{2,1,0:T(8,128)(2,1)}, f32[10,112]{1,0:T(8,128)}) custom-call(f32[32,45,112]{2,1,0:T(8,128)S(1)} %all-to-all-done.refs_0_, bf16[10,128,112]{2,1,0:T(8,128)(2,1)} %query.1.refs_1_, bf16[128,1120]{1,0:T(8,128)(2,1)} %bitcast.18), custom_call_target="tpu_custom_call" | custom-call | tf_op jit(solution)/shard_map/numerator/pallas_call | solution.py:64
  35.9 7.3 %all-to-all-start.1 = ((f32[32,70,112]{2,1,0:T(8,128)}), f32[32,70,112]{2,1,0:T(8,128)S(1)}, u32[]{:S(2)}, u32[]{:S(2)}) async-start(f32[32,70,112]{2,1,0:T(8,128)} %get-tuple-element.74), calls=%async_computation.1 | async-start | bytes 2359296 | tf_op jit(solution)/shard_map/all_to_all | solution.py:324
  47.3 14.7 %all-to-all-done.1.refs_0_.got = f32[32,70,112]{2,1,0:T(8,128)S(1)} async-done(((f32[32,70,112]{2,1,0:T(8,128)}), f32[32,70,112]{2,1,0:T(8,128)S(1)}, u32[]{:S(2)}, u32[]{:S(2)}) %all-to-all-start.1) | async-done | bytes 1003552 | tf_op jit(solution)/shard_map/all_to_all | solution.py:324
  61.9 3.6 %total_grad.1 = (f32[32,45,112]{2,1,0:T(8,128)}, f32[128,10]{1,0:T(8,128)}) custom-call(f32[32,70,112]{2,1,0:T(8,128)S(1)} %all-to-all-done.1.refs_0_.got, bf16[10,128,112]{2,1,0:T(8,128)(2,1)} %query.1.refs_1_, bf16[128,1120]{1,0:T(8,128)(2,1)} %bitcast.19, f32[10,112]{1,0:T(8,128)} %get-tuple-element.76.refs_3_.total), custom_call_target="tpu_custom_call" | custom-call | tf_op jit(solution)/shard_map/total_grad/pallas_call | solution.py:64
  66.4 4.6 %collective-permute-done.2.refs_4_ = f32[1120,128]{1,0:T(8,128)} collective-permute-done((f32[1120,128]{1,0:T(8,128)S(1)}, f32[1120,128]{1,0:T(8,128)}, u32[]{:S(2)}, u32[]{:S(2)}) %collective-permute-start.2) | collective-permute-done | bytes 573472 | tf_op jit(solution)/shard_map/ppermute | solution.py:328
  72.0 7.3 %all-to-all-start.2 = ((f32[32,45,112]{2,1,0:T(8,128)}), f32[32,45,112]{2,1,0:T(8,128)S(1)}, u32[]{:S(2)}, u32[]{:S(2)}) async-start(f32[32,45,112]{2,1,0:T(8,128)} %get-tuple-element.84), calls=%async_computation.2 | async-start | bytes 1572864 | tf_op jit(solution)/shard_map/all_to_all | solution.py:324
  79.3 2.9 %query_grad.1 = (bf16[128,1120]{1,0:T(8,128)(2,1)}, f32[128,256]{1,0:T(8,128)}, f32[128,256]{1,0:T(8,128)}, f32[128,256]{1,0:T(8,128)}, f32[128,256]{1,0:T(8,128)}, /*index=5*/f32[4,128,24]{2,1,0:T(8,128)}) custom-call(s32[1]{0:T(128)} %bitcast.place, f32[32,70,112]{2,1,0:T(8,128)S(1)} %all-to-all-done.1.refs_0_.got, bf16[10,128,112]{2,1,0:T(8,128)(2,1)} %query.1.refs_1_, ...), custom_call_target="tpu_custom_call" | custom-call | tf_op jit(solution)/shard_map/query_grad/pallas_call | solution.py:64
  85.0 2.3 %collective-permute-start.8 = (f32[128,256]{1,0:T(8,128)}, f32[128,256]{1,0:T(8,128)S(1)}, u32[]{:S(2)}, u32[]{:S(2)}) collective-permute-start(f32[128,256]{1,0:T(8,128)} %get-tuple-element.92), channel_id=1, source_target_pairs={{0,96},{32,0},{64,32},{96,64},{1,97},{33,1},{65,33},{97,65},{2,98}... | collective-permute-start | bytes 393224 | tf_op jit(solution)/shard_map/ppermute | solution.py:328
  88.3 3.5 %join.1.refs_1_ = bf16[2240,512]{1,0:T(8,128)(2,1)} custom-call(f32[1120,128]{1,0:T(8,128)} %get-tuple-element.83.refs_0_, f32[1120,128]{1,0:T(8,128)} %get-tuple-element.82.refs_1_, f32[1120,128]{1,0:T(8,128)S(1)} %collective-permute-done.refs_2_, f32[1120,128]{1,0:T(8,128)S(1)} %copy-done.1, f32[1120,128]{1,0:T(8,128)} %collective-permute-done.2.refs_4_, ...), custom_call_target="tpu_custom_call" | custom-call | tf_op jit(solution)/shard_map/join/pallas_call | solution.py:64
  93.1 3.6 %weight_grad.2 = (f32[16,72,256]{2,1,0:T(8,128)}, f32[16,72,256]{2,1,0:T(8,128)}) custom-call(s32[1]{0:T(128)} %bitcast.3.refs_0_, bf16[2240,512]{1,0:T(8,128)(2,1)} %join.1.refs_1_, f32[128,256]{1,0:T(8,128)} %get-tuple-element.89.refs_2_, f32[128,256]{1,0:T(8,128)S(1)} %collective-permute-done.6.refs_3_, f32[128,256]{1,0:T(8,128)S(1)} %collective-permute-done.7.refs_4_, ...), custom_call_target="tpu_custom_call" | custom-call | tf_op jit(solution)/shard_map/weight_grad/pallas_call | solution.py:64
  96.7 4.0 %key_value_grad.1 = (bf16[128,1120]{1,0:T(8,128)(2,1)}, bf16[128,1120]{1,0:T(8,128)(2,1)}, f32[128,584]{1,0:T(8,128)}, f32[128,584]{1,0:T(8,128)}, f32[128,584]{1,0:T(8,128)}, /*index=5*/f32[128,584]{1,0:T(8,128)}) custom-call(s32[1]{0:T(128)} %bitcast.place, f32[32,45,112]{2,1,0:T(8,128)S(1)} %all-to-all-done.2.got, ...), custom_call_target="tpu_custom_call" | custom-call | tf_op jit(solution)/shard_map/key_value_grad/pallas_call | solution.py:64
  100.6 3.1 %collective-permute-done.9 = f32[16,72,256]{2,1,0:T(8,128)S(1)} collective-permute-done((f32[16,72,256]{2,1,0:T(8,128)}, f32[16,72,256]{2,1,0:T(8,128)S(1)}, u32[]{:S(2)}, u32[]{:S(2)}) %collective-permute-start.9) | collective-permute-done | bytes 1179680 | tf_op jit(solution)/shard_map/ppermute | solution.py:336
  104.9 7.1 %all-to-all-start.3 = ((f32[16,72,256]{2,1,0:T(8,128)}), f32[16,72,256]{2,1,0:T(8,128)S(1)}, u32[]{:S(2)}, u32[]{:S(2)}) async-start(f32[16,72,256]{2,1,0:T(8,128)} %add.14), calls=%async_computation.3 | async-start | bytes 2359296 | tf_op jit(solution)/shard_map/all_to_all | solution.py:324
  116.5 6.2 %collective-permute-done.10.refs_3_ = f32[128,584]{1,0:T(8,128)S(1)} collective-permute-done((f32[128,584]{1,0:T(8,128)S(1)}, f32[128,584]{1,0:T(8,128)S(1)}, u32[]{:S(2)}, u32[]{:S(2)}) %collective-permute-start.10) | collective-permute-done | bytes 299040 | tf_op jit(solution)/shard_map/ppermute | solution.py:328
  122.7 2.7 %collective-permute-done.11.refs_4_ = f32[128,584]{1,0:T(8,128)S(1)} collective-permute-done((f32[128,584]{1,0:T(8,128)S(1)}, f32[128,584]{1,0:T(8,128)S(1)}, u32[]{:S(2)}, u32[]{:S(2)}) %collective-permute-start.11) | collective-permute-done | bytes 299040 | tf_op jit(solution)/shard_map/ppermute | solution.py:328
  125.4 5.5 %collective-permute-done.12.refs_5_ = f32[128,584]{1,0:T(8,128)S(1)} collective-permute-done((f32[128,584]{1,0:T(8,128)S(1)}, f32[128,584]{1,0:T(8,128)S(1)}, u32[]{:S(2)}, u32[]{:S(2)}) %collective-permute-start.12) | collective-permute-done | bytes 299040 | tf_op jit(solution)/shard_map/ppermute | solution.py:328
  132.1 5.3 %weight_grad.3 = (f32[16,72,584]{2,1,0:T(8,128)}, f32[16,72,584]{2,1,0:T(8,128)}) custom-call(s32[1]{0:T(128)} %bitcast.3.refs_0_, bf16[2240,512]{1,0:T(8,128)(2,1)} %join.1.refs_1_, f32[128,584]{1,0:T(8,128)} %get-tuple-element.113.refs_2_, f32[128,584]{1,0:T(8,128)S(1)} %collective-permute-done.10.refs_3_, f32[128,584]{1,0:T(8,128)S(1)} %collective-permute-done.11.refs_4_, ...), custom_call_target="tpu_custom_call" | custom-call | tf_op jit(solution)/shard_map/weight_grad/pallas_call | solution.py:64
  137.5 5.6 %collective-permute-done.13.got = f32[16,72,584]{2,1,0:T(8,128)} collective-permute-done((f32[16,72,584]{2,1,0:T(8,128)}, f32[16,72,584]{2,1,0:T(8,128)}, u32[]{:S(2)}, u32[]{:S(2)}) %collective-permute-start.13) | collective-permute-done | bytes 2691104 | tf_op jit(solution)/shard_map/ppermute | solution.py:336
  143.1 4.5 %first_stage.1 = (f32[4,40,584]{2,1,0:T(8,128)}, f32[4,40,584]{2,1,0:T(8,128)}, f32[4,40,584]{2,1,0:T(8,128)}, f32[4,40,584]{2,1,0:T(8,128)}, f32[4,4,32,584]{3,2,1,0:T(8,128)}) custom-call(s32[2]{0:T(128)S(1)} %pad_add_fusion.spot, f32[16,72,584]{2,1,0:T(8,128)} %get-tuple-element.117.kept, f32[16,72,584]{2,1,0:T(8,128)} %collective-permute-done.13.got), custom_call_target="tpu_custom_call" | custom-call | tf_op jit(solution)/shard_map/first_stage/pallas_call | solution.py:64
  147.6 3.7 %all-to-all-start.4 = ((f32[4,4,32,584]{3,2,1,0:T(8,128)}), f32[4,4,32,584]{3,2,1,0:T(8,128)S(1)}, u32[]{:S(2)}, u32[]{:S(2)}) async-start(f32[4,4,32,584]{3,2,1,0:T(8,128)} %get-tuple-element.123), calls=%async_computation.4 | async-start | bytes 2621440 | tf_op jit(solution)/shard_map/all_to_all | solution.py:324
  151.3 4.2 %fusion.1 = f32[128,2240]{0,1:T(8,128)S(1)} fusion(bf16[128,1120]{1,0:T(8,128)(2,1)S(1)} %copy-done.5, bf16[2240,1120]{1,0:T(8,128)(2,1)} %weight.1), kind=kOutput, calls=%fused_computation.4 | convolution fusion | flops 642252800 | bytes 6451200 | tf_op jit(solution)/shard_map/dot_general | solution.py:70
  156.7 2.7 %collective-permute-start.15 = (f32[4,40,584]{2,1,0:T(8,128)S(1)}, f32[4,40,584]{2,1,0:T(8,128)S(1)}, u32[]{:S(2)}, u32[]{:S(2)}) collective-permute-start(f32[4,40,584]{2,1,0:T(8,128)S(1)} %copy-done.8), channel_id=1, source_target_pairs={{0,4},{2,6},{4,0},{6,2},{1,5},{3,7},{5,1},{7,3},{8,12},{10,14},{12... | collective-permute-start | bytes 1121288 | tf_op jit(solution)/shard_map/ppermute | solution.py:328
  160.8 2.6 %convolution_add_fusion.1 = f32[128,2240]{0,1:T(8,128)} fusion(f32[128,2240]{0,1:T(8,128)S(1)} %fusion.1, bf16[128,1120]{1,0:T(8,128)(2,1)S(1)} %copy-done.6, bf16[2240,1120]{1,0:T(8,128)(2,1)S(1)} %bitcast.14), kind=kOutput, calls=%fused_computation.1 | convolution fusion | flops 642539520 | bytes 7598080 | tf_op jit(solution)/shard_map/dot_general | solution.py:70
  163.5 5.7 %collective-permute-done.14.refs_1_ = f32[4,40,584]{2,1,0:T(8,128)S(1)} collective-permute-done((f32[4,40,584]{2,1,0:T(8,128)S(1)}, f32[4,40,584]{2,1,0:T(8,128)S(1)}, u32[]{:S(2)}, u32[]{:S(2)}) %collective-permute-start.14) | collective-permute-done | bytes 373792 | tf_op jit(solution)/shard_map/ppermute | solution.py:328
  169.2 8.1 %collective-permute-done.15.refs_2_ = f32[4,40,584]{2,1,0:T(8,128)S(1)} collective-permute-done((f32[4,40,584]{2,1,0:T(8,128)S(1)}, f32[4,40,584]{2,1,0:T(8,128)S(1)}, u32[]{:S(2)}, u32[]{:S(2)}) %collective-permute-start.15) | collective-permute-done | bytes 373792 | tf_op jit(solution)/shard_map/ppermute | solution.py:328
  181.4 4.5 %all-to-all-start.5 = ((f32[4,40,584]{2,1,0:T(8,128)}), f32[4,40,584]{2,1,0:T(8,128)S(1)}, u32[]{:S(2)}, u32[]{:S(2)}) async-start(f32[4,40,584]{2,1,0:T(8,128)} %get-tuple-element.128), calls=%async_computation.5 | async-start | bytes 819200 | tf_op jit(solution)/shard_map/all_to_all | solution.py:324
  187.6 2.4 %collective-permute-start.18 = (f32[32,584]{1,0:T(8,128)}, f32[32,584]{1,0:T(8,128)S(1)}, u32[]{:S(2)}, u32[]{:S(2)}) collective-permute-start(f32[32,584]{1,0:T(8,128)} %get-tuple-element.126), channel_id=1, source_target_pairs={{0,4},{2,6},{4,0},{6,2},{1,5},{3,7},{5,1},{7,3},{8,12},{10,14},{12... | collective-permute-start | bytes 224264 | tf_op jit(solution)/shard_map/ppermute | solution.py:328
  190.9 4.4 %fusion = bf16[128,2240]{0,1:T(8,128)(2,1)S(1)} fusion(f32[128,2240]{0,1:T(8,128)} %convolution_add_fusion.1, bf16[128,1120]{1,0:T(8,128)(2,1)} %get-tuple-element.100, bf16[2240,1120]{1,0:T(8,128)(2,1)} %value_weight.1), kind=kOutput, calls=%fused_computation.2 | convolution fusion | flops 642826240 | bytes 7024640 | tf_op jit(solution)/shard_map/dot_general | solution.py:70
  (70 shorter events, 35.3 us)
Async XLA Ops:
  8.8 22.7 %all-to-all-start = ((f32[32,45,112]{2,1,0:T(8,128)}), f32[32,45,112]{2,1,0:T(8,128)S(1)}, u32[]{:S(2)}, u32[]{:S(2)}) async-start(f32[32,45,112]{2,1,0:T(8,128)} %get-tuple-element.69), calls=%async_computation | async-start | bytes 1572864 | tf_op jit(solution)/shard_map/all_to_all | solution.py:324
  19.2 15.8 %collective-permute-start = (f32[1120,128]{1,0:T(8,128)}, f32[1120,128]{1,0:T(8,128)S(1)}, u32[]{:S(2)}, u32[]{:S(2)}) collective-permute-start(f32[1120,128]{1,0:T(8,128)} %get-tuple-element.83.refs_0_), channel_id=1, source_target_pairs={{0,32},{32,64},{64,96},{96,0},{1,33},{33,65},{65,97},{97,1},{2,34}... | collective-permute-start | bytes 1720328 | tf_op jit(solution)/shard_map/ppermute | solution.py:328
  20.8 15.1 %collective-permute-start.1 = (f32[1120,128]{1,0:T(8,128)}, f32[1120,128]{1,0:T(8,128)S(1)}, u32[]{:S(2)}, u32[]{:S(2)}) collective-permute-start(f32[1120,128]{1,0:T(8,128)} %get-tuple-element.82.refs_1_), channel_id=1, source_target_pairs={{0,96},{32,0},{64,32},{96,64},{1,97},{33,1},{65,33},{97,65},{2,98}... | collective-permute-start | bytes 1720328 | tf_op jit(solution)/shard_map/ppermute | solution.py:328
  35.9 26.1 %all-to-all-start.1 = ((f32[32,70,112]{2,1,0:T(8,128)}), f32[32,70,112]{2,1,0:T(8,128)S(1)}, u32[]{:S(2)}, u32[]{:S(2)}) async-start(f32[32,70,112]{2,1,0:T(8,128)} %get-tuple-element.74), calls=%async_computation.1 | async-start | bytes 2359296 | tf_op jit(solution)/shard_map/all_to_all | solution.py:324
  43.1 22.4 %collective-permute-start.4 = (f32[1120,128]{1,0:T(8,128)}, f32[1120,128]{1,0:T(8,128)S(1)}, u32[]{:S(2)}, u32[]{:S(2)}) collective-permute-start(f32[1120,128]{1,0:T(8,128)} %get-tuple-element.82.refs_1_), channel_id=1, source_target_pairs={{0,32},{32,64},{64,96},{96,0},{1,33},{33,65},{65,97},{97,1},{2,34}... | collective-permute-start | bytes 1720328 | tf_op jit(solution)/shard_map/ppermute | solution.py:328
  44.5 21.9 %collective-permute-start.5 = (f32[1120,128]{1,0:T(8,128)}, f32[1120,128]{1,0:T(8,128)}, u32[]{:S(2)}, u32[]{:S(2)}) collective-permute-start(f32[1120,128]{1,0:T(8,128)} %get-tuple-element.83.refs_0_), channel_id=1, source_target_pairs={{0,96},{32,0},{64,32},{96,64},{1,97},{33,1},{65,33},{97,65},{2,98}... | collective-permute-start | bytes 1720328 | tf_op jit(solution)/shard_map/ppermute | solution.py:328
  45.2 25.7 %collective-permute-start.2 = (f32[1120,128]{1,0:T(8,128)S(1)}, f32[1120,128]{1,0:T(8,128)}, u32[]{:S(2)}, u32[]{:S(2)}) collective-permute-start(f32[1120,128]{1,0:T(8,128)S(1)} %collective-permute-done.refs_2_), channel_id=1, source_target_pairs={{0,32},{32,64},{64,96},{96,0},{1,33},{33,65},{65,97},{97,1},{2,34}... | collective-permute-start | bytes 1720328 | tf_op jit(solution)/shard_map/ppermute | solution.py:328
  46.5 25.5 %collective-permute-start.3 = (f32[1120,128]{1,0:T(8,128)S(1)}, f32[1120,128]{1,0:T(8,128)}, u32[]{:S(2)}, u32[]{:S(2)}) collective-permute-start(f32[1120,128]{1,0:T(8,128)S(1)} %collective-permute-done.1.refs_7_), channel_id=1, source_target_pairs={{0,96},{32,0},{64,32},{96,64},{1,97},{33,1},{65,33},{97,65},{2,98}... | collective-permute-start | bytes 1720328 | tf_op jit(solution)/shard_map/ppermute | solution.py:328
  72.0 24.7 %all-to-all-start.2 = ((f32[32,45,112]{2,1,0:T(8,128)}), f32[32,45,112]{2,1,0:T(8,128)S(1)}, u32[]{:S(2)}, u32[]{:S(2)}) async-start(f32[32,45,112]{2,1,0:T(8,128)} %get-tuple-element.84), calls=%async_computation.2 | async-start | bytes 1572864 | tf_op jit(solution)/shard_map/all_to_all | solution.py:324
  82.1 9.7 %collective-permute-start.6 = (f32[128,256]{1,0:T(8,128)}, f32[128,256]{1,0:T(8,128)S(1)}, u32[]{:S(2)}, u32[]{:S(2)}) collective-permute-start(f32[128,256]{1,0:T(8,128)} %get-tuple-element.90), channel_id=1, source_target_pairs={{0,32},{32,64},{64,96},{96,0},{1,33},{33,65},{65,97},{97,1},{2,34}... | collective-permute-start | bytes 393224 | tf_op jit(solution)/shard_map/ppermute | solution.py:328
  83.6 8.2 %collective-permute-start.7 = (f32[128,256]{1,0:T(8,128)}, f32[128,256]{1,0:T(8,128)S(1)}, u32[]{:S(2)}, u32[]{:S(2)}) collective-permute-start(f32[128,256]{1,0:T(8,128)} %get-tuple-element.91), channel_id=1, source_target_pairs={{0,64},{32,96},{64,0},{96,32},{1,65},{33,97},{65,1},{97,33},{2,66}... | collective-permute-start | bytes 393224 | tf_op jit(solution)/shard_map/ppermute | solution.py:328
  85.0 8.1 %collective-permute-start.8 = (f32[128,256]{1,0:T(8,128)}, f32[128,256]{1,0:T(8,128)S(1)}, u32[]{:S(2)}, u32[]{:S(2)}) collective-permute-start(f32[128,256]{1,0:T(8,128)} %get-tuple-element.92), channel_id=1, source_target_pairs={{0,96},{32,0},{64,32},{96,64},{1,97},{33,1},{65,33},{97,65},{2,98}... | collective-permute-start | bytes 393224 | tf_op jit(solution)/shard_map/ppermute | solution.py:328
  100.6 3.1 %collective-permute-start.9 = (f32[16,72,256]{2,1,0:T(8,128)}, f32[16,72,256]{2,1,0:T(8,128)S(1)}, u32[]{:S(2)}, u32[]{:S(2)}) collective-permute-start(f32[16,72,256]{2,1,0:T(8,128)} %get-tuple-element.107), channel_id=1, source_target_pairs={{0,8},{8,0},{1,9},{9,1},{2,10},{10,2},{3,11},{11,3},{4,12},{12,4},... | collective-permute-start | bytes 3538952 | tf_op jit(solution)/shard_map/ppermute | solution.py:336
  104.9 8.3 %copy-start.11 = (f32[128,584]{1,0:T(8,128)S(1)}, f32[128,584]{1,0:T(8,128)}, u32[]{:S(2)}) copy-start(f32[128,584]{1,0:T(8,128)} %get-tuple-element.110) | copy-start | bytes 897028
  104.9 10.1 %copy-start.10 = (f32[128,584]{1,0:T(8,128)S(1)}, f32[128,584]{1,0:T(8,128)}, u32[]{:S(2)}) copy-start(f32[128,584]{1,0:T(8,128)} %get-tuple-element.111) | copy-start | bytes 897028
  104.9 27.2 %all-to-all-start.3 = ((f32[16,72,256]{2,1,0:T(8,128)}), f32[16,72,256]{2,1,0:T(8,128)S(1)}, u32[]{:S(2)}, u32[]{:S(2)}) async-start(f32[16,72,256]{2,1,0:T(8,128)} %add.14), calls=%async_computation.3 | async-start | bytes 2359296 | tf_op jit(solution)/shard_map/all_to_all | solution.py:324
  112.0 10.7 %collective-permute-start.10 = (f32[128,584]{1,0:T(8,128)S(1)}, f32[128,584]{1,0:T(8,128)S(1)}, u32[]{:S(2)}, u32[]{:S(2)}) collective-permute-start(f32[128,584]{1,0:T(8,128)S(1)} %copy-done.12), channel_id=1, source_target_pairs={{0,32},{32,64},{64,96},{96,0},{1,33},{33,65},{65,97},{97,1},{2,34}... | collective-permute-start | bytes 897032 | tf_op jit(solution)/shard_map/ppermute | solution.py:328
  113.2 12.2 %collective-permute-start.11 = (f32[128,584]{1,0:T(8,128)S(1)}, f32[128,584]{1,0:T(8,128)S(1)}, u32[]{:S(2)}, u32[]{:S(2)}) collective-permute-start(f32[128,584]{1,0:T(8,128)S(1)} %copy-done.11), channel_id=1, source_target_pairs={{0,64},{32,96},{64,0},{96,32},{1,65},{33,97},{65,1},{97,33},{2,66}... | collective-permute-start | bytes 897032 | tf_op jit(solution)/shard_map/ppermute | solution.py:328
  115.0 15.9 %collective-permute-start.12 = (f32[128,584]{1,0:T(8,128)S(1)}, f32[128,584]{1,0:T(8,128)S(1)}, u32[]{:S(2)}, u32[]{:S(2)}) collective-permute-start(f32[128,584]{1,0:T(8,128)S(1)} %copy-done.10), channel_id=1, source_target_pairs={{0,96},{32,0},{64,32},{96,64},{1,97},{33,1},{65,33},{97,65},{2,98}... | collective-permute-start | bytes 897032 | tf_op jit(solution)/shard_map/ppermute | solution.py:328
  137.4 5.7 %collective-permute-start.13 = (f32[16,72,584]{2,1,0:T(8,128)}, f32[16,72,584]{2,1,0:T(8,128)}, u32[]{:S(2)}, u32[]{:S(2)}) collective-permute-start(f32[16,72,584]{2,1,0:T(8,128)} %get-tuple-element.118), channel_id=1, source_target_pairs={{0,8},{8,0},{1,9},{9,1},{2,10},{10,2},{3,11},{11,3},{4,12},{12,4},... | collective-permute-start | bytes 8073224 | tf_op jit(solution)/shard_map/ppermute | solution.py:336
  147.6 30.9 %all-to-all-start.4 = ((f32[4,4,32,584]{3,2,1,0:T(8,128)}), f32[4,4,32,584]{3,2,1,0:T(8,128)S(1)}, u32[]{:S(2)}, u32[]{:S(2)}) async-start(f32[4,4,32,584]{3,2,1,0:T(8,128)} %get-tuple-element.123), calls=%async_computation.4 | async-start | bytes 2621440 | tf_op jit(solution)/shard_map/all_to_all | solution.py:324
  151.3 9.6 %slice-start = ((s8[5160960]{0:T(1024)(128)(4,1)}), s8[4194304]{0:T(1024)(128)(4,1)S(1)}, s32[]{:S(2)}) async-start(s8[5160960]{0:T(1024)(128)(4,1)} %bitcast.13), calls=%async_computation.6 | async-start | bytes 8388608
  151.3 8.1 %copy-start.7 = (f32[4,40,584]{2,1,0:T(8,128)S(1)}, f32[4,40,584]{2,1,0:T(8,128)}, u32[]{:S(2)}) copy-start(f32[4,40,584]{2,1,0:T(8,128)} %get-tuple-element.122) | copy-start | bytes 1121284
  151.3 9.5 %slice-start.1 = ((s8[5160960]{0:T(1024)(128)(4,1)}), s8[966656]{0:T(1024)(128)(4,1)S(1)}, s32[]{:S(2)}) async-start(s8[5160960]{0:T(1024)(128)(4,1)} %bitcast.13), calls=%async_computation.7 | async-start | bytes 1933312
  151.3 9.5 %copy-start.6 = (bf16[128,1120]{1,0:T(8,128)(2,1)S(1)}, bf16[128,1120]{1,0:T(8,128)(2,1)}, u32[]{:S(2)}) copy-start(bf16[128,1120]{1,0:T(8,128)(2,1)} %get-tuple-element.99) | copy-start | bytes 860164
  155.5 13.7 %collective-permute-start.14 = (f32[4,40,584]{2,1,0:T(8,128)S(1)}, f32[4,40,584]{2,1,0:T(8,128)S(1)}, u32[]{:S(2)}, u32[]{:S(2)}) collective-permute-start(f32[4,40,584]{2,1,0:T(8,128)S(1)} %copy-done.9), channel_id=1, source_target_pairs={{0,2},{2,4},{4,6},{6,0},{1,3},{3,5},{5,7},{7,1},{8,10},{10,12},{12... | collective-permute-start | bytes 1121288 | tf_op jit(solution)/shard_map/ppermute | solution.py:328
  156.7 20.6 %collective-permute-start.15 = (f32[4,40,584]{2,1,0:T(8,128)S(1)}, f32[4,40,584]{2,1,0:T(8,128)S(1)}, u32[]{:S(2)}, u32[]{:S(2)}) collective-permute-start(f32[4,40,584]{2,1,0:T(8,128)S(1)} %copy-done.8), channel_id=1, source_target_pairs={{0,4},{2,6},{4,0},{6,2},{1,5},{3,7},{5,1},{7,3},{8,12},{10,14},{12... | collective-permute-start | bytes 1121288 | tf_op jit(solution)/shard_map/ppermute | solution.py:328
  159.4 18.3 %collective-permute-start.16 = (f32[4,40,584]{2,1,0:T(8,128)S(1)}, f32[4,40,584]{2,1,0:T(8,128)S(1)}, u32[]{:S(2)}, u32[]{:S(2)}) collective-permute-start(f32[4,40,584]{2,1,0:T(8,128)S(1)} %copy-done.7), channel_id=1, source_target_pairs={{0,6},{2,0},{4,2},{6,4},{1,7},{3,1},{5,3},{7,5},{8,14},{10,8},{12,... | collective-permute-start | bytes 1121288 | tf_op jit(solution)/shard_map/ppermute | solution.py:328
  181.4 14.9 %all-to-all-start.5 = ((f32[4,40,584]{2,1,0:T(8,128)}), f32[4,40,584]{2,1,0:T(8,128)S(1)}, u32[]{:S(2)}, u32[]{:S(2)}) async-start(f32[4,40,584]{2,1,0:T(8,128)} %get-tuple-element.128), calls=%async_computation.5 | async-start | bytes 819200 | tf_op jit(solution)/shard_map/all_to_all | solution.py:324
  185.9 10.5 %collective-permute-start.17 = (f32[32,584]{1,0:T(8,128)}, f32[32,584]{1,0:T(8,128)S(1)}, u32[]{:S(2)}, u32[]{:S(2)}) collective-permute-start(f32[32,584]{1,0:T(8,128)} %get-tuple-element.125), channel_id=1, source_target_pairs={{0,2},{2,4},{4,6},{6,0},{1,3},{3,5},{5,7},{7,1},{8,10},{10,12},{12... | collective-permute-start | bytes 224264 | tf_op jit(solution)/shard_map/ppermute | solution.py:328
  187.6 8.8 %collective-permute-start.18 = (f32[32,584]{1,0:T(8,128)}, f32[32,584]{1,0:T(8,128)S(1)}, u32[]{:S(2)}, u32[]{:S(2)}) collective-permute-start(f32[32,584]{1,0:T(8,128)} %get-tuple-element.126), channel_id=1, source_target_pairs={{0,4},{2,6},{4,0},{6,2},{1,5},{3,7},{5,1},{7,3},{8,12},{10,14},{12... | collective-permute-start | bytes 224264 | tf_op jit(solution)/shard_map/ppermute | solution.py:328
  190.0 6.4 %collective-permute-start.19 = (f32[32,584]{1,0:T(8,128)}, f32[32,584]{1,0:T(8,128)S(1)}, u32[]{:S(2)}, u32[]{:S(2)}) collective-permute-start(f32[32,584]{1,0:T(8,128)} %get-tuple-element.127), channel_id=1, source_target_pairs={{0,6},{2,0},{4,2},{6,4},{1,7},{3,1},{5,3},{7,5},{8,14},{10,8},{12,... | collective-permute-start | bytes 224264 | tf_op jit(solution)/shard_map/ppermute | solution.py:328
  (9 other events, 31.1 us)

commit v5 on v4

--- a/solution.py
+++ b/solution.py
@@ -17,7 +17,6 @@
 CORES = 2
 ROWS = D // TILES
 PADDED_ROWS = 72
-SPLIT = 40
 REPLICAS = 4
 RING = 4
 COLS = HW // REPLICAS
@@ -35,6 +34,7 @@
 BF16 = jnp.bfloat16
 BLOCK = pl.BlockSpec()
 IN_SMEM = pl.BlockSpec(memory_space=pltpu.SMEM)
+ANYWHERE = pl.BlockSpec(memory_space=pl.ANY)
 IN_HBM = pl.BlockSpec(memory_space=pltpu.HBM)
 
 
@@ -269,7 +269,7 @@
         out[rows : rows + D // 2, at] = half[...].astype(BF16)
 
 
-def weight_grad_kernel(normalizer, core, tokens, own, first, second, third, kept, sent, columns):
+def weight_grad_kernel(normalizer, core, tokens, own, first, second, third, after, kept, sent, columns):
     for slot, block in enumerate((own, first, second, third)):
         columns[slot * TOKENS : (slot + 1) * TOKENS, :] = block[...].astype(BF16)
     right = columns[...]
@@ -282,42 +282,29 @@
                 out[half * span + index, :ROWS, :] = product[index * ROWS : (index + 1) * ROWS]
 
 
-def first_stage_kernel(spot, kept, got, *outs):
-    for slot in range(RING):
+def first_stage_kernel(spot, kept, got, after, *outs):
+    for slot, out in enumerate(outs):
         across = lax.rem(spot[0] + slot, RING)
         for other in range(RING):
             at = (other // 2) * (2 * RING) + across * 2 + other % 2
-            outs[slot][other] = kept[at, :SPLIT, :] + got[at, :SPLIT, :]
-            at = (slot // 2) * (2 * RING) + other * 2 + slot % 2
-            outs[RING][slot, other] = kept[at, SPLIT:, :] + got[at, SPLIT:, :]
-
-
-def second_stage_kernel(spot, *refs):
-    uppers, lowers, outs = refs[:RING], refs[RING], refs[RING + 1 :]
-    for slot in range(RING):
-        outs[RING][slot] = sum_at(uppers, slot)
-        across = lax.rem(spot[0] + slot, RING)
-        outs[slot][...] = (lowers[0, across] + lowers[1, across]) + (
-            lowers[2, across] + lowers[3, across]
-        )
-
-
-def sum_at(refs, at):
-    return (refs[0][at] + refs[1][at]) + (refs[2][at] + refs[3][at])
-
-
-def last_kernel(query, *refs):
-    lowers, uppers, query_out, key_out, value_out = refs[:RING], *refs[RING:]
-    total = query[0]
+            out[other] = kept[at] + got[at]
+
+
+def second_stage_kernel(spot, own, first, second, third, *outs):
+    for slot, out in enumerate(outs):
+        along = lax.rem(spot[1] + slot, RING)
+        out[...] = (own[along] + first[along]) + (second[along] + third[along])
+
+
+def last_kernel(key_value, own, first, second, third, query_out, key_out, value_out):
+    total = key_value[0]
     for index in range(1, PLANE_SIZE):
-        total = total + query[index]
+        total = total + key_value[index]
+    key_out[...] = total[:ROWS, :COLS]
+    value_out[...] = total[:ROWS, COLS : 2 * COLS]
+    query_out[:, EARLY:] = total[:ROWS, 2 * COLS :]
+    total = (own[...] + first[...]) + (second[...] + third[...])
     query_out[:, :EARLY] = total[:ROWS]
-    upper = (uppers[0] + uppers[1]) + (uppers[2] + uppers[3])
-    lower = (lowers[0][...] + lowers[1][...]) + (lowers[2][...] + lowers[3][...])
-    for total, rows, size in ((upper, 0, SPLIT), (lower, SPLIT, ROWS - SPLIT)):
-        key_out[rows : rows + size, :] = total[:size, :COLS]
-        value_out[rows : rows + size, :] = total[:size, COLS : 2 * COLS]
-        query_out[rows : rows + size, EARLY:] = total[:size, 2 * COLS :]
 
 
 def exchange(blocks, axes):
@@ -383,7 +370,7 @@
         [shaped((TILES, 2 * PART, HD)), heads, shaped((HEADS, HD))],
         [BLOCK] * 3,
         [state],
-        arrived=(0,),
+        arrived=(0, 1, 2),
     )(got, query, upstream)
     sent, left_top, right_bottom, later_top, later_bottom = lax.optimization_barrier(
         (sent, left_top, right_bottom, top, bottom)
@@ -399,7 +386,7 @@
         [shaped((TILES, PART + HEADS, HD)), shaped((TOKENS, HEADS))],
         [BLOCK] * 4,
         [state, totals],
-        arrived=(0,),
+        arrived=(0, 1, 2, 3),
     )(got_state, query, upstream, total)
     sent, far_top, far_bottom, left_bottom, right_top = lax.optimization_barrier(
         (sent, far_top, far_bottom, left_bottom, right_top)
@@ -419,21 +406,20 @@
     (all_tokens,) = call(
         join_kernel, "join", [shaped((D, REPLICAS * TOKENS), BF16)], [BLOCK] * 8, arrived=(2, 3, 4, 5, 6, 7)
     )(top, bottom, left_top, left_bottom, far_top, far_bottom, right_top, right_bottom)
-    def partial_products(columns):
+    def partial_products(all_tokens, columns, after):
         width = columns[0].shape[1]
         half = shaped((PLANE_SIZE, PADDED_ROWS, width))
         return call(
             lambda *refs: weight_grad_kernel(normalizer, *refs),
             "weight_grad",
             [half, half],
-            [IN_SMEM] + [BLOCK] * 5,
+            [IN_SMEM] + [BLOCK] * 5 + [ANYWHERE],
             [pltpu.VMEM((REPLICAS * TOKENS, width), BF16)],
             vmem=24,
-            arrived=(3, 4, 5),
-        )(core, all_tokens, *columns)
-
-    query_kept, query_given = partial_products(query_columns)
-    got, query_kept, query_given = lax.optimization_barrier((got, query_kept, query_given))
+            arrived=(3, 4, 5, 6),
+        )(core, all_tokens, *columns, after)
+
+    got, all_tokens, query_columns = lax.optimization_barrier((got, all_tokens, query_columns))
 
     block = shaped((TOKENS, WIDE))
     grad_key, grad_value, *key_value_columns = call(
@@ -442,40 +428,34 @@
         [flat, flat, block, block, block, block],
         [IN_SMEM] + [BLOCK] * 4,
         [state, wide, wide, blocks],
-        arrived=(1,),
+        arrived=(1, 2, 3, 4),
     )(place, got, key, value, late)
-    key_value_columns, query_given = lax.optimization_barrier((key_value_columns, query_given))
     key_value_columns = shifted(key_value_columns, "dp")
 
-    query_out = exchange(query_kept + swap_cores(query_given), PLANE)
-    query_out, key_value_columns = lax.optimization_barrier((query_out, key_value_columns))
-
-    kept, given = partial_products(key_value_columns)
+    query_kept, query_given = partial_products(all_tokens, query_columns, key_value_columns[1])
+    query_got = swap_cores(query_given)
+    kept, given = partial_products(all_tokens, key_value_columns, place)
     got = swap_cores(given)
-    rest = PADDED_ROWS - SPLIT
-    *uppers, lowers = call(
+    slots = call(
         first_stage_kernel,
         "first_stage",
-        [shaped((RING, SPLIT, WIDE))] * RING + [shaped((RING, RING, rest, WIDE))],
-        [IN_SMEM, BLOCK, BLOCK],
-        vmem=24,
-        arrived=(2,),
-    )(spot, kept, got)
-    lowers = exchange(lowers, ("zh", "zl"))
-    uppers = shifted(uppers, "x")
-    *lowers, uppers = call(
+        [shaped((RING, PADDED_ROWS, EARLY))] * RING,
+        [IN_SMEM, BLOCK, BLOCK, ANYWHERE],
+        arrived=(2, 3),
+    )(spot, query_kept, query_got, given)
+    key_value_out = exchange(kept + got, PLANE)
+    slots = call(
         second_stage_kernel,
         "second_stage",
-        [shaped((rest, WIDE))] * RING + [shaped((RING, SPLIT, WIDE))],
-        [IN_SMEM] + [BLOCK] * (RING + 1),
-        arrived=(2, 3, 4, 5),
-    )(spot, *uppers, lowers)
-    uppers = exchange(uppers, ("zh", "zl"))
-    lowers = shifted(lowers, "x")
+        [shaped((PADDED_ROWS, EARLY))] * RING,
+        [IN_SMEM] + [BLOCK] * RING,
+        arrived=(2, 3, 4),
+    )(spot, *shifted(slots, "x"))
+    slots = shifted(slots, ("zh", "zl"))
     block = shaped((ROWS, COLS))
     query_out, key_out, value_out = call(
-        last_kernel, "last", [block] * 3, [BLOCK] * (RING + 2), arrived=(0, 2, 3, 4, 5)
-    )(query_out, *lowers, uppers)
+        last_kernel, "last", [block] * 3, [BLOCK] * 5, arrived=(0, 2, 3, 4)
+    )(key_value_out, *slots)
 
     summed = back_project(grad_query, query_weight) + back_project(grad_key, key_weight)
     summed = summed + back_project(grad_value, value_weight)

time: 199 us -> 204 us (1.025)
  waiting for transfers between devices: 66.8 us -> 81.2 us
  starting transfers between devices: 64 us -> 57.2 us
  Pallas kernels: 49.2 us -> 44.2 us
  other arithmetic: 1.29 us -> 3.82 us
    ppermute x18, waiting for transfers between devices: 36.3 us -> 54.5 us  [shift(): lax.ppermute(values, axis, [(i, (i + by) % RING) for i in range(RING)])]
    all_to_all x6 -> x4, starting transfers between devices: 38 us -> 29.1 us  [exchange(): return lax.all_to_all(blocks, axes, 0, 0, tiled=True)]
    pallas_call x13, Pallas kernels: 49.2 us -> 44.2 us  [with_placed(): return run(*placed)]
    ppermute x2, waiting for transfers between devices: 8.7 us -> 5.59 us  [swap_cores(): return lax.ppermute(values, 'core', [(0, 1), (1, 0)])]
    add x1, other arithmetic: 1.21 us -> 3.74 us  [body(): key_value_out = exchange(kept + got, PLANE)]
    all_to_all x6 -> x4, waiting for transfers between devices: 21.7 us -> 21.1 us  [exchange(): return lax.all_to_all(blocks, axes, 0, 0, tiled=True)]
  transfers between devices with their start and end apart: 26 -> 24, of which waited for: 15 -> 15; matrix products, arithmetic and copies ran while one was open for 6% -> 6% of each run, Pallas kernels for 12% -> 13%
where the time goes in v5:
time: 204 us; the launch traced here: 203 us
  waiting for transfers between devices  81.2 us (40%)
  starting transfers between devices  57.2 us (28%)
  Pallas kernels  44.2 us (22%)
  matrix products  10.8 us (5%)
  local copies, waits for them, and re-layouts  4.73 us (2%)
  other arithmetic  3.82 us (2%)
    ppermute x18, waiting for transfers between devices, shift(): lax.ppermute(values, axis, [(i, (i + by) % RING) for i in range(RING)])  54.5 us
    pallas_call x13, Pallas kernels, with_placed(): return run(*placed)  44.2 us
    all_to_all x4, starting transfers between devices, exchange(): return lax.all_to_all(blocks, axes, 0, 0, tiled=True)  29.1 us
    ppermute x18, starting transfers between devices, shift(): lax.ppermute(values, axis, [(i, (i + by) % RING) for i in range(RING)])  28.1 us
    all_to_all x4, waiting for transfers between devices, exchange(): return lax.all_to_all(blocks, axes, 0, 0, tiled=True)  21.1 us
    dot_general x3, matrix products, dot(): lax.dot_general(left, right, (((left_dim,), (right_dim,)), ((), ())), pre...  10.8 us
    ppermute x2, waiting for transfers between devices, swap_cores(): return lax.ppermute(values, 'core', [(0, 1), (1, 0)])  5.59 us
  transfers between devices with their start and end apart: 24, of which 15 were waited for; matrix products, arithmetic and copies ran while one was open for 6% of the time, Pallas kernels for 13%

profile of v5, /device:TPU:8, one launch (start us, length us, event | category | flops | bytes accessed | tf_op | source)
XLA Modules:
  0.0 202.9 jit_solution(10101403605456175101)
XLA Ops:
  0.6 8.1 %key_value.1 = (bf16[10,128,112]{2,1,0:T(8,128)(2,1)}, bf16[10,128,112]{2,1,0:T(8,128)(2,1)}, f32[32,45,112]{2,1,0:T(8,128)}) custom-call(bf16[128,2240]{1,0:T(8,128)(2,1)} %bitcast.17, bf16[2240,1120]{1,0:T(8,128)(2,1)} %key_weight.1, bf16[2240,1120]{1,0:T(8,128)(2,1)} %value_weight.1), custom_call_target="tpu_custom_call" | custom-call | tf_op jit(solution)/shard_map/key_value/pallas_call | solution.py:64
  8.7 8.2 %all-to-all-start = ((f32[32,45,112]{2,1,0:T(8,128)}), f32[32,45,112]{2,1,0:T(8,128)S(1)}, u32[]{:S(2)}, u32[]{:S(2)}) async-start(f32[32,45,112]{2,1,0:T(8,128)} %get-tuple-element.60), calls=%async_computation | async-start | bytes 1572864 | tf_op jit(solution)/shard_map/all_to_all | solution.py:311
  16.9 2.2 %turn.1 = (f32[1120,128]{1,0:T(8,128)}, f32[1120,128]{1,0:T(8,128)}) custom-call(bf16[128,2240]{1,0:T(8,128)(2,1)} %bitcast.18), custom_call_target="tpu_custom_call" | custom-call | tf_op jit(solution)/shard_map/turn/pallas_call | solution.py:64
  21.2 4.4 %query.1.refs_1_ = bf16[10,128,112]{2,1,0:T(8,128)(2,1)} custom-call(bf16[128,2240]{1,0:T(8,128)(2,1)} %bitcast.19, bf16[2240,1120]{1,0:T(8,128)(2,1)} %weight.1), custom_call_target="tpu_custom_call" | custom-call | tf_op jit(solution)/shard_map/query/pallas_call | solution.py:64
  25.6 5.8 %all-to-all-done.refs_0_ = f32[32,45,112]{2,1,0:T(8,128)S(1)} async-done(((f32[32,45,112]{2,1,0:T(8,128)}), f32[32,45,112]{2,1,0:T(8,128)S(1)}, u32[]{:S(2)}, u32[]{:S(2)}) %all-to-all-start) | async-done | bytes 645152 | tf_op jit(solution)/shard_map/all_to_all | solution.py:311
  32.4 2.4 %numerator.1 = (f32[32,70,112]{2,1,0:T(8,128)}, bf16[10,128,112]{2,1,0:T(8,128)(2,1)}, f32[10,112]{1,0:T(8,128)}) custom-call(f32[32,45,112]{2,1,0:T(8,128)S(1)} %all-to-all-done.refs_0_, bf16[10,128,112]{2,1,0:T(8,128)(2,1)S(1)} %copy-done, bf16[128,1120]{1,0:T(8,128)(2,1)S(1)} %bitcast.13), custom_call_target="tpu_custom_call" | custom-call | tf_op jit(solution)/shard_map/numerator/pallas_call | solution.py:64
  35.8 7.3 %all-to-all-start.1 = ((f32[32,70,112]{2,1,0:T(8,128)}), f32[32,70,112]{2,1,0:T(8,128)S(1)}, u32[]{:S(2)}, u32[]{:S(2)}) async-start(f32[32,70,112]{2,1,0:T(8,128)} %get-tuple-element.65), calls=%async_computation.1 | async-start | bytes 2359296 | tf_op jit(solution)/shard_map/all_to_all | solution.py:311
  47.2 14.7 %all-to-all-done.1.refs_0_.got = f32[32,70,112]{2,1,0:T(8,128)S(1)} async-done(((f32[32,70,112]{2,1,0:T(8,128)}), f32[32,70,112]{2,1,0:T(8,128)S(1)}, u32[]{:S(2)}, u32[]{:S(2)}) %all-to-all-start.1) | async-done | bytes 1003552 | tf_op jit(solution)/shard_map/all_to_all | solution.py:311
  62.6 2.6 %total_grad.1 = (f32[32,45,112]{2,1,0:T(8,128)}, f32[128,10]{1,0:T(8,128)}) custom-call(f32[32,70,112]{2,1,0:T(8,128)S(1)} %all-to-all-done.1.refs_0_.got, bf16[10,128,112]{2,1,0:T(8,128)(2,1)S(1)} %copy-done.1, bf16[128,1120]{1,0:T(8,128)(2,1)S(1)} %bitcast.14, f32[10,112]{1,0:T(8,128)S(1)} %copy-done.9), custom_call_target="tpu_custom_call" | custom-call | tf_op jit(solution)/shard_map/total_grad/pallas_call | solution.py:64
  65.2 5.8 %collective-permute-done.2.refs_4_ = f32[1120,128]{1,0:T(8,128)} collective-permute-done((f32[1120,128]{1,0:T(8,128)S(1)}, f32[1120,128]{1,0:T(8,128)}, u32[]{:S(2)}, u32[]{:S(2)}) %collective-permute-start.2) | collective-permute-done | bytes 573472 | tf_op jit(solution)/shard_map/ppermute | solution.py:315
  72.0 7.3 %all-to-all-start.2 = ((f32[32,45,112]{2,1,0:T(8,128)}), f32[32,45,112]{2,1,0:T(8,128)S(1)}, u32[]{:S(2)}, u32[]{:S(2)}) async-start(f32[32,45,112]{2,1,0:T(8,128)} %get-tuple-element.75), calls=%async_computation.2 | async-start | bytes 1572864 | tf_op jit(solution)/shard_map/all_to_all | solution.py:311
  79.2 2.9 %query_grad.1 = (bf16[128,1120]{1,0:T(8,128)(2,1)}, f32[128,256]{1,0:T(8,128)}, f32[128,256]{1,0:T(8,128)}, f32[128,256]{1,0:T(8,128)}, f32[128,256]{1,0:T(8,128)}, /*index=5*/f32[4,128,24]{2,1,0:T(8,128)}) custom-call(s32[1]{0:T(128)} %bitcast.place.refs_6_, f32[32,70,112]{2,1,0:T(8,128)S(1)} %all-to-all-done.1.refs_0_.got, ...), custom_call_target="tpu_custom_call" | custom-call | tf_op jit(solution)/shard_map/query_grad/pallas_call | solution.py:64
  85.0 2.3 %collective-permute-start.8 = (f32[128,256]{1,0:T(8,128)}, f32[128,256]{1,0:T(8,128)S(1)}, u32[]{:S(2)}, u32[]{:S(2)}) collective-permute-start(f32[128,256]{1,0:T(8,128)} %get-tuple-element.83), channel_id=1, source_target_pairs={{0,96},{32,0},{64,32},{96,64},{1,97},{33,1},{65,33},{97,65},{2,98}... | collective-permute-start | bytes 393224 | tf_op jit(solution)/shard_map/ppermute | solution.py:315
  87.3 3.6 %join.1.refs_1_ = bf16[2240,512]{1,0:T(8,128)(2,1)} custom-call(f32[1120,128]{1,0:T(8,128)} %get-tuple-element.74.refs_0_, f32[1120,128]{1,0:T(8,128)} %get-tuple-element.73.refs_1_, f32[1120,128]{1,0:T(8,128)S(1)} %collective-permute-done.refs_2_, f32[1120,128]{1,0:T(8,128)} %collective-permute-done.4.refs_3_, f32[1120,128]{1,0:T(8,128)} %collective-permute-done.2.refs_4_, ...), custom_call_target="tpu_custom_call" | custom-call | tf_op jit(solution)/shard_map/join/pallas_call | solution.py:64
  93.8 2.8 %key_value_grad.1 = (bf16[128,1120]{1,0:T(8,128)(2,1)}, bf16[128,1120]{1,0:T(8,128)(2,1)}, f32[128,584]{1,0:T(8,128)}, f32[128,584]{1,0:T(8,128)}, f32[128,584]{1,0:T(8,128)}, /*index=5*/f32[128,584]{1,0:T(8,128)}) custom-call(s32[1]{0:T(128)} %bitcast.place.refs_6_, f32[32,45,112]{2,1,0:T(8,128)S(1)} %all-to-all-done.2.got, ...), custom_call_target="tpu_custom_call" | custom-call | tf_op jit(solution)/shard_map/key_value_grad/pallas_call | solution.py:64
  99.4 2.3 %collective-permute-start.11 = (f32[128,584]{1,0:T(8,128)}, f32[128,584]{1,0:T(8,128)S(1)}, u32[]{:S(2)}, u32[]{:S(2)}) collective-permute-start(f32[128,584]{1,0:T(8,128)} %get-tuple-element.94), channel_id=1, source_target_pairs={{0,96},{32,0},{64,32},{96,64},{1,97},{33,1},{65,33},{97,65},{2,98}... | collective-permute-start | bytes 897032 | tf_op jit(solution)/shard_map/ppermute | solution.py:315
  101.7 5.7 %collective-permute-done.9.refs_3_.refs_6_ = f32[128,584]{1,0:T(8,128)S(1)} collective-permute-done((f32[128,584]{1,0:T(8,128)}, f32[128,584]{1,0:T(8,128)S(1)}, u32[]{:S(2)}, u32[]{:S(2)}) %collective-permute-start.9) | collective-permute-done | bytes 299040 | tf_op jit(solution)/shard_map/ppermute | solution.py:315
  107.4 3.0 %collective-permute-done.10.refs_4_ = f32[128,584]{1,0:T(8,128)S(1)} collective-permute-done((f32[128,584]{1,0:T(8,128)}, f32[128,584]{1,0:T(8,128)S(1)}, u32[]{:S(2)}, u32[]{:S(2)}) %collective-permute-start.10) | collective-permute-done | bytes 299040 | tf_op jit(solution)/shard_map/ppermute | solution.py:315
  110.4 4.3 %collective-permute-done.11.refs_5_ = f32[128,584]{1,0:T(8,128)S(1)} collective-permute-done((f32[128,584]{1,0:T(8,128)}, f32[128,584]{1,0:T(8,128)S(1)}, u32[]{:S(2)}, u32[]{:S(2)}) %collective-permute-start.11) | collective-permute-done | bytes 299040 | tf_op jit(solution)/shard_map/ppermute | solution.py:315
  114.7 5.3 %weight_grad.2 = (f32[16,72,584]{2,1,0:T(8,128)}, f32[16,72,584]{2,1,0:T(8,128)}) custom-call(s32[1]{0:T(128)} %bitcast.4.refs_0_, bf16[2240,512]{1,0:T(8,128)(2,1)} %join.1.refs_1_, f32[128,584]{1,0:T(8,128)} %get-tuple-element.91.refs_2_, f32[128,584]{1,0:T(8,128)S(1)} %collective-permute-done.9.refs_3_.refs_6_, ...), custom_call_target="tpu_custom_call" | custom-call | tf_op jit(solution)/shard_map/weight_grad/pallas_call | solution.py:64
  120.0 5.6 %collective-permute-done.12 = f32[16,72,584]{2,1,0:T(8,128)S(1)} collective-permute-done((f32[16,72,584]{2,1,0:T(8,128)}, f32[16,72,584]{2,1,0:T(8,128)S(1)}, u32[]{:S(2)}, u32[]{:S(2)}) %collective-permute-start.12) | collective-permute-done | bytes 2691104 | tf_op jit(solution)/shard_map/ppermute | solution.py:323
  125.6 3.7 %add.14 = f32[16,72,584]{2,1,0:T(8,128)} add(f32[16,72,584]{2,1,0:T(8,128)} %get-tuple-element.95, f32[16,72,584]{2,1,0:T(8,128)S(1)} %collective-permute-done.12) | non-fusion elementwise | flops 672768 | bytes 8073216 | tf_op jit(solution)/shard_map/add | solution.py:446
  129.3 6.4 %all-to-all-start.3 = ((f32[16,72,584]{2,1,0:T(8,128)}), f32[16,72,584]{2,1,0:T(8,128)S(1)}, u32[]{:S(2)}, u32[]{:S(2)}) async-start(f32[16,72,584]{2,1,0:T(8,128)} %add.14), calls=%async_computation.3 | async-start | bytes 5898240 | tf_op jit(solution)/shard_map/all_to_all | solution.py:311
  136.7 3.5 %weight_grad.3 = (f32[16,72,256]{2,1,0:T(8,128)}, f32[16,72,256]{2,1,0:T(8,128)}) custom-call(s32[1]{0:T(128)} %bitcast.4.refs_0_, bf16[2240,512]{1,0:T(8,128)(2,1)} %join.1.refs_1_, f32[128,256]{1,0:T(8,128)} %get-tuple-element.97.refs_2_, f32[128,256]{1,0:T(8,128)S(1)} %collective-permute-done.6.refs_3_, f32[128,256]{1,0:T(8,128)S(1)} %collective-permute-done.7.refs_4_, ...), custom_call_target="tpu_custom_call" | custom-call | tf_op jit(solution)/shard_map/weight_grad/pallas_call | solution.py:64
  140.2 4.2 %fusion.1 = f32[128,2240]{0,1:T(8,128)S(1)} fusion(bf16[128,1120]{1,0:T(8,128)(2,1)} %get-tuple-element.69, bf16[2240,1120]{1,0:T(8,128)(2,1)} %weight.1), kind=kOutput, calls=%fused_computation.4 | convolution fusion | flops 642252800 | bytes 6451200 | tf_op jit(solution)/shard_map/dot_general | solution.py:70
  144.5 2.9 %first_stage.1 = (f32[4,72,256]{2,1,0:T(8,128)}, f32[4,72,256]{2,1,0:T(8,128)}, f32[4,72,256]{2,1,0:T(8,128)}, f32[4,72,256]{2,1,0:T(8,128)}) custom-call(s32[2]{0:T(128)S(1)} %pad_add_fusion.spot, f32[16,72,256]{2,1,0:T(8,128)} %get-tuple-element.101.kept, f32[16,72,256]{2,1,0:T(8,128)} %collective-permute-done.13.got, f32[16,72,584]{2,1,0:T(8,128)S(1)} %copy-done.2), custom_call_target="tpu_custom_call" | custom-call | tf_op jit(solution)/shard_map/first_stage/pallas_call | solution.py:64
  149.3 2.7 %collective-permute-start.15 = (f32[4,72,256]{2,1,0:T(8,128)}, f32[4,72,256]{2,1,0:T(8,128)S(1)}, u32[]{:S(2)}, u32[]{:S(2)}) collective-permute-start(f32[4,72,256]{2,1,0:T(8,128)} %get-tuple-element.105), channel_id=1, source_target_pairs={{0,4},{2,6},{4,0},{6,2},{1,5},{3,7},{5,1},{7,3},{8,12},{10,14},{12... | collective-permute-start | bytes 884744 | tf_op jit(solution)/shard_map/ppermute | solution.py:315
  153.4 4.2 %convolution_add_fusion.1 = f32[128,2240]{0,1:T(8,128)S(1)} fusion(f32[128,2240]{0,1:T(8,128)S(1)} %fusion.1, bf16[128,1120]{1,0:T(8,128)(2,1)S(1)} %copy-done.11, bf16[2240,1120]{1,0:T(8,128)(2,1)} %key_weight.1), kind=kOutput, calls=%fused_computation.1 | convolution fusion | flops 642539520 | bytes 7598080 | tf_op jit(solution)/shard_map/dot_general | solution.py:70
  157.6 24.0 %collective-permute-done.14.first = f32[4,72,256]{2,1,0:T(8,128)S(1)} collective-permute-done((f32[4,72,256]{2,1,0:T(8,128)}, f32[4,72,256]{2,1,0:T(8,128)S(1)}, u32[]{:S(2)}, u32[]{:S(2)}) %collective-permute-start.14) | collective-permute-done | bytes 294944 | tf_op jit(solution)/shard_map/ppermute | solution.py:315
  181.7 6.8 %collective-permute-done.15.second = f32[4,72,256]{2,1,0:T(8,128)S(1)} collective-permute-done((f32[4,72,256]{2,1,0:T(8,128)}, f32[4,72,256]{2,1,0:T(8,128)S(1)}, u32[]{:S(2)}, u32[]{:S(2)}) %collective-permute-start.15) | collective-permute-done | bytes 294944 | tf_op jit(solution)/shard_map/ppermute | solution.py:315
  192.6 2.6 %collective-permute-start.18 = (f32[72,256]{1,0:T(8,128)}, f32[72,256]{1,0:T(8,128)S(1)}, u32[]{:S(2)}, u32[]{:S(2)}) collective-permute-start(f32[72,256]{1,0:T(8,128)} %get-tuple-element.109), channel_id=1, source_target_pairs={{0,16},{1,17},{16,0},{17,1},{2,18},{3,19},{18,2},{19,3},{4,20},{5,... | collective-permute-start | bytes 221192 | tf_op jit(solution)/shard_map/ppermute | solution.py:315
  196.6 2.4 %fusion = bf16[128,2240]{0,1:T(8,128)(2,1)} fusion(f32[128,2240]{0,1:T(8,128)S(1)} %convolution_add_fusion.1, bf16[128,1120]{1,0:T(8,128)(2,1)S(1)} %copy-done.10, bf16[2240,1120]{1,0:T(8,128)(2,1)S(1)} %bitcast.16), kind=kOutput, calls=%fused_computation.2 | convolution fusion | flops 642826240 | bytes 7024640 | tf_op jit(solution)/shard_map/dot_general | solution.py:70
  (64 shorter events, 32.0 us)
Async XLA Ops:
  8.7 22.7 %all-to-all-start = ((f32[32,45,112]{2,1,0:T(8,128)}), f32[32,45,112]{2,1,0:T(8,128)S(1)}, u32[]{:S(2)}, u32[]{:S(2)}) async-start(f32[32,45,112]{2,1,0:T(8,128)} %get-tuple-element.60), calls=%async_computation | async-start | bytes 1572864 | tf_op jit(solution)/shard_map/all_to_all | solution.py:311
  19.2 15.7 %collective-permute-start = (f32[1120,128]{1,0:T(8,128)}, f32[1120,128]{1,0:T(8,128)S(1)}, u32[]{:S(2)}, u32[]{:S(2)}) collective-permute-start(f32[1120,128]{1,0:T(8,128)} %get-tuple-element.74.refs_0_), channel_id=1, source_target_pairs={{0,32},{32,64},{64,96},{96,0},{1,33},{33,65},{65,97},{97,1},{2,34}... | collective-permute-start | bytes 1720328 | tf_op jit(solution)/shard_map/ppermute | solution.py:315
  20.7 10.7 %copy-start.3 = (bf16[1,16,8,1120]{3,2,1,0:T(8,128)(2,1)S(1)}, bf16[1,16,8,1120]{3,2,1,0:T(8,128)(2,1)}, u32[]{:S(2)}) copy-start(bf16[1,16,8,1120]{3,2,1,0:T(8,128)(2,1)} %param.9) | copy-start | bytes 860164
  20.7 15.1 %collective-permute-start.1 = (f32[1120,128]{1,0:T(8,128)}, f32[1120,128]{1,0:T(8,128)S(1)}, u32[]{:S(2)}, u32[]{:S(2)}) collective-permute-start(f32[1120,128]{1,0:T(8,128)} %get-tuple-element.73.refs_1_), channel_id=1, source_target_pairs={{0,96},{32,0},{64,32},{96,64},{1,97},{33,1},{65,33},{97,65},{2,98}... | collective-permute-start | bytes 1720328 | tf_op jit(solution)/shard_map/ppermute | solution.py:315
  32.4 29.5 %copy-start.1 = (bf16[10,128,112]{2,1,0:T(8,128)(2,1)S(1)}, bf16[10,128,112]{2,1,0:T(8,128)(2,1)}, u32[]{:S(2)}) copy-start(bf16[10,128,112]{2,1,0:T(8,128)(2,1)} %query.1.refs_1_) | copy-start | bytes 860164
  35.8 26.1 %all-to-all-start.1 = ((f32[32,70,112]{2,1,0:T(8,128)}), f32[32,70,112]{2,1,0:T(8,128)S(1)}, u32[]{:S(2)}, u32[]{:S(2)}) async-start(f32[32,70,112]{2,1,0:T(8,128)} %get-tuple-element.65), calls=%async_computation.1 | async-start | bytes 2359296 | tf_op jit(solution)/shard_map/all_to_all | solution.py:311
  43.1 22.1 %collective-permute-start.4 = (f32[1120,128]{1,0:T(8,128)}, f32[1120,128]{1,0:T(8,128)}, u32[]{:S(2)}, u32[]{:S(2)}) collective-permute-start(f32[1120,128]{1,0:T(8,128)} %get-tuple-element.73.refs_1_), channel_id=1, source_target_pairs={{0,32},{32,64},{64,96},{96,0},{1,33},{33,65},{65,97},{97,1},{2,34}... | collective-permute-start | bytes 1720328 | tf_op jit(solution)/shard_map/ppermute | solution.py:315
  44.5 20.7 %collective-permute-start.5 = (f32[1120,128]{1,0:T(8,128)}, f32[1120,128]{1,0:T(8,128)}, u32[]{:S(2)}, u32[]{:S(2)}) collective-permute-start(f32[1120,128]{1,0:T(8,128)} %get-tuple-element.74.refs_0_), channel_id=1, source_target_pairs={{0,96},{32,0},{64,32},{96,64},{1,97},{33,1},{65,33},{97,65},{2,98}... | collective-permute-start | bytes 1720328 | tf_op jit(solution)/shard_map/ppermute | solution.py:315
  45.2 25.7 %collective-permute-start.2 = (f32[1120,128]{1,0:T(8,128)S(1)}, f32[1120,128]{1,0:T(8,128)}, u32[]{:S(2)}, u32[]{:S(2)}) collective-permute-start(f32[1120,128]{1,0:T(8,128)S(1)} %collective-permute-done.refs_2_), channel_id=1, source_target_pairs={{0,32},{32,64},{64,96},{96,0},{1,33},{33,65},{65,97},{97,1},{2,34}... | collective-permute-start | bytes 1720328 | tf_op jit(solution)/shard_map/ppermute | solution.py:315
  46.5 25.5 %collective-permute-start.3 = (f32[1120,128]{1,0:T(8,128)S(1)}, f32[1120,128]{1,0:T(8,128)}, u32[]{:S(2)}, u32[]{:S(2)}) collective-permute-start(f32[1120,128]{1,0:T(8,128)S(1)} %collective-permute-done.1.refs_7_), channel_id=1, source_target_pairs={{0,96},{32,0},{64,32},{96,64},{1,97},{33,1},{65,33},{97,65},{2,98}... | collective-permute-start | bytes 1720328 | tf_op jit(solution)/shard_map/ppermute | solution.py:315
  72.0 21.8 %all-to-all-start.2 = ((f32[32,45,112]{2,1,0:T(8,128)}), f32[32,45,112]{2,1,0:T(8,128)S(1)}, u32[]{:S(2)}, u32[]{:S(2)}) async-start(f32[32,45,112]{2,1,0:T(8,128)} %get-tuple-element.75), calls=%async_computation.2 | async-start | bytes 1572864 | tf_op jit(solution)/shard_map/all_to_all | solution.py:311
  82.1 8.8 %collective-permute-start.6 = (f32[128,256]{1,0:T(8,128)}, f32[128,256]{1,0:T(8,128)S(1)}, u32[]{:S(2)}, u32[]{:S(2)}) collective-permute-start(f32[128,256]{1,0:T(8,128)} %get-tuple-element.81), channel_id=1, source_target_pairs={{0,32},{32,64},{64,96},{96,0},{1,33},{33,65},{65,97},{97,1},{2,34}... | collective-permute-start | bytes 393224 | tf_op jit(solution)/shard_map/ppermute | solution.py:315
  83.6 8.1 %collective-permute-start.7 = (f32[128,256]{1,0:T(8,128)}, f32[128,256]{1,0:T(8,128)S(1)}, u32[]{:S(2)}, u32[]{:S(2)}) collective-permute-start(f32[128,256]{1,0:T(8,128)} %get-tuple-element.82), channel_id=1, source_target_pairs={{0,64},{32,96},{64,0},{96,32},{1,65},{33,97},{65,1},{97,33},{2,66}... | collective-permute-start | bytes 393224 | tf_op jit(solution)/shard_map/ppermute | solution.py:315
  85.0 8.8 %copy-start.5 = (bf16[10,128,112]{2,1,0:T(8,128)(2,1)S(1)}, bf16[10,128,112]{2,1,0:T(8,128)(2,1)}, u32[]{:S(2)}) copy-start(bf16[10,128,112]{2,1,0:T(8,128)(2,1)} %get-tuple-element.86.value) | copy-start | bytes 860164
  85.0 8.8 %copy-start.6 = (f32[4,128,24]{2,1,0:T(8,128)S(1)}, f32[4,128,24]{2,1,0:T(8,128)}, u32[]{:S(2)}) copy-start(f32[4,128,24]{2,1,0:T(8,128)} %get-tuple-element.87.late) | copy-start | bytes 147460
  85.0 8.1 %collective-permute-start.8 = (f32[128,256]{1,0:T(8,128)}, f32[128,256]{1,0:T(8,128)S(1)}, u32[]{:S(2)}, u32[]{:S(2)}) collective-permute-start(f32[128,256]{1,0:T(8,128)} %get-tuple-element.83), channel_id=1, source_target_pairs={{0,96},{32,0},{64,32},{96,64},{1,97},{33,1},{65,33},{97,65},{2,98}... | collective-permute-start | bytes 393224 | tf_op jit(solution)/shard_map/ppermute | solution.py:315
  96.6 10.9 %collective-permute-start.9 = (f32[128,584]{1,0:T(8,128)}, f32[128,584]{1,0:T(8,128)S(1)}, u32[]{:S(2)}, u32[]{:S(2)}) collective-permute-start(f32[128,584]{1,0:T(8,128)} %get-tuple-element.92), channel_id=1, source_target_pairs={{0,32},{32,64},{64,96},{96,0},{1,33},{33,65},{65,97},{97,1},{2,34}... | collective-permute-start | bytes 897032 | tf_op jit(solution)/shard_map/ppermute | solution.py:315
  98.1 12.4 %collective-permute-start.10 = (f32[128,584]{1,0:T(8,128)}, f32[128,584]{1,0:T(8,128)S(1)}, u32[]{:S(2)}, u32[]{:S(2)}) collective-permute-start(f32[128,584]{1,0:T(8,128)} %get-tuple-element.93), channel_id=1, source_target_pairs={{0,64},{32,96},{64,0},{96,32},{1,65},{33,97},{65,1},{97,33},{2,66}... | collective-permute-start | bytes 897032 | tf_op jit(solution)/shard_map/ppermute | solution.py:315
  99.4 15.3 %collective-permute-start.11 = (f32[128,584]{1,0:T(8,128)}, f32[128,584]{1,0:T(8,128)S(1)}, u32[]{:S(2)}, u32[]{:S(2)}) collective-permute-start(f32[128,584]{1,0:T(8,128)} %get-tuple-element.94), channel_id=1, source_target_pairs={{0,96},{32,0},{64,32},{96,64},{1,97},{33,1},{65,33},{97,65},{2,98}... | collective-permute-start | bytes 897032 | tf_op jit(solution)/shard_map/ppermute | solution.py:315
  120.0 5.6 %collective-permute-start.12 = (f32[16,72,584]{2,1,0:T(8,128)}, f32[16,72,584]{2,1,0:T(8,128)S(1)}, u32[]{:S(2)}, u32[]{:S(2)}) collective-permute-start(f32[16,72,584]{2,1,0:T(8,128)} %get-tuple-element.96.after), channel_id=1, source_target_pairs={{0,8},{8,0},{1,9},{9,1},{2,10},{10,2},{3,11},{11,3},{4,12},{12,4},... | collective-permute-start | bytes 8073224 | tf_op jit(solution)/shard_map/ppermute | solution.py:323
  129.3 71.8 %all-to-all-start.3 = ((f32[16,72,584]{2,1,0:T(8,128)}), f32[16,72,584]{2,1,0:T(8,128)S(1)}, u32[]{:S(2)}, u32[]{:S(2)}) async-start(f32[16,72,584]{2,1,0:T(8,128)} %add.14), calls=%async_computation.3 | async-start | bytes 5898240 | tf_op jit(solution)/shard_map/all_to_all | solution.py:311
  140.2 4.3 %collective-permute-start.13 = (f32[16,72,256]{2,1,0:T(8,128)}, f32[16,72,256]{2,1,0:T(8,128)}, u32[]{:S(2)}, u32[]{:S(2)}) collective-permute-start(f32[16,72,256]{2,1,0:T(8,128)} %get-tuple-element.102), channel_id=1, source_target_pairs={{0,8},{8,0},{1,9},{9,1},{2,10},{10,2},{3,11},{11,3},{4,12},{12,4},... | collective-permute-start | bytes 3538952 | tf_op jit(solution)/shard_map/ppermute | solution.py:323
  144.5 9.0 %copy-start.11 = (bf16[128,1120]{1,0:T(8,128)(2,1)S(1)}, bf16[128,1120]{1,0:T(8,128)(2,1)}, u32[]{:S(2)}) copy-start(bf16[128,1120]{1,0:T(8,128)(2,1)} %get-tuple-element.88) | copy-start | bytes 860164
  144.5 52.1 %slice-start = ((s8[5160960]{0:T(1024)(128)(4,1)}), s8[966656]{0:T(1024)(128)(4,1)S(1)}, s32[]{:S(2)}) async-start(s8[5160960]{0:T(1024)(128)(4,1)} %bitcast.15), calls=%async_computation.4 | async-start | bytes 1933312
  147.4 34.3 %collective-permute-start.14 = (f32[4,72,256]{2,1,0:T(8,128)}, f32[4,72,256]{2,1,0:T(8,128)S(1)}, u32[]{:S(2)}, u32[]{:S(2)}) collective-permute-start(f32[4,72,256]{2,1,0:T(8,128)} %get-tuple-element.104), channel_id=1, source_target_pairs={{0,2},{2,4},{4,6},{6,0},{1,3},{3,5},{5,7},{7,1},{8,10},{10,12},{12... | collective-permute-start | bytes 884744 | tf_op jit(solution)/shard_map/ppermute | solution.py:315
  149.3 39.2 %collective-permute-start.15 = (f32[4,72,256]{2,1,0:T(8,128)}, f32[4,72,256]{2,1,0:T(8,128)S(1)}, u32[]{:S(2)}, u32[]{:S(2)}) collective-permute-start(f32[4,72,256]{2,1,0:T(8,128)} %get-tuple-element.105), channel_id=1, source_target_pairs={{0,4},{2,6},{4,0},{6,2},{1,5},{3,7},{5,1},{7,3},{8,12},{10,14},{12... | collective-permute-start | bytes 884744 | tf_op jit(solution)/shard_map/ppermute | solution.py:315
  152.0 37.2 %collective-permute-start.16 = (f32[4,72,256]{2,1,0:T(8,128)}, f32[4,72,256]{2,1,0:T(8,128)S(1)}, u32[]{:S(2)}, u32[]{:S(2)}) collective-permute-start(f32[4,72,256]{2,1,0:T(8,128)} %get-tuple-element.106), channel_id=1, source_target_pairs={{0,6},{2,0},{4,2},{6,4},{1,7},{3,1},{5,3},{7,5},{8,14},{10,8},{12,... | collective-permute-start | bytes 884744 | tf_op jit(solution)/shard_map/ppermute | solution.py:315
  153.4 43.1 %slice-start.1 = ((s8[5160960]{0:T(1024)(128)(4,1)}), s8[4194304]{0:T(1024)(128)(4,1)S(1)}, s32[]{:S(2)}) async-start(s8[5160960]{0:T(1024)(128)(4,1)} %bitcast.15), calls=%async_computation.5 | async-start | bytes 8388608
  153.4 43.1 %copy-start.10 = (bf16[128,1120]{1,0:T(8,128)(2,1)S(1)}, bf16[128,1120]{1,0:T(8,128)(2,1)}, u32[]{:S(2)}) copy-start(bf16[128,1120]{1,0:T(8,128)(2,1)} %get-tuple-element.89) | copy-start | bytes 860164
  191.0 10.1 %collective-permute-start.17 = (f32[72,256]{1,0:T(8,128)}, f32[72,256]{1,0:T(8,128)S(1)}, u32[]{:S(2)}, u32[]{:S(2)}) collective-permute-start(f32[72,256]{1,0:T(8,128)} %get-tuple-element.108), channel_id=1, source_target_pairs={{0,1},{1,16},{16,17},{17,0},{2,3},{3,18},{18,19},{19,2},{4,5},{5,2... | collective-permute-start | bytes 221192 | tf_op jit(solution)/shard_map/ppermute | solution.py:315
  192.6 8.5 %collective-permute-start.18 = (f32[72,256]{1,0:T(8,128)}, f32[72,256]{1,0:T(8,128)S(1)}, u32[]{:S(2)}, u32[]{:S(2)}) collective-permute-start(f32[72,256]{1,0:T(8,128)} %get-tuple-element.109), channel_id=1, source_target_pairs={{0,16},{1,17},{16,0},{17,1},{2,18},{3,19},{18,2},{19,3},{4,20},{5,... | collective-permute-start | bytes 221192 | tf_op jit(solution)/shard_map/ppermute | solution.py:315
  195.2 5.9 %collective-permute-start.19 = (f32[72,256]{1,0:T(8,128)}, f32[72,256]{1,0:T(8,128)S(1)}, u32[]{:S(2)}, u32[]{:S(2)}) collective-permute-start(f32[72,256]{1,0:T(8,128)} %get-tuple-element.110), channel_id=1, source_target_pairs={{0,17},{1,0},{16,1},{17,16},{2,19},{3,2},{18,3},{19,18},{4,21},{5,... | collective-permute-start | bytes 221192 | tf_op jit(solution)/shard_map/ppermute | solution.py:315
  (6 other events, 19.1 us)

commit v6 on v5

--- a/solution.py
+++ b/solution.py
@@ -17,6 +17,7 @@
 CORES = 2
 ROWS = D // TILES
 PADDED_ROWS = 72
+HALF = D // 4
 REPLICAS = 4
 RING = 4
 COLS = HW // REPLICAS
@@ -261,39 +262,56 @@
             bottom[at : at + turned.shape[0] - cut, :] = turned[cut:]
 
 
-def join_kernel(*refs):
-    out = refs[-1]
-    for index, half in enumerate(refs[:-1]):
-        slot, rows = index // 2, index % 2 * (D // 2)
+def join_kernel(core, *refs):
+    parts, kept, given = refs[:-2], refs[-2], refs[-1]
+    mine = pl.multiple_of(core[0] * HALF, 16)
+    other = pl.multiple_of((1 - core[0]) * HALF, 16)
+    for index, part in enumerate(parts):
+        slot, rows = index // 2, slice(index % 2 * HALF, (index % 2 + 1) * HALF)
         at = slice(slot * TOKENS, (slot + 1) * TOKENS)
-        out[rows : rows + D // 2, at] = half[...].astype(BF16)
-
-
-def weight_grad_kernel(normalizer, core, tokens, own, first, second, third, after, kept, sent, columns):
-    for slot, block in enumerate((own, first, second, third)):
-        columns[slot * TOKENS : (slot + 1) * TOKENS, :] = block[...].astype(BF16)
-    right = columns[...]
+        kept[rows, at] = part[pl.ds(mine, HALF), :].astype(BF16)
+        given[rows, at] = part[pl.ds(other, HALF), :]
+
+
+def fill_columns(columns, blocks):
+    for index, block in enumerate(blocks):
+        columns[index * TOKENS : (index + 1) * TOKENS, :] = block[...].astype(BF16)
+
+
+def row_products(normalizer, kept, got, columns, rows):
+    own = dot(kept[rows, :], columns[: REPLICAS * TOKENS, :], 1, 0)
+    other = dot(got[rows, :].astype(BF16), columns[REPLICAS * TOKENS :, :], 1, 0)
+    return (own + other) * normalizer
+
+
+def query_product_kernel(normalizer, across, kept, got, *refs):
+    blocks, outs, columns, product = refs[: 2 * REPLICAS], refs[2 * REPLICAS : -2], refs[-2], refs[-1]
+    fill_columns(columns, blocks)
     span = PLANE_SIZE // CORES
-    for out, which in ((sent, 1 - core[0]), (kept, core[0])):
-        for half in range(CORES):
-            start = pl.multiple_of((half * CORES + which) * (span * ROWS), 16)
-            product = dot(tokens[pl.ds(start, span * ROWS), :], right, 1, 0) * normalizer
-            for index in range(span):
-                out[half * span + index, :ROWS, :] = product[index * ROWS : (index + 1) * ROWS]
-
-
-def first_stage_kernel(spot, kept, got, after, *outs):
+    for half in range(CORES):
+        values = row_products(normalizer, kept, got, columns, slice(half * HALF, (half + 1) * HALF))
+        for index in range(span):
+            product[half * span + index, :ROWS, :] = values[index * ROWS : (index + 1) * ROWS]
     for slot, out in enumerate(outs):
-        across = lax.rem(spot[0] + slot, RING)
+        at = lax.rem(across[0] + slot, RING)
         for other in range(RING):
-            at = (other // 2) * (2 * RING) + across * 2 + other % 2
-            out[other] = kept[at] + got[at]
-
-
-def second_stage_kernel(spot, own, first, second, third, *outs):
+            out[other] = product[(other // 2) * span + at * 2 + other % 2]
+
+
+def key_value_product_kernel(normalizer, kept, got, *refs):
+    blocks, out, columns = refs[: 2 * REPLICAS], refs[-2], refs[-1]
+    fill_columns(columns, blocks)
+    span = PLANE_SIZE // CORES
+    for half in range(CORES):
+        values = row_products(normalizer, kept, got, columns, slice(half * HALF, (half + 1) * HALF))
+        for index in range(span):
+            out[half * span + index, :ROWS, :] = values[index * ROWS : (index + 1) * ROWS]
+
+
+def second_stage_kernel(along, own, first, second, third, *outs):
     for slot, out in enumerate(outs):
-        along = lax.rem(spot[1] + slot, RING)
-        out[...] = (own[along] + first[along]) + (second[along] + third[along])
+        at = lax.rem(along[0] + slot, RING)
+        out[...] = (own[at] + first[at]) + (second[at] + third[at])
 
 
 def last_kernel(key_value, own, first, second, third, query_out, key_out, value_out):
@@ -323,6 +341,10 @@
     return lax.ppermute(values, "core", [(0, 1), (1, 0)])
 
 
+def both_cores(blocks):
+    return blocks + [swap_cores(block) for block in blocks]
+
+
 def back_project(gradient, weight):
     return dot(gradient, weight, 1, 1)
 
@@ -335,7 +357,8 @@
     upstream = upstream_grad.reshape(TOKENS, HW)
     place = lax.axis_index("dp").reshape(1)
     core = lax.axis_index("core").reshape(1)
-    spot = jnp.stack([lax.axis_index("x"), lax.axis_index(("zh", "zl"))])
+    across = lax.axis_index("x").reshape(1)
+    along = lax.axis_index(("zh", "zl")).reshape(1)
     heads = shaped((HEADS, TOKENS, HD), BF16)
     flat = shaped((TOKENS, HW), BF16)
     state = pltpu.VMEM((HW, HD), F32)
@@ -403,24 +426,19 @@
         arrived=(1,),
     )(place, got_state, query, numer, total, grad_denom)
     query_columns = shifted(query_columns, "dp")
-    (all_tokens,) = call(
-        join_kernel, "join", [shaped((D, REPLICAS * TOKENS), BF16)], [BLOCK] * 8, arrived=(2, 3, 4, 5, 6, 7)
-    )(top, bottom, left_top, left_bottom, far_top, far_bottom, right_top, right_bottom)
-    def partial_products(all_tokens, columns, after):
-        width = columns[0].shape[1]
-        half = shaped((PLANE_SIZE, PADDED_ROWS, width))
-        return call(
-            lambda *refs: weight_grad_kernel(normalizer, *refs),
-            "weight_grad",
-            [half, half],
-            [IN_SMEM] + [BLOCK] * 5 + [ANYWHERE],
-            [pltpu.VMEM((REPLICAS * TOKENS, width), BF16)],
-            vmem=24,
-            arrived=(3, 4, 5, 6),
-        )(core, all_tokens, *columns, after)
-
-    got, all_tokens, query_columns = lax.optimization_barrier((got, all_tokens, query_columns))
-
+    half_rows = CORES * HALF
+    kept_rows, given_rows = call(
+        join_kernel,
+        "join",
+        [shaped((half_rows, REPLICAS * TOKENS), BF16), shaped((half_rows, REPLICAS * TOKENS))],
+        [IN_SMEM] + [BLOCK] * 8,
+        arrived=(3, 4, 5, 6, 7, 8),
+    )(core, top, bottom, left_top, left_bottom, far_top, far_bottom, right_top, right_bottom)
+    got_rows = swap_cores(given_rows)
+    query_columns = both_cores(query_columns)
+    got, kept_rows, got_rows, query_columns = lax.optimization_barrier(
+        (got, kept_rows, got_rows, query_columns)
+    )
     block = shaped((TOKENS, WIDE))
     grad_key, grad_value, *key_value_columns = call(
         key_value_grad_kernel,
@@ -430,27 +448,38 @@
         [state, wide, wide, blocks],
         arrived=(1, 2, 3, 4),
     )(place, got, key, value, late)
-    key_value_columns = shifted(key_value_columns, "dp")
-
-    query_kept, query_given = partial_products(all_tokens, query_columns, key_value_columns[1])
-    query_got = swap_cores(query_given)
-    kept, given = partial_products(all_tokens, key_value_columns, place)
-    got = swap_cores(given)
     slots = call(
-        first_stage_kernel,
-        "first_stage",
+        lambda *refs: query_product_kernel(normalizer, *refs),
+        "query_product",
         [shaped((RING, PADDED_ROWS, EARLY))] * RING,
-        [IN_SMEM, BLOCK, BLOCK, ANYWHERE],
-        arrived=(2, 3),
-    )(spot, query_kept, query_got, given)
-    key_value_out = exchange(kept + got, PLANE)
+        [IN_SMEM] + [BLOCK] * (2 + 2 * REPLICAS),
+        [
+            pltpu.VMEM((2 * REPLICAS * TOKENS, EARLY), BF16),
+            pltpu.VMEM((PLANE_SIZE, PADDED_ROWS, EARLY), F32),
+        ],
+        vmem=24,
+        arrived=tuple(range(2, 11)),
+    )(across, kept_rows, got_rows, *query_columns)
+    slots = shifted(slots, "x")
+
+    key_value_columns = both_cores(shifted(key_value_columns, "dp"))
+    (product,) = call(
+        lambda *refs: key_value_product_kernel(normalizer, *refs[:10], *refs[13:]),
+        "key_value_product",
+        [shaped((PLANE_SIZE, PADDED_ROWS, WIDE))],
+        [BLOCK] * (2 + 2 * REPLICAS) + [ANYWHERE] * 3,
+        [pltpu.VMEM((2 * REPLICAS * TOKENS, WIDE), BF16)],
+        vmem=24,
+        arrived=tuple(range(1, 13)),
+    )(kept_rows, got_rows, *key_value_columns, *slots[1:])
+    key_value_out = exchange(product, PLANE)
     slots = call(
         second_stage_kernel,
         "second_stage",
         [shaped((PADDED_ROWS, EARLY))] * RING,
         [IN_SMEM] + [BLOCK] * RING,
         arrived=(2, 3, 4),
-    )(spot, *shifted(slots, "x"))
+    )(along, *slots)
     slots = shifted(slots, ("zh", "zl"))
     block = shaped((ROWS, COLS))
     query_out, key_out, value_out = call(

time: 204 us -> 202 us (level)
  local copies, waits for them, and re-layouts: 4.73 us -> 19.2 us
  waiting for transfers between devices: 81.2 us -> 71.7 us
  other arithmetic: 3.82 us -> 0.01 us
    unnamed x28 -> x64, local copies, waits for them, and re-layouts: 2.61 us -> 17 us
    ppermute x18, waiting for transfers between devices: 54.5 us -> 47.7 us  [shift(): lax.ppermute(values, axis, [(i, (i + by) % RING) for i in range(RING)])]
    ppermute x2 -> x9, waiting for transfers between devices: 5.59 us -> 0.02 us  [swap_cores(): return lax.ppermute(values, 'core', [(0, 1), (1, 0)])]
    add x1 -> x0, other arithmetic: 3.74 us -> none  [body(): key_value_out = exchange(kept + got, PLANE)]
    all_to_all x4, waiting for transfers between devices: 21.1 us -> 24 us  [exchange(): return lax.all_to_all(blocks, axes, 0, 0, tiled=True)]
    pallas_call x13 -> x12, Pallas kernels: 44.2 us -> 42.2 us  [with_placed(): return run(*placed)]
  transfers between devices with their start and end apart: 24 -> 31, of which waited for: 15 -> 13; matrix products, arithmetic and copies ran while one was open for 6% -> 6% of each run, Pallas kernels for 13% -> 10%
where the time goes in v6:
time: 202 us; the launch traced here: 200 us
  waiting for transfers between devices  71.7 us (35%)
  starting transfers between devices  55.5 us (27%)
  Pallas kernels  42.2 us (21%)
  local copies, waits for them, and re-layouts  19.2 us (10%)
  matrix products  10.7 us (5%)
    ppermute x18, waiting for transfers between devices, shift(): lax.ppermute(values, axis, [(i, (i + by) % RING) for i in range(RING)])  47.7 us
    pallas_call x12, Pallas kernels, with_placed(): return run(*placed)  42.2 us
    all_to_all x4, starting transfers between devices, exchange(): return lax.all_to_all(blocks, axes, 0, 0, tiled=True)  28.4 us
    ppermute x18, starting transfers between devices, shift(): lax.ppermute(values, axis, [(i, (i + by) % RING) for i in range(RING)])  26.1 us
    all_to_all x4, waiting for transfers between devices, exchange(): return lax.all_to_all(blocks, axes, 0, 0, tiled=True)  24 us
    unnamed x64, local copies, waits for them, and re-layouts  17 us
    dot_general x3, matrix products, dot(): lax.dot_general(left, right, (((left_dim,), (right_dim,)), ((), ())), pre...  10.7 us
  transfers between devices with their start and end apart: 31, of which 13 were waited for; matrix products, arithmetic and copies ran while one was open for 6% of the time, Pallas kernels for 10%

profile of v6, /device:TPU:8, one launch (start us, length us, event | category | flops | bytes accessed | tf_op | source)
XLA Modules:
  0.0 200.1 jit_solution(17489365934425711105)
XLA Ops:
  0.6 8.2 %key_value.1 = (bf16[10,128,112]{2,1,0:T(8,128)(2,1)}, bf16[10,128,112]{2,1,0:T(8,128)(2,1)}, f32[32,45,112]{2,1,0:T(8,128)}) custom-call(bf16[128,2240]{1,0:T(8,128)(2,1)} %bitcast.17, bf16[2240,1120]{1,0:T(8,128)(2,1)} %key_weight.1, bf16[2240,1120]{1,0:T(8,128)(2,1)} %value_weight.1), custom_call_target="tpu_custom_call" | custom-call | tf_op jit(solution)/shard_map/key_value/pallas_call | solution.py:65
  8.8 8.2 %all-to-all-start = ((f32[32,45,112]{2,1,0:T(8,128)}), f32[32,45,112]{2,1,0:T(8,128)S(1)}, u32[]{:S(2)}, u32[]{:S(2)}) async-start(f32[32,45,112]{2,1,0:T(8,128)} %get-tuple-element.63), calls=%async_computation | async-start | bytes 1572864 | tf_op jit(solution)/shard_map/all_to_all | solution.py:329
  17.0 2.2 %turn.1 = (f32[1120,128]{1,0:T(8,128)}, f32[1120,128]{1,0:T(8,128)}) custom-call(bf16[128,2240]{1,0:T(8,128)(2,1)} %bitcast.18), custom_call_target="tpu_custom_call" | custom-call | tf_op jit(solution)/shard_map/turn/pallas_call | solution.py:65
  21.3 4.4 %query.1.refs_1_ = bf16[10,128,112]{2,1,0:T(8,128)(2,1)} custom-call(bf16[128,2240]{1,0:T(8,128)(2,1)} %bitcast.19, bf16[2240,1120]{1,0:T(8,128)(2,1)} %weight.1), custom_call_target="tpu_custom_call" | custom-call | tf_op jit(solution)/shard_map/query/pallas_call | solution.py:65
  25.7 5.8 %all-to-all-done.refs_0_ = f32[32,45,112]{2,1,0:T(8,128)S(1)} async-done(((f32[32,45,112]{2,1,0:T(8,128)}), f32[32,45,112]{2,1,0:T(8,128)S(1)}, u32[]{:S(2)}, u32[]{:S(2)}) %all-to-all-start) | async-done | bytes 645152 | tf_op jit(solution)/shard_map/all_to_all | solution.py:329
  32.5 2.4 %numerator.1 = (f32[32,70,112]{2,1,0:T(8,128)}, bf16[10,128,112]{2,1,0:T(8,128)(2,1)}, f32[10,112]{1,0:T(8,128)}) custom-call(f32[32,45,112]{2,1,0:T(8,128)S(1)} %all-to-all-done.refs_0_, bf16[10,128,112]{2,1,0:T(8,128)(2,1)S(1)} %copy-done, bf16[128,1120]{1,0:T(8,128)(2,1)S(1)} %bitcast.13), custom_call_target="tpu_custom_call" | custom-call | tf_op jit(solution)/shard_map/numerator/pallas_call | solution.py:65
  35.9 7.3 %all-to-all-start.1 = ((f32[32,70,112]{2,1,0:T(8,128)}), f32[32,70,112]{2,1,0:T(8,128)S(1)}, u32[]{:S(2)}, u32[]{:S(2)}) async-start(f32[32,70,112]{2,1,0:T(8,128)} %get-tuple-element.68), calls=%async_computation.1 | async-start | bytes 2359296 | tf_op jit(solution)/shard_map/all_to_all | solution.py:329
  47.3 14.7 %all-to-all-done.1.refs_0_.got = f32[32,70,112]{2,1,0:T(8,128)S(1)} async-done(((f32[32,70,112]{2,1,0:T(8,128)}), f32[32,70,112]{2,1,0:T(8,128)S(1)}, u32[]{:S(2)}, u32[]{:S(2)}) %all-to-all-start.1) | async-done | bytes 1003552 | tf_op jit(solution)/shard_map/all_to_all | solution.py:329
  62.7 2.6 %total_grad.1 = (f32[32,45,112]{2,1,0:T(8,128)}, f32[128,10]{1,0:T(8,128)}) custom-call(f32[32,70,112]{2,1,0:T(8,128)S(1)} %all-to-all-done.1.refs_0_.got, bf16[10,128,112]{2,1,0:T(8,128)(2,1)S(1)} %copy-done.1, bf16[128,1120]{1,0:T(8,128)(2,1)S(1)} %bitcast.14, f32[10,112]{1,0:T(8,128)S(1)} %copy-done.26), custom_call_target="tpu_custom_call" | custom-call | tf_op jit(solution)/shard_map/total_grad/pallas_call | solution.py:65
  65.3 5.6 %collective-permute-done.4.refs_3_ = f32[1120,128]{1,0:T(8,128)} collective-permute-done((f32[1120,128]{1,0:T(8,128)}, f32[1120,128]{1,0:T(8,128)}, u32[]{:S(2)}, u32[]{:S(2)}) %collective-permute-start.4) | collective-permute-done | bytes 573472 | tf_op jit(solution)/shard_map/ppermute | solution.py:333
  71.8 4.0 %join.1 = (bf16[1120,512]{1,0:T(8,128)(2,1)}, f32[1120,512]{1,0:T(8,128)}) custom-call(s32[1]{0:T(128)} %bitcast.3.core, f32[1120,128]{1,0:T(8,128)} %get-tuple-element.77.refs_0_, f32[1120,128]{1,0:T(8,128)} %get-tuple-element.76.refs_1_, f32[1120,128]{1,0:T(8,128)S(1)} %collective-permute-done.refs_2_, f32[1120,128]{1,0:T(8,128)} %collective-permute-done.4.refs_3_, ...), custom_call_target="tpu_custom_call" | custom-call | tf_op jit(solution)/shard_map/join/pallas_call | solution.py:65
  75.9 7.5 %all-to-all-start.2 = ((f32[32,45,112]{2,1,0:T(8,128)}), f32[32,45,112]{2,1,0:T(8,128)}, u32[]{:S(2)}, u32[]{:S(2)}) async-start(f32[32,45,112]{2,1,0:T(8,128)} %get-tuple-element.78), calls=%async_computation.2 | async-start | bytes 1572864 | tf_op jit(solution)/shard_map/all_to_all | solution.py:329
  83.4 2.8 %query_grad.1 = (bf16[128,1120]{1,0:T(8,128)(2,1)}, f32[128,256]{1,0:T(8,128)}, f32[128,256]{1,0:T(8,128)}, f32[128,256]{1,0:T(8,128)}, f32[128,256]{1,0:T(8,128)}, /*index=5*/f32[4,128,24]{2,1,0:T(8,128)}) custom-call(s32[1]{0:T(128)} %bitcast.place, f32[32,70,112]{2,1,0:T(8,128)S(1)} %all-to-all-done.1.refs_0_.got, bf16[10,128,112]{2,1,0:T(8,128)(2,1)} %query.1.refs_1_, ...), custom_call_target="tpu_custom_call" | custom-call | tf_op jit(solution)/shard_map/query_grad/pallas_call | solution.py:65
  89.0 2.3 %collective-permute-start.9 = (f32[128,256]{1,0:T(8,128)}, f32[128,256]{1,0:T(8,128)S(1)}, u32[]{:S(2)}, u32[]{:S(2)}) collective-permute-start(f32[128,256]{1,0:T(8,128)} %get-tuple-element.88), channel_id=1, source_target_pairs={{0,96},{32,0},{64,32},{96,64},{1,97},{33,1},{65,33},{97,65},{2,98}... | collective-permute-start | bytes 393224 | tf_op jit(solution)/shard_map/ppermute | solution.py:333
  92.0 3.8 %collective-permute-done.8.refs_5_ = f32[128,256]{1,0:T(8,128)S(1)} collective-permute-done((f32[128,256]{1,0:T(8,128)}, f32[128,256]{1,0:T(8,128)S(1)}, u32[]{:S(2)}, u32[]{:S(2)}) %collective-permute-start.8) | collective-permute-done | bytes 131104 | tf_op jit(solution)/shard_map/ppermute | solution.py:333
  103.3 3.9 %key_value_grad.1 = (bf16[128,1120]{1,0:T(8,128)(2,1)}, bf16[128,1120]{1,0:T(8,128)(2,1)}, f32[128,584]{1,0:T(8,128)}, f32[128,584]{1,0:T(8,128)}, f32[128,584]{1,0:T(8,128)}, /*index=5*/f32[128,584]{1,0:T(8,128)}) custom-call(s32[1]{0:T(128)} %bitcast.place, f32[32,45,112]{2,1,0:T(8,128)} %all-to-all-done.2.got, bf16[10,128,112]{2,1,0:T(8,128)(2,1)S(1)} %copy-done.10, ...), custom_call_target="tpu_custom_call" | custom-call | tf_op jit(solution)/shard_map/key_value_grad/pallas_call | solution.py:65
  108.3 3.0 %collective-permute-start.15 = (f32[128,584]{1,0:T(8,128)}, f32[128,584]{1,0:T(8,128)S(1)}, u32[]{:S(2)}, u32[]{:S(2)}) collective-permute-start(f32[128,584]{1,0:T(8,128)} %get-tuple-element.99), channel_id=1, source_target_pairs={{0,64},{32,96},{64,0},{96,32},{1,65},{33,97},{65,1},{97,33},{2,66}... | collective-permute-start | bytes 897032 | tf_op jit(solution)/shard_map/ppermute | solution.py:333
  118.0 3.2 %query_product.1 = (f32[4,72,256]{2,1,0:T(8,128)}, f32[4,72,256]{2,1,0:T(8,128)}, f32[4,72,256]{2,1,0:T(8,128)}, f32[4,72,256]{2,1,0:T(8,128)}) custom-call(s32[1]{0:T(128)} %bitcast.5.refs_0_, bf16[1120,512]{1,0:T(8,128)(2,1)} %get-tuple-element.95.refs_1_.refs_0_, f32[1120,512]{1,0:T(8,128)S(1)} %collective-permute-done.6.refs_2_.refs_1_, ...), custom_call_target="tpu_custom_call" | custom-call | tf_op jit(solution)/shard_map/query_product/pallas_call | solution.py:65
  122.9 2.7 %collective-permute-start.22 = (f32[4,72,256]{2,1,0:T(8,128)}, f32[4,72,256]{2,1,0:T(8,128)S(1)}, u32[]{:S(2)}, u32[]{:S(2)}) collective-permute-start(f32[4,72,256]{2,1,0:T(8,128)} %get-tuple-element.110), channel_id=1, source_target_pairs={{0,4},{2,6},{4,0},{6,2},{1,5},{3,7},{5,1},{7,3},{8,12},{10,14},{12... | collective-permute-start | bytes 884744 | tf_op jit(solution)/shard_map/ppermute | solution.py:333
  125.6 5.9 %collective-permute-done.21.refs_10_.first = f32[4,72,256]{2,1,0:T(8,128)S(1)} collective-permute-done((f32[4,72,256]{2,1,0:T(8,128)}, f32[4,72,256]{2,1,0:T(8,128)S(1)}, u32[]{:S(2)}, u32[]{:S(2)}) %collective-permute-start.21) | collective-permute-done | bytes 294944 | tf_op jit(solution)/shard_map/ppermute | solution.py:333
  132.5 6.2 %collective-permute-done.22.refs_11_.second = f32[4,72,256]{2,1,0:T(8,128)S(1)} collective-permute-done((f32[4,72,256]{2,1,0:T(8,128)}, f32[4,72,256]{2,1,0:T(8,128)S(1)}, u32[]{:S(2)}, u32[]{:S(2)}) %collective-permute-start.22) | collective-permute-done | bytes 294944 | tf_op jit(solution)/shard_map/ppermute | solution.py:333
  138.7 7.9 %collective-permute-done.23.refs_12_.third = f32[4,72,256]{2,1,0:T(8,128)S(1)} collective-permute-done((f32[4,72,256]{2,1,0:T(8,128)}, f32[4,72,256]{2,1,0:T(8,128)S(1)}, u32[]{:S(2)}, u32[]{:S(2)}) %collective-permute-start.23) | collective-permute-done | bytes 294944 | tf_op jit(solution)/shard_map/ppermute | solution.py:333
  146.6 4.9 %key_value_product.1 = f32[16,72,584]{2,1,0:T(8,128)} custom-call(bf16[1120,512]{1,0:T(8,128)(2,1)} %get-tuple-element.95.refs_1_.refs_0_, f32[1120,512]{1,0:T(8,128)S(1)} %collective-permute-done.6.refs_2_.refs_1_, f32[128,584]{1,0:T(8,128)S(1)} %copy-done.9, f32[128,584]{1,0:T(8,128)S(1)} %collective-permute-done.14.refs_3_, ...), custom_call_target="tpu_custom_call" | custom-call | tf_op jit(solution)/shard_map/key_value_product/pallas_call | solution.py:65
  153.6 5.5 %all-to-all-start.3 = ((f32[16,72,584]{2,1,0:T(8,128)}), f32[16,72,584]{2,1,0:T(8,128)S(1)}, u32[]{:S(2)}, u32[]{:S(2)}) async-start(f32[16,72,584]{2,1,0:T(8,128)} %key_value_product.1), calls=%async_computation.3 | async-start | bytes 5898240 | tf_op jit(solution)/shard_map/all_to_all | solution.py:329
  159.1 4.2 %fusion.1 = f32[128,2240]{0,1:T(8,128)S(1)} fusion(bf16[128,1120]{1,0:T(8,128)(2,1)S(1)} %copy-done.27, bf16[2240,1120]{1,0:T(8,128)(2,1)} %weight.1), kind=kOutput, calls=%fused_computation.3 | convolution fusion | flops 642252800 | bytes 6451200 | tf_op jit(solution)/shard_map/dot_general | solution.py:71
  163.4 4.1 %convolution_add_fusion.1 = f32[128,2240]{0,1:T(8,128)S(1)} fusion(f32[128,2240]{0,1:T(8,128)S(1)} %fusion.1, bf16[128,1120]{1,0:T(8,128)(2,1)S(1)} %copy-done.29, bf16[2240,1120]{1,0:T(8,128)(2,1)} %key_weight.1), kind=kOutput, calls=%fused_computation.1 | convolution fusion | flops 642539520 | bytes 7598080 | tf_op jit(solution)/shard_map/dot_general | solution.py:71
  169.3 1.9 collective-permute-start.24
  171.2 2.7 %collective-permute-start.25 = (f32[72,256]{1,0:T(8,128)}, f32[72,256]{1,0:T(8,128)S(1)}, u32[]{:S(2)}, u32[]{:S(2)}) collective-permute-start(f32[72,256]{1,0:T(8,128)} %get-tuple-element.115), channel_id=1, source_target_pairs={{0,16},{1,17},{16,0},{17,1},{2,18},{3,19},{18,2},{19,3},{4,20},{5,... | collective-permute-start | bytes 221192 | tf_op jit(solution)/shard_map/ppermute | solution.py:333
  175.3 2.4 %fusion = bf16[128,2240]{0,1:T(8,128)(2,1)} fusion(f32[128,2240]{0,1:T(8,128)S(1)} %convolution_add_fusion.1, bf16[128,1120]{1,0:T(8,128)(2,1)S(1)} %copy-done.28, bf16[2240,1120]{1,0:T(8,128)(2,1)S(1)} %bitcast.16), kind=kOutput, calls=%fused_computation.2 | convolution fusion | flops 642826240 | bytes 7024640 | tf_op jit(solution)/shard_map/dot_general | solution.py:71
  177.7 2.1 %copy.10 = bf16[128,2240]{1,0:T(8,128)(2,1)} copy(bf16[128,2240]{0,1:T(8,128)(2,1)} %fusion) | data formatting | bytes 1146880 | tf_op jit(solution)/shard_map/convert_element_type | solution.py:491
  179.8 15.0 %collective-permute-done.24.first = f32[72,256]{1,0:T(8,128)S(1)} collective-permute-done((f32[72,256]{1,0:T(8,128)}, f32[72,256]{1,0:T(8,128)S(1)}, u32[]{:S(2)}, u32[]{:S(2)}) %collective-permute-start.24) | collective-permute-done | bytes 73760 | tf_op jit(solution)/shard_map/ppermute | solution.py:333
  194.9 3.5 %all-to-all-done.3.key_value = f32[16,72,584]{2,1,0:T(8,128)S(1)} async-done(((f32[16,72,584]{2,1,0:T(8,128)}), f32[16,72,584]{2,1,0:T(8,128)S(1)}, u32[]{:S(2)}, u32[]{:S(2)}) %all-to-all-start.3) | async-done | bytes 2691104 | tf_op jit(solution)/shard_map/all_to_all | solution.py:329
  (111 shorter events, 38.4 us)
Async XLA Ops:
  8.8 22.7 %all-to-all-start = ((f32[32,45,112]{2,1,0:T(8,128)}), f32[32,45,112]{2,1,0:T(8,128)S(1)}, u32[]{:S(2)}, u32[]{:S(2)}) async-start(f32[32,45,112]{2,1,0:T(8,128)} %get-tuple-element.63), calls=%async_computation | async-start | bytes 1572864 | tf_op jit(solution)/shard_map/all_to_all | solution.py:329
  19.3 15.7 %collective-permute-start = (f32[1120,128]{1,0:T(8,128)}, f32[1120,128]{1,0:T(8,128)S(1)}, u32[]{:S(2)}, u32[]{:S(2)}) collective-permute-start(f32[1120,128]{1,0:T(8,128)} %get-tuple-element.77.refs_0_), channel_id=1, source_target_pairs={{0,32},{32,64},{64,96},{96,0},{1,33},{33,65},{65,97},{97,1},{2,34}... | collective-permute-start | bytes 1720328 | tf_op jit(solution)/shard_map/ppermute | solution.py:333
  20.8 15.1 %collective-permute-start.1 = (f32[1120,128]{1,0:T(8,128)}, f32[1120,128]{1,0:T(8,128)S(1)}, u32[]{:S(2)}, u32[]{:S(2)}) collective-permute-start(f32[1120,128]{1,0:T(8,128)} %get-tuple-element.76.refs_1_), channel_id=1, source_target_pairs={{0,96},{32,0},{64,32},{96,64},{1,97},{33,1},{65,33},{97,65},{2,98}... | collective-permute-start | bytes 1720328 | tf_op jit(solution)/shard_map/ppermute | solution.py:333
  32.5 29.5 %copy-start.1 = (bf16[10,128,112]{2,1,0:T(8,128)(2,1)S(1)}, bf16[10,128,112]{2,1,0:T(8,128)(2,1)}, u32[]{:S(2)}) copy-start(bf16[10,128,112]{2,1,0:T(8,128)(2,1)} %query.1.refs_1_) | copy-start | bytes 860164
  35.9 26.1 %all-to-all-start.1 = ((f32[32,70,112]{2,1,0:T(8,128)}), f32[32,70,112]{2,1,0:T(8,128)S(1)}, u32[]{:S(2)}, u32[]{:S(2)}) async-start(f32[32,70,112]{2,1,0:T(8,128)} %get-tuple-element.68), calls=%async_computation.1 | async-start | bytes 2359296 | tf_op jit(solution)/shard_map/all_to_all | solution.py:329
  43.2 22.0 %collective-permute-start.2 = (f32[1120,128]{1,0:T(8,128)S(1)}, f32[1120,128]{1,0:T(8,128)S(1)}, u32[]{:S(2)}, u32[]{:S(2)}) collective-permute-start(f32[1120,128]{1,0:T(8,128)S(1)} %collective-permute-done.refs_2_), channel_id=1, source_target_pairs={{0,32},{32,64},{64,96},{96,0},{1,33},{33,65},{65,97},{97,1},{2,34}... | collective-permute-start | bytes 1720328 | tf_op jit(solution)/shard_map/ppermute | solution.py:333
  44.6 20.7 %collective-permute-start.3 = (f32[1120,128]{1,0:T(8,128)S(1)}, f32[1120,128]{1,0:T(8,128)}, u32[]{:S(2)}, u32[]{:S(2)}) collective-permute-start(f32[1120,128]{1,0:T(8,128)S(1)} %collective-permute-done.1.refs_7_), channel_id=1, source_target_pairs={{0,96},{32,0},{64,32},{96,64},{1,97},{33,1},{65,33},{97,65},{2,98}... | collective-permute-start | bytes 1720328 | tf_op jit(solution)/shard_map/ppermute | solution.py:333
  45.3 25.5 %collective-permute-start.4 = (f32[1120,128]{1,0:T(8,128)}, f32[1120,128]{1,0:T(8,128)}, u32[]{:S(2)}, u32[]{:S(2)}) collective-permute-start(f32[1120,128]{1,0:T(8,128)} %get-tuple-element.76.refs_1_), channel_id=1, source_target_pairs={{0,32},{32,64},{64,96},{96,0},{1,33},{33,65},{65,97},{97,1},{2,34}... | collective-permute-start | bytes 1720328 | tf_op jit(solution)/shard_map/ppermute | solution.py:333
  46.6 25.2 %collective-permute-start.5 = (f32[1120,128]{1,0:T(8,128)}, f32[1120,128]{1,0:T(8,128)}, u32[]{:S(2)}, u32[]{:S(2)}) collective-permute-start(f32[1120,128]{1,0:T(8,128)} %get-tuple-element.77.refs_0_), channel_id=1, source_target_pairs={{0,96},{32,0},{64,32},{96,64},{1,97},{33,1},{65,33},{97,65},{2,98}... | collective-permute-start | bytes 1720328 | tf_op jit(solution)/shard_map/ppermute | solution.py:333
  75.9 24.6 %collective-permute-start.6 = (f32[1120,512]{1,0:T(8,128)}, f32[1120,512]{1,0:T(8,128)S(1)}, u32[]{:S(2)}, u32[]{:S(2)}) collective-permute-start(f32[1120,512]{1,0:T(8,128)} %get-tuple-element.84), channel_id=1, source_target_pairs={{0,8},{8,0},{1,9},{9,1},{2,10},{10,2},{3,11},{11,3},{4,12},{12,4},... | collective-permute-start | bytes 6881288 | tf_op jit(solution)/shard_map/ppermute | solution.py:341
  75.9 24.6 %all-to-all-start.2 = ((f32[32,45,112]{2,1,0:T(8,128)}), f32[32,45,112]{2,1,0:T(8,128)}, u32[]{:S(2)}, u32[]{:S(2)}) async-start(f32[32,45,112]{2,1,0:T(8,128)} %get-tuple-element.78), calls=%async_computation.2 | async-start | bytes 1572864 | tf_op jit(solution)/shard_map/all_to_all | solution.py:329
  86.2 5.8 %collective-permute-start.7 = (f32[128,256]{1,0:T(8,128)}, f32[128,256]{1,0:T(8,128)S(1)}, u32[]{:S(2)}, u32[]{:S(2)}) collective-permute-start(f32[128,256]{1,0:T(8,128)} %get-tuple-element.86), channel_id=1, source_target_pairs={{0,32},{32,64},{64,96},{96,0},{1,33},{33,65},{65,97},{97,1},{2,34}... | collective-permute-start | bytes 393224 | tf_op jit(solution)/shard_map/ppermute | solution.py:333
  87.7 8.1 %collective-permute-start.8 = (f32[128,256]{1,0:T(8,128)}, f32[128,256]{1,0:T(8,128)S(1)}, u32[]{:S(2)}, u32[]{:S(2)}) collective-permute-start(f32[128,256]{1,0:T(8,128)} %get-tuple-element.87), channel_id=1, source_target_pairs={{0,64},{32,96},{64,0},{96,32},{1,65},{33,97},{65,1},{97,33},{2,66}... | collective-permute-start | bytes 393224 | tf_op jit(solution)/shard_map/ppermute | solution.py:333
  89.0 8.1 %collective-permute-start.9 = (f32[128,256]{1,0:T(8,128)}, f32[128,256]{1,0:T(8,128)S(1)}, u32[]{:S(2)}, u32[]{:S(2)}) collective-permute-start(f32[128,256]{1,0:T(8,128)} %get-tuple-element.88), channel_id=1, source_target_pairs={{0,96},{32,0},{64,32},{96,64},{1,97},{33,1},{65,33},{97,65},{2,98}... | collective-permute-start | bytes 393224 | tf_op jit(solution)/shard_map/ppermute | solution.py:333
  91.4 6.4 %collective-permute-start.10 = (f32[128,256]{1,0:T(8,128)}, f32[128,256]{1,0:T(8,128)S(1)}, u32[]{:S(2)}, u32[]{:S(2)}) collective-permute-start(f32[128,256]{1,0:T(8,128)} %get-tuple-element.101.refs_3_), channel_id=1, source_target_pairs={{0,8},{8,0},{1,9},{9,1},{2,10},{10,2},{3,11},{11,3},{4,12},{12,4},... | collective-permute-start | bytes 393224 | tf_op jit(solution)/shard_map/ppermute | solution.py:341
  92.0 6.4 %collective-permute-start.11 = (f32[128,256]{1,0:T(8,128)S(1)}, f32[128,256]{1,0:T(8,128)S(1)}, u32[]{:S(2)}, u32[]{:S(2)}) collective-permute-start(f32[128,256]{1,0:T(8,128)S(1)} %collective-permute-done.7.refs_4_), channel_id=1, source_target_pairs={{0,8},{8,0},{1,9},{9,1},{2,10},{10,2},{3,11},{11,3},{4,12},{12,4},... | collective-permute-start | bytes 393224 | tf_op jit(solution)/shard_map/ppermute | solution.py:341
  95.8 3.3 %collective-permute-start.12 = (f32[128,256]{1,0:T(8,128)S(1)}, f32[128,256]{1,0:T(8,128)S(1)}, u32[]{:S(2)}, u32[]{:S(2)}) collective-permute-start(f32[128,256]{1,0:T(8,128)S(1)} %collective-permute-done.8.refs_5_), channel_id=1, source_target_pairs={{0,8},{8,0},{1,9},{9,1},{2,10},{10,2},{3,11},{11,3},{4,12},{12,4},... | collective-permute-start | bytes 393224 | tf_op jit(solution)/shard_map/ppermute | solution.py:341
  97.1 2.7 %collective-permute-start.13 = (f32[128,256]{1,0:T(8,128)S(1)}, f32[128,256]{1,0:T(8,128)S(1)}, u32[]{:S(2)}, u32[]{:S(2)}) collective-permute-start(f32[128,256]{1,0:T(8,128)S(1)} %collective-permute-done.9.refs_6_), channel_id=1, source_target_pairs={{0,8},{8,0},{1,9},{9,1},{2,10},{10,2},{3,11},{11,3},{4,12},{12,4},... | collective-permute-start | bytes 393224 | tf_op jit(solution)/shard_map/ppermute | solution.py:341
  107.3 24.2 %collective-permute-start.14 = (f32[128,584]{1,0:T(8,128)}, f32[128,584]{1,0:T(8,128)S(1)}, u32[]{:S(2)}, u32[]{:S(2)}) collective-permute-start(f32[128,584]{1,0:T(8,128)} %get-tuple-element.98), channel_id=1, source_target_pairs={{0,32},{32,64},{64,96},{96,0},{1,33},{33,65},{65,97},{97,1},{2,34}... | collective-permute-start | bytes 897032 | tf_op jit(solution)/shard_map/ppermute | solution.py:333
  108.3 23.7 %collective-permute-start.15 = (f32[128,584]{1,0:T(8,128)}, f32[128,584]{1,0:T(8,128)S(1)}, u32[]{:S(2)}, u32[]{:S(2)}) collective-permute-start(f32[128,584]{1,0:T(8,128)} %get-tuple-element.99), channel_id=1, source_target_pairs={{0,64},{32,96},{64,0},{96,32},{1,65},{33,97},{65,1},{97,33},{2,66}... | collective-permute-start | bytes 897032 | tf_op jit(solution)/shard_map/ppermute | solution.py:333
  111.3 20.7 %collective-permute-start.16 = (f32[128,584]{1,0:T(8,128)}, f32[128,584]{1,0:T(8,128)}, u32[]{:S(2)}, u32[]{:S(2)}) collective-permute-start(f32[128,584]{1,0:T(8,128)} %get-tuple-element.100), channel_id=1, source_target_pairs={{0,96},{32,0},{64,32},{96,64},{1,97},{33,1},{65,33},{97,65},{2,98}... | collective-permute-start | bytes 897032 | tf_op jit(solution)/shard_map/ppermute | solution.py:333
  121.2 10.2 %collective-permute-start.21 = (f32[4,72,256]{2,1,0:T(8,128)}, f32[4,72,256]{2,1,0:T(8,128)S(1)}, u32[]{:S(2)}, u32[]{:S(2)}) collective-permute-start(f32[4,72,256]{2,1,0:T(8,128)} %get-tuple-element.109), channel_id=1, source_target_pairs={{0,2},{2,4},{4,6},{6,0},{1,3},{3,5},{5,7},{7,1},{8,10},{10,12},{12... | collective-permute-start | bytes 884744 | tf_op jit(solution)/shard_map/ppermute | solution.py:333
  122.9 15.8 %collective-permute-start.22 = (f32[4,72,256]{2,1,0:T(8,128)}, f32[4,72,256]{2,1,0:T(8,128)S(1)}, u32[]{:S(2)}, u32[]{:S(2)}) collective-permute-start(f32[4,72,256]{2,1,0:T(8,128)} %get-tuple-element.110), channel_id=1, source_target_pairs={{0,4},{2,6},{4,0},{6,2},{1,5},{3,7},{5,1},{7,3},{8,12},{10,14},{12... | collective-permute-start | bytes 884744 | tf_op jit(solution)/shard_map/ppermute | solution.py:333
  131.5 15.1 %collective-permute-start.17 = (f32[128,584]{1,0:T(8,128)S(1)}, f32[128,584]{1,0:T(8,128)S(1)}, u32[]{:S(2)}, u32[]{:S(2)}) collective-permute-start(f32[128,584]{1,0:T(8,128)S(1)} %copy-done.9), channel_id=1, source_target_pairs={{0,8},{8,0},{1,9},{9,1},{2,10},{10,2},{3,11},{11,3},{4,12},{12,4},... | collective-permute-start | bytes 897032 | tf_op jit(solution)/shard_map/ppermute | solution.py:341
  131.5 15.1 %collective-permute-start.18 = (f32[128,584]{1,0:T(8,128)S(1)}, f32[128,584]{1,0:T(8,128)S(1)}, u32[]{:S(2)}, u32[]{:S(2)}) collective-permute-start(f32[128,584]{1,0:T(8,128)S(1)} %collective-permute-done.14.refs_3_), channel_id=1, source_target_pairs={{0,8},{8,0},{1,9},{9,1},{2,10},{10,2},{3,11},{11,3},{4,12},{12,4},... | collective-permute-start | bytes 897032 | tf_op jit(solution)/shard_map/ppermute | solution.py:341
  132.0 14.6 %collective-permute-start.19 = (f32[128,584]{1,0:T(8,128)S(1)}, f32[128,584]{1,0:T(8,128)S(1)}, u32[]{:S(2)}, u32[]{:S(2)}) collective-permute-start(f32[128,584]{1,0:T(8,128)S(1)} %collective-permute-done.15.refs_4_), channel_id=1, source_target_pairs={{0,8},{8,0},{1,9},{9,1},{2,10},{10,2},{3,11},{11,3},{4,12},{12,4},... | collective-permute-start | bytes 897032 | tf_op jit(solution)/shard_map/ppermute | solution.py:341
  132.1 14.5 %collective-permute-start.20 = (f32[128,584]{1,0:T(8,128)}, f32[128,584]{1,0:T(8,128)S(1)}, u32[]{:S(2)}, u32[]{:S(2)}) collective-permute-start(f32[128,584]{1,0:T(8,128)} %collective-permute-done.16.refs_5_), channel_id=1, source_target_pairs={{0,8},{8,0},{1,9},{9,1},{2,10},{10,2},{3,11},{11,3},{4,12},{12,4},... | collective-permute-start | bytes 897032 | tf_op jit(solution)/shard_map/ppermute | solution.py:341
  138.7 7.9 %collective-permute-start.23 = (f32[4,72,256]{2,1,0:T(8,128)}, f32[4,72,256]{2,1,0:T(8,128)S(1)}, u32[]{:S(2)}, u32[]{:S(2)}) collective-permute-start(f32[4,72,256]{2,1,0:T(8,128)} %get-tuple-element.111), channel_id=1, source_target_pairs={{0,6},{2,0},{4,2},{6,4},{1,7},{3,1},{5,3},{7,5},{8,14},{10,8},{12,... | collective-permute-start | bytes 884744 | tf_op jit(solution)/shard_map/ppermute | solution.py:333
  153.6 44.8 %all-to-all-start.3 = ((f32[16,72,584]{2,1,0:T(8,128)}), f32[16,72,584]{2,1,0:T(8,128)S(1)}, u32[]{:S(2)}, u32[]{:S(2)}) async-start(f32[16,72,584]{2,1,0:T(8,128)} %key_value_product.1), calls=%async_computation.3 | async-start | bytes 5898240 | tf_op jit(solution)/shard_map/all_to_all | solution.py:329
  169.3 25.6 %collective-permute-start.24 = (f32[72,256]{1,0:T(8,128)}, f32[72,256]{1,0:T(8,128)S(1)}, u32[]{:S(2)}, u32[]{:S(2)}) collective-permute-start(f32[72,256]{1,0:T(8,128)} %get-tuple-element.114), channel_id=1, source_target_pairs={{0,1},{1,16},{16,17},{17,0},{2,3},{3,18},{18,19},{19,2},{4,5},{5,2... | collective-permute-start | bytes 221192 | tf_op jit(solution)/shard_map/ppermute | solution.py:333
  171.2 23.7 %collective-permute-start.25 = (f32[72,256]{1,0:T(8,128)}, f32[72,256]{1,0:T(8,128)S(1)}, u32[]{:S(2)}, u32[]{:S(2)}) collective-permute-start(f32[72,256]{1,0:T(8,128)} %get-tuple-element.115), channel_id=1, source_target_pairs={{0,16},{1,17},{16,0},{17,1},{2,18},{3,19},{18,2},{19,3},{4,20},{5,... | collective-permute-start | bytes 221192 | tf_op jit(solution)/shard_map/ppermute | solution.py:333
  173.9 21.0 %collective-permute-start.26 = (f32[72,256]{1,0:T(8,128)}, f32[72,256]{1,0:T(8,128)S(1)}, u32[]{:S(2)}, u32[]{:S(2)}) collective-permute-start(f32[72,256]{1,0:T(8,128)} %get-tuple-element.116), channel_id=1, source_target_pairs={{0,17},{1,0},{16,1},{17,16},{2,19},{3,2},{18,3},{19,18},{4,21},{5,... | collective-permute-start | bytes 221192 | tf_op jit(solution)/shard_map/ppermute | solution.py:333
  (31 other events, 114.5 us)

commit v7 on v6

--- a/solution.py
+++ b/solution.py
@@ -24,6 +24,7 @@
 EARLY = 256
 LATE = COLS - EARLY
 WIDE = 2 * COLS + LATE
+LANES = 640
 TOKENS = 128
 
 EPSILON = 1e-15
@@ -219,13 +220,11 @@
         flat[:, part] = values.astype(F32)
     split_columns(flat, blocks)
     place_columns(place, blocks, (own, first, second, third), 0, 0, EARLY)
-    for slot in range(REPLICAS):
-        late[slot] = blocks[lax.rem(place[0] + slot, REPLICAS)][:, EARLY:]
-
-
-def key_value_grad_kernel(
-    place, got, key, value, late, grad_key, grad_value, own, first, second, third, state, flat_key, flat_value, blocks
-):
+    for block in range(REPLICAS):
+        late[block] = blocks[block][:, EARLY:]
+
+
+def key_value_grad_kernel(got, key, value, late, grad_key, grad_value, sent, state, flat_key, flat_value):
     load_parts(state, got)
     totals = got[0, PART : PART + HEADS, :]
     for tile in range(1, TILES):
@@ -242,68 +241,60 @@
         values = jnp.where(key_head.astype(F32) > 0, values, 0.0).astype(BF16)
         grad_key[:, part] = values
         flat_key[:, part] = values.astype(F32)
-    outs = (own, first, second, third)
-    split_columns(flat_key, blocks)
-    place_columns(place, blocks, outs, 0)
-    split_columns(flat_value, blocks)
-    place_columns(place, blocks, outs, COLS)
-    for slot, out in enumerate(outs):
-        out[:, 2 * COLS :] = late[slot]
-
-
-def turn_kernel(tokens, top, bottom):
+    for block in range(REPLICAS):
+        part = slice(block * COLS, (block + 1) * COLS)
+        sent[block, :, :COLS] = flat_key[:, part]
+        sent[block, :, COLS : 2 * COLS] = flat_value[:, part]
+        sent[block, :, 2 * COLS : WIDE] = late[block]
+        sent[block, :, WIDE:] = jnp.zeros((TOKENS, LANES - WIDE), F32)
+
+
+def turn_kernel(core, tokens, mine, other, turned):
     for start in range(0, D, 128):
-        turned = tokens[:, start : min(start + 128, D)].astype(F32).T
-        cut = min(max(D // 2 - start, 0), turned.shape[0])
-        if cut > 0:
-            top[start : start + cut, :] = turned[:cut]
-        if cut < turned.shape[0]:
-            at = start + cut - D // 2
-            bottom[at : at + turned.shape[0] - cut, :] = turned[cut:]
-
-
-def join_kernel(core, *refs):
-    parts, kept, given = refs[:-2], refs[-2], refs[-1]
-    mine = pl.multiple_of(core[0] * HALF, 16)
-    other = pl.multiple_of((1 - core[0]) * HALF, 16)
-    for index, part in enumerate(parts):
-        slot, rows = index // 2, slice(index % 2 * HALF, (index % 2 + 1) * HALF)
-        at = slice(slot * TOKENS, (slot + 1) * TOKENS)
-        kept[rows, at] = part[pl.ds(mine, HALF), :].astype(BF16)
-        given[rows, at] = part[pl.ds(other, HALF), :]
-
-
-def fill_columns(columns, blocks):
-    for index, block in enumerate(blocks):
-        columns[index * TOKENS : (index + 1) * TOKENS, :] = block[...].astype(BF16)
-
-
-def row_products(normalizer, kept, got, columns, rows):
-    own = dot(kept[rows, :], columns[: REPLICAS * TOKENS, :], 1, 0)
-    other = dot(got[rows, :].astype(BF16), columns[REPLICAS * TOKENS :, :], 1, 0)
-    return (own + other) * normalizer
-
-
-def query_product_kernel(normalizer, across, kept, got, *refs):
-    blocks, outs, columns, product = refs[: 2 * REPLICAS], refs[2 * REPLICAS : -2], refs[-2], refs[-1]
-    fill_columns(columns, blocks)
+        size = min(128, D - start)
+        turned[start : start + size, :] = tokens[:, start : start + size].astype(F32).T
+    for half in range(CORES):
+        rows = slice(half * HALF, (half + 1) * HALF)
+        for out, which in ((mine, core[0]), (other, 1 - core[0])):
+            start = pl.multiple_of((half * CORES + which) * HALF, 16)
+            out[rows, :] = turned[pl.ds(start, HALF), :]
+
+
+def join_kernel(*refs):
+    for slot, part in enumerate(refs[:-1]):
+        refs[-1][:, slot * TOKENS : (slot + 1) * TOKENS] = part[...].astype(BF16)
+
+
+def pack_kernel(*refs):
+    out = refs[-1]
+    for slot, part in enumerate(refs[:-1]):
+        out[slot * TOKENS : (slot + 1) * TOKENS, :] = part[...].astype(out.dtype)
+
+
+def query_product_kernel(normalizer, across, rows, own, other, *refs):
+    outs, columns, product = refs[:-2], refs[-2], refs[-1]
+    columns[: REPLICAS * TOKENS, :] = own[...].astype(BF16)
+    columns[REPLICAS * TOKENS :, :] = other[...].astype(BF16)
     span = PLANE_SIZE // CORES
     for half in range(CORES):
-        values = row_products(normalizer, kept, got, columns, slice(half * HALF, (half + 1) * HALF))
+        values = dot(rows[half * HALF : (half + 1) * HALF, :], columns[...], 1, 0) * normalizer
         for index in range(span):
             product[half * span + index, :ROWS, :] = values[index * ROWS : (index + 1) * ROWS]
     for slot, out in enumerate(outs):
         at = lax.rem(across[0] + slot, RING)
-        for other in range(RING):
-            out[other] = product[(other // 2) * span + at * 2 + other % 2]
-
-
-def key_value_product_kernel(normalizer, kept, got, *refs):
-    blocks, out, columns = refs[: 2 * REPLICAS], refs[-2], refs[-1]
-    fill_columns(columns, blocks)
+        for block in range(RING):
+            out[block] = product[(block // 2) * span + at * 2 + block % 2]
+
+
+def key_value_product_kernel(normalizer, place, rows, own, other, out, columns):
+    for core, blocks in enumerate((own, other)):
+        for slot in range(REPLICAS):
+            at = (core * REPLICAS + slot) * TOKENS
+            source = lax.rem(place[0] + REPLICAS - slot, REPLICAS)
+            columns[at : at + TOKENS, :] = blocks[source].astype(BF16)
     span = PLANE_SIZE // CORES
     for half in range(CORES):
-        values = row_products(normalizer, kept, got, columns, slice(half * HALF, (half + 1) * HALF))
+        values = dot(rows[half * HALF : (half + 1) * HALF, :], columns[...], 1, 0) * normalizer
         for index in range(span):
             out[half * span + index, :ROWS, :] = values[index * ROWS : (index + 1) * ROWS]
 
@@ -320,7 +311,7 @@
         total = total + key_value[index]
     key_out[...] = total[:ROWS, :COLS]
     value_out[...] = total[:ROWS, COLS : 2 * COLS]
-    query_out[:, EARLY:] = total[:ROWS, 2 * COLS :]
+    query_out[:, EARLY:] = total[:ROWS, 2 * COLS : WIDE]
     total = (own[...] + first[...]) + (second[...] + third[...])
     query_out[:, :EARLY] = total[:ROWS]
 
@@ -377,7 +368,10 @@
     )(tokens, key_weight, value_weight)
     sent, later_tokens = lax.optimization_barrier((sent, tokens))
     half = shaped((D // 2, TOKENS))
-    top, bottom = call(turn_kernel, "turn", [half, half], [BLOCK])(later_tokens)
+    top, bottom = call(
+        turn_kernel, "turn", [half, half], [IN_SMEM, BLOCK], [pltpu.VMEM((D, TOKENS), F32)]
+    )(core, later_tokens)
+    bottom = swap_cores(bottom)
     left_top = shift(top, 1, "dp")
     right_bottom = shift(bottom, 3, "dp")
     got = exchange(sent, IMAGE)
@@ -426,53 +420,45 @@
         arrived=(1,),
     )(place, got_state, query, numer, total, grad_denom)
     query_columns = shifted(query_columns, "dp")
-    half_rows = CORES * HALF
-    kept_rows, given_rows = call(
+    (rows,) = call(
         join_kernel,
         "join",
-        [shaped((half_rows, REPLICAS * TOKENS), BF16), shaped((half_rows, REPLICAS * TOKENS))],
-        [IN_SMEM] + [BLOCK] * 8,
-        arrived=(3, 4, 5, 6, 7, 8),
-    )(core, top, bottom, left_top, left_bottom, far_top, far_bottom, right_top, right_bottom)
-    got_rows = swap_cores(given_rows)
-    query_columns = both_cores(query_columns)
-    got, kept_rows, got_rows, query_columns = lax.optimization_barrier(
-        (got, kept_rows, got_rows, query_columns)
-    )
-    block = shaped((TOKENS, WIDE))
-    grad_key, grad_value, *key_value_columns = call(
+        [shaped((CORES * HALF, 2 * REPLICAS * TOKENS), BF16)],
+        [BLOCK] * 8,
+        arrived=tuple(range(1, 8)),
+    )(top, left_top, far_top, right_top, bottom, left_bottom, far_bottom, right_bottom)
+    (query_columns,) = call(
+        pack_kernel,
+        "pack_query",
+        [shaped((REPLICAS * TOKENS, EARLY))],
+        [BLOCK] * RING,
+        arrived=(1, 2, 3),
+    )(*query_columns)
+    got, rows, query_columns = lax.optimization_barrier((got, rows, query_columns))
+
+    grad_key, grad_value, sent = call(
         key_value_grad_kernel,
         "key_value_grad",
-        [flat, flat, block, block, block, block],
-        [IN_SMEM] + [BLOCK] * 4,
-        [state, wide, wide, blocks],
-        arrived=(1, 2, 3, 4),
-    )(place, got, key, value, late)
+        [flat, flat, shaped((REPLICAS, TOKENS, LANES))],
+        [BLOCK] * 4,
+        [state, wide, wide],
+        arrived=(0, 1, 2, 3),
+    )(got, key, value, late)
+    own_columns = exchange(sent, "dp")
     slots = call(
-        lambda *refs: query_product_kernel(normalizer, *refs),
+        lambda *refs: query_product_kernel(normalizer, *refs[:4], *refs[5:]),
         "query_product",
         [shaped((RING, PADDED_ROWS, EARLY))] * RING,
-        [IN_SMEM] + [BLOCK] * (2 + 2 * REPLICAS),
+        [IN_SMEM, BLOCK, BLOCK, BLOCK, ANYWHERE],
         [
             pltpu.VMEM((2 * REPLICAS * TOKENS, EARLY), BF16),
             pltpu.VMEM((PLANE_SIZE, PADDED_ROWS, EARLY), F32),
         ],
         vmem=24,
-        arrived=tuple(range(2, 11)),
-    )(across, kept_rows, got_rows, *query_columns)
+        arrived=(3,),
+    )(across, rows, query_columns, swap_cores(query_columns), sent)
     slots = shifted(slots, "x")
-
-    key_value_columns = both_cores(shifted(key_value_columns, "dp"))
-    (product,) = call(
-        lambda *refs: key_value_product_kernel(normalizer, *refs[:10], *refs[13:]),
-        "key_value_product",
-        [shaped((PLANE_SIZE, PADDED_ROWS, WIDE))],
-        [BLOCK] * (2 + 2 * REPLICAS) + [ANYWHERE] * 3,
-        [pltpu.VMEM((2 * REPLICAS * TOKENS, WIDE), BF16)],
-        vmem=24,
-        arrived=tuple(range(1, 13)),
-    )(kept_rows, got_rows, *key_value_columns, *slots[1:])
-    key_value_out = exchange(product, PLANE)
+    own_columns, slots = lax.optimization_barrier((own_columns, slots))
     slots = call(
         second_stage_kernel,
         "second_stage",
@@ -480,6 +466,16 @@
         [IN_SMEM] + [BLOCK] * RING,
         arrived=(2, 3, 4),
     )(along, *slots)
+    (product,) = call(
+        lambda *refs: key_value_product_kernel(normalizer, *refs[:4], *refs[5:]),
+        "key_value_product",
+        [shaped((PLANE_SIZE, PADDED_ROWS, LANES))],
+        [IN_SMEM, BLOCK, BLOCK, BLOCK, ANYWHERE],
+        [pltpu.VMEM((2 * REPLICAS * TOKENS, LANES), BF16)],
+        vmem=24,
+        arrived=(2, 3),
+    )(place, rows, own_columns, swap_cores(own_columns), slots[0])
+    key_value_out = exchange(product, PLANE)
     slots = shifted(slots, ("zh", "zl"))
     block = shaped((ROWS, COLS))
     query_out, key_out, value_out = call(

time: 202 us -> 185 us (0.916)
  local copies, waits for them, and re-layouts: 19.2 us -> 3.16 us
    unnamed x64 -> x32, local copies, waits for them, and re-layouts: 17 us -> 1.05 us
    ppermute x18 -> x15, waiting for transfers between devices: 47.7 us -> 39.9 us  [shift(): lax.ppermute(values, axis, [(i, (i + by) % RING) for i in range(RING)])]
    all_to_all x4 -> x5, starting transfers between devices: 28.4 us -> 32.5 us  [exchange(): return lax.all_to_all(blocks, axes, 0, 0, tiled=True)]
    all_to_all x4 -> x5, waiting for transfers between devices: 24 us -> 27.2 us  [exchange(): return lax.all_to_all(blocks, axes, 0, 0, tiled=True)]
    ppermute x9 -> x3, waiting for transfers between devices: 0.02 us -> 3.21 us  [swap_cores(): return lax.ppermute(values, 'core', [(0, 1), (1, 0)])]
    ppermute x18 -> x15, starting transfers between devices: 26.1 us -> 23.4 us  [shift(): lax.ppermute(values, axis, [(i, (i + by) % RING) for i in range(RING)])]
    pallas_call x12 -> x13, Pallas kernels: 42.2 us -> 43.1 us  [with_placed(): return run(*placed)]
  transfers between devices with their start and end apart: 31 -> 23, of which waited for: 13 -> 12; matrix products, arithmetic and copies ran while one was open for 6% -> 7% of each run, Pallas kernels for 10% -> 13%
where the time goes in v7:
time: 185 us; the launch traced here: 184 us
  waiting for transfers between devices  70.3 us (38%)
  starting transfers between devices  55.9 us (30%)
  Pallas kernels  43.1 us (23%)
  matrix products  10.7 us (6%)
  local copies, waits for them, and re-layouts  3.16 us (2%)
    pallas_call x13, Pallas kernels, with_placed(): return run(*placed)  43.1 us
    ppermute x15, waiting for transfers between devices, shift(): lax.ppermute(values, axis, [(i, (i + by) % RING) for i in range(RING)])  39.9 us
    all_to_all x5, starting transfers between devices, exchange(): return lax.all_to_all(blocks, axes, 0, 0, tiled=True)  32.5 us
    all_to_all x5, waiting for transfers between devices, exchange(): return lax.all_to_all(blocks, axes, 0, 0, tiled=True)  27.2 us
    ppermute x15, starting transfers between devices, shift(): lax.ppermute(values, axis, [(i, (i + by) % RING) for i in range(RING)])  23.4 us
    dot_general x3, matrix products, dot(): lax.dot_general(left, right, (((left_dim,), (right_dim,)), ((), ())), pre...  10.7 us
  transfers between devices with their start and end apart: 23, of which 12 were waited for; matrix products, arithmetic and copies ran while one was open for 7% of the time, Pallas kernels for 13%

profile of v7, /device:TPU:8, one launch (start us, length us, event | category | flops | bytes accessed | tf_op | source)
XLA Modules:
  0.0 184.0 jit_solution(15007375546527813614)
XLA Ops:
  0.6 8.1 %key_value.1 = (bf16[10,128,112]{2,1,0:T(8,128)(2,1)}, bf16[10,128,112]{2,1,0:T(8,128)(2,1)}, f32[32,45,112]{2,1,0:T(8,128)}) custom-call(bf16[128,2240]{1,0:T(8,128)(2,1)} %bitcast.17, bf16[2240,1120]{1,0:T(8,128)(2,1)} %key_weight.1, bf16[2240,1120]{1,0:T(8,128)(2,1)} %value_weight.1), custom_call_target="tpu_custom_call" | custom-call | tf_op jit(solution)/shard_map/key_value/pallas_call | solution.py:66
  8.8 2.3 %turn.1 = (f32[1120,128]{1,0:T(8,128)}, f32[1120,128]{1,0:T(8,128)}) custom-call(s32[1]{0:T(128)} %bitcast.3.core, bf16[128,2240]{1,0:T(8,128)(2,1)} %bitcast.18), custom_call_target="tpu_custom_call" | custom-call | tf_op jit(solution)/shard_map/turn/pallas_call | solution.py:66
  11.1 8.3 %all-to-all-start = ((f32[32,45,112]{2,1,0:T(8,128)}), f32[32,45,112]{2,1,0:T(8,128)S(1)}, u32[]{:S(2)}, u32[]{:S(2)}) async-start(f32[32,45,112]{2,1,0:T(8,128)} %get-tuple-element.55), calls=%async_computation | async-start | bytes 1572864 | tf_op jit(solution)/shard_map/all_to_all | solution.py:320
  21.5 4.4 %query.1.refs_1_ = bf16[10,128,112]{2,1,0:T(8,128)(2,1)} custom-call(bf16[128,2240]{1,0:T(8,128)(2,1)} %bitcast.19, bf16[2240,1120]{1,0:T(8,128)(2,1)} %weight.1), custom_call_target="tpu_custom_call" | custom-call | tf_op jit(solution)/shard_map/query/pallas_call | solution.py:66
  25.9 8.0 %all-to-all-done.refs_0_ = f32[32,45,112]{2,1,0:T(8,128)S(1)} async-done(((f32[32,45,112]{2,1,0:T(8,128)}), f32[32,45,112]{2,1,0:T(8,128)S(1)}, u32[]{:S(2)}, u32[]{:S(2)}) %all-to-all-start) | async-done | bytes 645152 | tf_op jit(solution)/shard_map/all_to_all | solution.py:320
  34.9 2.4 %numerator.1 = (f32[32,70,112]{2,1,0:T(8,128)}, bf16[10,128,112]{2,1,0:T(8,128)(2,1)}, f32[10,112]{1,0:T(8,128)}) custom-call(f32[32,45,112]{2,1,0:T(8,128)S(1)} %all-to-all-done.refs_0_, bf16[10,128,112]{2,1,0:T(8,128)(2,1)S(1)} %copy-done, bf16[128,1120]{1,0:T(8,128)(2,1)S(1)} %bitcast.13), custom_call_target="tpu_custom_call" | custom-call | tf_op jit(solution)/shard_map/numerator/pallas_call | solution.py:66
  37.3 6.0 %all-to-all-start.1 = ((f32[32,70,112]{2,1,0:T(8,128)}), f32[32,70,112]{2,1,0:T(8,128)S(1)}, u32[]{:S(2)}, u32[]{:S(2)}) async-start(f32[32,70,112]{2,1,0:T(8,128)} %get-tuple-element.60), calls=%async_computation.1 | async-start | bytes 2359296 | tf_op jit(solution)/shard_map/all_to_all | solution.py:320
  47.5 14.7 %all-to-all-done.1.refs_0_.got = f32[32,70,112]{2,1,0:T(8,128)S(1)} async-done(((f32[32,70,112]{2,1,0:T(8,128)}), f32[32,70,112]{2,1,0:T(8,128)S(1)}, u32[]{:S(2)}, u32[]{:S(2)}) %all-to-all-start.1) | async-done | bytes 1003552 | tf_op jit(solution)/shard_map/all_to_all | solution.py:320
  62.1 2.6 %total_grad.1 = (f32[32,45,112]{2,1,0:T(8,128)}, f32[128,10]{1,0:T(8,128)}) custom-call(f32[32,70,112]{2,1,0:T(8,128)S(1)} %all-to-all-done.1.refs_0_.got, bf16[10,128,112]{2,1,0:T(8,128)(2,1)S(1)} %copy-done.1, bf16[128,1120]{1,0:T(8,128)(2,1)S(1)} %bitcast.14, f32[10,112]{1,0:T(8,128)S(1)} %copy-done.6), custom_call_target="tpu_custom_call" | custom-call | tf_op jit(solution)/shard_map/total_grad/pallas_call | solution.py:66
  64.7 6.3 %collective-permute-done.5.refs_5_ = f32[1120,128]{1,0:T(8,128)} collective-permute-done((f32[1120,128]{1,0:T(8,128)S(1)}, f32[1120,128]{1,0:T(8,128)}, u32[]{:S(2)}, u32[]{:S(2)}) %collective-permute-start.5) | collective-permute-done | bytes 573472 | tf_op jit(solution)/shard_map/ppermute | solution.py:324
  72.2 7.3 %all-to-all-start.2 = ((f32[32,45,112]{2,1,0:T(8,128)}), f32[32,45,112]{2,1,0:T(8,128)S(1)}, u32[]{:S(2)}, u32[]{:S(2)}) async-start(f32[32,45,112]{2,1,0:T(8,128)} %get-tuple-element.70), calls=%async_computation.2 | async-start | bytes 1572864 | tf_op jit(solution)/shard_map/all_to_all | solution.py:320
  79.5 2.9 %query_grad.1 = (bf16[128,1120]{1,0:T(8,128)(2,1)}, f32[128,256]{1,0:T(8,128)}, f32[128,256]{1,0:T(8,128)}, f32[128,256]{1,0:T(8,128)}, f32[128,256]{1,0:T(8,128)}, /*index=5*/f32[4,128,24]{2,1,0:T(8,128)}) custom-call(s32[1]{0:T(128)} %bitcast.place.refs_0_, f32[32,70,112]{2,1,0:T(8,128)S(1)} %all-to-all-done.1.refs_0_.got, ...), custom_call_target="tpu_custom_call" | custom-call | tf_op jit(solution)/shard_map/query_grad/pallas_call | solution.py:66
  85.2 2.4 %collective-permute-start.9 = (f32[128,256]{1,0:T(8,128)}, f32[128,256]{1,0:T(8,128)S(1)}, u32[]{:S(2)}, u32[]{:S(2)}) collective-permute-start(f32[128,256]{1,0:T(8,128)} %get-tuple-element.78), channel_id=1, source_target_pairs={{0,96},{32,0},{64,32},{96,64},{1,97},{33,1},{65,33},{97,65},{2,98}... | collective-permute-start | bytes 393224 | tf_op jit(solution)/shard_map/ppermute | solution.py:324
  87.6 3.9 %join.1.refs_1_ = bf16[1120,1024]{1,0:T(8,128)(2,1)} custom-call(f32[1120,128]{1,0:T(8,128)} %get-tuple-element.69.refs_0_, f32[1120,128]{1,0:T(8,128)S(1)} %collective-permute-done.refs_1_, f32[1120,128]{1,0:T(8,128)} %collective-permute-done.3.refs_2_, f32[1120,128]{1,0:T(8,128)} %collective-permute-done.6.refs_3_, ...), custom_call_target="tpu_custom_call" | custom-call | tf_op jit(solution)/shard_map/join/pallas_call | solution.py:66
  95.3 2.2 %key_value_grad.1 = (bf16[128,1120]{1,0:T(8,128)(2,1)}, bf16[128,1120]{1,0:T(8,128)(2,1)}, f32[4,128,640]{2,1,0:T(8,128)}) custom-call(f32[32,45,112]{2,1,0:T(8,128)S(1)} %all-to-all-done.2.got, bf16[10,128,112]{2,1,0:T(8,128)(2,1)S(1)} %copy-done.3, bf16[10,128,112]{2,1,0:T(8,128)(2,1)S(1)} %copy-done.4, f32[4,128,24]{2,1,0:T(8,128)S(1)} %copy-done.5), custom_call_target="tpu_custom_call" | custom-call | tf_op jit(solution)/shard_map/key_value_grad/pallas_call | solution.py:66
  97.5 4.4 %all-to-all-start.3 = ((f32[4,128,640]{2,1,0:T(8,128)}), f32[4,128,640]{2,1,0:T(8,128)S(1)}, u32[]{:S(2)}, u32[]{:S(2)}) async-start(f32[4,128,640]{2,1,0:T(8,128)} %get-tuple-element.86.refs_4_), calls=%async_computation.3 | async-start | bytes 2621440 | tf_op jit(solution)/shard_map/all_to_all | solution.py:320
  101.9 1.9 %collective-permute-done.10.refs_3_ = f32[512,256]{1,0:T(8,128)S(1)} collective-permute-done((f32[512,256]{1,0:T(8,128)S(1)}, f32[512,256]{1,0:T(8,128)S(1)}, u32[]{:S(2)}, u32[]{:S(2)}) %collective-permute-start.10) | collective-permute-done | bytes 524320 | tf_op jit(solution)/shard_map/ppermute | solution.py:332
  103.8 3.7 %query_product.1 = (f32[4,72,256]{2,1,0:T(8,128)}, f32[4,72,256]{2,1,0:T(8,128)}, f32[4,72,256]{2,1,0:T(8,128)}, f32[4,72,256]{2,1,0:T(8,128)}) custom-call(s32[1]{0:T(128)} %bitcast.5.refs_0_, bf16[1120,1024]{1,0:T(8,128)(2,1)} %join.1.refs_1_, f32[512,256]{1,0:T(8,128)} %pack_query.1.refs_2_, f32[512,256]{1,0:T(8,128)S(1)} %collective-permute-done.10.refs_3_, ...), custom_call_target="tpu_custom_call" | custom-call | tf_op jit(solution)/shard_map/query_product/pallas_call | solution.py:66
  109.1 2.7 %collective-permute-start.12 = (f32[4,72,256]{2,1,0:T(8,128)}, f32[4,72,256]{2,1,0:T(8,128)S(1)}, u32[]{:S(2)}, u32[]{:S(2)}) collective-permute-start(f32[4,72,256]{2,1,0:T(8,128)} %get-tuple-element.90), channel_id=1, source_target_pairs={{0,4},{2,6},{4,0},{6,2},{1,5},{3,7},{5,1},{7,3},{8,12},{10,14},{12... | collective-permute-start | bytes 884744 | tf_op jit(solution)/shard_map/ppermute | solution.py:324
  113.3 4.7 %collective-permute-done.11.first = f32[4,72,256]{2,1,0:T(8,128)S(1)} collective-permute-done((f32[4,72,256]{2,1,0:T(8,128)}, f32[4,72,256]{2,1,0:T(8,128)S(1)}, u32[]{:S(2)}, u32[]{:S(2)}) %collective-permute-start.11) | collective-permute-done | bytes 294944 | tf_op jit(solution)/shard_map/ppermute | solution.py:324
  117.9 7.4 %collective-permute-done.12.second = f32[4,72,256]{2,1,0:T(8,128)S(1)} collective-permute-done((f32[4,72,256]{2,1,0:T(8,128)}, f32[4,72,256]{2,1,0:T(8,128)S(1)}, u32[]{:S(2)}, u32[]{:S(2)}) %collective-permute-start.12) | collective-permute-done | bytes 294944 | tf_op jit(solution)/shard_map/ppermute | solution.py:324
  128.4 5.2 %key_value_product.1 = f32[16,72,640]{2,1,0:T(8,128)} custom-call(s32[1]{0:T(128)} %bitcast.place.refs_0_, bf16[1120,1024]{1,0:T(8,128)(2,1)} %join.1.refs_1_, f32[4,128,640]{2,1,0:T(8,128)S(1)} %all-to-all-done.3.refs_2_, f32[4,128,640]{2,1,0:T(8,128)S(1)} %collective-permute-done.14.refs_3_, f32[72,256]{1,0:T(8,128)} %get-tuple-element.97.refs_4_.own), custom_call_target="tpu_custom_call" | custom-call | tf_op jit(solution)/shard_map/key_value_product/pallas_call | solution.py:66
  133.6 6.6 %all-to-all-start.4 = ((f32[16,72,640]{2,1,0:T(8,128)}), f32[16,72,640]{2,1,0:T(8,128)S(1)}, u32[]{:S(2)}, u32[]{:S(2)}) async-start(f32[16,72,640]{2,1,0:T(8,128)} %key_value_product.1), calls=%async_computation.4 | async-start | bytes 5898240 | tf_op jit(solution)/shard_map/all_to_all | solution.py:320
  140.3 4.2 %fusion.1 = f32[128,2240]{0,1:T(8,128)S(1)} fusion(bf16[128,1120]{1,0:T(8,128)(2,1)S(1)} %copy-done.8, bf16[2240,1120]{1,0:T(8,128)(2,1)} %weight.1), kind=kOutput, calls=%fused_computation.3 | convolution fusion | flops 642252800 | bytes 6451200 | tf_op jit(solution)/shard_map/dot_general | solution.py:72
  144.6 4.1 %convolution_add_fusion.1 = f32[128,2240]{0,1:T(8,128)S(1)} fusion(f32[128,2240]{0,1:T(8,128)S(1)} %fusion.1, bf16[128,1120]{1,0:T(8,128)(2,1)S(1)} %copy-done.10, bf16[2240,1120]{1,0:T(8,128)(2,1)} %key_weight.1), kind=kOutput, calls=%fused_computation.1 | convolution fusion | flops 642539520 | bytes 7598080 | tf_op jit(solution)/shard_map/dot_general | solution.py:72
  148.7 2.0 %collective-permute-start.15 = (f32[72,256]{1,0:T(8,128)S(1)}, f32[72,256]{1,0:T(8,128)S(1)}, u32[]{:S(2)}, u32[]{:S(2)}) collective-permute-start(f32[72,256]{1,0:T(8,128)S(1)} %copy-done.13), channel_id=1, source_target_pairs={{0,1},{1,16},{16,17},{17,0},{2,3},{3,18},{18,19},{19,2},{4,5},{5,2... | collective-permute-start | bytes 221192 | tf_op jit(solution)/shard_map/ppermute | solution.py:324
  150.7 2.7 %collective-permute-start.16 = (f32[72,256]{1,0:T(8,128)S(1)}, f32[72,256]{1,0:T(8,128)S(1)}, u32[]{:S(2)}, u32[]{:S(2)}) collective-permute-start(f32[72,256]{1,0:T(8,128)S(1)} %copy-done.12), channel_id=1, source_target_pairs={{0,16},{1,17},{16,0},{17,1},{2,18},{3,19},{18,2},{19,3},{4,20},{5,... | collective-permute-start | bytes 221192 | tf_op jit(solution)/shard_map/ppermute | solution.py:324
  154.8 2.4 %fusion = bf16[128,2240]{0,1:T(8,128)(2,1)} fusion(f32[128,2240]{0,1:T(8,128)S(1)} %convolution_add_fusion.1, bf16[128,1120]{1,0:T(8,128)(2,1)S(1)} %copy-done.9, bf16[2240,1120]{1,0:T(8,128)(2,1)S(1)} %bitcast.16), kind=kOutput, calls=%fused_computation.2 | convolution fusion | flops 642826240 | bytes 7024640 | tf_op jit(solution)/shard_map/dot_general | solution.py:72
  157.2 2.1 %copy.10 = bf16[128,2240]{1,0:T(8,128)(2,1)} copy(bf16[128,2240]{0,1:T(8,128)(2,1)} %fusion) | data formatting | bytes 1146880 | tf_op jit(solution)/shard_map/convert_element_type | solution.py:487
  159.3 18.4 %collective-permute-done.15.first = f32[72,256]{1,0:T(8,128)S(1)} collective-permute-done((f32[72,256]{1,0:T(8,128)S(1)}, f32[72,256]{1,0:T(8,128)S(1)}, u32[]{:S(2)}, u32[]{:S(2)}) %collective-permute-start.15) | collective-permute-done | bytes 73760 | tf_op jit(solution)/shard_map/ppermute | solution.py:324
  177.7 4.6 %all-to-all-done.4.key_value = f32[16,72,640]{2,1,0:T(8,128)S(1)} async-done(((f32[16,72,640]{2,1,0:T(8,128)}), f32[16,72,640]{2,1,0:T(8,128)S(1)}, u32[]{:S(2)}, u32[]{:S(2)}) %all-to-all-start.4) | async-done | bytes 2949152 | tf_op jit(solution)/shard_map/all_to_all | solution.py:320
  182.3 1.7 last.1
  (64 shorter events, 22.6 us)
Async XLA Ops:
  11.1 9.9 %collective-permute-start.1 = (f32[1120,128]{1,0:T(8,128)}, f32[1120,128]{1,0:T(8,128)S(1)}, u32[]{:S(2)}, u32[]{:S(2)}) collective-permute-start(f32[1120,128]{1,0:T(8,128)} %get-tuple-element.59), channel_id=1, source_target_pairs={{0,8},{8,0},{1,9},{9,1},{2,10},{10,2},{3,11},{11,3},{4,12},{12,4},... | collective-permute-start | bytes 1720328 | tf_op jit(solution)/shard_map/ppermute | solution.py:332
  11.1 22.8 %all-to-all-start = ((f32[32,45,112]{2,1,0:T(8,128)}), f32[32,45,112]{2,1,0:T(8,128)S(1)}, u32[]{:S(2)}, u32[]{:S(2)}) async-start(f32[32,45,112]{2,1,0:T(8,128)} %get-tuple-element.55), calls=%async_computation | async-start | bytes 1572864 | tf_op jit(solution)/shard_map/all_to_all | solution.py:320
  19.4 14.5 %copy-start.2 = (bf16[1,16,8,1120]{3,2,1,0:T(8,128)(2,1)S(1)}, bf16[1,16,8,1120]{3,2,1,0:T(8,128)(2,1)}, u32[]{:S(2)}) copy-start(bf16[1,16,8,1120]{3,2,1,0:T(8,128)(2,1)} %param.9) | copy-start | bytes 860164
  19.4 17.9 %collective-permute-start = (f32[1120,128]{1,0:T(8,128)}, f32[1120,128]{1,0:T(8,128)S(1)}, u32[]{:S(2)}, u32[]{:S(2)}) collective-permute-start(f32[1120,128]{1,0:T(8,128)} %get-tuple-element.69.refs_0_), channel_id=1, source_target_pairs={{0,32},{32,64},{64,96},{96,0},{1,33},{33,65},{65,97},{97,1},{2,34}... | collective-permute-start | bytes 1720328 | tf_op jit(solution)/shard_map/ppermute | solution.py:324
  21.1 16.3 %collective-permute-start.2 = (f32[1120,128]{1,0:T(8,128)S(1)}, f32[1120,128]{1,0:T(8,128)}, u32[]{:S(2)}, u32[]{:S(2)}) collective-permute-start(f32[1120,128]{1,0:T(8,128)S(1)} %collective-permute-done.1.refs_4_), channel_id=1, source_target_pairs={{0,96},{32,0},{64,32},{96,64},{1,97},{33,1},{65,33},{97,65},{2,98}... | collective-permute-start | bytes 1720328 | tf_op jit(solution)/shard_map/ppermute | solution.py:324
  34.9 27.2 %copy-start.1 = (bf16[10,128,112]{2,1,0:T(8,128)(2,1)S(1)}, bf16[10,128,112]{2,1,0:T(8,128)(2,1)}, u32[]{:S(2)}) copy-start(bf16[10,128,112]{2,1,0:T(8,128)(2,1)} %query.1.refs_1_) | copy-start | bytes 860164
  37.3 24.8 %copy-start.6 = (f32[10,112]{1,0:T(8,128)S(1)}, f32[10,112]{1,0:T(8,128)}, u32[]{:S(2)}) copy-start(f32[10,112]{1,0:T(8,128)} %get-tuple-element.62.refs_3_.total) | copy-start | bytes 13444
  37.3 24.8 %all-to-all-start.1 = ((f32[32,70,112]{2,1,0:T(8,128)}), f32[32,70,112]{2,1,0:T(8,128)S(1)}, u32[]{:S(2)}, u32[]{:S(2)}) async-start(f32[32,70,112]{2,1,0:T(8,128)} %get-tuple-element.60), calls=%async_computation.1 | async-start | bytes 2359296 | tf_op jit(solution)/shard_map/all_to_all | solution.py:320
  43.3 21.4 %collective-permute-start.3 = (f32[1120,128]{1,0:T(8,128)S(1)}, f32[1120,128]{1,0:T(8,128)}, u32[]{:S(2)}, u32[]{:S(2)}) collective-permute-start(f32[1120,128]{1,0:T(8,128)S(1)} %collective-permute-done.refs_1_), channel_id=1, source_target_pairs={{0,32},{32,64},{64,96},{96,0},{1,33},{33,65},{65,97},{97,1},{2,34}... | collective-permute-start | bytes 1720328 | tf_op jit(solution)/shard_map/ppermute | solution.py:324
  44.7 20.0 %collective-permute-start.4 = (f32[1120,128]{1,0:T(8,128)}, f32[1120,128]{1,0:T(8,128)}, u32[]{:S(2)}, u32[]{:S(2)}) collective-permute-start(f32[1120,128]{1,0:T(8,128)} %collective-permute-done.2.refs_7_), channel_id=1, source_target_pairs={{0,96},{32,0},{64,32},{96,64},{1,97},{33,1},{65,33},{97,65},{2,98}... | collective-permute-start | bytes 1720328 | tf_op jit(solution)/shard_map/ppermute | solution.py:324
  45.4 25.5 %collective-permute-start.5 = (f32[1120,128]{1,0:T(8,128)S(1)}, f32[1120,128]{1,0:T(8,128)}, u32[]{:S(2)}, u32[]{:S(2)}) collective-permute-start(f32[1120,128]{1,0:T(8,128)S(1)} %collective-permute-done.1.refs_4_), channel_id=1, source_target_pairs={{0,32},{32,64},{64,96},{96,0},{1,33},{33,65},{65,97},{97,1},{2,34}... | collective-permute-start | bytes 1720328 | tf_op jit(solution)/shard_map/ppermute | solution.py:324
  46.7 25.5 %collective-permute-start.6 = (f32[1120,128]{1,0:T(8,128)}, f32[1120,128]{1,0:T(8,128)}, u32[]{:S(2)}, u32[]{:S(2)}) collective-permute-start(f32[1120,128]{1,0:T(8,128)} %get-tuple-element.69.refs_0_), channel_id=1, source_target_pairs={{0,96},{32,0},{64,32},{96,64},{1,97},{33,1},{65,33},{97,65},{2,98}... | collective-permute-start | bytes 1720328 | tf_op jit(solution)/shard_map/ppermute | solution.py:324
  72.2 23.1 %all-to-all-start.2 = ((f32[32,45,112]{2,1,0:T(8,128)}), f32[32,45,112]{2,1,0:T(8,128)S(1)}, u32[]{:S(2)}, u32[]{:S(2)}) async-start(f32[32,45,112]{2,1,0:T(8,128)} %get-tuple-element.70), calls=%async_computation.2 | async-start | bytes 1572864 | tf_op jit(solution)/shard_map/all_to_all | solution.py:320
  82.4 9.2 %collective-permute-start.7 = (f32[128,256]{1,0:T(8,128)}, f32[128,256]{1,0:T(8,128)S(1)}, u32[]{:S(2)}, u32[]{:S(2)}) collective-permute-start(f32[128,256]{1,0:T(8,128)} %get-tuple-element.76), channel_id=1, source_target_pairs={{0,32},{32,64},{64,96},{96,0},{1,33},{33,65},{65,97},{97,1},{2,34}... | collective-permute-start | bytes 393224 | tf_op jit(solution)/shard_map/ppermute | solution.py:324
  84.0 8.1 %collective-permute-start.8 = (f32[128,256]{1,0:T(8,128)}, f32[128,256]{1,0:T(8,128)S(1)}, u32[]{:S(2)}, u32[]{:S(2)}) collective-permute-start(f32[128,256]{1,0:T(8,128)} %get-tuple-element.77), channel_id=1, source_target_pairs={{0,64},{32,96},{64,0},{96,32},{1,65},{33,97},{65,1},{97,33},{2,66}... | collective-permute-start | bytes 393224 | tf_op jit(solution)/shard_map/ppermute | solution.py:324
  85.2 10.0 %copy-start.3 = (bf16[10,128,112]{2,1,0:T(8,128)(2,1)S(1)}, bf16[10,128,112]{2,1,0:T(8,128)(2,1)}, u32[]{:S(2)}) copy-start(bf16[10,128,112]{2,1,0:T(8,128)(2,1)} %get-tuple-element.80.key) | copy-start | bytes 860164
  85.2 10.0 %copy-start.4 = (bf16[10,128,112]{2,1,0:T(8,128)(2,1)S(1)}, bf16[10,128,112]{2,1,0:T(8,128)(2,1)}, u32[]{:S(2)}) copy-start(bf16[10,128,112]{2,1,0:T(8,128)(2,1)} %get-tuple-element.81.value) | copy-start | bytes 860164
  85.2 10.0 %copy-start.5 = (f32[4,128,24]{2,1,0:T(8,128)S(1)}, f32[4,128,24]{2,1,0:T(8,128)}, u32[]{:S(2)}) copy-start(f32[4,128,24]{2,1,0:T(8,128)} %get-tuple-element.82.late) | copy-start | bytes 147460
  85.2 8.3 %collective-permute-start.9 = (f32[128,256]{1,0:T(8,128)}, f32[128,256]{1,0:T(8,128)S(1)}, u32[]{:S(2)}, u32[]{:S(2)}) collective-permute-start(f32[128,256]{1,0:T(8,128)} %get-tuple-element.78), channel_id=1, source_target_pairs={{0,96},{32,0},{64,32},{96,64},{1,97},{33,1},{65,33},{97,65},{2,98}... | collective-permute-start | bytes 393224 | tf_op jit(solution)/shard_map/ppermute | solution.py:324
  97.5 27.9 %all-to-all-start.3 = ((f32[4,128,640]{2,1,0:T(8,128)}), f32[4,128,640]{2,1,0:T(8,128)S(1)}, u32[]{:S(2)}, u32[]{:S(2)}) async-start(f32[4,128,640]{2,1,0:T(8,128)} %get-tuple-element.86.refs_4_), calls=%async_computation.3 | async-start | bytes 2621440 | tf_op jit(solution)/shard_map/all_to_all | solution.py:320
  101.9 1.9 %collective-permute-start.10 = (f32[512,256]{1,0:T(8,128)S(1)}, f32[512,256]{1,0:T(8,128)S(1)}, u32[]{:S(2)}, u32[]{:S(2)}) collective-permute-start(f32[512,256]{1,0:T(8,128)S(1)} %copy-done.7), channel_id=1, source_target_pairs={{0,8},{8,0},{1,9},{9,1},{2,10},{10,2},{3,11},{11,3},{4,12},{12,4},... | collective-permute-start | bytes 1572872 | tf_op jit(solution)/shard_map/ppermute | solution.py:332
  107.5 10.5 %collective-permute-start.11 = (f32[4,72,256]{2,1,0:T(8,128)}, f32[4,72,256]{2,1,0:T(8,128)S(1)}, u32[]{:S(2)}, u32[]{:S(2)}) collective-permute-start(f32[4,72,256]{2,1,0:T(8,128)} %get-tuple-element.89), channel_id=1, source_target_pairs={{0,2},{2,4},{4,6},{6,0},{1,3},{3,5},{5,7},{7,1},{8,10},{10,12},{12... | collective-permute-start | bytes 884744 | tf_op jit(solution)/shard_map/ppermute | solution.py:324
  109.1 16.2 %collective-permute-start.12 = (f32[4,72,256]{2,1,0:T(8,128)}, f32[4,72,256]{2,1,0:T(8,128)S(1)}, u32[]{:S(2)}, u32[]{:S(2)}) collective-permute-start(f32[4,72,256]{2,1,0:T(8,128)} %get-tuple-element.90), channel_id=1, source_target_pairs={{0,4},{2,6},{4,0},{6,2},{1,5},{3,7},{5,1},{7,3},{8,12},{10,14},{12... | collective-permute-start | bytes 884744 | tf_op jit(solution)/shard_map/ppermute | solution.py:324
  111.8 13.6 %collective-permute-start.13 = (f32[4,72,256]{2,1,0:T(8,128)}, f32[4,72,256]{2,1,0:T(8,128)S(1)}, u32[]{:S(2)}, u32[]{:S(2)}) collective-permute-start(f32[4,72,256]{2,1,0:T(8,128)} %get-tuple-element.91), channel_id=1, source_target_pairs={{0,6},{2,0},{4,2},{6,4},{1,7},{3,1},{5,3},{7,5},{8,14},{10,8},{12,... | collective-permute-start | bytes 884744 | tf_op jit(solution)/shard_map/ppermute | solution.py:324
  125.4 3.0 %collective-permute-start.14 = (f32[4,128,640]{2,1,0:T(8,128)S(1)}, f32[4,128,640]{2,1,0:T(8,128)S(1)}, u32[]{:S(2)}, u32[]{:S(2)}) collective-permute-start(f32[4,128,640]{2,1,0:T(8,128)S(1)} %all-to-all-done.3.refs_2_), channel_id=1, source_target_pairs={{0,8},{8,0},{1,9},{9,1},{2,10},{10,2},{3,11},{11,3},{4,12},{12,4},... | collective-permute-start | bytes 3932168 | tf_op jit(solution)/shard_map/ppermute | solution.py:332
  133.6 48.6 %all-to-all-start.4 = ((f32[16,72,640]{2,1,0:T(8,128)}), f32[16,72,640]{2,1,0:T(8,128)S(1)}, u32[]{:S(2)}, u32[]{:S(2)}) async-start(f32[16,72,640]{2,1,0:T(8,128)} %key_value_product.1), calls=%async_computation.4 | async-start | bytes 5898240 | tf_op jit(solution)/shard_map/all_to_all | solution.py:320
  140.3 14.5 %slice-start = ((s8[5160960]{0:T(1024)(128)(4,1)}), s8[4194304]{0:T(1024)(128)(4,1)S(1)}, s32[]{:S(2)}) async-start(s8[5160960]{0:T(1024)(128)(4,1)} %bitcast.15), calls=%async_computation.5 | async-start | bytes 8388608
  144.5 10.3 %slice-start.1 = ((s8[5160960]{0:T(1024)(128)(4,1)}), s8[966656]{0:T(1024)(128)(4,1)S(1)}, s32[]{:S(2)}) async-start(s8[5160960]{0:T(1024)(128)(4,1)} %bitcast.15), calls=%async_computation.6 | async-start | bytes 1933312
  144.6 10.3 %copy-start.9 = (bf16[128,1120]{1,0:T(8,128)(2,1)S(1)}, bf16[128,1120]{1,0:T(8,128)(2,1)}, u32[]{:S(2)}) copy-start(bf16[128,1120]{1,0:T(8,128)(2,1)} %get-tuple-element.84) | copy-start | bytes 860164
  148.7 29.0 %collective-permute-start.15 = (f32[72,256]{1,0:T(8,128)S(1)}, f32[72,256]{1,0:T(8,128)S(1)}, u32[]{:S(2)}, u32[]{:S(2)}) collective-permute-start(f32[72,256]{1,0:T(8,128)S(1)} %copy-done.13), channel_id=1, source_target_pairs={{0,1},{1,16},{16,17},{17,0},{2,3},{3,18},{18,19},{19,2},{4,5},{5,2... | collective-permute-start | bytes 221192 | tf_op jit(solution)/shard_map/ppermute | solution.py:324
  150.7 27.0 %collective-permute-start.16 = (f32[72,256]{1,0:T(8,128)S(1)}, f32[72,256]{1,0:T(8,128)S(1)}, u32[]{:S(2)}, u32[]{:S(2)}) collective-permute-start(f32[72,256]{1,0:T(8,128)S(1)} %copy-done.12), channel_id=1, source_target_pairs={{0,16},{1,17},{16,0},{17,1},{2,18},{3,19},{18,2},{19,3},{4,20},{5,... | collective-permute-start | bytes 221192 | tf_op jit(solution)/shard_map/ppermute | solution.py:324
  153.4 24.3 %collective-permute-start.17 = (f32[72,256]{1,0:T(8,128)S(1)}, f32[72,256]{1,0:T(8,128)S(1)}, u32[]{:S(2)}, u32[]{:S(2)}) collective-permute-start(f32[72,256]{1,0:T(8,128)S(1)} %copy-done.11), channel_id=1, source_target_pairs={{0,17},{1,0},{16,1},{17,16},{2,19},{3,2},{18,3},{19,18},{4,21},{5,... | collective-permute-start | bytes 221192 | tf_op jit(solution)/shard_map/ppermute | solution.py:324
  (7 other events, 37.6 us)

commit v8 on v7

--- a/solution.py
+++ b/solution.py
@@ -394,8 +394,6 @@
     )
     far_top = shift(left_top, 1, "dp")
     far_bottom = shift(right_bottom, 3, "dp")
-    left_bottom = shift(later_bottom, 1, "dp")
-    right_top = shift(later_top, 3, "dp")
     got_state = exchange(sent, IMAGE)
     sent, grad_denom = call(
         lambda *refs: total_grad_kernel(loss_scale, *refs),
@@ -405,9 +403,11 @@
         [state, totals],
         arrived=(0, 1, 2, 3),
     )(got_state, query, upstream, total)
-    sent, far_top, far_bottom, left_bottom, right_top = lax.optimization_barrier(
-        (sent, far_top, far_bottom, left_bottom, right_top)
+    sent, far_top, far_bottom, later_top, later_bottom = lax.optimization_barrier(
+        (sent, far_top, far_bottom, later_top, later_bottom)
     )
+    left_bottom = shift(later_bottom, 1, "dp")
+    right_top = shift(later_top, 3, "dp")
     got = exchange(sent, IMAGE)
 
     block = shaped((TOKENS, EARLY))

time: 185 us -> 189 us (1.022)
  waiting for transfers between devices: 70.3 us -> 72.8 us
    all_to_all x5, waiting for transfers between devices: 27.2 us -> 29.3 us  [exchange(): return lax.all_to_all(blocks, axes, 0, 0, tiled=True)]
  transfers between devices with their start and end apart: 23 -> 23, of which waited for: 12 -> 10; matrix products, arithmetic and copies ran while one was open for 7% -> 7% of each run, Pallas kernels for 13% -> 12%
where the time goes in v8:
time: 189 us; the launch traced here: 188 us
  waiting for transfers between devices  72.8 us (39%)
  starting transfers between devices  57.1 us (30%)
  Pallas kernels  43.2 us (23%)
  matrix products  10.7 us (6%)
  local copies, waits for them, and re-layouts  3.16 us (2%)
    pallas_call x13, Pallas kernels, with_placed(): return run(*placed)  43.2 us
    ppermute x15, waiting for transfers between devices, shift(): lax.ppermute(values, axis, [(i, (i + by) % RING) for i in range(RING)])  40.4 us
    all_to_all x5, starting transfers between devices, exchange(): return lax.all_to_all(blocks, axes, 0, 0, tiled=True)  32.7 us
    all_to_all x5, waiting for transfers between devices, exchange(): return lax.all_to_all(blocks, axes, 0, 0, tiled=True)  29.3 us
    ppermute x15, starting transfers between devices, shift(): lax.ppermute(values, axis, [(i, (i + by) % RING) for i in range(RING)])  24.4 us
    dot_general x3, matrix products, dot(): lax.dot_general(left, right, (((left_dim,), (right_dim,)), ((), ())), pre...  10.7 us
  transfers between devices with their start and end apart: 23, of which 10 were waited for; matrix products, arithmetic and copies ran while one was open for 7% of the time, Pallas kernels for 12%

profile of v8, /device:TPU:8, one launch (start us, length us, event | category | flops | bytes accessed | tf_op | source)
XLA Modules:
  0.0 187.8 jit_solution(3041009173269810328)
XLA Ops:
  0.6 8.2 %key_value.1 = (bf16[10,128,112]{2,1,0:T(8,128)(2,1)}, bf16[10,128,112]{2,1,0:T(8,128)(2,1)}, f32[32,45,112]{2,1,0:T(8,128)}) custom-call(bf16[128,2240]{1,0:T(8,128)(2,1)} %bitcast.17, bf16[2240,1120]{1,0:T(8,128)(2,1)} %key_weight.1, bf16[2240,1120]{1,0:T(8,128)(2,1)} %value_weight.1), custom_call_target="tpu_custom_call" | custom-call | tf_op jit(solution)/shard_map/key_value/pallas_call | solution.py:66
  8.8 2.4 %turn.1 = (f32[1120,128]{1,0:T(8,128)}, f32[1120,128]{1,0:T(8,128)}) custom-call(s32[1]{0:T(128)} %bitcast.3.core, bf16[128,2240]{1,0:T(8,128)(2,1)} %bitcast.18), custom_call_target="tpu_custom_call" | custom-call | tf_op jit(solution)/shard_map/turn/pallas_call | solution.py:66
  11.2 8.3 %all-to-all-start = ((f32[32,45,112]{2,1,0:T(8,128)}), f32[32,45,112]{2,1,0:T(8,128)S(1)}, u32[]{:S(2)}, u32[]{:S(2)}) async-start(f32[32,45,112]{2,1,0:T(8,128)} %get-tuple-element.55), calls=%async_computation | async-start | bytes 1572864 | tf_op jit(solution)/shard_map/all_to_all | solution.py:320
  21.5 4.4 %query.1.refs_1_ = bf16[10,128,112]{2,1,0:T(8,128)(2,1)} custom-call(bf16[128,2240]{1,0:T(8,128)(2,1)} %bitcast.19, bf16[2240,1120]{1,0:T(8,128)(2,1)} %weight.1), custom_call_target="tpu_custom_call" | custom-call | tf_op jit(solution)/shard_map/query/pallas_call | solution.py:66
  25.9 8.0 %all-to-all-done.refs_0_ = f32[32,45,112]{2,1,0:T(8,128)S(1)} async-done(((f32[32,45,112]{2,1,0:T(8,128)}), f32[32,45,112]{2,1,0:T(8,128)S(1)}, u32[]{:S(2)}, u32[]{:S(2)}) %all-to-all-start) | async-done | bytes 645152 | tf_op jit(solution)/shard_map/all_to_all | solution.py:320
  34.9 2.4 %numerator.1 = (f32[32,70,112]{2,1,0:T(8,128)}, bf16[10,128,112]{2,1,0:T(8,128)(2,1)}, f32[10,112]{1,0:T(8,128)}) custom-call(f32[32,45,112]{2,1,0:T(8,128)S(1)} %all-to-all-done.refs_0_, bf16[10,128,112]{2,1,0:T(8,128)(2,1)S(1)} %copy-done, bf16[128,1120]{1,0:T(8,128)(2,1)S(1)} %bitcast.13), custom_call_target="tpu_custom_call" | custom-call | tf_op jit(solution)/shard_map/numerator/pallas_call | solution.py:66
  37.4 6.0 %all-to-all-start.1 = ((f32[32,70,112]{2,1,0:T(8,128)}), f32[32,70,112]{2,1,0:T(8,128)S(1)}, u32[]{:S(2)}, u32[]{:S(2)}) async-start(f32[32,70,112]{2,1,0:T(8,128)} %get-tuple-element.60), calls=%async_computation.1 | async-start | bytes 2359296 | tf_op jit(solution)/shard_map/all_to_all | solution.py:320
  45.5 16.7 %all-to-all-done.1.refs_0_.got = f32[32,70,112]{2,1,0:T(8,128)S(1)} async-done(((f32[32,70,112]{2,1,0:T(8,128)}), f32[32,70,112]{2,1,0:T(8,128)S(1)}, u32[]{:S(2)}, u32[]{:S(2)}) %all-to-all-start.1) | async-done | bytes 1003552 | tf_op jit(solution)/shard_map/all_to_all | solution.py:320
  62.2 2.6 %total_grad.1 = (f32[32,45,112]{2,1,0:T(8,128)}, f32[128,10]{1,0:T(8,128)}) custom-call(f32[32,70,112]{2,1,0:T(8,128)S(1)} %all-to-all-done.1.refs_0_.got, bf16[10,128,112]{2,1,0:T(8,128)(2,1)S(1)} %copy-done.1, bf16[128,1120]{1,0:T(8,128)(2,1)S(1)} %bitcast.14, f32[10,112]{1,0:T(8,128)S(1)} %copy-done.6), custom_call_target="tpu_custom_call" | custom-call | tf_op jit(solution)/shard_map/total_grad/pallas_call | solution.py:66
  64.7 4.1 %all-to-all-start.2 = ((f32[32,45,112]{2,1,0:T(8,128)}), f32[32,45,112]{2,1,0:T(8,128)S(1)}, u32[]{:S(2)}, u32[]{:S(2)}) async-start(f32[32,45,112]{2,1,0:T(8,128)} %get-tuple-element.70), calls=%async_computation.2 | async-start | bytes 1572864 | tf_op jit(solution)/shard_map/all_to_all | solution.py:320
  71.0 2.9 %query_grad.1 = (bf16[128,1120]{1,0:T(8,128)(2,1)}, f32[128,256]{1,0:T(8,128)}, f32[128,256]{1,0:T(8,128)}, f32[128,256]{1,0:T(8,128)}, f32[128,256]{1,0:T(8,128)}, /*index=5*/f32[4,128,24]{2,1,0:T(8,128)}) custom-call(s32[1]{0:T(128)} %bitcast.place.refs_0_, f32[32,70,112]{2,1,0:T(8,128)S(1)} %all-to-all-done.1.refs_0_.got, ...), custom_call_target="tpu_custom_call" | custom-call | tf_op jit(solution)/shard_map/query_grad/pallas_call | solution.py:66
  75.2 2.3 %collective-permute-start.8 = (f32[128,256]{1,0:T(8,128)}, f32[128,256]{1,0:T(8,128)S(1)}, u32[]{:S(2)}, u32[]{:S(2)}) collective-permute-start(f32[128,256]{1,0:T(8,128)} %get-tuple-element.77), channel_id=1, source_target_pairs={{0,64},{32,96},{64,0},{96,32},{1,65},{33,97},{65,1},{97,33},{2,66}... | collective-permute-start | bytes 393224 | tf_op jit(solution)/shard_map/ppermute | solution.py:324
  77.5 2.6 %collective-permute-start.9 = (f32[128,256]{1,0:T(8,128)}, f32[128,256]{1,0:T(8,128)S(1)}, u32[]{:S(2)}, u32[]{:S(2)}) collective-permute-start(f32[128,256]{1,0:T(8,128)} %get-tuple-element.78), channel_id=1, source_target_pairs={{0,96},{32,0},{64,32},{96,64},{1,97},{33,1},{65,33},{97,65},{2,98}... | collective-permute-start | bytes 393224 | tf_op jit(solution)/shard_map/ppermute | solution.py:324
  80.0 9.0 %collective-permute-done.7.refs_1_ = f32[128,256]{1,0:T(8,128)S(1)} collective-permute-done((f32[128,256]{1,0:T(8,128)}, f32[128,256]{1,0:T(8,128)S(1)}, u32[]{:S(2)}, u32[]{:S(2)}) %collective-permute-start.7) | collective-permute-done | bytes 131104 | tf_op jit(solution)/shard_map/ppermute | solution.py:324
  91.7 4.0 %join.1.refs_1_ = bf16[1120,1024]{1,0:T(8,128)(2,1)} custom-call(f32[1120,128]{1,0:T(8,128)} %get-tuple-element.72.refs_0_, f32[1120,128]{1,0:T(8,128)S(1)} %collective-permute-done.refs_1_, f32[1120,128]{1,0:T(8,128)} %collective-permute-done.3.refs_2_, f32[1120,128]{1,0:T(8,128)} %collective-permute-done.5.refs_3_, ...), custom_call_target="tpu_custom_call" | custom-call | tf_op jit(solution)/shard_map/join/pallas_call | solution.py:66
  95.7 2.2 %key_value_grad.1 = (bf16[128,1120]{1,0:T(8,128)(2,1)}, bf16[128,1120]{1,0:T(8,128)(2,1)}, f32[4,128,640]{2,1,0:T(8,128)}) custom-call(f32[32,45,112]{2,1,0:T(8,128)S(1)} %all-to-all-done.2.got, bf16[10,128,112]{2,1,0:T(8,128)(2,1)S(1)} %copy-done.3, bf16[10,128,112]{2,1,0:T(8,128)(2,1)S(1)} %copy-done.4, f32[4,128,24]{2,1,0:T(8,128)S(1)} %copy-done.5), custom_call_target="tpu_custom_call" | custom-call | tf_op jit(solution)/shard_map/key_value_grad/pallas_call | solution.py:66
  98.0 7.7 %all-to-all-start.3 = ((f32[4,128,640]{2,1,0:T(8,128)}), f32[4,128,640]{2,1,0:T(8,128)S(1)}, u32[]{:S(2)}, u32[]{:S(2)}) async-start(f32[4,128,640]{2,1,0:T(8,128)} %get-tuple-element.86.refs_4_), calls=%async_computation.3 | async-start | bytes 2621440 | tf_op jit(solution)/shard_map/all_to_all | solution.py:320
  105.7 1.9 %collective-permute-done.10.refs_3_ = f32[512,256]{1,0:T(8,128)S(1)} collective-permute-done((f32[512,256]{1,0:T(8,128)S(1)}, f32[512,256]{1,0:T(8,128)S(1)}, u32[]{:S(2)}, u32[]{:S(2)}) %collective-permute-start.10) | collective-permute-done | bytes 524320 | tf_op jit(solution)/shard_map/ppermute | solution.py:332
  107.6 3.7 %query_product.1 = (f32[4,72,256]{2,1,0:T(8,128)}, f32[4,72,256]{2,1,0:T(8,128)}, f32[4,72,256]{2,1,0:T(8,128)}, f32[4,72,256]{2,1,0:T(8,128)}) custom-call(s32[1]{0:T(128)} %bitcast.5.refs_0_, bf16[1120,1024]{1,0:T(8,128)(2,1)} %join.1.refs_1_, f32[512,256]{1,0:T(8,128)} %pack_query.1.refs_2_, f32[512,256]{1,0:T(8,128)S(1)} %collective-permute-done.10.refs_3_, ...), custom_call_target="tpu_custom_call" | custom-call | tf_op jit(solution)/shard_map/query_product/pallas_call | solution.py:66
  112.9 2.7 %collective-permute-start.12 = (f32[4,72,256]{2,1,0:T(8,128)}, f32[4,72,256]{2,1,0:T(8,128)S(1)}, u32[]{:S(2)}, u32[]{:S(2)}) collective-permute-start(f32[4,72,256]{2,1,0:T(8,128)} %get-tuple-element.90), channel_id=1, source_target_pairs={{0,4},{2,6},{4,0},{6,2},{1,5},{3,7},{5,1},{7,3},{8,12},{10,14},{12... | collective-permute-start | bytes 884744 | tf_op jit(solution)/shard_map/ppermute | solution.py:324
  117.1 4.7 %collective-permute-done.11.first = f32[4,72,256]{2,1,0:T(8,128)S(1)} collective-permute-done((f32[4,72,256]{2,1,0:T(8,128)}, f32[4,72,256]{2,1,0:T(8,128)S(1)}, u32[]{:S(2)}, u32[]{:S(2)}) %collective-permute-start.11) | collective-permute-done | bytes 294944 | tf_op jit(solution)/shard_map/ppermute | solution.py:324
  121.7 7.4 %collective-permute-done.12.second = f32[4,72,256]{2,1,0:T(8,128)S(1)} collective-permute-done((f32[4,72,256]{2,1,0:T(8,128)}, f32[4,72,256]{2,1,0:T(8,128)S(1)}, u32[]{:S(2)}, u32[]{:S(2)}) %collective-permute-start.12) | collective-permute-done | bytes 294944 | tf_op jit(solution)/shard_map/ppermute | solution.py:324
  132.2 5.2 %key_value_product.1 = f32[16,72,640]{2,1,0:T(8,128)} custom-call(s32[1]{0:T(128)} %bitcast.place.refs_0_, bf16[1120,1024]{1,0:T(8,128)(2,1)} %join.1.refs_1_, f32[4,128,640]{2,1,0:T(8,128)S(1)} %all-to-all-done.3.refs_2_, f32[4,128,640]{2,1,0:T(8,128)S(1)} %collective-permute-done.14.refs_3_, f32[72,256]{1,0:T(8,128)} %get-tuple-element.97.refs_4_.own), custom_call_target="tpu_custom_call" | custom-call | tf_op jit(solution)/shard_map/key_value_product/pallas_call | solution.py:66
  137.5 6.6 %all-to-all-start.4 = ((f32[16,72,640]{2,1,0:T(8,128)}), f32[16,72,640]{2,1,0:T(8,128)S(1)}, u32[]{:S(2)}, u32[]{:S(2)}) async-start(f32[16,72,640]{2,1,0:T(8,128)} %key_value_product.1), calls=%async_computation.4 | async-start | bytes 5898240 | tf_op jit(solution)/shard_map/all_to_all | solution.py:320
  144.1 4.2 %fusion.1 = f32[128,2240]{0,1:T(8,128)S(1)} fusion(bf16[128,1120]{1,0:T(8,128)(2,1)S(1)} %copy-done.8, bf16[2240,1120]{1,0:T(8,128)(2,1)} %weight.1), kind=kOutput, calls=%fused_computation.3 | convolution fusion | flops 642252800 | bytes 6451200 | tf_op jit(solution)/shard_map/dot_general | solution.py:72
  148.4 4.1 %convolution_add_fusion.1 = f32[128,2240]{0,1:T(8,128)S(1)} fusion(f32[128,2240]{0,1:T(8,128)S(1)} %fusion.1, bf16[128,1120]{1,0:T(8,128)(2,1)S(1)} %copy-done.10, bf16[2240,1120]{1,0:T(8,128)(2,1)} %key_weight.1), kind=kOutput, calls=%fused_computation.1 | convolution fusion | flops 642539520 | bytes 7598080 | tf_op jit(solution)/shard_map/dot_general | solution.py:72
  152.5 2.0 %collective-permute-start.15 = (f32[72,256]{1,0:T(8,128)S(1)}, f32[72,256]{1,0:T(8,128)S(1)}, u32[]{:S(2)}, u32[]{:S(2)}) collective-permute-start(f32[72,256]{1,0:T(8,128)S(1)} %copy-done.13), channel_id=1, source_target_pairs={{0,1},{1,16},{16,17},{17,0},{2,3},{3,18},{18,19},{19,2},{4,5},{5,2... | collective-permute-start | bytes 221192 | tf_op jit(solution)/shard_map/ppermute | solution.py:324
  154.5 2.7 %collective-permute-start.16 = (f32[72,256]{1,0:T(8,128)S(1)}, f32[72,256]{1,0:T(8,128)S(1)}, u32[]{:S(2)}, u32[]{:S(2)}) collective-permute-start(f32[72,256]{1,0:T(8,128)S(1)} %copy-done.12), channel_id=1, source_target_pairs={{0,16},{1,17},{16,0},{17,1},{2,18},{3,19},{18,2},{19,3},{4,20},{5,... | collective-permute-start | bytes 221192 | tf_op jit(solution)/shard_map/ppermute | solution.py:324
  158.7 2.4 %fusion = bf16[128,2240]{0,1:T(8,128)(2,1)} fusion(f32[128,2240]{0,1:T(8,128)S(1)} %convolution_add_fusion.1, bf16[128,1120]{1,0:T(8,128)(2,1)S(1)} %copy-done.9, bf16[2240,1120]{1,0:T(8,128)(2,1)S(1)} %bitcast.16), kind=kOutput, calls=%fused_computation.2 | convolution fusion | flops 642826240 | bytes 7024640 | tf_op jit(solution)/shard_map/dot_general | solution.py:72
  161.1 2.1 %copy.10 = bf16[128,2240]{1,0:T(8,128)(2,1)} copy(bf16[128,2240]{0,1:T(8,128)(2,1)} %fusion) | data formatting | bytes 1146880 | tf_op jit(solution)/shard_map/convert_element_type | solution.py:487
  163.2 18.3 %collective-permute-done.15.first = f32[72,256]{1,0:T(8,128)S(1)} collective-permute-done((f32[72,256]{1,0:T(8,128)S(1)}, f32[72,256]{1,0:T(8,128)S(1)}, u32[]{:S(2)}, u32[]{:S(2)}) %collective-permute-start.15) | collective-permute-done | bytes 73760 | tf_op jit(solution)/shard_map/ppermute | solution.py:324
  181.5 4.6 %all-to-all-done.4.key_value = f32[16,72,640]{2,1,0:T(8,128)S(1)} async-done(((f32[16,72,640]{2,1,0:T(8,128)}), f32[16,72,640]{2,1,0:T(8,128)S(1)}, u32[]{:S(2)}, u32[]{:S(2)}) %all-to-all-start.4) | async-done | bytes 2949152 | tf_op jit(solution)/shard_map/all_to_all | solution.py:320
  (64 shorter events, 20.7 us)
Async XLA Ops:
  11.2 9.9 %collective-permute-start.1 = (f32[1120,128]{1,0:T(8,128)}, f32[1120,128]{1,0:T(8,128)S(1)}, u32[]{:S(2)}, u32[]{:S(2)}) collective-permute-start(f32[1120,128]{1,0:T(8,128)} %get-tuple-element.59), channel_id=1, source_target_pairs={{0,8},{8,0},{1,9},{9,1},{2,10},{10,2},{3,11},{11,3},{4,12},{12,4},... | collective-permute-start | bytes 1720328 | tf_op jit(solution)/shard_map/ppermute | solution.py:332
  11.2 22.8 %all-to-all-start = ((f32[32,45,112]{2,1,0:T(8,128)}), f32[32,45,112]{2,1,0:T(8,128)S(1)}, u32[]{:S(2)}, u32[]{:S(2)}) async-start(f32[32,45,112]{2,1,0:T(8,128)} %get-tuple-element.55), calls=%async_computation | async-start | bytes 1572864 | tf_op jit(solution)/shard_map/all_to_all | solution.py:320
  19.4 14.5 %copy-start.2 = (bf16[1,16,8,1120]{3,2,1,0:T(8,128)(2,1)S(1)}, bf16[1,16,8,1120]{3,2,1,0:T(8,128)(2,1)}, u32[]{:S(2)}) copy-start(bf16[1,16,8,1120]{3,2,1,0:T(8,128)(2,1)} %param.9) | copy-start | bytes 860164
  19.4 17.9 %collective-permute-start = (f32[1120,128]{1,0:T(8,128)}, f32[1120,128]{1,0:T(8,128)S(1)}, u32[]{:S(2)}, u32[]{:S(2)}) collective-permute-start(f32[1120,128]{1,0:T(8,128)} %get-tuple-element.72.refs_0_), channel_id=1, source_target_pairs={{0,32},{32,64},{64,96},{96,0},{1,33},{33,65},{65,97},{97,1},{2,34}... | collective-permute-start | bytes 1720328 | tf_op jit(solution)/shard_map/ppermute | solution.py:324
  21.1 16.3 %collective-permute-start.2 = (f32[1120,128]{1,0:T(8,128)S(1)}, f32[1120,128]{1,0:T(8,128)}, u32[]{:S(2)}, u32[]{:S(2)}) collective-permute-start(f32[1120,128]{1,0:T(8,128)S(1)} %collective-permute-done.1.refs_4_), channel_id=1, source_target_pairs={{0,96},{32,0},{64,32},{96,64},{1,97},{33,1},{65,33},{97,65},{2,98}... | collective-permute-start | bytes 1720328 | tf_op jit(solution)/shard_map/ppermute | solution.py:324
  34.9 27.2 %copy-start.1 = (bf16[10,128,112]{2,1,0:T(8,128)(2,1)S(1)}, bf16[10,128,112]{2,1,0:T(8,128)(2,1)}, u32[]{:S(2)}) copy-start(bf16[10,128,112]{2,1,0:T(8,128)(2,1)} %query.1.refs_1_) | copy-start | bytes 860164
  37.4 24.8 %copy-start.6 = (f32[10,112]{1,0:T(8,128)S(1)}, f32[10,112]{1,0:T(8,128)}, u32[]{:S(2)}) copy-start(f32[10,112]{1,0:T(8,128)} %get-tuple-element.62.refs_3_.total) | copy-start | bytes 13444
  37.4 24.8 %all-to-all-start.1 = ((f32[32,70,112]{2,1,0:T(8,128)}), f32[32,70,112]{2,1,0:T(8,128)S(1)}, u32[]{:S(2)}, u32[]{:S(2)}) async-start(f32[32,70,112]{2,1,0:T(8,128)} %get-tuple-element.60), calls=%async_computation.1 | async-start | bytes 2359296 | tf_op jit(solution)/shard_map/all_to_all | solution.py:320
  43.4 21.4 %collective-permute-start.3 = (f32[1120,128]{1,0:T(8,128)S(1)}, f32[1120,128]{1,0:T(8,128)}, u32[]{:S(2)}, u32[]{:S(2)}) collective-permute-start(f32[1120,128]{1,0:T(8,128)S(1)} %collective-permute-done.refs_1_), channel_id=1, source_target_pairs={{0,32},{32,64},{64,96},{96,0},{1,33},{33,65},{65,97},{97,1},{2,34}... | collective-permute-start | bytes 1720328 | tf_op jit(solution)/shard_map/ppermute | solution.py:324
  44.7 20.0 %collective-permute-start.4 = (f32[1120,128]{1,0:T(8,128)}, f32[1120,128]{1,0:T(8,128)}, u32[]{:S(2)}, u32[]{:S(2)}) collective-permute-start(f32[1120,128]{1,0:T(8,128)} %collective-permute-done.2.refs_7_), channel_id=1, source_target_pairs={{0,96},{32,0},{64,32},{96,64},{1,97},{33,1},{65,33},{97,65},{2,98}... | collective-permute-start | bytes 1720328 | tf_op jit(solution)/shard_map/ppermute | solution.py:324
  64.7 31.0 %all-to-all-start.2 = ((f32[32,45,112]{2,1,0:T(8,128)}), f32[32,45,112]{2,1,0:T(8,128)S(1)}, u32[]{:S(2)}, u32[]{:S(2)}) async-start(f32[32,45,112]{2,1,0:T(8,128)} %get-tuple-element.70), calls=%async_computation.2 | async-start | bytes 1572864 | tf_op jit(solution)/shard_map/all_to_all | solution.py:320
  68.9 22.8 %collective-permute-start.5 = (f32[1120,128]{1,0:T(8,128)}, f32[1120,128]{1,0:T(8,128)}, u32[]{:S(2)}, u32[]{:S(2)}) collective-permute-start(f32[1120,128]{1,0:T(8,128)} %get-tuple-element.72.refs_0_), channel_id=1, source_target_pairs={{0,96},{32,0},{64,32},{96,64},{1,97},{33,1},{65,33},{97,65},{2,98}... | collective-permute-start | bytes 1720328 | tf_op jit(solution)/shard_map/ppermute | solution.py:324
  69.5 22.2 %collective-permute-start.6 = (f32[1120,128]{1,0:T(8,128)S(1)}, f32[1120,128]{1,0:T(8,128)}, u32[]{:S(2)}, u32[]{:S(2)}) collective-permute-start(f32[1120,128]{1,0:T(8,128)S(1)} %collective-permute-done.1.refs_4_), channel_id=1, source_target_pairs={{0,32},{32,64},{64,96},{96,0},{1,33},{33,65},{65,97},{97,1},{2,34}... | collective-permute-start | bytes 1720328 | tf_op jit(solution)/shard_map/ppermute | solution.py:324
  73.9 15.1 %collective-permute-start.7 = (f32[128,256]{1,0:T(8,128)}, f32[128,256]{1,0:T(8,128)S(1)}, u32[]{:S(2)}, u32[]{:S(2)}) collective-permute-start(f32[128,256]{1,0:T(8,128)} %get-tuple-element.76), channel_id=1, source_target_pairs={{0,32},{32,64},{64,96},{96,0},{1,33},{33,65},{65,97},{97,1},{2,34}... | collective-permute-start | bytes 393224 | tf_op jit(solution)/shard_map/ppermute | solution.py:324
  75.2 13.8 %collective-permute-start.8 = (f32[128,256]{1,0:T(8,128)}, f32[128,256]{1,0:T(8,128)S(1)}, u32[]{:S(2)}, u32[]{:S(2)}) collective-permute-start(f32[128,256]{1,0:T(8,128)} %get-tuple-element.77), channel_id=1, source_target_pairs={{0,64},{32,96},{64,0},{96,32},{1,65},{33,97},{65,1},{97,33},{2,66}... | collective-permute-start | bytes 393224 | tf_op jit(solution)/shard_map/ppermute | solution.py:324
  77.5 12.5 %collective-permute-start.9 = (f32[128,256]{1,0:T(8,128)}, f32[128,256]{1,0:T(8,128)S(1)}, u32[]{:S(2)}, u32[]{:S(2)}) collective-permute-start(f32[128,256]{1,0:T(8,128)} %get-tuple-element.78), channel_id=1, source_target_pairs={{0,96},{32,0},{64,32},{96,64},{1,97},{33,1},{65,33},{97,65},{2,98}... | collective-permute-start | bytes 393224 | tf_op jit(solution)/shard_map/ppermute | solution.py:324
  95.7 10.0 %copy-start.7 = (f32[512,256]{1,0:T(8,128)S(1)}, f32[512,256]{1,0:T(8,128)}, u32[]{:S(2)}) copy-start(f32[512,256]{1,0:T(8,128)} %pack_query.1.refs_2_) | copy-start | bytes 1572868
  98.0 31.2 %all-to-all-start.3 = ((f32[4,128,640]{2,1,0:T(8,128)}), f32[4,128,640]{2,1,0:T(8,128)S(1)}, u32[]{:S(2)}, u32[]{:S(2)}) async-start(f32[4,128,640]{2,1,0:T(8,128)} %get-tuple-element.86.refs_4_), calls=%async_computation.3 | async-start | bytes 2621440 | tf_op jit(solution)/shard_map/all_to_all | solution.py:320
  105.7 1.9 %collective-permute-start.10 = (f32[512,256]{1,0:T(8,128)S(1)}, f32[512,256]{1,0:T(8,128)S(1)}, u32[]{:S(2)}, u32[]{:S(2)}) collective-permute-start(f32[512,256]{1,0:T(8,128)S(1)} %copy-done.7), channel_id=1, source_target_pairs={{0,8},{8,0},{1,9},{9,1},{2,10},{10,2},{3,11},{11,3},{4,12},{12,4},... | collective-permute-start | bytes 1572872 | tf_op jit(solution)/shard_map/ppermute | solution.py:332
  111.3 10.5 %collective-permute-start.11 = (f32[4,72,256]{2,1,0:T(8,128)}, f32[4,72,256]{2,1,0:T(8,128)S(1)}, u32[]{:S(2)}, u32[]{:S(2)}) collective-permute-start(f32[4,72,256]{2,1,0:T(8,128)} %get-tuple-element.89), channel_id=1, source_target_pairs={{0,2},{2,4},{4,6},{6,0},{1,3},{3,5},{5,7},{7,1},{8,10},{10,12},{12... | collective-permute-start | bytes 884744 | tf_op jit(solution)/shard_map/ppermute | solution.py:324
  112.9 16.2 %collective-permute-start.12 = (f32[4,72,256]{2,1,0:T(8,128)}, f32[4,72,256]{2,1,0:T(8,128)S(1)}, u32[]{:S(2)}, u32[]{:S(2)}) collective-permute-start(f32[4,72,256]{2,1,0:T(8,128)} %get-tuple-element.90), channel_id=1, source_target_pairs={{0,4},{2,6},{4,0},{6,2},{1,5},{3,7},{5,1},{7,3},{8,12},{10,14},{12... | collective-permute-start | bytes 884744 | tf_op jit(solution)/shard_map/ppermute | solution.py:324
  115.6 13.6 %collective-permute-start.13 = (f32[4,72,256]{2,1,0:T(8,128)}, f32[4,72,256]{2,1,0:T(8,128)S(1)}, u32[]{:S(2)}, u32[]{:S(2)}) collective-permute-start(f32[4,72,256]{2,1,0:T(8,128)} %get-tuple-element.91), channel_id=1, source_target_pairs={{0,6},{2,0},{4,2},{6,4},{1,7},{3,1},{5,3},{7,5},{8,14},{10,8},{12,... | collective-permute-start | bytes 884744 | tf_op jit(solution)/shard_map/ppermute | solution.py:324
  129.2 3.0 %collective-permute-start.14 = (f32[4,128,640]{2,1,0:T(8,128)S(1)}, f32[4,128,640]{2,1,0:T(8,128)S(1)}, u32[]{:S(2)}, u32[]{:S(2)}) collective-permute-start(f32[4,128,640]{2,1,0:T(8,128)S(1)} %all-to-all-done.3.refs_2_), channel_id=1, source_target_pairs={{0,8},{8,0},{1,9},{9,1},{2,10},{10,2},{3,11},{11,3},{4,12},{12,4},... | collective-permute-start | bytes 3932168 | tf_op jit(solution)/shard_map/ppermute | solution.py:332
  137.4 6.6 %copy-start.8 = (bf16[128,1120]{1,0:T(8,128)(2,1)S(1)}, bf16[128,1120]{1,0:T(8,128)(2,1)}, u32[]{:S(2)}) copy-start(bf16[128,1120]{1,0:T(8,128)(2,1)} %get-tuple-element.64) | copy-start | bytes 860164
  137.5 48.6 %all-to-all-start.4 = ((f32[16,72,640]{2,1,0:T(8,128)}), f32[16,72,640]{2,1,0:T(8,128)S(1)}, u32[]{:S(2)}, u32[]{:S(2)}) async-start(f32[16,72,640]{2,1,0:T(8,128)} %key_value_product.1), calls=%async_computation.4 | async-start | bytes 5898240 | tf_op jit(solution)/shard_map/all_to_all | solution.py:320
  144.1 14.5 %slice-start = ((s8[5160960]{0:T(1024)(128)(4,1)}), s8[4194304]{0:T(1024)(128)(4,1)S(1)}, s32[]{:S(2)}) async-start(s8[5160960]{0:T(1024)(128)(4,1)} %bitcast.15), calls=%async_computation.5 | async-start | bytes 8388608
  148.3 8.8 %copy-start.11 = (f32[72,256]{1,0:T(8,128)S(1)}, f32[72,256]{1,0:T(8,128)}, u32[]{:S(2)}) copy-start(f32[72,256]{1,0:T(8,128)} %get-tuple-element.100) | copy-start | bytes 221188
  148.3 10.3 %slice-start.1 = ((s8[5160960]{0:T(1024)(128)(4,1)}), s8[966656]{0:T(1024)(128)(4,1)S(1)}, s32[]{:S(2)}) async-start(s8[5160960]{0:T(1024)(128)(4,1)} %bitcast.15), calls=%async_computation.6 | async-start | bytes 1933312
  148.4 10.3 %copy-start.9 = (bf16[128,1120]{1,0:T(8,128)(2,1)S(1)}, bf16[128,1120]{1,0:T(8,128)(2,1)}, u32[]{:S(2)}) copy-start(bf16[128,1120]{1,0:T(8,128)(2,1)} %get-tuple-element.84) | copy-start | bytes 860164
  152.5 29.0 %collective-permute-start.15 = (f32[72,256]{1,0:T(8,128)S(1)}, f32[72,256]{1,0:T(8,128)S(1)}, u32[]{:S(2)}, u32[]{:S(2)}) collective-permute-start(f32[72,256]{1,0:T(8,128)S(1)} %copy-done.13), channel_id=1, source_target_pairs={{0,1},{1,16},{16,17},{17,0},{2,3},{3,18},{18,19},{19,2},{4,5},{5,2... | collective-permute-start | bytes 221192 | tf_op jit(solution)/shard_map/ppermute | solution.py:324
  154.5 27.0 %collective-permute-start.16 = (f32[72,256]{1,0:T(8,128)S(1)}, f32[72,256]{1,0:T(8,128)S(1)}, u32[]{:S(2)}, u32[]{:S(2)}) collective-permute-start(f32[72,256]{1,0:T(8,128)S(1)} %copy-done.12), channel_id=1, source_target_pairs={{0,16},{1,17},{16,0},{17,1},{2,18},{3,19},{18,2},{19,3},{4,20},{5,... | collective-permute-start | bytes 221192 | tf_op jit(solution)/shard_map/ppermute | solution.py:324
  157.2 24.3 %collective-permute-start.17 = (f32[72,256]{1,0:T(8,128)S(1)}, f32[72,256]{1,0:T(8,128)S(1)}, u32[]{:S(2)}, u32[]{:S(2)}) collective-permute-start(f32[72,256]{1,0:T(8,128)S(1)} %copy-done.11), channel_id=1, source_target_pairs={{0,17},{1,0},{16,1},{17,16},{2,19},{3,2},{18,3},{19,18},{4,21},{5,... | collective-permute-start | bytes 221192 | tf_op jit(solution)/shard_map/ppermute | solution.py:324
  (7 other events, 27.6 us)

commit v9 on v8

--- a/solution.py
+++ b/solution.py
@@ -261,8 +261,15 @@
 
 
 def join_kernel(*refs):
-    for slot, part in enumerate(refs[:-1]):
-        refs[-1][:, slot * TOKENS : (slot + 1) * TOKENS] = part[...].astype(BF16)
+    parts, out = refs[:-1], refs[-1]
+    for core in range(CORES):
+        own, left, far_upper, far_lower, right = parts[core * 5 : core * 5 + 5]
+        at = core * REPLICAS * TOKENS
+        out[:, at : at + TOKENS] = own[...].astype(BF16)
+        out[:, at + TOKENS : at + 2 * TOKENS] = left[...].astype(BF16)
+        out[:HALF, at + 2 * TOKENS : at + 3 * TOKENS] = far_upper[...].astype(BF16)
+        out[HALF:, at + 2 * TOKENS : at + 3 * TOKENS] = far_lower[...].astype(BF16)
+        out[:, at + 3 * TOKENS : at + 4 * TOKENS] = right[...].astype(BF16)
 
 
 def pack_kernel(*refs):
@@ -372,8 +379,7 @@
         turn_kernel, "turn", [half, half], [IN_SMEM, BLOCK], [pltpu.VMEM((D, TOKENS), F32)]
     )(core, later_tokens)
     bottom = swap_cores(bottom)
-    left_top = shift(top, 1, "dp")
-    right_bottom = shift(bottom, 3, "dp")
+    top_left, top_right = shift(top, 1, "dp"), shift(top, 3, "dp")
     got = exchange(sent, IMAGE)
     (query,) = call(
         query_kernel,
@@ -387,13 +393,13 @@
         [shaped((TILES, 2 * PART, HD)), heads, shaped((HEADS, HD))],
         [BLOCK] * 3,
         [state],
-        arrived=(0, 1, 2),
+        arrived=(0, 2),
     )(got, query, upstream)
-    sent, left_top, right_bottom, later_top, later_bottom = lax.optimization_barrier(
-        (sent, left_top, right_bottom, top, bottom)
+    sent, top_left, top_right, bottom = lax.optimization_barrier(
+        (sent, top_left, top_right, bottom)
     )
-    far_top = shift(left_top, 1, "dp")
-    far_bottom = shift(right_bottom, 3, "dp")
+    bottom_left, bottom_right = shift(bottom, 1, "dp"), shift(bottom, 3, "dp")
+    top_far = shift(top_left[:HALF], 1, "dp"), shift(top_right[HALF:], 3, "dp")
     got_state = exchange(sent, IMAGE)
     sent, grad_denom = call(
         lambda *refs: total_grad_kernel(loss_scale, *refs),
@@ -403,11 +409,10 @@
         [state, totals],
         arrived=(0, 1, 2, 3),
     )(got_state, query, upstream, total)
-    sent, far_top, far_bottom, later_top, later_bottom = lax.optimization_barrier(
-        (sent, far_top, far_bottom, later_top, later_bottom)
+    sent, top_far, bottom_left, bottom_right = lax.optimization_barrier(
+        (sent, top_far, bottom_left, bottom_right)
     )
-    left_bottom = shift(later_bottom, 1, "dp")
-    right_top = shift(later_top, 3, "dp")
+    bottom_far = shift(bottom_left[:HALF], 1, "dp"), shift(bottom_right[HALF:], 3, "dp")
     got = exchange(sent, IMAGE)
 
     block = shaped((TOKENS, EARLY))
@@ -424,16 +429,16 @@
         join_kernel,
         "join",
         [shaped((CORES * HALF, 2 * REPLICAS * TOKENS), BF16)],
-        [BLOCK] * 8,
-        arrived=tuple(range(1, 8)),
-    )(top, left_top, far_top, right_top, bottom, left_bottom, far_bottom, right_bottom)
+        [BLOCK] * 10,
+        arrived=tuple(range(1, 10)),
+    )(top, top_left, *top_far, top_right, bottom, bottom_left, *bottom_far, bottom_right)
     (query_columns,) = call(
-        pack_kernel,
+        lambda *refs: pack_kernel(*refs[:RING], refs[-1]),
         "pack_query",
         [shaped((REPLICAS * TOKENS, EARLY))],
-        [BLOCK] * RING,
+        [BLOCK] * RING + [ANYWHERE],
         arrived=(1, 2, 3),
-    )(*query_columns)
+    )(*query_columns, rows)
     got, rows, query_columns = lax.optimization_barrier((got, rows, query_columns))
 
     grad_key, grad_value, sent = call(

time: 189 us -> 187 us (0.989)
  waiting for transfers between devices: 72.8 us -> 62.7 us
  local copies, waits for them, and re-layouts: 3.16 us -> 7.04 us
  starting transfers between devices: 57.1 us -> 60.7 us
    all_to_all x5, waiting for transfers between devices: 29.3 us -> 22.3 us  [exchange(): return lax.all_to_all(blocks, axes, 0, 0, tiled=True)]
    slice x0 -> x4, local copies, waits for them, and re-layouts: none -> 4.86 us  [the longest x1 1.72 us: body(): bottom_left[:HALF]]
    ppermute x15 -> x17, waiting for transfers between devices: 40.4 us -> 37.2 us  [shift(): lax.ppermute(values, axis, [(i, (i + by) % RING) for i in range(RING)])]
    all_to_all x5, starting transfers between devices: 32.7 us -> 35 us  [exchange(): return lax.all_to_all(blocks, axes, 0, 0, tiled=True)]
    ppermute x15 -> x17, starting transfers between devices: 24.4 us -> 25.4 us  [shift(): lax.ppermute(values, axis, [(i, (i + by) % RING) for i in range(RING)])]
  transfers between devices with their start and end apart: 23 -> 25, of which waited for: 10 -> 13; matrix products, arithmetic and copies ran while one was open for 7% -> 9% of each run, Pallas kernels for 12% -> 14%
where the time goes in v9:
time: 187 us; the launch traced here: 186 us
  waiting for transfers between devices  62.7 us (34%)
  starting transfers between devices  60.7 us (32%)
  Pallas kernels  44.2 us (24%)
  matrix products  10.7 us (6%)
  local copies, waits for them, and re-layouts  7.04 us (4%)
    pallas_call x13, Pallas kernels, with_placed(): return run(*placed)  44.2 us
    ppermute x17, waiting for transfers between devices, shift(): lax.ppermute(values, axis, [(i, (i + by) % RING) for i in range(RING)])  37.2 us
    all_to_all x5, starting transfers between devices, exchange(): return lax.all_to_all(blocks, axes, 0, 0, tiled=True)  35 us
    ppermute x17, starting transfers between devices, shift(): lax.ppermute(values, axis, [(i, (i + by) % RING) for i in range(RING)])  25.4 us
    all_to_all x5, waiting for transfers between devices, exchange(): return lax.all_to_all(blocks, axes, 0, 0, tiled=True)  22.3 us
    dot_general x3, matrix products, dot(): lax.dot_general(left, right, (((left_dim,), (right_dim,)), ((), ())), pre...  10.7 us
  transfers between devices with their start and end apart: 25, of which 13 were waited for; matrix products, arithmetic and copies ran while one was open for 9% of the time, Pallas kernels for 14%

profile of v9, /device:TPU:8, one launch (start us, length us, event | category | flops | bytes accessed | tf_op | source)
XLA Modules:
  0.0 186.2 jit_solution(6006449314862022508)
XLA Ops:
  0.6 8.1 %key_value.1 = (bf16[10,128,112]{2,1,0:T(8,128)(2,1)}, bf16[10,128,112]{2,1,0:T(8,128)(2,1)}, f32[32,45,112]{2,1,0:T(8,128)}) custom-call(bf16[128,2240]{1,0:T(8,128)(2,1)} %bitcast.17, bf16[2240,1120]{1,0:T(8,128)(2,1)} %key_weight.1, bf16[2240,1120]{1,0:T(8,128)(2,1)} %value_weight.1), custom_call_target="tpu_custom_call" | custom-call | tf_op jit(solution)/shard_map/key_value/pallas_call | solution.py:66
  8.8 8.2 %all-to-all-start = ((f32[32,45,112]{2,1,0:T(8,128)}), f32[32,45,112]{2,1,0:T(8,128)S(1)}, u32[]{:S(2)}, u32[]{:S(2)}) async-start(f32[32,45,112]{2,1,0:T(8,128)} %get-tuple-element.54), calls=%async_computation | async-start | bytes 1572864 | tf_op jit(solution)/shard_map/all_to_all | solution.py:327
  17.0 2.4 %turn.1 = (f32[1120,128]{1,0:T(8,128)}, f32[1120,128]{1,0:T(8,128)}) custom-call(s32[1]{0:T(128)} %bitcast.3.core, bf16[128,2240]{1,0:T(8,128)(2,1)} %bitcast.18), custom_call_target="tpu_custom_call" | custom-call | tf_op jit(solution)/shard_map/turn/pallas_call | solution.py:66
  21.6 4.4 %query.1.refs_1_ = bf16[10,128,112]{2,1,0:T(8,128)(2,1)} custom-call(bf16[128,2240]{1,0:T(8,128)(2,1)} %bitcast.19, bf16[2240,1120]{1,0:T(8,128)(2,1)} %weight.1), custom_call_target="tpu_custom_call" | custom-call | tf_op jit(solution)/shard_map/query/pallas_call | solution.py:66
  26.0 5.5 %all-to-all-done.refs_0_ = f32[32,45,112]{2,1,0:T(8,128)S(1)} async-done(((f32[32,45,112]{2,1,0:T(8,128)}), f32[32,45,112]{2,1,0:T(8,128)S(1)}, u32[]{:S(2)}, u32[]{:S(2)}) %all-to-all-start) | async-done | bytes 645152 | tf_op jit(solution)/shard_map/all_to_all | solution.py:327
  31.5 3.5 %numerator.1 = (f32[32,70,112]{2,1,0:T(8,128)}, bf16[10,128,112]{2,1,0:T(8,128)(2,1)}, f32[10,112]{1,0:T(8,128)}) custom-call(f32[32,45,112]{2,1,0:T(8,128)S(1)} %all-to-all-done.refs_0_, bf16[10,128,112]{2,1,0:T(8,128)(2,1)} %query.1.refs_1_, bf16[128,1120]{1,0:T(8,128)(2,1)S(1)} %bitcast.13), custom_call_target="tpu_custom_call" | custom-call | tf_op jit(solution)/shard_map/numerator/pallas_call | solution.py:66
  36.4 7.4 %all-to-all-start.1 = ((f32[32,70,112]{2,1,0:T(8,128)}), f32[32,70,112]{2,1,0:T(8,128)S(1)}, u32[]{:S(2)}, u32[]{:S(2)}) async-start(f32[32,70,112]{2,1,0:T(8,128)} %get-tuple-element.59), calls=%async_computation.1 | async-start | bytes 2359296 | tf_op jit(solution)/shard_map/all_to_all | solution.py:327
  43.8 3.0 %collective-permute-start.6 = (f32[1120,128]{1,0:T(8,128)}, f32[1120,128]{1,0:T(8,128)}, u32[]{:S(2)}, u32[]{:S(2)}) collective-permute-start(f32[1120,128]{1,0:T(8,128)} %collective-permute-done.2.refs_5_), channel_id=1, source_target_pairs={{0,96},{32,0},{64,32},{96,64},{1,97},{33,1},{65,33},{97,65},{2,98}... | collective-permute-start | bytes 1720328 | tf_op jit(solution)/shard_map/ppermute | solution.py:331
  48.2 2.0 %collective-permute-start.4 = (f32[560,128]{1,0:T(8,128)}, f32[560,128]{1,0:T(8,128)S(1)}, u32[]{:S(2)}, u32[]{:S(2)}) collective-permute-start(f32[560,128]{1,0:T(8,128)} %slice.13), channel_id=1, source_target_pairs={{0,96},{32,0},{64,32},{96,64},{1,97},{33,1},{65,33},{97,65},{2,98}... | collective-permute-start | bytes 860168 | tf_op jit(solution)/shard_map/ppermute | solution.py:331
  50.3 12.3 %all-to-all-done.1.refs_0_.got = f32[32,70,112]{2,1,0:T(8,128)S(1)} async-done(((f32[32,70,112]{2,1,0:T(8,128)}), f32[32,70,112]{2,1,0:T(8,128)S(1)}, u32[]{:S(2)}, u32[]{:S(2)}) %all-to-all-start.1) | async-done | bytes 1003552 | tf_op jit(solution)/shard_map/all_to_all | solution.py:327
  62.6 2.6 %total_grad.1 = (f32[32,45,112]{2,1,0:T(8,128)}, f32[128,10]{1,0:T(8,128)}) custom-call(f32[32,70,112]{2,1,0:T(8,128)S(1)} %all-to-all-done.1.refs_0_.got, bf16[10,128,112]{2,1,0:T(8,128)(2,1)S(1)} %copy-done, bf16[128,1120]{1,0:T(8,128)(2,1)S(1)} %bitcast.14, f32[10,112]{1,0:T(8,128)S(1)} %copy-done.5), custom_call_target="tpu_custom_call" | custom-call | tf_op jit(solution)/shard_map/total_grad/pallas_call | solution.py:66
  65.9 2.2 %collective-permute-done.3.refs_2_ = f32[560,128]{1,0:T(8,128)} collective-permute-done((f32[560,128]{1,0:T(8,128)}, f32[560,128]{1,0:T(8,128)}, u32[]{:S(2)}, u32[]{:S(2)}) %collective-permute-start.3) | collective-permute-done | bytes 286752 | tf_op jit(solution)/shard_map/ppermute | solution.py:331
  68.1 7.3 %all-to-all-start.2 = ((f32[32,45,112]{2,1,0:T(8,128)}), f32[32,45,112]{2,1,0:T(8,128)S(1)}, u32[]{:S(2)}, u32[]{:S(2)}) async-start(f32[32,45,112]{2,1,0:T(8,128)} %get-tuple-element.68), calls=%async_computation.2 | async-start | bytes 1572864 | tf_op jit(solution)/shard_map/all_to_all | solution.py:327
  80.8 2.9 %query_grad.1 = (bf16[128,1120]{1,0:T(8,128)(2,1)}, f32[128,256]{1,0:T(8,128)}, f32[128,256]{1,0:T(8,128)}, f32[128,256]{1,0:T(8,128)}, f32[128,256]{1,0:T(8,128)}, /*index=5*/f32[4,128,24]{2,1,0:T(8,128)}) custom-call(s32[1]{0:T(128)} %bitcast.place.refs_0_, f32[32,70,112]{2,1,0:T(8,128)S(1)} %all-to-all-done.1.refs_0_.got, ...), custom_call_target="tpu_custom_call" | custom-call | tf_op jit(solution)/shard_map/query_grad/pallas_call | solution.py:66
  84.1 3.3 %collective-permute-start.10 = (f32[128,256]{1,0:T(8,128)}, f32[128,256]{1,0:T(8,128)S(1)}, u32[]{:S(2)}, u32[]{:S(2)}) collective-permute-start(f32[128,256]{1,0:T(8,128)} %get-tuple-element.75), channel_id=1, source_target_pairs={{0,64},{32,96},{64,0},{96,32},{1,65},{33,97},{65,1},{97,33},{2,66}... | collective-permute-start | bytes 393224 | tf_op jit(solution)/shard_map/ppermute | solution.py:331
  90.4 3.9 %join.1.refs_4_.refs_1_ = bf16[1120,1024]{1,0:T(8,128)(2,1)} custom-call(f32[1120,128]{1,0:T(8,128)} %get-tuple-element.57.refs_0_, f32[1120,128]{1,0:T(8,128)S(1)} %collective-permute-done.refs_1_, f32[560,128]{1,0:T(8,128)} %collective-permute-done.3.refs_2_, f32[560,128]{1,0:T(8,128)S(1)} %collective-permute-done.4.refs_3_, ...), custom_call_target="tpu_custom_call" | custom-call | tf_op jit(solution)/shard_map/join/pallas_call | solution.py:66
  96.1 2.3 %key_value_grad.1 = (bf16[128,1120]{1,0:T(8,128)(2,1)}, bf16[128,1120]{1,0:T(8,128)(2,1)}, f32[4,128,640]{2,1,0:T(8,128)}) custom-call(f32[32,45,112]{2,1,0:T(8,128)S(1)} %all-to-all-done.2.got, bf16[10,128,112]{2,1,0:T(8,128)(2,1)S(1)} %copy-done.2, bf16[10,128,112]{2,1,0:T(8,128)(2,1)S(1)} %copy-done.3, f32[4,128,24]{2,1,0:T(8,128)S(1)} %copy-done.4), custom_call_target="tpu_custom_call" | custom-call | tf_op jit(solution)/shard_map/key_value_grad/pallas_call | solution.py:66
  98.5 5.6 %all-to-all-start.3 = ((f32[4,128,640]{2,1,0:T(8,128)}), f32[4,128,640]{2,1,0:T(8,128)S(1)}, u32[]{:S(2)}, u32[]{:S(2)}) async-start(f32[4,128,640]{2,1,0:T(8,128)} %get-tuple-element.84.refs_4_), calls=%async_computation.3 | async-start | bytes 2621440 | tf_op jit(solution)/shard_map/all_to_all | solution.py:327
  106.0 3.7 %query_product.1 = (f32[4,72,256]{2,1,0:T(8,128)}, f32[4,72,256]{2,1,0:T(8,128)}, f32[4,72,256]{2,1,0:T(8,128)}, f32[4,72,256]{2,1,0:T(8,128)}) custom-call(s32[1]{0:T(128)} %bitcast.5.refs_0_, bf16[1120,1024]{1,0:T(8,128)(2,1)} %join.1.refs_4_.refs_1_, f32[512,256]{1,0:T(8,128)} %pack_query.1.refs_2_, f32[512,256]{1,0:T(8,128)S(1)} %collective-permute-done.12.refs_3_, ...), custom_call_target="tpu_custom_call" | custom-call | tf_op jit(solution)/shard_map/query_product/pallas_call | solution.py:66
  111.3 2.7 %collective-permute-start.14 = (f32[4,72,256]{2,1,0:T(8,128)}, f32[4,72,256]{2,1,0:T(8,128)S(1)}, u32[]{:S(2)}, u32[]{:S(2)}) collective-permute-start(f32[4,72,256]{2,1,0:T(8,128)} %get-tuple-element.88), channel_id=1, source_target_pairs={{0,4},{2,6},{4,0},{6,2},{1,5},{3,7},{5,1},{7,3},{8,12},{10,14},{12... | collective-permute-start | bytes 884744 | tf_op jit(solution)/shard_map/ppermute | solution.py:331
  115.4 4.7 %collective-permute-done.13.first = f32[4,72,256]{2,1,0:T(8,128)S(1)} collective-permute-done((f32[4,72,256]{2,1,0:T(8,128)}, f32[4,72,256]{2,1,0:T(8,128)S(1)}, u32[]{:S(2)}, u32[]{:S(2)}) %collective-permute-start.13) | collective-permute-done | bytes 294944 | tf_op jit(solution)/shard_map/ppermute | solution.py:331
  120.1 7.4 %collective-permute-done.14.second = f32[4,72,256]{2,1,0:T(8,128)S(1)} collective-permute-done((f32[4,72,256]{2,1,0:T(8,128)}, f32[4,72,256]{2,1,0:T(8,128)S(1)}, u32[]{:S(2)}, u32[]{:S(2)}) %collective-permute-start.14) | collective-permute-done | bytes 294944 | tf_op jit(solution)/shard_map/ppermute | solution.py:331
  130.6 5.3 %key_value_product.1 = f32[16,72,640]{2,1,0:T(8,128)} custom-call(s32[1]{0:T(128)} %bitcast.place.refs_0_, bf16[1120,1024]{1,0:T(8,128)(2,1)} %join.1.refs_4_.refs_1_, f32[4,128,640]{2,1,0:T(8,128)S(1)} %all-to-all-done.3.refs_2_, f32[4,128,640]{2,1,0:T(8,128)S(1)} %collective-permute-done.16.refs_3_, f32[72,256]{1,0:T(8,128)} %get-tuple-element.95.refs_4_.own), custom_call_target="tpu_custom_call" | custom-call | tf_op jit(solution)/shard_map/key_value_product/pallas_call | solution.py:66
  135.8 6.6 %all-to-all-start.4 = ((f32[16,72,640]{2,1,0:T(8,128)}), f32[16,72,640]{2,1,0:T(8,128)S(1)}, u32[]{:S(2)}, u32[]{:S(2)}) async-start(f32[16,72,640]{2,1,0:T(8,128)} %key_value_product.1), calls=%async_computation.4 | async-start | bytes 5898240 | tf_op jit(solution)/shard_map/all_to_all | solution.py:327
  142.5 4.2 %fusion.1 = f32[128,2240]{0,1:T(8,128)S(1)} fusion(bf16[128,1120]{1,0:T(8,128)(2,1)S(1)} %copy-done.7, bf16[2240,1120]{1,0:T(8,128)(2,1)} %weight.1), kind=kOutput, calls=%fused_computation.3 | convolution fusion | flops 642252800 | bytes 6451200 | tf_op jit(solution)/shard_map/dot_general | solution.py:72
  146.8 4.1 %convolution_add_fusion.1 = f32[128,2240]{0,1:T(8,128)S(1)} fusion(f32[128,2240]{0,1:T(8,128)S(1)} %fusion.1, bf16[128,1120]{1,0:T(8,128)(2,1)S(1)} %copy-done.9, bf16[2240,1120]{1,0:T(8,128)(2,1)} %key_weight.1), kind=kOutput, calls=%fused_computation.1 | convolution fusion | flops 642539520 | bytes 7598080 | tf_op jit(solution)/shard_map/dot_general | solution.py:72
  150.9 2.0 %collective-permute-start.17 = (f32[72,256]{1,0:T(8,128)S(1)}, f32[72,256]{1,0:T(8,128)S(1)}, u32[]{:S(2)}, u32[]{:S(2)}) collective-permute-start(f32[72,256]{1,0:T(8,128)S(1)} %copy-done.12), channel_id=1, source_target_pairs={{0,1},{1,16},{16,17},{17,0},{2,3},{3,18},{18,19},{19,2},{4,5},{5,2... | collective-permute-start | bytes 221192 | tf_op jit(solution)/shard_map/ppermute | solution.py:331
  152.9 2.7 %collective-permute-start.18 = (f32[72,256]{1,0:T(8,128)S(1)}, f32[72,256]{1,0:T(8,128)S(1)}, u32[]{:S(2)}, u32[]{:S(2)}) collective-permute-start(f32[72,256]{1,0:T(8,128)S(1)} %copy-done.11), channel_id=1, source_target_pairs={{0,16},{1,17},{16,0},{17,1},{2,18},{3,19},{18,2},{19,3},{4,20},{5,... | collective-permute-start | bytes 221192 | tf_op jit(solution)/shard_map/ppermute | solution.py:331
  157.0 2.4 %fusion = bf16[128,2240]{0,1:T(8,128)(2,1)} fusion(f32[128,2240]{0,1:T(8,128)S(1)} %convolution_add_fusion.1, bf16[128,1120]{1,0:T(8,128)(2,1)S(1)} %copy-done.8, bf16[2240,1120]{1,0:T(8,128)(2,1)S(1)} %bitcast.16), kind=kOutput, calls=%fused_computation.2 | convolution fusion | flops 642826240 | bytes 7024640 | tf_op jit(solution)/shard_map/dot_general | solution.py:72
  159.4 2.1 %copy.10 = bf16[128,2240]{1,0:T(8,128)(2,1)} copy(bf16[128,2240]{0,1:T(8,128)(2,1)} %fusion) | data formatting | bytes 1146880 | tf_op jit(solution)/shard_map/convert_element_type | solution.py:492
  161.5 18.4 %collective-permute-done.17.first = f32[72,256]{1,0:T(8,128)S(1)} collective-permute-done((f32[72,256]{1,0:T(8,128)S(1)}, f32[72,256]{1,0:T(8,128)S(1)}, u32[]{:S(2)}, u32[]{:S(2)}) %collective-permute-start.17) | collective-permute-done | bytes 73760 | tf_op jit(solution)/shard_map/ppermute | solution.py:331
  179.9 4.6 %all-to-all-done.4.key_value = f32[16,72,640]{2,1,0:T(8,128)S(1)} async-done(((f32[16,72,640]{2,1,0:T(8,128)}), f32[16,72,640]{2,1,0:T(8,128)S(1)}, u32[]{:S(2)}, u32[]{:S(2)}) %all-to-all-start.4) | async-done | bytes 2949152 | tf_op jit(solution)/shard_map/all_to_all | solution.py:327
  (70 shorter events, 27.9 us)
Async XLA Ops:
  8.8 22.7 %all-to-all-start = ((f32[32,45,112]{2,1,0:T(8,128)}), f32[32,45,112]{2,1,0:T(8,128)S(1)}, u32[]{:S(2)}, u32[]{:S(2)}) async-start(f32[32,45,112]{2,1,0:T(8,128)} %get-tuple-element.54), calls=%async_computation | async-start | bytes 1572864 | tf_op jit(solution)/shard_map/all_to_all | solution.py:327
  19.3 15.6 %collective-permute-start.2 = (f32[1120,128]{1,0:T(8,128)}, f32[1120,128]{1,0:T(8,128)}, u32[]{:S(2)}, u32[]{:S(2)}) collective-permute-start(f32[1120,128]{1,0:T(8,128)} %get-tuple-element.58), channel_id=1, source_target_pairs={{0,8},{8,0},{1,9},{9,1},{2,10},{10,2},{3,11},{11,3},{4,12},{12,4},... | collective-permute-start | bytes 1720328 | tf_op jit(solution)/shard_map/ppermute | solution.py:339
  19.6 11.9 %copy-start.1 = (bf16[1,16,8,1120]{3,2,1,0:T(8,128)(2,1)S(1)}, bf16[1,16,8,1120]{3,2,1,0:T(8,128)(2,1)}, u32[]{:S(2)}) copy-start(bf16[1,16,8,1120]{3,2,1,0:T(8,128)(2,1)} %param.9) | copy-start | bytes 860164
  19.6 15.4 %collective-permute-start.1 = (f32[1120,128]{1,0:T(8,128)}, f32[1120,128]{1,0:T(8,128)S(1)}, u32[]{:S(2)}, u32[]{:S(2)}) collective-permute-start(f32[1120,128]{1,0:T(8,128)} %get-tuple-element.57.refs_0_), channel_id=1, source_target_pairs={{0,96},{32,0},{64,32},{96,64},{1,97},{33,1},{65,33},{97,65},{2,98}... | collective-permute-start | bytes 1720328 | tf_op jit(solution)/shard_map/ppermute | solution.py:331
  20.0 16.4 %collective-permute-start = (f32[1120,128]{1,0:T(8,128)}, f32[1120,128]{1,0:T(8,128)S(1)}, u32[]{:S(2)}, u32[]{:S(2)}) collective-permute-start(f32[1120,128]{1,0:T(8,128)} %get-tuple-element.57.refs_0_), channel_id=1, source_target_pairs={{0,32},{32,64},{64,96},{96,0},{1,33},{33,65},{65,97},{97,1},{2,34}... | collective-permute-start | bytes 1720328 | tf_op jit(solution)/shard_map/ppermute | solution.py:331
  31.5 31.1 %copy-start = (bf16[10,128,112]{2,1,0:T(8,128)(2,1)S(1)}, bf16[10,128,112]{2,1,0:T(8,128)(2,1)}, u32[]{:S(2)}) copy-start(bf16[10,128,112]{2,1,0:T(8,128)(2,1)} %query.1.refs_1_) | copy-start | bytes 860164
  34.9 27.6 %copy-start.5 = (f32[10,112]{1,0:T(8,128)S(1)}, f32[10,112]{1,0:T(8,128)}, u32[]{:S(2)}) copy-start(f32[10,112]{1,0:T(8,128)} %get-tuple-element.61.refs_3_.total) | copy-start | bytes 13444
  36.4 26.2 %all-to-all-start.1 = ((f32[32,70,112]{2,1,0:T(8,128)}), f32[32,70,112]{2,1,0:T(8,128)S(1)}, u32[]{:S(2)}, u32[]{:S(2)}) async-start(f32[32,70,112]{2,1,0:T(8,128)} %get-tuple-element.59), calls=%async_computation.1 | async-start | bytes 2359296 | tf_op jit(solution)/shard_map/all_to_all | solution.py:327
  43.8 24.3 %collective-permute-start.6 = (f32[1120,128]{1,0:T(8,128)}, f32[1120,128]{1,0:T(8,128)}, u32[]{:S(2)}, u32[]{:S(2)}) collective-permute-start(f32[1120,128]{1,0:T(8,128)} %collective-permute-done.2.refs_5_), channel_id=1, source_target_pairs={{0,96},{32,0},{64,32},{96,64},{1,97},{33,1},{65,33},{97,65},{2,98}... | collective-permute-start | bytes 1720328 | tf_op jit(solution)/shard_map/ppermute | solution.py:331
  46.8 21.3 %collective-permute-start.5 = (f32[1120,128]{1,0:T(8,128)}, f32[1120,128]{1,0:T(8,128)}, u32[]{:S(2)}, u32[]{:S(2)}) collective-permute-start(f32[1120,128]{1,0:T(8,128)} %collective-permute-done.2.refs_5_), channel_id=1, source_target_pairs={{0,32},{32,64},{64,96},{96,0},{1,33},{33,65},{65,97},{97,1},{2,34}... | collective-permute-start | bytes 1720328 | tf_op jit(solution)/shard_map/ppermute | solution.py:331
  48.2 17.7 %collective-permute-start.4 = (f32[560,128]{1,0:T(8,128)}, f32[560,128]{1,0:T(8,128)S(1)}, u32[]{:S(2)}, u32[]{:S(2)}) collective-permute-start(f32[560,128]{1,0:T(8,128)} %slice.13), channel_id=1, source_target_pairs={{0,96},{32,0},{64,32},{96,64},{1,97},{33,1},{65,33},{97,65},{2,98}... | collective-permute-start | bytes 860168 | tf_op jit(solution)/shard_map/ppermute | solution.py:331
  50.3 17.9 %collective-permute-start.3 = (f32[560,128]{1,0:T(8,128)}, f32[560,128]{1,0:T(8,128)}, u32[]{:S(2)}, u32[]{:S(2)}) collective-permute-start(f32[560,128]{1,0:T(8,128)} %slice.12), channel_id=1, source_target_pairs={{0,32},{32,64},{64,96},{96,0},{1,33},{33,65},{65,97},{97,1},{2,34}... | collective-permute-start | bytes 860168 | tf_op jit(solution)/shard_map/ppermute | solution.py:331
  68.1 28.0 %all-to-all-start.2 = ((f32[32,45,112]{2,1,0:T(8,128)}), f32[32,45,112]{2,1,0:T(8,128)S(1)}, u32[]{:S(2)}, u32[]{:S(2)}) async-start(f32[32,45,112]{2,1,0:T(8,128)} %get-tuple-element.68), calls=%async_computation.2 | async-start | bytes 1572864 | tf_op jit(solution)/shard_map/all_to_all | solution.py:327
  78.8 10.8 %collective-permute-start.8 = (f32[560,128]{1,0:T(8,128)}, f32[560,128]{1,0:T(8,128)}, u32[]{:S(2)}, u32[]{:S(2)}) collective-permute-start(f32[560,128]{1,0:T(8,128)} %slice.15), channel_id=1, source_target_pairs={{0,96},{32,0},{64,32},{96,64},{1,97},{33,1},{65,33},{97,65},{2,98}... | collective-permute-start | bytes 860168 | tf_op jit(solution)/shard_map/ppermute | solution.py:331
  80.4 10.0 %collective-permute-start.7 = (f32[560,128]{1,0:T(8,128)}, f32[560,128]{1,0:T(8,128)}, u32[]{:S(2)}, u32[]{:S(2)}) collective-permute-start(f32[560,128]{1,0:T(8,128)} %slice.14), channel_id=1, source_target_pairs={{0,32},{32,64},{64,96},{96,0},{1,33},{33,65},{65,97},{97,1},{2,34}... | collective-permute-start | bytes 860168 | tf_op jit(solution)/shard_map/ppermute | solution.py:331
  83.7 10.5 %collective-permute-start.9 = (f32[128,256]{1,0:T(8,128)}, f32[128,256]{1,0:T(8,128)S(1)}, u32[]{:S(2)}, u32[]{:S(2)}) collective-permute-start(f32[128,256]{1,0:T(8,128)} %get-tuple-element.74), channel_id=1, source_target_pairs={{0,32},{32,64},{64,96},{96,0},{1,33},{33,65},{65,97},{97,1},{2,34}... | collective-permute-start | bytes 393224 | tf_op jit(solution)/shard_map/ppermute | solution.py:331
  84.1 10.2 %collective-permute-start.10 = (f32[128,256]{1,0:T(8,128)}, f32[128,256]{1,0:T(8,128)S(1)}, u32[]{:S(2)}, u32[]{:S(2)}) collective-permute-start(f32[128,256]{1,0:T(8,128)} %get-tuple-element.75), channel_id=1, source_target_pairs={{0,64},{32,96},{64,0},{96,32},{1,65},{33,97},{65,1},{97,33},{2,66}... | collective-permute-start | bytes 393224 | tf_op jit(solution)/shard_map/ppermute | solution.py:331
  87.4 6.9 %collective-permute-start.11 = (f32[128,256]{1,0:T(8,128)}, f32[128,256]{1,0:T(8,128)S(1)}, u32[]{:S(2)}, u32[]{:S(2)}) collective-permute-start(f32[128,256]{1,0:T(8,128)} %get-tuple-element.76), channel_id=1, source_target_pairs={{0,96},{32,0},{64,32},{96,64},{1,97},{33,1},{65,33},{97,65},{2,98}... | collective-permute-start | bytes 393224 | tf_op jit(solution)/shard_map/ppermute | solution.py:331
  98.5 29.0 %all-to-all-start.3 = ((f32[4,128,640]{2,1,0:T(8,128)}), f32[4,128,640]{2,1,0:T(8,128)S(1)}, u32[]{:S(2)}, u32[]{:S(2)}) async-start(f32[4,128,640]{2,1,0:T(8,128)} %get-tuple-element.84.refs_4_), calls=%async_computation.3 | async-start | bytes 2621440 | tf_op jit(solution)/shard_map/all_to_all | solution.py:327
  104.1 1.9 %collective-permute-start.12 = (f32[512,256]{1,0:T(8,128)S(1)}, f32[512,256]{1,0:T(8,128)S(1)}, u32[]{:S(2)}, u32[]{:S(2)}) collective-permute-start(f32[512,256]{1,0:T(8,128)S(1)} %copy-done.6), channel_id=1, source_target_pairs={{0,8},{8,0},{1,9},{9,1},{2,10},{10,2},{3,11},{11,3},{4,12},{12,4},... | collective-permute-start | bytes 1572872 | tf_op jit(solution)/shard_map/ppermute | solution.py:339
  109.6 10.5 %collective-permute-start.13 = (f32[4,72,256]{2,1,0:T(8,128)}, f32[4,72,256]{2,1,0:T(8,128)S(1)}, u32[]{:S(2)}, u32[]{:S(2)}) collective-permute-start(f32[4,72,256]{2,1,0:T(8,128)} %get-tuple-element.87), channel_id=1, source_target_pairs={{0,2},{2,4},{4,6},{6,0},{1,3},{3,5},{5,7},{7,1},{8,10},{10,12},{12... | collective-permute-start | bytes 884744 | tf_op jit(solution)/shard_map/ppermute | solution.py:331
  111.3 16.2 %collective-permute-start.14 = (f32[4,72,256]{2,1,0:T(8,128)}, f32[4,72,256]{2,1,0:T(8,128)S(1)}, u32[]{:S(2)}, u32[]{:S(2)}) collective-permute-start(f32[4,72,256]{2,1,0:T(8,128)} %get-tuple-element.88), channel_id=1, source_target_pairs={{0,4},{2,6},{4,0},{6,2},{1,5},{3,7},{5,1},{7,3},{8,12},{10,14},{12... | collective-permute-start | bytes 884744 | tf_op jit(solution)/shard_map/ppermute | solution.py:331
  114.0 13.6 %collective-permute-start.15 = (f32[4,72,256]{2,1,0:T(8,128)}, f32[4,72,256]{2,1,0:T(8,128)S(1)}, u32[]{:S(2)}, u32[]{:S(2)}) collective-permute-start(f32[4,72,256]{2,1,0:T(8,128)} %get-tuple-element.89), channel_id=1, source_target_pairs={{0,6},{2,0},{4,2},{6,4},{1,7},{3,1},{5,3},{7,5},{8,14},{10,8},{12,... | collective-permute-start | bytes 884744 | tf_op jit(solution)/shard_map/ppermute | solution.py:331
  127.5 3.0 %collective-permute-start.16 = (f32[4,128,640]{2,1,0:T(8,128)S(1)}, f32[4,128,640]{2,1,0:T(8,128)S(1)}, u32[]{:S(2)}, u32[]{:S(2)}) collective-permute-start(f32[4,128,640]{2,1,0:T(8,128)S(1)} %all-to-all-done.3.refs_2_), channel_id=1, source_target_pairs={{0,8},{8,0},{1,9},{9,1},{2,10},{10,2},{3,11},{11,3},{4,12},{12,4},... | collective-permute-start | bytes 3932168 | tf_op jit(solution)/shard_map/ppermute | solution.py:339
  135.8 48.6 %all-to-all-start.4 = ((f32[16,72,640]{2,1,0:T(8,128)}), f32[16,72,640]{2,1,0:T(8,128)S(1)}, u32[]{:S(2)}, u32[]{:S(2)}) async-start(f32[16,72,640]{2,1,0:T(8,128)} %key_value_product.1), calls=%async_computation.4 | async-start | bytes 5898240 | tf_op jit(solution)/shard_map/all_to_all | solution.py:327
  142.5 14.5 %slice-start = ((s8[5160960]{0:T(1024)(128)(4,1)}), s8[4194304]{0:T(1024)(128)(4,1)S(1)}, s32[]{:S(2)}) async-start(s8[5160960]{0:T(1024)(128)(4,1)} %bitcast.15), calls=%async_computation.5 | async-start | bytes 8388608
  146.7 8.8 %copy-start.10 = (f32[72,256]{1,0:T(8,128)S(1)}, f32[72,256]{1,0:T(8,128)}, u32[]{:S(2)}) copy-start(f32[72,256]{1,0:T(8,128)} %get-tuple-element.98) | copy-start | bytes 221188
  146.7 10.3 %slice-start.1 = ((s8[5160960]{0:T(1024)(128)(4,1)}), s8[966656]{0:T(1024)(128)(4,1)S(1)}, s32[]{:S(2)}) async-start(s8[5160960]{0:T(1024)(128)(4,1)} %bitcast.15), calls=%async_computation.6 | async-start | bytes 1933312
  146.8 10.3 %copy-start.8 = (bf16[128,1120]{1,0:T(8,128)(2,1)S(1)}, bf16[128,1120]{1,0:T(8,128)(2,1)}, u32[]{:S(2)}) copy-start(bf16[128,1120]{1,0:T(8,128)(2,1)} %get-tuple-element.82) | copy-start | bytes 860164
  150.9 29.0 %collective-permute-start.17 = (f32[72,256]{1,0:T(8,128)S(1)}, f32[72,256]{1,0:T(8,128)S(1)}, u32[]{:S(2)}, u32[]{:S(2)}) collective-permute-start(f32[72,256]{1,0:T(8,128)S(1)} %copy-done.12), channel_id=1, source_target_pairs={{0,1},{1,16},{16,17},{17,0},{2,3},{3,18},{18,19},{19,2},{4,5},{5,2... | collective-permute-start | bytes 221192 | tf_op jit(solution)/shard_map/ppermute | solution.py:331
  152.9 27.0 %collective-permute-start.18 = (f32[72,256]{1,0:T(8,128)S(1)}, f32[72,256]{1,0:T(8,128)S(1)}, u32[]{:S(2)}, u32[]{:S(2)}) collective-permute-start(f32[72,256]{1,0:T(8,128)S(1)} %copy-done.11), channel_id=1, source_target_pairs={{0,16},{1,17},{16,0},{17,1},{2,18},{3,19},{18,2},{19,3},{4,20},{5,... | collective-permute-start | bytes 221192 | tf_op jit(solution)/shard_map/ppermute | solution.py:331
  155.6 24.3 %collective-permute-start.19 = (f32[72,256]{1,0:T(8,128)S(1)}, f32[72,256]{1,0:T(8,128)S(1)}, u32[]{:S(2)}, u32[]{:S(2)}) collective-permute-start(f32[72,256]{1,0:T(8,128)S(1)} %copy-done.10), channel_id=1, source_target_pairs={{0,17},{1,0},{16,1},{17,16},{2,19},{3,2},{18,3},{19,18},{4,21},{5,... | collective-permute-start | bytes 221192 | tf_op jit(solution)/shard_map/ppermute | solution.py:331
  (8 other events, 34.7 us)

commit v10 on v7

--- a/solution.py
+++ b/solution.py
@@ -17,6 +17,7 @@
 CORES = 2
 ROWS = D // TILES
 PADDED_ROWS = 72
+SPLIT = 40
 HALF = D // 4
 REPLICAS = 4
 RING = 4
@@ -30,7 +31,7 @@
 EPSILON = 1e-15
 IMAGE = ("zh", "core", "x", "zl")
 PLANE = ("zh", "x", "zl")
-CHUNKS = [(start, min(384, D - start)) for start in range(0, D, 384)]
+CHUNKS = [(0, 1152), (1152, D - 1152)]
 
 F32 = jnp.float32
 BF16 = jnp.bfloat16
@@ -44,14 +45,14 @@
     return pltpu.HBM(shape, dtype)
 
 
-def call(kernel, name, outs, in_specs, scratch=(), vmem=12, arrived=()):
+def call(kernel, name, outs, in_specs, scratch=(), vmem=12, arrived=(), steps=1, out_specs=None):
     run = pl.pallas_call(
         kernel,
         name=name,
-        grid=(1,),
+        grid=(steps,),
         out_shape=outs,
         in_specs=in_specs,
-        out_specs=[BLOCK] * len(outs),
+        out_specs=out_specs or [BLOCK] * len(outs),
         scratch_shapes=list(scratch),
         compiler_params=pltpu.CompilerParams(vmem_limit_bytes=vmem * 1024 * 1024),
     )
@@ -280,29 +281,37 @@
         values = dot(rows[half * HALF : (half + 1) * HALF, :], columns[...], 1, 0) * normalizer
         for index in range(span):
             product[half * span + index, :ROWS, :] = values[index * ROWS : (index + 1) * ROWS]
-    for slot, out in enumerate(outs):
+    for slot in range(RING):
         at = lax.rem(across[0] + slot, RING)
         for block in range(RING):
-            out[block] = product[(block // 2) * span + at * 2 + block % 2]
+            values = product[(block // 2) * span + at * 2 + block % 2]
+            if slot == 2:
+                outs[2][block] = values[:SPLIT]
+                outs[4][block] = values[SPLIT:]
+            else:
+                outs[slot][block] = values
 
 
 def key_value_product_kernel(normalizer, place, rows, own, other, out, columns):
-    for core, blocks in enumerate((own, other)):
-        for slot in range(REPLICAS):
-            at = (core * REPLICAS + slot) * TOKENS
-            source = lax.rem(place[0] + REPLICAS - slot, REPLICAS)
-            columns[at : at + TOKENS, :] = blocks[source].astype(BF16)
-    span = PLANE_SIZE // CORES
-    for half in range(CORES):
-        values = dot(rows[half * HALF : (half + 1) * HALF, :], columns[...], 1, 0) * normalizer
-        for index in range(span):
-            out[half * span + index, :ROWS, :] = values[index * ROWS : (index + 1) * ROWS]
-
-
-def second_stage_kernel(along, own, first, second, third, *outs):
+    @pl.when(pl.program_id(0) == 0)
+    def _():
+        for core, blocks in enumerate((own, other)):
+            for slot in range(REPLICAS):
+                at = (core * REPLICAS + slot) * TOKENS
+                source = lax.rem(place[0] + REPLICAS - slot, REPLICAS)
+                columns[at : at + TOKENS, :] = blocks[source].astype(BF16)
+
+    values = dot(rows[...], columns[...], 1, 0) * normalizer
+    for index in range(PLANE_SIZE // CORES):
+        out[index, :ROWS, :] = values[index * ROWS : (index + 1) * ROWS]
+
+
+def second_stage_kernel(along, own, first, upper, third, lower, *outs):
     for slot, out in enumerate(outs):
         at = lax.rem(along[0] + slot, RING)
-        out[...] = (own[at] + first[at]) + (second[at] + third[at])
+        total = (own[at] + first[at]) + third[at]
+        out[:SPLIT, :] = total[:SPLIT] + upper[at]
+        out[SPLIT:, :] = total[SPLIT:] + lower[at]
 
 
 def last_kernel(key_value, own, first, second, third, query_out, key_out, value_out):
@@ -448,7 +457,11 @@
     slots = call(
         lambda *refs: query_product_kernel(normalizer, *refs[:4], *refs[5:]),
         "query_product",
-        [shaped((RING, PADDED_ROWS, EARLY))] * RING,
+        [
+            shaped((RING, SPLIT if slot == 2 else PADDED_ROWS, EARLY))
+            for slot in range(RING)
+        ]
+        + [shaped((RING, PADDED_ROWS - SPLIT, EARLY))],
         [IN_SMEM, BLOCK, BLOCK, BLOCK, ANYWHERE],
         [
             pltpu.VMEM((2 * REPLICAS * TOKENS, EARLY), BF16),
@@ -457,23 +470,35 @@
         vmem=24,
         arrived=(3,),
     )(across, rows, query_columns, swap_cores(query_columns), sent)
-    slots = shifted(slots, "x")
+    upper, lower = slots[2], slots[4]
+    lower = shift(shift(lower, 3, "x"), 3, "x")
+    slots = [slots[0], shift(slots[1], 1, "x"), shift(upper, 2, "x"), shift(slots[3], 3, "x"), lower]
     own_columns, slots = lax.optimization_barrier((own_columns, slots))
     slots = call(
         second_stage_kernel,
         "second_stage",
         [shaped((PADDED_ROWS, EARLY))] * RING,
-        [IN_SMEM] + [BLOCK] * RING,
-        arrived=(2, 3, 4),
+        [IN_SMEM] + [BLOCK] * (RING + 1),
+        arrived=(2, 3, 4, 5),
     )(along, *slots)
     (product,) = call(
         lambda *refs: key_value_product_kernel(normalizer, *refs[:4], *refs[5:]),
         "key_value_product",
         [shaped((PLANE_SIZE, PADDED_ROWS, LANES))],
-        [IN_SMEM, BLOCK, BLOCK, BLOCK, ANYWHERE],
+        [
+            IN_SMEM,
+            pl.BlockSpec((HALF, 2 * REPLICAS * TOKENS), lambda half: (half, 0)),
+            BLOCK,
+            BLOCK,
+            ANYWHERE,
+        ],
         [pltpu.VMEM((2 * REPLICAS * TOKENS, LANES), BF16)],
         vmem=24,
         arrived=(2, 3),
+        steps=CORES,
+        out_specs=[
+            pl.BlockSpec((PLANE_SIZE // CORES, PADDED_ROWS, LANES), lambda half: (half, 0, 0))
+        ],
     )(place, rows, own_columns, swap_cores(own_columns), slots[0])
     key_value_out = exchange(product, PLANE)
     slots = shifted(slots, ("zh", "zl"))

time: 185 us -> 189 us (1.022)
  starting transfers between devices: 55.9 us -> 61.4 us
    ppermute x15 -> x17, starting transfers between devices: 23.4 us -> 27.4 us  [shift(): lax.ppermute(values, axis, [(i, (i + by) % RING) for i in range(RING)])]
    ppermute x15 -> x17, waiting for transfers between devices: 39.9 us -> 39.1 us  [shift(): lax.ppermute(values, axis, [(i, (i + by) % RING) for i in range(RING)])]
  transfers between devices with their start and end apart: 23 -> 25, of which waited for: 12 -> 12; matrix products, arithmetic and copies ran while one was open for 7% -> 7% of each run, Pallas kernels for 13% -> 12%
where the time goes in v10:
time: 189 us; the launch traced here: 188 us
  waiting for transfers between devices  69.5 us (37%)
  starting transfers between devices  61.4 us (32%)
  Pallas kernels  42.1 us (22%)
  matrix products  10.7 us (6%)
  local copies, waits for them, and re-layouts  3.16 us (2%)
    pallas_call x13, Pallas kernels, with_placed(): return run(*placed)  42.1 us
    ppermute x17, waiting for transfers between devices, shift(): lax.ppermute(values, axis, [(i, (i + by) % RING) for i in range(RING)])  39.1 us
    all_to_all x5, starting transfers between devices, exchange(): return lax.all_to_all(blocks, axes, 0, 0, tiled=True)  34 us
    ppermute x17, starting transfers between devices, shift(): lax.ppermute(values, axis, [(i, (i + by) % RING) for i in range(RING)])  27.4 us
    all_to_all x5, waiting for transfers between devices, exchange(): return lax.all_to_all(blocks, axes, 0, 0, tiled=True)  27.2 us
    dot_general x3, matrix products, dot(): lax.dot_general(left, right, (((left_dim,), (right_dim,)), ((), ())), pre...  10.7 us
  transfers between devices with their start and end apart: 25, of which 12 were waited for; matrix products, arithmetic and copies ran while one was open for 7% of the time, Pallas kernels for 12%

profile of v10, /device:TPU:8, one launch (start us, length us, event | category | flops | bytes accessed | tf_op | source)
XLA Modules:
  0.0 187.7 jit_solution(15625097500083356403)
XLA Ops:
  0.6 7.7 %key_value.1 = (bf16[10,128,112]{2,1,0:T(8,128)(2,1)}, bf16[10,128,112]{2,1,0:T(8,128)(2,1)}, f32[32,45,112]{2,1,0:T(8,128)}) custom-call(bf16[128,2240]{1,0:T(8,128)(2,1)} %bitcast.17, bf16[2240,1120]{1,0:T(8,128)(2,1)} %key_weight.1, bf16[2240,1120]{1,0:T(8,128)(2,1)} %value_weight.1), custom_call_target="tpu_custom_call" | custom-call | tf_op jit(solution)/shard_map/key_value/pallas_call | solution.py:67
  8.4 2.3 %turn.1 = (f32[1120,128]{1,0:T(8,128)}, f32[1120,128]{1,0:T(8,128)}) custom-call(s32[1]{0:T(128)} %bitcast.3.core, bf16[128,2240]{1,0:T(8,128)(2,1)} %bitcast.18), custom_call_target="tpu_custom_call" | custom-call | tf_op jit(solution)/shard_map/turn/pallas_call | solution.py:67
  10.7 8.3 %all-to-all-start = ((f32[32,45,112]{2,1,0:T(8,128)}), f32[32,45,112]{2,1,0:T(8,128)S(1)}, u32[]{:S(2)}, u32[]{:S(2)}) async-start(f32[32,45,112]{2,1,0:T(8,128)} %get-tuple-element.57), calls=%async_computation | async-start | bytes 1572864 | tf_op jit(solution)/shard_map/all_to_all | solution.py:329
  21.1 4.4 %query.1.refs_1_ = bf16[10,128,112]{2,1,0:T(8,128)(2,1)} custom-call(bf16[128,2240]{1,0:T(8,128)(2,1)} %bitcast.19, bf16[2240,1120]{1,0:T(8,128)(2,1)} %weight.1), custom_call_target="tpu_custom_call" | custom-call | tf_op jit(solution)/shard_map/query/pallas_call | solution.py:67
  25.5 8.0 %all-to-all-done.refs_0_ = f32[32,45,112]{2,1,0:T(8,128)S(1)} async-done(((f32[32,45,112]{2,1,0:T(8,128)}), f32[32,45,112]{2,1,0:T(8,128)S(1)}, u32[]{:S(2)}, u32[]{:S(2)}) %all-to-all-start) | async-done | bytes 645152 | tf_op jit(solution)/shard_map/all_to_all | solution.py:329
  34.5 2.4 %numerator.1 = (f32[32,70,112]{2,1,0:T(8,128)}, bf16[10,128,112]{2,1,0:T(8,128)(2,1)}, f32[10,112]{1,0:T(8,128)}) custom-call(f32[32,45,112]{2,1,0:T(8,128)S(1)} %all-to-all-done.refs_0_, bf16[10,128,112]{2,1,0:T(8,128)(2,1)S(1)} %copy-done, bf16[128,1120]{1,0:T(8,128)(2,1)S(1)} %bitcast.13), custom_call_target="tpu_custom_call" | custom-call | tf_op jit(solution)/shard_map/numerator/pallas_call | solution.py:67
  36.9 6.0 %all-to-all-start.1 = ((f32[32,70,112]{2,1,0:T(8,128)}), f32[32,70,112]{2,1,0:T(8,128)S(1)}, u32[]{:S(2)}, u32[]{:S(2)}) async-start(f32[32,70,112]{2,1,0:T(8,128)} %get-tuple-element.62), calls=%async_computation.1 | async-start | bytes 2359296 | tf_op jit(solution)/shard_map/all_to_all | solution.py:329
  47.0 14.7 %all-to-all-done.1.refs_0_.got = f32[32,70,112]{2,1,0:T(8,128)S(1)} async-done(((f32[32,70,112]{2,1,0:T(8,128)}), f32[32,70,112]{2,1,0:T(8,128)S(1)}, u32[]{:S(2)}, u32[]{:S(2)}) %all-to-all-start.1) | async-done | bytes 1003552 | tf_op jit(solution)/shard_map/all_to_all | solution.py:329
  61.7 2.6 %total_grad.1 = (f32[32,45,112]{2,1,0:T(8,128)}, f32[128,10]{1,0:T(8,128)}) custom-call(f32[32,70,112]{2,1,0:T(8,128)S(1)} %all-to-all-done.1.refs_0_.got, bf16[10,128,112]{2,1,0:T(8,128)(2,1)S(1)} %copy-done.1, bf16[128,1120]{1,0:T(8,128)(2,1)S(1)} %bitcast.14, f32[10,112]{1,0:T(8,128)S(1)} %copy-done.6), custom_call_target="tpu_custom_call" | custom-call | tf_op jit(solution)/shard_map/total_grad/pallas_call | solution.py:67
  64.3 6.3 %collective-permute-done.5.refs_5_ = f32[1120,128]{1,0:T(8,128)} collective-permute-done((f32[1120,128]{1,0:T(8,128)S(1)}, f32[1120,128]{1,0:T(8,128)}, u32[]{:S(2)}, u32[]{:S(2)}) %collective-permute-start.5) | collective-permute-done | bytes 573472 | tf_op jit(solution)/shard_map/ppermute | solution.py:333
  71.8 7.3 %all-to-all-start.2 = ((f32[32,45,112]{2,1,0:T(8,128)}), f32[32,45,112]{2,1,0:T(8,128)S(1)}, u32[]{:S(2)}, u32[]{:S(2)}) async-start(f32[32,45,112]{2,1,0:T(8,128)} %get-tuple-element.72), calls=%async_computation.2 | async-start | bytes 1572864 | tf_op jit(solution)/shard_map/all_to_all | solution.py:329
  79.0 2.9 %query_grad.1 = (bf16[128,1120]{1,0:T(8,128)(2,1)}, f32[128,256]{1,0:T(8,128)}, f32[128,256]{1,0:T(8,128)}, f32[128,256]{1,0:T(8,128)}, f32[128,256]{1,0:T(8,128)}, /*index=5*/f32[4,128,24]{2,1,0:T(8,128)}) custom-call(s32[1]{0:T(128)} %bitcast.place.refs_0_, f32[32,70,112]{2,1,0:T(8,128)S(1)} %all-to-all-done.1.refs_0_.got, ...), custom_call_target="tpu_custom_call" | custom-call | tf_op jit(solution)/shard_map/query_grad/pallas_call | solution.py:67
  84.8 2.4 %collective-permute-start.9 = (f32[128,256]{1,0:T(8,128)}, f32[128,256]{1,0:T(8,128)S(1)}, u32[]{:S(2)}, u32[]{:S(2)}) collective-permute-start(f32[128,256]{1,0:T(8,128)} %get-tuple-element.80), channel_id=1, source_target_pairs={{0,96},{32,0},{64,32},{96,64},{1,97},{33,1},{65,33},{97,65},{2,98}... | collective-permute-start | bytes 393224 | tf_op jit(solution)/shard_map/ppermute | solution.py:333
  87.2 3.9 %join.1.refs_1_ = bf16[1120,1024]{1,0:T(8,128)(2,1)} custom-call(f32[1120,128]{1,0:T(8,128)} %get-tuple-element.71.refs_0_, f32[1120,128]{1,0:T(8,128)S(1)} %collective-permute-done.refs_1_, f32[1120,128]{1,0:T(8,128)} %collective-permute-done.3.refs_2_, f32[1120,128]{1,0:T(8,128)} %collective-permute-done.6.refs_3_, ...), custom_call_target="tpu_custom_call" | custom-call | tf_op jit(solution)/shard_map/join/pallas_call | solution.py:67
  94.8 2.2 %key_value_grad.1 = (bf16[128,1120]{1,0:T(8,128)(2,1)}, bf16[128,1120]{1,0:T(8,128)(2,1)}, f32[4,128,640]{2,1,0:T(8,128)}) custom-call(f32[32,45,112]{2,1,0:T(8,128)S(1)} %all-to-all-done.2.got, bf16[10,128,112]{2,1,0:T(8,128)(2,1)S(1)} %copy-done.3, bf16[10,128,112]{2,1,0:T(8,128)(2,1)S(1)} %copy-done.4, f32[4,128,24]{2,1,0:T(8,128)S(1)} %copy-done.5), custom_call_target="tpu_custom_call" | custom-call | tf_op jit(solution)/shard_map/key_value_grad/pallas_call | solution.py:67
  97.1 4.4 %all-to-all-start.3 = ((f32[4,128,640]{2,1,0:T(8,128)}), f32[4,128,640]{2,1,0:T(8,128)S(1)}, u32[]{:S(2)}, u32[]{:S(2)}) async-start(f32[4,128,640]{2,1,0:T(8,128)} %get-tuple-element.88.refs_4_), calls=%async_computation.3 | async-start | bytes 2621440 | tf_op jit(solution)/shard_map/all_to_all | solution.py:329
  101.4 1.9 %collective-permute-done.10.refs_3_ = f32[512,256]{1,0:T(8,128)S(1)} collective-permute-done((f32[512,256]{1,0:T(8,128)S(1)}, f32[512,256]{1,0:T(8,128)S(1)}, u32[]{:S(2)}, u32[]{:S(2)}) %collective-permute-start.10) | collective-permute-done | bytes 524320 | tf_op jit(solution)/shard_map/ppermute | solution.py:341
  103.3 3.7 %query_product.1 = (f32[4,72,256]{2,1,0:T(8,128)}, f32[4,72,256]{2,1,0:T(8,128)}, f32[4,40,256]{2,1,0:T(8,128)}, f32[4,72,256]{2,1,0:T(8,128)}, f32[4,32,256]{2,1,0:T(8,128)}) custom-call(s32[1]{0:T(128)} %bitcast.5.refs_0_, bf16[1120,1024]{1,0:T(8,128)(2,1)} %join.1.refs_1_, f32[512,256]{1,0:T(8,128)} %pack_query.1.refs_2_, ...), custom_call_target="tpu_custom_call" | custom-call | tf_op jit(solution)/shard_map/query_product/pallas_call | solution.py:67
  112.8 8.8 %collective-permute-done.14 = f32[4,32,256]{2,1,0:T(8,128)S(1)} collective-permute-done((f32[4,32,256]{2,1,0:T(8,128)}, f32[4,32,256]{2,1,0:T(8,128)S(1)}, u32[]{:S(2)}, u32[]{:S(2)}) %collective-permute-start.14) | collective-permute-done | bytes 131104 | tf_op jit(solution)/shard_map/ppermute | solution.py:333
  121.6 4.0 %collective-permute-start.15 = (f32[4,32,256]{2,1,0:T(8,128)S(1)}, f32[4,32,256]{2,1,0:T(8,128)S(1)}, u32[]{:S(2)}, u32[]{:S(2)}) collective-permute-start(f32[4,32,256]{2,1,0:T(8,128)S(1)} %collective-permute-done.14), channel_id=1, source_target_pairs={{0,6},{2,0},{4,2},{6,4},{1,7},{3,1},{5,3},{7,5},{8,14},{10,8},{12,... | collective-permute-start | bytes 393224 | tf_op jit(solution)/shard_map/ppermute | solution.py:333
  125.7 2.5 %collective-permute-done.15.lower = f32[4,32,256]{2,1,0:T(8,128)S(1)} collective-permute-done((f32[4,32,256]{2,1,0:T(8,128)S(1)}, f32[4,32,256]{2,1,0:T(8,128)S(1)}, u32[]{:S(2)}, u32[]{:S(2)}) %collective-permute-start.15) | collective-permute-done | bytes 131104 | tf_op jit(solution)/shard_map/ppermute | solution.py:333
  131.3 4.7 %key_value_product.1 = f32[16,72,640]{2,1,0:T(8,128)} custom-call(s32[1]{0:T(128)} %bitcast.place.refs_0_, bf16[1120,1024]{1,0:T(8,128)(2,1)} %join.1.refs_1_, f32[4,128,640]{2,1,0:T(8,128)S(1)} %all-to-all-done.3.refs_2_, f32[4,128,640]{2,1,0:T(8,128)S(1)} %collective-permute-done.16.refs_3_, f32[72,256]{1,0:T(8,128)} %get-tuple-element.101.refs_4_.own), custom_call_target="tpu_custom_call" | custom-call | tf_op jit(solution)/shard_map/key_value_product/pallas_call | solution.py:67
  136.0 8.1 %all-to-all-start.4 = ((f32[16,72,640]{2,1,0:T(8,128)}), f32[16,72,640]{2,1,0:T(8,128)S(1)}, u32[]{:S(2)}, u32[]{:S(2)}) async-start(f32[16,72,640]{2,1,0:T(8,128)} %key_value_product.1), calls=%async_computation.4 | async-start | bytes 5898240 | tf_op jit(solution)/shard_map/all_to_all | solution.py:329
  144.1 4.2 %fusion.1 = f32[128,2240]{0,1:T(8,128)S(1)} fusion(bf16[128,1120]{1,0:T(8,128)(2,1)S(1)} %copy-done.8, bf16[2240,1120]{1,0:T(8,128)(2,1)} %weight.1), kind=kOutput, calls=%fused_computation.3 | convolution fusion | flops 642252800 | bytes 6451200 | tf_op jit(solution)/shard_map/dot_general | solution.py:73
  148.3 4.1 %convolution_add_fusion.1 = f32[128,2240]{0,1:T(8,128)S(1)} fusion(f32[128,2240]{0,1:T(8,128)S(1)} %fusion.1, bf16[128,1120]{1,0:T(8,128)(2,1)S(1)} %copy-done.10, bf16[2240,1120]{1,0:T(8,128)(2,1)} %key_weight.1), kind=kOutput, calls=%fused_computation.1 | convolution fusion | flops 642539520 | bytes 7598080 | tf_op jit(solution)/shard_map/dot_general | solution.py:73
  152.4 2.0 %collective-permute-start.17 = (f32[72,256]{1,0:T(8,128)S(1)}, f32[72,256]{1,0:T(8,128)S(1)}, u32[]{:S(2)}, u32[]{:S(2)}) collective-permute-start(f32[72,256]{1,0:T(8,128)S(1)} %copy-done.13), channel_id=1, source_target_pairs={{0,1},{1,16},{16,17},{17,0},{2,3},{3,18},{18,19},{19,2},{4,5},{5,2... | collective-permute-start | bytes 221192 | tf_op jit(solution)/shard_map/ppermute | solution.py:333
  154.4 2.7 %collective-permute-start.18 = (f32[72,256]{1,0:T(8,128)S(1)}, f32[72,256]{1,0:T(8,128)S(1)}, u32[]{:S(2)}, u32[]{:S(2)}) collective-permute-start(f32[72,256]{1,0:T(8,128)S(1)} %copy-done.12), channel_id=1, source_target_pairs={{0,16},{1,17},{16,0},{17,1},{2,18},{3,19},{18,2},{19,3},{4,20},{5,... | collective-permute-start | bytes 221192 | tf_op jit(solution)/shard_map/ppermute | solution.py:333
  158.6 2.4 %fusion = bf16[128,2240]{0,1:T(8,128)(2,1)} fusion(f32[128,2240]{0,1:T(8,128)S(1)} %convolution_add_fusion.1, bf16[128,1120]{1,0:T(8,128)(2,1)S(1)} %copy-done.9, bf16[2240,1120]{1,0:T(8,128)(2,1)S(1)} %bitcast.16), kind=kOutput, calls=%fused_computation.2 | convolution fusion | flops 642826240 | bytes 7024640 | tf_op jit(solution)/shard_map/dot_general | solution.py:73
  161.0 2.1 %copy.10 = bf16[128,2240]{1,0:T(8,128)(2,1)} copy(bf16[128,2240]{0,1:T(8,128)(2,1)} %fusion) | data formatting | bytes 1146880 | tf_op jit(solution)/shard_map/convert_element_type | solution.py:512
  163.1 18.4 %collective-permute-done.17.first = f32[72,256]{1,0:T(8,128)S(1)} collective-permute-done((f32[72,256]{1,0:T(8,128)S(1)}, f32[72,256]{1,0:T(8,128)S(1)}, u32[]{:S(2)}, u32[]{:S(2)}) %collective-permute-start.17) | collective-permute-done | bytes 73760 | tf_op jit(solution)/shard_map/ppermute | solution.py:333
  181.4 4.5 %all-to-all-done.4.key_value = f32[16,72,640]{2,1,0:T(8,128)S(1)} async-done(((f32[16,72,640]{2,1,0:T(8,128)}), f32[16,72,640]{2,1,0:T(8,128)S(1)}, u32[]{:S(2)}, u32[]{:S(2)}) %all-to-all-start.4) | async-done | bytes 2949152 | tf_op jit(solution)/shard_map/all_to_all | solution.py:329
  186.0 1.7 last.1
  (68 shorter events, 25.3 us)
Async XLA Ops:
  10.7 9.9 %collective-permute-start.1 = (f32[1120,128]{1,0:T(8,128)}, f32[1120,128]{1,0:T(8,128)S(1)}, u32[]{:S(2)}, u32[]{:S(2)}) collective-permute-start(f32[1120,128]{1,0:T(8,128)} %get-tuple-element.61), channel_id=1, source_target_pairs={{0,8},{8,0},{1,9},{9,1},{2,10},{10,2},{3,11},{11,3},{4,12},{12,4},... | collective-permute-start | bytes 1720328 | tf_op jit(solution)/shard_map/ppermute | solution.py:341
  10.7 22.8 %all-to-all-start = ((f32[32,45,112]{2,1,0:T(8,128)}), f32[32,45,112]{2,1,0:T(8,128)S(1)}, u32[]{:S(2)}, u32[]{:S(2)}) async-start(f32[32,45,112]{2,1,0:T(8,128)} %get-tuple-element.57), calls=%async_computation | async-start | bytes 1572864 | tf_op jit(solution)/shard_map/all_to_all | solution.py:329
  19.0 14.5 %copy-start.2 = (bf16[1,16,8,1120]{3,2,1,0:T(8,128)(2,1)S(1)}, bf16[1,16,8,1120]{3,2,1,0:T(8,128)(2,1)}, u32[]{:S(2)}) copy-start(bf16[1,16,8,1120]{3,2,1,0:T(8,128)(2,1)} %param.9) | copy-start | bytes 860164
  19.0 17.9 %collective-permute-start = (f32[1120,128]{1,0:T(8,128)}, f32[1120,128]{1,0:T(8,128)S(1)}, u32[]{:S(2)}, u32[]{:S(2)}) collective-permute-start(f32[1120,128]{1,0:T(8,128)} %get-tuple-element.71.refs_0_), channel_id=1, source_target_pairs={{0,32},{32,64},{64,96},{96,0},{1,33},{33,65},{65,97},{97,1},{2,34}... | collective-permute-start | bytes 1720328 | tf_op jit(solution)/shard_map/ppermute | solution.py:333
  20.6 16.3 %collective-permute-start.2 = (f32[1120,128]{1,0:T(8,128)S(1)}, f32[1120,128]{1,0:T(8,128)}, u32[]{:S(2)}, u32[]{:S(2)}) collective-permute-start(f32[1120,128]{1,0:T(8,128)S(1)} %collective-permute-done.1.refs_4_), channel_id=1, source_target_pairs={{0,96},{32,0},{64,32},{96,64},{1,97},{33,1},{65,33},{97,65},{2,98}... | collective-permute-start | bytes 1720328 | tf_op jit(solution)/shard_map/ppermute | solution.py:333
  34.5 27.2 %copy-start.1 = (bf16[10,128,112]{2,1,0:T(8,128)(2,1)S(1)}, bf16[10,128,112]{2,1,0:T(8,128)(2,1)}, u32[]{:S(2)}) copy-start(bf16[10,128,112]{2,1,0:T(8,128)(2,1)} %query.1.refs_1_) | copy-start | bytes 860164
  36.9 24.8 %copy-start.6 = (f32[10,112]{1,0:T(8,128)S(1)}, f32[10,112]{1,0:T(8,128)}, u32[]{:S(2)}) copy-start(f32[10,112]{1,0:T(8,128)} %get-tuple-element.64.refs_3_.total) | copy-start | bytes 13444
  36.9 24.8 %all-to-all-start.1 = ((f32[32,70,112]{2,1,0:T(8,128)}), f32[32,70,112]{2,1,0:T(8,128)S(1)}, u32[]{:S(2)}, u32[]{:S(2)}) async-start(f32[32,70,112]{2,1,0:T(8,128)} %get-tuple-element.62), calls=%async_computation.1 | async-start | bytes 2359296 | tf_op jit(solution)/shard_map/all_to_all | solution.py:329
  42.9 21.3 %collective-permute-start.3 = (f32[1120,128]{1,0:T(8,128)S(1)}, f32[1120,128]{1,0:T(8,128)}, u32[]{:S(2)}, u32[]{:S(2)}) collective-permute-start(f32[1120,128]{1,0:T(8,128)S(1)} %collective-permute-done.refs_1_), channel_id=1, source_target_pairs={{0,32},{32,64},{64,96},{96,0},{1,33},{33,65},{65,97},{97,1},{2,34}... | collective-permute-start | bytes 1720328 | tf_op jit(solution)/shard_map/ppermute | solution.py:333
  44.3 20.0 %collective-permute-start.4 = (f32[1120,128]{1,0:T(8,128)}, f32[1120,128]{1,0:T(8,128)}, u32[]{:S(2)}, u32[]{:S(2)}) collective-permute-start(f32[1120,128]{1,0:T(8,128)} %collective-permute-done.2.refs_7_), channel_id=1, source_target_pairs={{0,96},{32,0},{64,32},{96,64},{1,97},{33,1},{65,33},{97,65},{2,98}... | collective-permute-start | bytes 1720328 | tf_op jit(solution)/shard_map/ppermute | solution.py:333
  45.0 25.5 %collective-permute-start.5 = (f32[1120,128]{1,0:T(8,128)S(1)}, f32[1120,128]{1,0:T(8,128)}, u32[]{:S(2)}, u32[]{:S(2)}) collective-permute-start(f32[1120,128]{1,0:T(8,128)S(1)} %collective-permute-done.1.refs_4_), channel_id=1, source_target_pairs={{0,32},{32,64},{64,96},{96,0},{1,33},{33,65},{65,97},{97,1},{2,34}... | collective-permute-start | bytes 1720328 | tf_op jit(solution)/shard_map/ppermute | solution.py:333
  46.3 25.5 %collective-permute-start.6 = (f32[1120,128]{1,0:T(8,128)}, f32[1120,128]{1,0:T(8,128)}, u32[]{:S(2)}, u32[]{:S(2)}) collective-permute-start(f32[1120,128]{1,0:T(8,128)} %get-tuple-element.71.refs_0_), channel_id=1, source_target_pairs={{0,96},{32,0},{64,32},{96,64},{1,97},{33,1},{65,33},{97,65},{2,98}... | collective-permute-start | bytes 1720328 | tf_op jit(solution)/shard_map/ppermute | solution.py:333
  71.8 23.0 %all-to-all-start.2 = ((f32[32,45,112]{2,1,0:T(8,128)}), f32[32,45,112]{2,1,0:T(8,128)S(1)}, u32[]{:S(2)}, u32[]{:S(2)}) async-start(f32[32,45,112]{2,1,0:T(8,128)} %get-tuple-element.72), calls=%async_computation.2 | async-start | bytes 1572864 | tf_op jit(solution)/shard_map/all_to_all | solution.py:329
  82.0 9.2 %collective-permute-start.7 = (f32[128,256]{1,0:T(8,128)}, f32[128,256]{1,0:T(8,128)S(1)}, u32[]{:S(2)}, u32[]{:S(2)}) collective-permute-start(f32[128,256]{1,0:T(8,128)} %get-tuple-element.78), channel_id=1, source_target_pairs={{0,32},{32,64},{64,96},{96,0},{1,33},{33,65},{65,97},{97,1},{2,34}... | collective-permute-start | bytes 393224 | tf_op jit(solution)/shard_map/ppermute | solution.py:333
  83.6 8.1 %collective-permute-start.8 = (f32[128,256]{1,0:T(8,128)}, f32[128,256]{1,0:T(8,128)S(1)}, u32[]{:S(2)}, u32[]{:S(2)}) collective-permute-start(f32[128,256]{1,0:T(8,128)} %get-tuple-element.79), channel_id=1, source_target_pairs={{0,64},{32,96},{64,0},{96,32},{1,65},{33,97},{65,1},{97,33},{2,66}... | collective-permute-start | bytes 393224 | tf_op jit(solution)/shard_map/ppermute | solution.py:333
  84.8 10.0 %copy-start.5 = (f32[4,128,24]{2,1,0:T(8,128)S(1)}, f32[4,128,24]{2,1,0:T(8,128)}, u32[]{:S(2)}) copy-start(f32[4,128,24]{2,1,0:T(8,128)} %get-tuple-element.84.late) | copy-start | bytes 147460
  84.8 8.3 %collective-permute-start.9 = (f32[128,256]{1,0:T(8,128)}, f32[128,256]{1,0:T(8,128)S(1)}, u32[]{:S(2)}, u32[]{:S(2)}) collective-permute-start(f32[128,256]{1,0:T(8,128)} %get-tuple-element.80), channel_id=1, source_target_pairs={{0,96},{32,0},{64,32},{96,64},{1,97},{33,1},{65,33},{97,65},{2,98}... | collective-permute-start | bytes 393224 | tf_op jit(solution)/shard_map/ppermute | solution.py:333
  97.1 31.1 %all-to-all-start.3 = ((f32[4,128,640]{2,1,0:T(8,128)}), f32[4,128,640]{2,1,0:T(8,128)S(1)}, u32[]{:S(2)}, u32[]{:S(2)}) async-start(f32[4,128,640]{2,1,0:T(8,128)} %get-tuple-element.88.refs_4_), calls=%async_computation.3 | async-start | bytes 2621440 | tf_op jit(solution)/shard_map/all_to_all | solution.py:329
  101.4 1.9 %collective-permute-start.10 = (f32[512,256]{1,0:T(8,128)S(1)}, f32[512,256]{1,0:T(8,128)S(1)}, u32[]{:S(2)}, u32[]{:S(2)}) collective-permute-start(f32[512,256]{1,0:T(8,128)S(1)} %copy-done.7), channel_id=1, source_target_pairs={{0,8},{8,0},{1,9},{9,1},{2,10},{10,2},{3,11},{11,3},{4,12},{12,4},... | collective-permute-start | bytes 1572872 | tf_op jit(solution)/shard_map/ppermute | solution.py:341
  107.0 21.1 %collective-permute-start.11 = (f32[4,72,256]{2,1,0:T(8,128)}, f32[4,72,256]{2,1,0:T(8,128)S(1)}, u32[]{:S(2)}, u32[]{:S(2)}) collective-permute-start(f32[4,72,256]{2,1,0:T(8,128)} %get-tuple-element.91), channel_id=1, source_target_pairs={{0,2},{2,4},{4,6},{6,0},{1,3},{3,5},{5,7},{7,1},{8,10},{10,12},{12... | collective-permute-start | bytes 884744 | tf_op jit(solution)/shard_map/ppermute | solution.py:333
  108.7 19.5 %collective-permute-start.13 = (f32[4,72,256]{2,1,0:T(8,128)}, f32[4,72,256]{2,1,0:T(8,128)S(1)}, u32[]{:S(2)}, u32[]{:S(2)}) collective-permute-start(f32[4,72,256]{2,1,0:T(8,128)} %get-tuple-element.93), channel_id=1, source_target_pairs={{0,6},{2,0},{4,2},{6,4},{1,7},{3,1},{5,3},{7,5},{8,14},{10,8},{12,... | collective-permute-start | bytes 884744 | tf_op jit(solution)/shard_map/ppermute | solution.py:333
  110.3 11.3 %collective-permute-start.14 = (f32[4,32,256]{2,1,0:T(8,128)}, f32[4,32,256]{2,1,0:T(8,128)S(1)}, u32[]{:S(2)}, u32[]{:S(2)}) collective-permute-start(f32[4,32,256]{2,1,0:T(8,128)} %get-tuple-element.94), channel_id=1, source_target_pairs={{0,6},{2,0},{4,2},{6,4},{1,7},{3,1},{5,3},{7,5},{8,14},{10,8},{12,... | collective-permute-start | bytes 393224 | tf_op jit(solution)/shard_map/ppermute | solution.py:333
  111.9 13.7 %collective-permute-start.12 = (f32[4,40,256]{2,1,0:T(8,128)}, f32[4,40,256]{2,1,0:T(8,128)S(1)}, u32[]{:S(2)}, u32[]{:S(2)}) collective-permute-start(f32[4,40,256]{2,1,0:T(8,128)} %get-tuple-element.92), channel_id=1, source_target_pairs={{0,4},{2,6},{4,0},{6,2},{1,5},{3,7},{5,1},{7,3},{8,12},{10,14},{12... | collective-permute-start | bytes 491528 | tf_op jit(solution)/shard_map/ppermute | solution.py:333
  121.6 6.6 %collective-permute-start.15 = (f32[4,32,256]{2,1,0:T(8,128)S(1)}, f32[4,32,256]{2,1,0:T(8,128)S(1)}, u32[]{:S(2)}, u32[]{:S(2)}) collective-permute-start(f32[4,32,256]{2,1,0:T(8,128)S(1)} %collective-permute-done.14), channel_id=1, source_target_pairs={{0,6},{2,0},{4,2},{6,4},{1,7},{3,1},{5,3},{7,5},{8,14},{10,8},{12,... | collective-permute-start | bytes 393224 | tf_op jit(solution)/shard_map/ppermute | solution.py:333
  128.2 3.1 %collective-permute-start.16 = (f32[4,128,640]{2,1,0:T(8,128)S(1)}, f32[4,128,640]{2,1,0:T(8,128)S(1)}, u32[]{:S(2)}, u32[]{:S(2)}) collective-permute-start(f32[4,128,640]{2,1,0:T(8,128)S(1)} %all-to-all-done.3.refs_2_), channel_id=1, source_target_pairs={{0,8},{8,0},{1,9},{9,1},{2,10},{10,2},{3,11},{11,3},{4,12},{12,4},... | collective-permute-start | bytes 3932168 | tf_op jit(solution)/shard_map/ppermute | solution.py:341
  136.0 50.0 %all-to-all-start.4 = ((f32[16,72,640]{2,1,0:T(8,128)}), f32[16,72,640]{2,1,0:T(8,128)S(1)}, u32[]{:S(2)}, u32[]{:S(2)}) async-start(f32[16,72,640]{2,1,0:T(8,128)} %key_value_product.1), calls=%async_computation.4 | async-start | bytes 5898240 | tf_op jit(solution)/shard_map/all_to_all | solution.py:329
  144.0 14.5 %slice-start = ((s8[5160960]{0:T(1024)(128)(4,1)}), s8[4194304]{0:T(1024)(128)(4,1)S(1)}, s32[]{:S(2)}) async-start(s8[5160960]{0:T(1024)(128)(4,1)} %bitcast.15), calls=%async_computation.5 | async-start | bytes 8388608
  148.3 10.3 %slice-start.1 = ((s8[5160960]{0:T(1024)(128)(4,1)}), s8[966656]{0:T(1024)(128)(4,1)S(1)}, s32[]{:S(2)}) async-start(s8[5160960]{0:T(1024)(128)(4,1)} %bitcast.15), calls=%async_computation.6 | async-start | bytes 1933312
  148.3 10.3 %copy-start.9 = (bf16[128,1120]{1,0:T(8,128)(2,1)S(1)}, bf16[128,1120]{1,0:T(8,128)(2,1)}, u32[]{:S(2)}) copy-start(bf16[128,1120]{1,0:T(8,128)(2,1)} %get-tuple-element.86) | copy-start | bytes 860164
  152.4 29.0 %collective-permute-start.17 = (f32[72,256]{1,0:T(8,128)S(1)}, f32[72,256]{1,0:T(8,128)S(1)}, u32[]{:S(2)}, u32[]{:S(2)}) collective-permute-start(f32[72,256]{1,0:T(8,128)S(1)} %copy-done.13), channel_id=1, source_target_pairs={{0,1},{1,16},{16,17},{17,0},{2,3},{3,18},{18,19},{19,2},{4,5},{5,2... | collective-permute-start | bytes 221192 | tf_op jit(solution)/shard_map/ppermute | solution.py:333
  154.4 27.0 %collective-permute-start.18 = (f32[72,256]{1,0:T(8,128)S(1)}, f32[72,256]{1,0:T(8,128)S(1)}, u32[]{:S(2)}, u32[]{:S(2)}) collective-permute-start(f32[72,256]{1,0:T(8,128)S(1)} %copy-done.12), channel_id=1, source_target_pairs={{0,16},{1,17},{16,0},{17,1},{2,18},{3,19},{18,2},{19,3},{4,20},{5,... | collective-permute-start | bytes 221192 | tf_op jit(solution)/shard_map/ppermute | solution.py:333
  157.1 24.3 %collective-permute-start.19 = (f32[72,256]{1,0:T(8,128)S(1)}, f32[72,256]{1,0:T(8,128)S(1)}, u32[]{:S(2)}, u32[]{:S(2)}) collective-permute-start(f32[72,256]{1,0:T(8,128)S(1)} %copy-done.11), channel_id=1, source_target_pairs={{0,17},{1,0},{16,1},{17,16},{2,19},{3,2},{18,3},{19,18},{4,21},{5,... | collective-permute-start | bytes 221192 | tf_op jit(solution)/shard_map/ppermute | solution.py:333
  (9 other events, 59.1 us)

commit v11 on v10

--- a/solution.py
+++ b/solution.py
@@ -17,7 +17,6 @@
 CORES = 2
 ROWS = D // TILES
 PADDED_ROWS = 72
-SPLIT = 40
 HALF = D // 4
 REPLICAS = 4
 RING = 4
@@ -281,15 +280,10 @@
         values = dot(rows[half * HALF : (half + 1) * HALF, :], columns[...], 1, 0) * normalizer
         for index in range(span):
             product[half * span + index, :ROWS, :] = values[index * ROWS : (index + 1) * ROWS]
-    for slot in range(RING):
+    for slot, out in enumerate(outs):
         at = lax.rem(across[0] + slot, RING)
         for block in range(RING):
-            values = product[(block // 2) * span + at * 2 + block % 2]
-            if slot == 2:
-                outs[2][block] = values[:SPLIT]
-                outs[4][block] = values[SPLIT:]
-            else:
-                outs[slot][block] = values
+            out[block] = product[(block // 2) * span + at * 2 + block % 2]
 
 
 def key_value_product_kernel(normalizer, place, rows, own, other, out, columns):
@@ -306,12 +300,10 @@
         out[index, :ROWS, :] = values[index * ROWS : (index + 1) * ROWS]
 
 
-def second_stage_kernel(along, own, first, upper, third, lower, *outs):
+def second_stage_kernel(along, own, first, second, third, *outs):
     for slot, out in enumerate(outs):
         at = lax.rem(along[0] + slot, RING)
-        total = (own[at] + first[at]) + third[at]
-        out[:SPLIT, :] = total[:SPLIT] + upper[at]
-        out[SPLIT:, :] = total[SPLIT:] + lower[at]
+        out[...] = (own[at] + first[at]) + (second[at] + third[at])
 
 
 def last_kernel(key_value, own, first, second, third, query_out, key_out, value_out):
@@ -407,13 +399,13 @@
     right_top = shift(later_top, 3, "dp")
     got_state = exchange(sent, IMAGE)
     sent, grad_denom = call(
-        lambda *refs: total_grad_kernel(loss_scale, *refs),
+        lambda *refs: total_grad_kernel(loss_scale, *refs[:4], *refs[6:]),
         "total_grad",
         [shaped((TILES, PART + HEADS, HD)), shaped((TOKENS, HEADS))],
-        [BLOCK] * 4,
+        [BLOCK] * 4 + [ANYWHERE] * 2,
         [state, totals],
-        arrived=(0, 1, 2, 3),
-    )(got_state, query, upstream, total)
+        arrived=(0, 1, 2, 3, 4, 5),
+    )(got_state, query, upstream, total, swap_cores(left_bottom), swap_cores(right_top))
     sent, far_top, far_bottom, left_bottom, right_top = lax.optimization_barrier(
         (sent, far_top, far_bottom, left_bottom, right_top)
     )
@@ -457,11 +449,7 @@
     slots = call(
         lambda *refs: query_product_kernel(normalizer, *refs[:4], *refs[5:]),
         "query_product",
-        [
-            shaped((RING, SPLIT if slot == 2 else PADDED_ROWS, EARLY))
-            for slot in range(RING)
-        ]
-        + [shaped((RING, PADDED_ROWS - SPLIT, EARLY))],
+        [shaped((RING, PADDED_ROWS, EARLY))] * RING,
         [IN_SMEM, BLOCK, BLOCK, BLOCK, ANYWHERE],
         [
             pltpu.VMEM((2 * REPLICAS * TOKENS, EARLY), BF16),
@@ -470,16 +458,14 @@
         vmem=24,
         arrived=(3,),
     )(across, rows, query_columns, swap_cores(query_columns), sent)
-    upper, lower = slots[2], slots[4]
-    lower = shift(shift(lower, 3, "x"), 3, "x")
-    slots = [slots[0], shift(slots[1], 1, "x"), shift(upper, 2, "x"), shift(slots[3], 3, "x"), lower]
+    slots = shifted(slots, "x")
     own_columns, slots = lax.optimization_barrier((own_columns, slots))
     slots = call(
         second_stage_kernel,
         "second_stage",
         [shaped((PADDED_ROWS, EARLY))] * RING,
-        [IN_SMEM] + [BLOCK] * (RING + 1),
-        arrived=(2, 3, 4, 5),
+        [IN_SMEM] + [BLOCK] * RING,
+        arrived=(2, 3, 4),
     )(along, *slots)
     (product,) = call(
         lambda *refs: key_value_product_kernel(normalizer, *refs[:4], *refs[5:]),

time: 189 us -> 180 us (0.952)
  starting transfers between devices: 61.4 us -> 54.6 us
  waiting for transfers between devices: 69.5 us -> 67.5 us
    all_to_all x5, waiting for transfers between devices: 27.2 us -> 21.9 us  [exchange(): return lax.all_to_all(blocks, axes, 0, 0, tiled=True)]
    ppermute x17 -> x15, starting transfers between devices: 27.4 us -> 22.8 us  [shift(): lax.ppermute(values, axis, [(i, (i + by) % RING) for i in range(RING)])]
    ppermute x17 -> x15, waiting for transfers between devices: 39.1 us -> 42.4 us  [shift(): lax.ppermute(values, axis, [(i, (i + by) % RING) for i in range(RING)])]
    all_to_all x5, starting transfers between devices: 34 us -> 31.7 us  [exchange(): return lax.all_to_all(blocks, axes, 0, 0, tiled=True)]
  transfers between devices with their start and end apart: 25 -> 25, of which waited for: 12 -> 14; matrix products, arithmetic and copies ran while one was open for 7% -> 7% of each run, Pallas kernels for 12% -> 13%
where the time goes in v11:
time: 180 us; the launch traced here: 179 us
  waiting for transfers between devices  67.5 us (38%)
  starting transfers between devices  54.6 us (30%)
  Pallas kernels  42.3 us (24%)
  matrix products  10.7 us (6%)
  local copies, waits for them, and re-layouts  3.17 us (2%)
    ppermute x15, waiting for transfers between devices, shift(): lax.ppermute(values, axis, [(i, (i + by) % RING) for i in range(RING)])  42.4 us
    pallas_call x13, Pallas kernels, with_placed(): return run(*placed)  42.3 us
    all_to_all x5, starting transfers between devices, exchange(): return lax.all_to_all(blocks, axes, 0, 0, tiled=True)  31.7 us
    ppermute x15, starting transfers between devices, shift(): lax.ppermute(values, axis, [(i, (i + by) % RING) for i in range(RING)])  22.8 us
    all_to_all x5, waiting for transfers between devices, exchange(): return lax.all_to_all(blocks, axes, 0, 0, tiled=True)  21.9 us
    dot_general x3, matrix products, dot(): lax.dot_general(left, right, (((left_dim,), (right_dim,)), ((), ())), pre...  10.7 us
  transfers between devices with their start and end apart: 25, of which 14 were waited for; matrix products, arithmetic and copies ran while one was open for 7% of the time, Pallas kernels for 13%

profile of v11, /device:TPU:8, one launch (start us, length us, event | category | flops | bytes accessed | tf_op | source)
XLA Modules:
  0.0 179.0 jit_solution(12608272453696853257)
XLA Ops:
  0.6 7.7 %key_value.1 = (bf16[10,128,112]{2,1,0:T(8,128)(2,1)}, bf16[10,128,112]{2,1,0:T(8,128)(2,1)}, f32[32,45,112]{2,1,0:T(8,128)}) custom-call(bf16[128,2240]{1,0:T(8,128)(2,1)} %bitcast.17, bf16[2240,1120]{1,0:T(8,128)(2,1)} %key_weight.1, bf16[2240,1120]{1,0:T(8,128)(2,1)} %value_weight.1), custom_call_target="tpu_custom_call" | custom-call | tf_op jit(solution)/shard_map/key_value/pallas_call | solution.py:66
  8.4 2.4 %turn.1 = (f32[1120,128]{1,0:T(8,128)}, f32[1120,128]{1,0:T(8,128)}) custom-call(s32[1]{0:T(128)} %bitcast.3.core, bf16[128,2240]{1,0:T(8,128)(2,1)} %bitcast.18), custom_call_target="tpu_custom_call" | custom-call | tf_op jit(solution)/shard_map/turn/pallas_call | solution.py:66
  10.7 8.3 %all-to-all-start = ((f32[32,45,112]{2,1,0:T(8,128)}), f32[32,45,112]{2,1,0:T(8,128)S(1)}, u32[]{:S(2)}, u32[]{:S(2)}) async-start(f32[32,45,112]{2,1,0:T(8,128)} %get-tuple-element.55), calls=%async_computation | async-start | bytes 1572864 | tf_op jit(solution)/shard_map/all_to_all | solution.py:321
  21.1 4.4 %query.1.refs_1_ = bf16[10,128,112]{2,1,0:T(8,128)(2,1)} custom-call(bf16[128,2240]{1,0:T(8,128)(2,1)} %bitcast.19, bf16[2240,1120]{1,0:T(8,128)(2,1)} %weight.1), custom_call_target="tpu_custom_call" | custom-call | tf_op jit(solution)/shard_map/query/pallas_call | solution.py:66
  25.6 8.0 %all-to-all-done.refs_0_ = f32[32,45,112]{2,1,0:T(8,128)S(1)} async-done(((f32[32,45,112]{2,1,0:T(8,128)}), f32[32,45,112]{2,1,0:T(8,128)S(1)}, u32[]{:S(2)}, u32[]{:S(2)}) %all-to-all-start) | async-done | bytes 645152 | tf_op jit(solution)/shard_map/all_to_all | solution.py:321
  34.5 2.5 %numerator.1 = (f32[32,70,112]{2,1,0:T(8,128)}, bf16[10,128,112]{2,1,0:T(8,128)(2,1)}, f32[10,112]{1,0:T(8,128)}) custom-call(f32[32,45,112]{2,1,0:T(8,128)S(1)} %all-to-all-done.refs_0_, bf16[10,128,112]{2,1,0:T(8,128)(2,1)S(1)} %copy-done, bf16[128,1120]{1,0:T(8,128)(2,1)S(1)} %bitcast.13), custom_call_target="tpu_custom_call" | custom-call | tf_op jit(solution)/shard_map/numerator/pallas_call | solution.py:66
  39.1 5.9 %all-to-all-start.1 = ((f32[32,70,112]{2,1,0:T(8,128)}), f32[32,70,112]{2,1,0:T(8,128)S(1)}, u32[]{:S(2)}, u32[]{:S(2)}) async-start(f32[32,70,112]{2,1,0:T(8,128)} %get-tuple-element.60), calls=%async_computation.1 | async-start | bytes 2359296 | tf_op jit(solution)/shard_map/all_to_all | solution.py:321
  45.0 6.1 %collective-permute-done.3.refs_5_ = f32[1120,128]{1,0:T(8,128)} collective-permute-done((f32[1120,128]{1,0:T(8,128)S(1)}, f32[1120,128]{1,0:T(8,128)}, u32[]{:S(2)}, u32[]{:S(2)}) %collective-permute-start.3) | collective-permute-done | bytes 573472 | tf_op jit(solution)/shard_map/ppermute | solution.py:325
  54.4 9.4 %all-to-all-done.1.refs_0_.got = f32[32,70,112]{2,1,0:T(8,128)S(1)} async-done(((f32[32,70,112]{2,1,0:T(8,128)}), f32[32,70,112]{2,1,0:T(8,128)S(1)}, u32[]{:S(2)}, u32[]{:S(2)}) %all-to-all-start.1) | async-done | bytes 1003552 | tf_op jit(solution)/shard_map/all_to_all | solution.py:321
  63.8 2.6 %total_grad.1 = (f32[32,45,112]{2,1,0:T(8,128)}, f32[128,10]{1,0:T(8,128)}) custom-call(f32[32,70,112]{2,1,0:T(8,128)S(1)} %all-to-all-done.1.refs_0_.got, bf16[10,128,112]{2,1,0:T(8,128)(2,1)S(1)} %copy-done.1, bf16[128,1120]{1,0:T(8,128)(2,1)S(1)} %bitcast.14, f32[10,112]{1,0:T(8,128)S(1)} %copy-done.6, f32[1120,128]{1,0:T(8,128)} %collective-permute-done.4.refs_4_, ...), custom_call_target="tpu_custom_call" | custom-call | tf_op jit(solution)/shard_map/total_grad/pallas_call | solution.py:66
  69.1 6.1 %all-to-all-start.2 = ((f32[32,45,112]{2,1,0:T(8,128)}), f32[32,45,112]{2,1,0:T(8,128)S(1)}, u32[]{:S(2)}, u32[]{:S(2)}) async-start(f32[32,45,112]{2,1,0:T(8,128)} %get-tuple-element.70), calls=%async_computation.2 | async-start | bytes 1572864 | tf_op jit(solution)/shard_map/all_to_all | solution.py:321
  75.2 3.0 %query_grad.1 = (bf16[128,1120]{1,0:T(8,128)(2,1)}, f32[128,256]{1,0:T(8,128)}, f32[128,256]{1,0:T(8,128)}, f32[128,256]{1,0:T(8,128)}, f32[128,256]{1,0:T(8,128)}, /*index=5*/f32[4,128,24]{2,1,0:T(8,128)}) custom-call(s32[1]{0:T(128)} %bitcast.place.refs_0_, f32[32,70,112]{2,1,0:T(8,128)S(1)} %all-to-all-done.1.refs_0_.got, ...), custom_call_target="tpu_custom_call" | custom-call | tf_op jit(solution)/shard_map/query_grad/pallas_call | solution.py:66
  78.1 2.7 %collective-permute-start.10 = (f32[128,256]{1,0:T(8,128)}, f32[128,256]{1,0:T(8,128)S(1)}, u32[]{:S(2)}, u32[]{:S(2)}) collective-permute-start(f32[128,256]{1,0:T(8,128)} %get-tuple-element.77), channel_id=1, source_target_pairs={{0,64},{32,96},{64,0},{96,32},{1,65},{33,97},{65,1},{97,33},{2,66}... | collective-permute-start | bytes 393224 | tf_op jit(solution)/shard_map/ppermute | solution.py:325
  82.8 4.0 %join.1.refs_1_ = bf16[1120,1024]{1,0:T(8,128)(2,1)} custom-call(f32[1120,128]{1,0:T(8,128)} %get-tuple-element.64.refs_0_, f32[1120,128]{1,0:T(8,128)S(1)} %collective-permute-done.refs_1_, f32[1120,128]{1,0:T(8,128)} %collective-permute-done.7.refs_2_, f32[1120,128]{1,0:T(8,128)} %collective-permute-done.5.refs_3_, ...), custom_call_target="tpu_custom_call" | custom-call | tf_op jit(solution)/shard_map/join/pallas_call | solution.py:66
  90.4 2.3 %key_value_grad.1 = (bf16[128,1120]{1,0:T(8,128)(2,1)}, bf16[128,1120]{1,0:T(8,128)(2,1)}, f32[4,128,640]{2,1,0:T(8,128)}) custom-call(f32[32,45,112]{2,1,0:T(8,128)S(1)} %all-to-all-done.2.got, bf16[10,128,112]{2,1,0:T(8,128)(2,1)S(1)} %copy-done.3, bf16[10,128,112]{2,1,0:T(8,128)(2,1)S(1)} %copy-done.4, f32[4,128,24]{2,1,0:T(8,128)S(1)} %copy-done.5), custom_call_target="tpu_custom_call" | custom-call | tf_op jit(solution)/shard_map/key_value_grad/pallas_call | solution.py:66
  92.7 4.8 %all-to-all-start.3 = ((f32[4,128,640]{2,1,0:T(8,128)}), f32[4,128,640]{2,1,0:T(8,128)S(1)}, u32[]{:S(2)}, u32[]{:S(2)}) async-start(f32[4,128,640]{2,1,0:T(8,128)} %get-tuple-element.86.refs_4_), calls=%async_computation.3 | async-start | bytes 2621440 | tf_op jit(solution)/shard_map/all_to_all | solution.py:321
  97.5 1.9 %collective-permute-done.12.refs_3_ = f32[512,256]{1,0:T(8,128)S(1)} collective-permute-done((f32[512,256]{1,0:T(8,128)S(1)}, f32[512,256]{1,0:T(8,128)S(1)}, u32[]{:S(2)}, u32[]{:S(2)}) %collective-permute-start.12) | collective-permute-done | bytes 524320 | tf_op jit(solution)/shard_map/ppermute | solution.py:333
  99.4 3.6 %query_product.1 = (f32[4,72,256]{2,1,0:T(8,128)}, f32[4,72,256]{2,1,0:T(8,128)}, f32[4,72,256]{2,1,0:T(8,128)}, f32[4,72,256]{2,1,0:T(8,128)}) custom-call(s32[1]{0:T(128)} %bitcast.5.refs_0_, bf16[1120,1024]{1,0:T(8,128)(2,1)} %join.1.refs_1_, f32[512,256]{1,0:T(8,128)} %pack_query.1.refs_2_, f32[512,256]{1,0:T(8,128)S(1)} %collective-permute-done.12.refs_3_, ...), custom_call_target="tpu_custom_call" | custom-call | tf_op jit(solution)/shard_map/query_product/pallas_call | solution.py:66
  104.7 2.7 %collective-permute-start.14 = (f32[4,72,256]{2,1,0:T(8,128)}, f32[4,72,256]{2,1,0:T(8,128)S(1)}, u32[]{:S(2)}, u32[]{:S(2)}) collective-permute-start(f32[4,72,256]{2,1,0:T(8,128)} %get-tuple-element.90), channel_id=1, source_target_pairs={{0,4},{2,6},{4,0},{6,2},{1,5},{3,7},{5,1},{7,3},{8,12},{10,14},{12... | collective-permute-start | bytes 884744 | tf_op jit(solution)/shard_map/ppermute | solution.py:325
  108.8 4.7 %collective-permute-done.13.first = f32[4,72,256]{2,1,0:T(8,128)S(1)} collective-permute-done((f32[4,72,256]{2,1,0:T(8,128)}, f32[4,72,256]{2,1,0:T(8,128)S(1)}, u32[]{:S(2)}, u32[]{:S(2)}) %collective-permute-start.13) | collective-permute-done | bytes 294944 | tf_op jit(solution)/shard_map/ppermute | solution.py:325
  113.5 7.4 %collective-permute-done.14.second = f32[4,72,256]{2,1,0:T(8,128)S(1)} collective-permute-done((f32[4,72,256]{2,1,0:T(8,128)}, f32[4,72,256]{2,1,0:T(8,128)S(1)}, u32[]{:S(2)}, u32[]{:S(2)}) %collective-permute-start.14) | collective-permute-done | bytes 294944 | tf_op jit(solution)/shard_map/ppermute | solution.py:325
  124.0 4.7 %key_value_product.1 = f32[16,72,640]{2,1,0:T(8,128)} custom-call(s32[1]{0:T(128)} %bitcast.place.refs_0_, bf16[1120,1024]{1,0:T(8,128)(2,1)} %join.1.refs_1_, f32[4,128,640]{2,1,0:T(8,128)S(1)} %all-to-all-done.3.refs_2_, f32[4,128,640]{2,1,0:T(8,128)S(1)} %collective-permute-done.16.refs_3_, f32[72,256]{1,0:T(8,128)} %get-tuple-element.97.refs_4_.own), custom_call_target="tpu_custom_call" | custom-call | tf_op jit(solution)/shard_map/key_value_product/pallas_call | solution.py:66
  128.6 6.6 %all-to-all-start.4 = ((f32[16,72,640]{2,1,0:T(8,128)}), f32[16,72,640]{2,1,0:T(8,128)S(1)}, u32[]{:S(2)}, u32[]{:S(2)}) async-start(f32[16,72,640]{2,1,0:T(8,128)} %key_value_product.1), calls=%async_computation.4 | async-start | bytes 5898240 | tf_op jit(solution)/shard_map/all_to_all | solution.py:321
  135.3 4.2 %fusion.1 = f32[128,2240]{0,1:T(8,128)S(1)} fusion(bf16[128,1120]{1,0:T(8,128)(2,1)S(1)} %copy-done.9, bf16[2240,1120]{1,0:T(8,128)(2,1)} %key_weight.1), kind=kOutput, calls=%fused_computation.3 | convolution fusion | flops 642252800 | bytes 6451200 | tf_op jit(solution)/shard_map/dot_general | solution.py:72
  139.6 4.1 %convolution_add_fusion.1 = f32[128,2240]{0,1:T(8,128)S(1)} fusion(f32[128,2240]{0,1:T(8,128)S(1)} %fusion.1, bf16[128,1120]{1,0:T(8,128)(2,1)S(1)} %copy-done.10, bf16[2240,1120]{1,0:T(8,128)(2,1)} %weight.1), kind=kOutput, calls=%fused_computation.1 | convolution fusion | flops 642539520 | bytes 7598080 | tf_op jit(solution)/shard_map/dot_general | solution.py:72
  143.7 2.0 %collective-permute-start.17 = (f32[72,256]{1,0:T(8,128)S(1)}, f32[72,256]{1,0:T(8,128)S(1)}, u32[]{:S(2)}, u32[]{:S(2)}) collective-permute-start(f32[72,256]{1,0:T(8,128)S(1)} %copy-done.14), channel_id=1, source_target_pairs={{0,1},{1,16},{16,17},{17,0},{2,3},{3,18},{18,19},{19,2},{4,5},{5,2... | collective-permute-start | bytes 221192 | tf_op jit(solution)/shard_map/ppermute | solution.py:325
  145.7 2.7 %collective-permute-start.18 = (f32[72,256]{1,0:T(8,128)S(1)}, f32[72,256]{1,0:T(8,128)S(1)}, u32[]{:S(2)}, u32[]{:S(2)}) collective-permute-start(f32[72,256]{1,0:T(8,128)S(1)} %copy-done.13), channel_id=1, source_target_pairs={{0,16},{1,17},{16,0},{17,1},{2,18},{3,19},{18,2},{19,3},{4,20},{5,... | collective-permute-start | bytes 221192 | tf_op jit(solution)/shard_map/ppermute | solution.py:325
  149.8 2.4 %fusion = bf16[128,2240]{0,1:T(8,128)(2,1)} fusion(f32[128,2240]{0,1:T(8,128)S(1)} %convolution_add_fusion.1, bf16[128,1120]{1,0:T(8,128)(2,1)S(1)} %copy-done.8, bf16[2240,1120]{1,0:T(8,128)(2,1)S(1)} %bitcast.16), kind=kOutput, calls=%fused_computation.2 | convolution fusion | flops 642826240 | bytes 7024640 | tf_op jit(solution)/shard_map/dot_general | solution.py:72
  152.2 2.1 %copy.10 = bf16[128,2240]{1,0:T(8,128)(2,1)} copy(bf16[128,2240]{0,1:T(8,128)(2,1)} %fusion) | data formatting | bytes 1146880 | tf_op jit(solution)/shard_map/convert_element_type | solution.py:498
  154.3 18.4 %collective-permute-done.17.first = f32[72,256]{1,0:T(8,128)S(1)} collective-permute-done((f32[72,256]{1,0:T(8,128)S(1)}, f32[72,256]{1,0:T(8,128)S(1)}, u32[]{:S(2)}, u32[]{:S(2)}) %collective-permute-start.17) | collective-permute-done | bytes 73760 | tf_op jit(solution)/shard_map/ppermute | solution.py:325
  172.7 4.5 %all-to-all-done.4.key_value = f32[16,72,640]{2,1,0:T(8,128)S(1)} async-done(((f32[16,72,640]{2,1,0:T(8,128)}), f32[16,72,640]{2,1,0:T(8,128)S(1)}, u32[]{:S(2)}, u32[]{:S(2)}) %all-to-all-start.4) | async-done | bytes 2949152 | tf_op jit(solution)/shard_map/all_to_all | solution.py:321
  177.3 1.7 last.1
  (70 shorter events, 24.5 us)
Async XLA Ops:
  10.7 10.0 %collective-permute-start.1 = (f32[1120,128]{1,0:T(8,128)}, f32[1120,128]{1,0:T(8,128)S(1)}, u32[]{:S(2)}, u32[]{:S(2)}) collective-permute-start(f32[1120,128]{1,0:T(8,128)} %get-tuple-element.59), channel_id=1, source_target_pairs={{0,8},{8,0},{1,9},{9,1},{2,10},{10,2},{3,11},{11,3},{4,12},{12,4},... | collective-permute-start | bytes 1720328 | tf_op jit(solution)/shard_map/ppermute | solution.py:333
  10.7 22.8 %all-to-all-start = ((f32[32,45,112]{2,1,0:T(8,128)}), f32[32,45,112]{2,1,0:T(8,128)S(1)}, u32[]{:S(2)}, u32[]{:S(2)}) async-start(f32[32,45,112]{2,1,0:T(8,128)} %get-tuple-element.55), calls=%async_computation | async-start | bytes 1572864 | tf_op jit(solution)/shard_map/all_to_all | solution.py:321
  19.0 14.5 %copy-start.2 = (bf16[1,16,8,1120]{3,2,1,0:T(8,128)(2,1)S(1)}, bf16[1,16,8,1120]{3,2,1,0:T(8,128)(2,1)}, u32[]{:S(2)}) copy-start(bf16[1,16,8,1120]{3,2,1,0:T(8,128)(2,1)} %param.9) | copy-start | bytes 860164
  19.0 19.6 %copy-start.11 = (f32[1120,128]{1,0:T(8,128)S(1)}, f32[1120,128]{1,0:T(8,128)}, u32[]{:S(2)}) copy-start(f32[1120,128]{1,0:T(8,128)} %get-tuple-element.64.refs_0_) | copy-start | bytes 1720324
  19.0 17.9 %collective-permute-start = (f32[1120,128]{1,0:T(8,128)}, f32[1120,128]{1,0:T(8,128)S(1)}, u32[]{:S(2)}, u32[]{:S(2)}) collective-permute-start(f32[1120,128]{1,0:T(8,128)} %get-tuple-element.64.refs_0_), channel_id=1, source_target_pairs={{0,32},{32,64},{64,96},{96,0},{1,33},{33,65},{65,97},{97,1},{2,34}... | collective-permute-start | bytes 1720328 | tf_op jit(solution)/shard_map/ppermute | solution.py:325
  20.7 16.3 %collective-permute-start.2 = (f32[1120,128]{1,0:T(8,128)S(1)}, f32[1120,128]{1,0:T(8,128)}, u32[]{:S(2)}, u32[]{:S(2)}) collective-permute-start(f32[1120,128]{1,0:T(8,128)S(1)} %collective-permute-done.1.refs_4_), channel_id=1, source_target_pairs={{0,96},{32,0},{64,32},{96,64},{1,97},{33,1},{65,33},{97,65},{2,98}... | collective-permute-start | bytes 1720328 | tf_op jit(solution)/shard_map/ppermute | solution.py:325
  34.5 29.3 %copy-start.1 = (bf16[10,128,112]{2,1,0:T(8,128)(2,1)S(1)}, bf16[10,128,112]{2,1,0:T(8,128)(2,1)}, u32[]{:S(2)}) copy-start(bf16[10,128,112]{2,1,0:T(8,128)(2,1)} %query.1.refs_1_) | copy-start | bytes 860164
  37.0 26.8 %copy-start.6 = (f32[10,112]{1,0:T(8,128)S(1)}, f32[10,112]{1,0:T(8,128)}, u32[]{:S(2)}) copy-start(f32[10,112]{1,0:T(8,128)} %get-tuple-element.62.refs_3_.total) | copy-start | bytes 13444
  37.0 14.1 %collective-permute-start.3 = (f32[1120,128]{1,0:T(8,128)S(1)}, f32[1120,128]{1,0:T(8,128)}, u32[]{:S(2)}, u32[]{:S(2)}) collective-permute-start(f32[1120,128]{1,0:T(8,128)S(1)} %collective-permute-done.1.refs_4_), channel_id=1, source_target_pairs={{0,32},{32,64},{64,96},{96,0},{1,33},{33,65},{65,97},{97,1},{2,34}... | collective-permute-start | bytes 1720328 | tf_op jit(solution)/shard_map/ppermute | solution.py:325
  38.6 13.7 %collective-permute-start.5 = (f32[1120,128]{1,0:T(8,128)S(1)}, f32[1120,128]{1,0:T(8,128)}, u32[]{:S(2)}, u32[]{:S(2)}) collective-permute-start(f32[1120,128]{1,0:T(8,128)S(1)} %copy-done.11), channel_id=1, source_target_pairs={{0,96},{32,0},{64,32},{96,64},{1,97},{33,1},{65,33},{97,65},{2,98}... | collective-permute-start | bytes 1720328 | tf_op jit(solution)/shard_map/ppermute | solution.py:325
  39.1 24.7 %all-to-all-start.1 = ((f32[32,70,112]{2,1,0:T(8,128)}), f32[32,70,112]{2,1,0:T(8,128)S(1)}, u32[]{:S(2)}, u32[]{:S(2)}) async-start(f32[32,70,112]{2,1,0:T(8,128)} %get-tuple-element.60), calls=%async_computation.1 | async-start | bytes 2359296 | tf_op jit(solution)/shard_map/all_to_all | solution.py:321
  51.1 12.7 %collective-permute-start.4 = (f32[1120,128]{1,0:T(8,128)}, f32[1120,128]{1,0:T(8,128)}, u32[]{:S(2)}, u32[]{:S(2)}) collective-permute-start(f32[1120,128]{1,0:T(8,128)} %collective-permute-done.3.refs_5_), channel_id=1, source_target_pairs={{0,8},{8,0},{1,9},{9,1},{2,10},{10,2},{3,11},{11,3},{4,12},{12,4},... | collective-permute-start | bytes 1720328 | tf_op jit(solution)/shard_map/ppermute | solution.py:333
  52.4 11.4 %collective-permute-start.6 = (f32[1120,128]{1,0:T(8,128)}, f32[1120,128]{1,0:T(8,128)}, u32[]{:S(2)}, u32[]{:S(2)}) collective-permute-start(f32[1120,128]{1,0:T(8,128)} %collective-permute-done.5.refs_3_), channel_id=1, source_target_pairs={{0,8},{8,0},{1,9},{9,1},{2,10},{10,2},{3,11},{11,3},{4,12},{12,4},... | collective-permute-start | bytes 1720328 | tf_op jit(solution)/shard_map/ppermute | solution.py:333
  52.4 15.5 %collective-permute-start.7 = (f32[1120,128]{1,0:T(8,128)S(1)}, f32[1120,128]{1,0:T(8,128)}, u32[]{:S(2)}, u32[]{:S(2)}) collective-permute-start(f32[1120,128]{1,0:T(8,128)S(1)} %collective-permute-done.refs_1_), channel_id=1, source_target_pairs={{0,32},{32,64},{64,96},{96,0},{1,33},{33,65},{65,97},{97,1},{2,34}... | collective-permute-start | bytes 1720328 | tf_op jit(solution)/shard_map/ppermute | solution.py:325
  53.7 15.4 %collective-permute-start.8 = (f32[1120,128]{1,0:T(8,128)}, f32[1120,128]{1,0:T(8,128)}, u32[]{:S(2)}, u32[]{:S(2)}) collective-permute-start(f32[1120,128]{1,0:T(8,128)} %collective-permute-done.2.refs_7_), channel_id=1, source_target_pairs={{0,96},{32,0},{64,32},{96,64},{1,97},{33,1},{65,33},{97,65},{2,98}... | collective-permute-start | bytes 1720328 | tf_op jit(solution)/shard_map/ppermute | solution.py:325
  69.1 21.3 %all-to-all-start.2 = ((f32[32,45,112]{2,1,0:T(8,128)}), f32[32,45,112]{2,1,0:T(8,128)S(1)}, u32[]{:S(2)}, u32[]{:S(2)}) async-start(f32[32,45,112]{2,1,0:T(8,128)} %get-tuple-element.70), calls=%async_computation.2 | async-start | bytes 1572864 | tf_op jit(solution)/shard_map/all_to_all | solution.py:321
  78.1 8.7 %collective-permute-start.10 = (f32[128,256]{1,0:T(8,128)}, f32[128,256]{1,0:T(8,128)S(1)}, u32[]{:S(2)}, u32[]{:S(2)}) collective-permute-start(f32[128,256]{1,0:T(8,128)} %get-tuple-element.77), channel_id=1, source_target_pairs={{0,64},{32,96},{64,0},{96,32},{1,65},{33,97},{65,1},{97,33},{2,66}... | collective-permute-start | bytes 393224 | tf_op jit(solution)/shard_map/ppermute | solution.py:325
  80.8 7.5 %collective-permute-start.11 = (f32[128,256]{1,0:T(8,128)}, f32[128,256]{1,0:T(8,128)S(1)}, u32[]{:S(2)}, u32[]{:S(2)}) collective-permute-start(f32[128,256]{1,0:T(8,128)} %get-tuple-element.78), channel_id=1, source_target_pairs={{0,96},{32,0},{64,32},{96,64},{1,97},{33,1},{65,33},{97,65},{2,98}... | collective-permute-start | bytes 393224 | tf_op jit(solution)/shard_map/ppermute | solution.py:325
  81.9 6.7 %collective-permute-start.9 = (f32[128,256]{1,0:T(8,128)}, f32[128,256]{1,0:T(8,128)S(1)}, u32[]{:S(2)}, u32[]{:S(2)}) collective-permute-start(f32[128,256]{1,0:T(8,128)} %get-tuple-element.76), channel_id=1, source_target_pairs={{0,32},{32,64},{64,96},{96,0},{1,33},{33,65},{65,97},{97,1},{2,34}... | collective-permute-start | bytes 393224 | tf_op jit(solution)/shard_map/ppermute | solution.py:325
  92.7 28.3 %all-to-all-start.3 = ((f32[4,128,640]{2,1,0:T(8,128)}), f32[4,128,640]{2,1,0:T(8,128)S(1)}, u32[]{:S(2)}, u32[]{:S(2)}) async-start(f32[4,128,640]{2,1,0:T(8,128)} %get-tuple-element.86.refs_4_), calls=%async_computation.3 | async-start | bytes 2621440 | tf_op jit(solution)/shard_map/all_to_all | solution.py:321
  97.5 1.9 %collective-permute-start.12 = (f32[512,256]{1,0:T(8,128)S(1)}, f32[512,256]{1,0:T(8,128)S(1)}, u32[]{:S(2)}, u32[]{:S(2)}) collective-permute-start(f32[512,256]{1,0:T(8,128)S(1)} %copy-done.7), channel_id=1, source_target_pairs={{0,8},{8,0},{1,9},{9,1},{2,10},{10,2},{3,11},{11,3},{4,12},{12,4},... | collective-permute-start | bytes 1572872 | tf_op jit(solution)/shard_map/ppermute | solution.py:333
  103.0 10.5 %collective-permute-start.13 = (f32[4,72,256]{2,1,0:T(8,128)}, f32[4,72,256]{2,1,0:T(8,128)S(1)}, u32[]{:S(2)}, u32[]{:S(2)}) collective-permute-start(f32[4,72,256]{2,1,0:T(8,128)} %get-tuple-element.89), channel_id=1, source_target_pairs={{0,2},{2,4},{4,6},{6,0},{1,3},{3,5},{5,7},{7,1},{8,10},{10,12},{12... | collective-permute-start | bytes 884744 | tf_op jit(solution)/shard_map/ppermute | solution.py:325
  104.7 16.2 %collective-permute-start.14 = (f32[4,72,256]{2,1,0:T(8,128)}, f32[4,72,256]{2,1,0:T(8,128)S(1)}, u32[]{:S(2)}, u32[]{:S(2)}) collective-permute-start(f32[4,72,256]{2,1,0:T(8,128)} %get-tuple-element.90), channel_id=1, source_target_pairs={{0,4},{2,6},{4,0},{6,2},{1,5},{3,7},{5,1},{7,3},{8,12},{10,14},{12... | collective-permute-start | bytes 884744 | tf_op jit(solution)/shard_map/ppermute | solution.py:325
  107.4 13.6 %collective-permute-start.15 = (f32[4,72,256]{2,1,0:T(8,128)}, f32[4,72,256]{2,1,0:T(8,128)S(1)}, u32[]{:S(2)}, u32[]{:S(2)}) collective-permute-start(f32[4,72,256]{2,1,0:T(8,128)} %get-tuple-element.91), channel_id=1, source_target_pairs={{0,6},{2,0},{4,2},{6,4},{1,7},{3,1},{5,3},{7,5},{8,14},{10,8},{12,... | collective-permute-start | bytes 884744 | tf_op jit(solution)/shard_map/ppermute | solution.py:325
  120.9 3.0 %collective-permute-start.16 = (f32[4,128,640]{2,1,0:T(8,128)S(1)}, f32[4,128,640]{2,1,0:T(8,128)S(1)}, u32[]{:S(2)}, u32[]{:S(2)}) collective-permute-start(f32[4,128,640]{2,1,0:T(8,128)S(1)} %all-to-all-done.3.refs_2_), channel_id=1, source_target_pairs={{0,8},{8,0},{1,9},{9,1},{2,10},{10,2},{3,11},{11,3},{4,12},{12,4},... | collective-permute-start | bytes 3932168 | tf_op jit(solution)/shard_map/ppermute | solution.py:333
  128.6 48.6 %all-to-all-start.4 = ((f32[16,72,640]{2,1,0:T(8,128)}), f32[16,72,640]{2,1,0:T(8,128)S(1)}, u32[]{:S(2)}, u32[]{:S(2)}) async-start(f32[16,72,640]{2,1,0:T(8,128)} %key_value_product.1), calls=%async_computation.4 | async-start | bytes 5898240 | tf_op jit(solution)/shard_map/all_to_all | solution.py:321
  135.3 14.5 %slice-start = ((s8[5160960]{0:T(1024)(128)(4,1)}), s8[4194304]{0:T(1024)(128)(4,1)S(1)}, s32[]{:S(2)}) async-start(s8[5160960]{0:T(1024)(128)(4,1)} %bitcast.15), calls=%async_computation.5 | async-start | bytes 8388608
  139.5 10.3 %slice-start.1 = ((s8[5160960]{0:T(1024)(128)(4,1)}), s8[966656]{0:T(1024)(128)(4,1)S(1)}, s32[]{:S(2)}) async-start(s8[5160960]{0:T(1024)(128)(4,1)} %bitcast.15), calls=%async_computation.6 | async-start | bytes 1933312
  139.6 10.3 %copy-start.8 = (bf16[128,1120]{1,0:T(8,128)(2,1)S(1)}, bf16[128,1120]{1,0:T(8,128)(2,1)}, u32[]{:S(2)}) copy-start(bf16[128,1120]{1,0:T(8,128)(2,1)} %get-tuple-element.84) | copy-start | bytes 860164
  143.7 29.0 %collective-permute-start.17 = (f32[72,256]{1,0:T(8,128)S(1)}, f32[72,256]{1,0:T(8,128)S(1)}, u32[]{:S(2)}, u32[]{:S(2)}) collective-permute-start(f32[72,256]{1,0:T(8,128)S(1)} %copy-done.14), channel_id=1, source_target_pairs={{0,1},{1,16},{16,17},{17,0},{2,3},{3,18},{18,19},{19,2},{4,5},{5,2... | collective-permute-start | bytes 221192 | tf_op jit(solution)/shard_map/ppermute | solution.py:325
  145.7 27.0 %collective-permute-start.18 = (f32[72,256]{1,0:T(8,128)S(1)}, f32[72,256]{1,0:T(8,128)S(1)}, u32[]{:S(2)}, u32[]{:S(2)}) collective-permute-start(f32[72,256]{1,0:T(8,128)S(1)} %copy-done.13), channel_id=1, source_target_pairs={{0,16},{1,17},{16,0},{17,1},{2,18},{3,19},{18,2},{19,3},{4,20},{5,... | collective-permute-start | bytes 221192 | tf_op jit(solution)/shard_map/ppermute | solution.py:325
  148.4 24.3 %collective-permute-start.19 = (f32[72,256]{1,0:T(8,128)S(1)}, f32[72,256]{1,0:T(8,128)S(1)}, u32[]{:S(2)}, u32[]{:S(2)}) collective-permute-start(f32[72,256]{1,0:T(8,128)S(1)} %copy-done.12), channel_id=1, source_target_pairs={{0,17},{1,0},{16,1},{17,16},{2,19},{3,2},{18,3},{19,18},{4,21},{5,... | collective-permute-start | bytes 221192 | tf_op jit(solution)/shard_map/ppermute | solution.py:325
  (10 other events, 63.4 us)

commit v12 on v11

--- a/solution.py
+++ b/solution.py
@@ -273,17 +273,19 @@
 
 def query_product_kernel(normalizer, across, rows, own, other, *refs):
     outs, columns, product = refs[:-2], refs[-2], refs[-1]
-    columns[: REPLICAS * TOKENS, :] = own[...].astype(BF16)
-    columns[REPLICAS * TOKENS :, :] = other[...].astype(BF16)
-    span = PLANE_SIZE // CORES
-    for half in range(CORES):
-        values = dot(rows[half * HALF : (half + 1) * HALF, :], columns[...], 1, 0) * normalizer
-        for index in range(span):
-            product[half * span + index, :ROWS, :] = values[index * ROWS : (index + 1) * ROWS]
+
+    @pl.when(pl.program_id(0) == 0)
+    def _():
+        columns[: REPLICAS * TOKENS, :] = own[...].astype(BF16)
+        columns[REPLICAS * TOKENS :, :] = other[...].astype(BF16)
+
+    values = dot(rows[...], columns[...], 1, 0) * normalizer
+    for index in range(PLANE_SIZE // CORES):
+        product[index, :ROWS, :] = values[index * ROWS : (index + 1) * ROWS]
     for slot, out in enumerate(outs):
         at = lax.rem(across[0] + slot, RING)
-        for block in range(RING):
-            out[block] = product[(block // 2) * span + at * 2 + block % 2]
+        for block in range(2):
+            out[block] = product[at * 2 + block]
 
 
 def key_value_product_kernel(normalizer, place, rows, own, other, out, columns):
@@ -450,15 +452,24 @@
         lambda *refs: query_product_kernel(normalizer, *refs[:4], *refs[5:]),
         "query_product",
         [shaped((RING, PADDED_ROWS, EARLY))] * RING,
-        [IN_SMEM, BLOCK, BLOCK, BLOCK, ANYWHERE],
+        [
+            IN_SMEM,
+            pl.BlockSpec((HALF, 2 * REPLICAS * TOKENS), lambda half: (half, 0)),
+            BLOCK,
+            BLOCK,
+            ANYWHERE,
+        ],
         [
             pltpu.VMEM((2 * REPLICAS * TOKENS, EARLY), BF16),
-            pltpu.VMEM((PLANE_SIZE, PADDED_ROWS, EARLY), F32),
+            pltpu.VMEM((PLANE_SIZE // CORES, PADDED_ROWS, EARLY), F32),
         ],
         vmem=24,
         arrived=(3,),
+        steps=CORES,
+        out_specs=[pl.BlockSpec((2, PADDED_ROWS, EARLY), lambda half: (half, 0, 0))] * RING,
     )(across, rows, query_columns, swap_cores(query_columns), sent)
-    slots = shifted(slots, "x")
+    far_slot = shift(slots[2], 2, "x")
+    slots = [slots[0], far_slot, shift(slots[1], 1, "x"), shift(slots[3], 3, "x")]
     own_columns, slots = lax.optimization_barrier((own_columns, slots))
     slots = call(
         second_stage_kernel,

time: 180 us -> 179 us (level)
  transfers between devices with their start and end apart: 25 -> 25, of which waited for: 14 -> 15; matrix products, arithmetic and copies ran while one was open for 7% -> 7% of each run, Pallas kernels for 13% -> 13%
where the time goes in v12:
time: 179 us; the launch traced here: 178 us
  waiting for transfers between devices  66.3 us (37%)
  starting transfers between devices  55.1 us (31%)
  Pallas kernels  42 us (23%)
  matrix products  10.7 us (6%)
  local copies, waits for them, and re-layouts  3.17 us (2%)
    pallas_call x13, Pallas kernels, with_placed(): return run(*placed)  42 us
    ppermute x15, waiting for transfers between devices, shift(): lax.ppermute(values, axis, [(i, (i + by) % RING) for i in range(RING)])  41.2 us
    all_to_all x5, starting transfers between devices, exchange(): return lax.all_to_all(blocks, axes, 0, 0, tiled=True)  31.7 us
    ppermute x15, starting transfers between devices, shift(): lax.ppermute(values, axis, [(i, (i + by) % RING) for i in range(RING)])  23.5 us
    all_to_all x5, waiting for transfers between devices, exchange(): return lax.all_to_all(blocks, axes, 0, 0, tiled=True)  21.9 us
    dot_general x3, matrix products, dot(): lax.dot_general(left, right, (((left_dim,), (right_dim,)), ((), ())), pre...  10.7 us
  transfers between devices with their start and end apart: 25, of which 15 were waited for; matrix products, arithmetic and copies ran while one was open for 7% of the time, Pallas kernels for 13%

profile of v12, /device:TPU:8, one launch (start us, length us, event | category | flops | bytes accessed | tf_op | source)
XLA Modules:
  0.0 178.1 jit_solution(15344730191784114618)
XLA Ops:
  0.6 7.7 %key_value.1 = (bf16[10,128,112]{2,1,0:T(8,128)(2,1)}, bf16[10,128,112]{2,1,0:T(8,128)(2,1)}, f32[32,45,112]{2,1,0:T(8,128)}) custom-call(bf16[128,2240]{1,0:T(8,128)(2,1)} %bitcast.17, bf16[2240,1120]{1,0:T(8,128)(2,1)} %key_weight.1, bf16[2240,1120]{1,0:T(8,128)(2,1)} %value_weight.1), custom_call_target="tpu_custom_call" | custom-call | tf_op jit(solution)/shard_map/key_value/pallas_call | solution.py:66
  8.4 2.4 %turn.1 = (f32[1120,128]{1,0:T(8,128)}, f32[1120,128]{1,0:T(8,128)}) custom-call(s32[1]{0:T(128)} %bitcast.3.core, bf16[128,2240]{1,0:T(8,128)(2,1)} %bitcast.18), custom_call_target="tpu_custom_call" | custom-call | tf_op jit(solution)/shard_map/turn/pallas_call | solution.py:66
  10.7 8.3 %all-to-all-start = ((f32[32,45,112]{2,1,0:T(8,128)}), f32[32,45,112]{2,1,0:T(8,128)S(1)}, u32[]{:S(2)}, u32[]{:S(2)}) async-start(f32[32,45,112]{2,1,0:T(8,128)} %get-tuple-element.55), calls=%async_computation | async-start | bytes 1572864 | tf_op jit(solution)/shard_map/all_to_all | solution.py:323
  21.1 4.4 %query.1.refs_1_ = bf16[10,128,112]{2,1,0:T(8,128)(2,1)} custom-call(bf16[128,2240]{1,0:T(8,128)(2,1)} %bitcast.19, bf16[2240,1120]{1,0:T(8,128)(2,1)} %weight.1), custom_call_target="tpu_custom_call" | custom-call | tf_op jit(solution)/shard_map/query/pallas_call | solution.py:66
  25.6 8.0 %all-to-all-done.refs_0_ = f32[32,45,112]{2,1,0:T(8,128)S(1)} async-done(((f32[32,45,112]{2,1,0:T(8,128)}), f32[32,45,112]{2,1,0:T(8,128)S(1)}, u32[]{:S(2)}, u32[]{:S(2)}) %all-to-all-start) | async-done | bytes 645152 | tf_op jit(solution)/shard_map/all_to_all | solution.py:323
  34.5 2.5 %numerator.1 = (f32[32,70,112]{2,1,0:T(8,128)}, bf16[10,128,112]{2,1,0:T(8,128)(2,1)}, f32[10,112]{1,0:T(8,128)}) custom-call(f32[32,45,112]{2,1,0:T(8,128)S(1)} %all-to-all-done.refs_0_, bf16[10,128,112]{2,1,0:T(8,128)(2,1)S(1)} %copy-done, bf16[128,1120]{1,0:T(8,128)(2,1)S(1)} %bitcast.13), custom_call_target="tpu_custom_call" | custom-call | tf_op jit(solution)/shard_map/numerator/pallas_call | solution.py:66
  39.1 5.9 %all-to-all-start.1 = ((f32[32,70,112]{2,1,0:T(8,128)}), f32[32,70,112]{2,1,0:T(8,128)S(1)}, u32[]{:S(2)}, u32[]{:S(2)}) async-start(f32[32,70,112]{2,1,0:T(8,128)} %get-tuple-element.60), calls=%async_computation.1 | async-start | bytes 2359296 | tf_op jit(solution)/shard_map/all_to_all | solution.py:323
  45.0 6.1 %collective-permute-done.3.refs_5_ = f32[1120,128]{1,0:T(8,128)} collective-permute-done((f32[1120,128]{1,0:T(8,128)S(1)}, f32[1120,128]{1,0:T(8,128)}, u32[]{:S(2)}, u32[]{:S(2)}) %collective-permute-start.3) | collective-permute-done | bytes 573472 | tf_op jit(solution)/shard_map/ppermute | solution.py:327
  54.4 9.4 %all-to-all-done.1.refs_0_.got = f32[32,70,112]{2,1,0:T(8,128)S(1)} async-done(((f32[32,70,112]{2,1,0:T(8,128)}), f32[32,70,112]{2,1,0:T(8,128)S(1)}, u32[]{:S(2)}, u32[]{:S(2)}) %all-to-all-start.1) | async-done | bytes 1003552 | tf_op jit(solution)/shard_map/all_to_all | solution.py:323
  63.8 2.6 %total_grad.1 = (f32[32,45,112]{2,1,0:T(8,128)}, f32[128,10]{1,0:T(8,128)}) custom-call(f32[32,70,112]{2,1,0:T(8,128)S(1)} %all-to-all-done.1.refs_0_.got, bf16[10,128,112]{2,1,0:T(8,128)(2,1)S(1)} %copy-done.1, bf16[128,1120]{1,0:T(8,128)(2,1)S(1)} %bitcast.14, f32[10,112]{1,0:T(8,128)S(1)} %copy-done.6, f32[1120,128]{1,0:T(8,128)} %collective-permute-done.4.refs_4_, ...), custom_call_target="tpu_custom_call" | custom-call | tf_op jit(solution)/shard_map/total_grad/pallas_call | solution.py:66
  69.1 6.1 %all-to-all-start.2 = ((f32[32,45,112]{2,1,0:T(8,128)}), f32[32,45,112]{2,1,0:T(8,128)S(1)}, u32[]{:S(2)}, u32[]{:S(2)}) async-start(f32[32,45,112]{2,1,0:T(8,128)} %get-tuple-element.70), calls=%async_computation.2 | async-start | bytes 1572864 | tf_op jit(solution)/shard_map/all_to_all | solution.py:323
  75.2 3.0 %query_grad.1 = (bf16[128,1120]{1,0:T(8,128)(2,1)}, f32[128,256]{1,0:T(8,128)}, f32[128,256]{1,0:T(8,128)}, f32[128,256]{1,0:T(8,128)}, f32[128,256]{1,0:T(8,128)}, /*index=5*/f32[4,128,24]{2,1,0:T(8,128)}) custom-call(s32[1]{0:T(128)} %bitcast.place.refs_0_, f32[32,70,112]{2,1,0:T(8,128)S(1)} %all-to-all-done.1.refs_0_.got, ...), custom_call_target="tpu_custom_call" | custom-call | tf_op jit(solution)/shard_map/query_grad/pallas_call | solution.py:66
  78.1 2.7 %collective-permute-start.10 = (f32[128,256]{1,0:T(8,128)}, f32[128,256]{1,0:T(8,128)S(1)}, u32[]{:S(2)}, u32[]{:S(2)}) collective-permute-start(f32[128,256]{1,0:T(8,128)} %get-tuple-element.77), channel_id=1, source_target_pairs={{0,64},{32,96},{64,0},{96,32},{1,65},{33,97},{65,1},{97,33},{2,66}... | collective-permute-start | bytes 393224 | tf_op jit(solution)/shard_map/ppermute | solution.py:327
  82.8 4.0 %join.1.refs_1_ = bf16[1120,1024]{1,0:T(8,128)(2,1)} custom-call(f32[1120,128]{1,0:T(8,128)} %get-tuple-element.64.refs_0_, f32[1120,128]{1,0:T(8,128)S(1)} %collective-permute-done.refs_1_, f32[1120,128]{1,0:T(8,128)} %collective-permute-done.7.refs_2_, f32[1120,128]{1,0:T(8,128)} %collective-permute-done.5.refs_3_, ...), custom_call_target="tpu_custom_call" | custom-call | tf_op jit(solution)/shard_map/join/pallas_call | solution.py:66
  90.4 2.3 %key_value_grad.1 = (bf16[128,1120]{1,0:T(8,128)(2,1)}, bf16[128,1120]{1,0:T(8,128)(2,1)}, f32[4,128,640]{2,1,0:T(8,128)}) custom-call(f32[32,45,112]{2,1,0:T(8,128)S(1)} %all-to-all-done.2.got, bf16[10,128,112]{2,1,0:T(8,128)(2,1)S(1)} %copy-done.3, bf16[10,128,112]{2,1,0:T(8,128)(2,1)S(1)} %copy-done.4, f32[4,128,24]{2,1,0:T(8,128)S(1)} %copy-done.5), custom_call_target="tpu_custom_call" | custom-call | tf_op jit(solution)/shard_map/key_value_grad/pallas_call | solution.py:66
  92.7 4.8 %all-to-all-start.3 = ((f32[4,128,640]{2,1,0:T(8,128)}), f32[4,128,640]{2,1,0:T(8,128)S(1)}, u32[]{:S(2)}, u32[]{:S(2)}) async-start(f32[4,128,640]{2,1,0:T(8,128)} %get-tuple-element.86.refs_4_), calls=%async_computation.3 | async-start | bytes 2621440 | tf_op jit(solution)/shard_map/all_to_all | solution.py:323
  97.5 1.9 %collective-permute-done.12.refs_3_ = f32[512,256]{1,0:T(8,128)S(1)} collective-permute-done((f32[512,256]{1,0:T(8,128)S(1)}, f32[512,256]{1,0:T(8,128)S(1)}, u32[]{:S(2)}, u32[]{:S(2)}) %collective-permute-start.12) | collective-permute-done | bytes 524320 | tf_op jit(solution)/shard_map/ppermute | solution.py:335
  99.4 3.4 %query_product.1 = (f32[4,72,256]{2,1,0:T(8,128)}, f32[4,72,256]{2,1,0:T(8,128)}, f32[4,72,256]{2,1,0:T(8,128)}, f32[4,72,256]{2,1,0:T(8,128)}) custom-call(s32[1]{0:T(128)} %bitcast.5.refs_0_, bf16[1120,1024]{1,0:T(8,128)(2,1)} %join.1.refs_1_, f32[512,256]{1,0:T(8,128)} %pack_query.1.refs_2_, f32[512,256]{1,0:T(8,128)S(1)} %collective-permute-done.12.refs_3_, ...), custom_call_target="tpu_custom_call" | custom-call | tf_op jit(solution)/shard_map/query_product/pallas_call | solution.py:66
  102.8 3.2 %collective-permute-start.13 = (f32[4,72,256]{2,1,0:T(8,128)}, f32[4,72,256]{2,1,0:T(8,128)S(1)}, u32[]{:S(2)}, u32[]{:S(2)}) collective-permute-start(f32[4,72,256]{2,1,0:T(8,128)} %get-tuple-element.89), channel_id=1, source_target_pairs={{0,4},{2,6},{4,0},{6,2},{1,5},{3,7},{5,1},{7,3},{8,12},{10,14},{12... | collective-permute-start | bytes 884744 | tf_op jit(solution)/shard_map/ppermute | solution.py:327
  106.5 2.7 %collective-permute-start.15 = (f32[4,72,256]{2,1,0:T(8,128)}, f32[4,72,256]{2,1,0:T(8,128)S(1)}, u32[]{:S(2)}, u32[]{:S(2)}) collective-permute-start(f32[4,72,256]{2,1,0:T(8,128)} %get-tuple-element.91), channel_id=1, source_target_pairs={{0,6},{2,0},{4,2},{6,4},{1,7},{3,1},{5,3},{7,5},{8,14},{10,8},{12,... | collective-permute-start | bytes 884744 | tf_op jit(solution)/shard_map/ppermute | solution.py:327
  109.2 5.2 %collective-permute-done.13.first = f32[4,72,256]{2,1,0:T(8,128)S(1)} collective-permute-done((f32[4,72,256]{2,1,0:T(8,128)}, f32[4,72,256]{2,1,0:T(8,128)S(1)}, u32[]{:S(2)}, u32[]{:S(2)}) %collective-permute-start.13) | collective-permute-done | bytes 294944 | tf_op jit(solution)/shard_map/ppermute | solution.py:327
  114.4 5.5 %collective-permute-done.14.second = f32[4,72,256]{2,1,0:T(8,128)S(1)} collective-permute-done((f32[4,72,256]{2,1,0:T(8,128)}, f32[4,72,256]{2,1,0:T(8,128)S(1)}, u32[]{:S(2)}, u32[]{:S(2)}) %collective-permute-start.14) | collective-permute-done | bytes 294944 | tf_op jit(solution)/shard_map/ppermute | solution.py:327
  123.1 4.7 %key_value_product.1 = f32[16,72,640]{2,1,0:T(8,128)} custom-call(s32[1]{0:T(128)} %bitcast.place.refs_0_, bf16[1120,1024]{1,0:T(8,128)(2,1)} %join.1.refs_1_, f32[4,128,640]{2,1,0:T(8,128)S(1)} %all-to-all-done.3.refs_2_, f32[4,128,640]{2,1,0:T(8,128)S(1)} %collective-permute-done.16.refs_3_, f32[72,256]{1,0:T(8,128)} %get-tuple-element.97.refs_4_.own), custom_call_target="tpu_custom_call" | custom-call | tf_op jit(solution)/shard_map/key_value_product/pallas_call | solution.py:66
  127.8 6.6 %all-to-all-start.4 = ((f32[16,72,640]{2,1,0:T(8,128)}), f32[16,72,640]{2,1,0:T(8,128)S(1)}, u32[]{:S(2)}, u32[]{:S(2)}) async-start(f32[16,72,640]{2,1,0:T(8,128)} %key_value_product.1), calls=%async_computation.4 | async-start | bytes 5898240 | tf_op jit(solution)/shard_map/all_to_all | solution.py:323
  134.5 4.2 %fusion.1 = f32[128,2240]{0,1:T(8,128)S(1)} fusion(bf16[128,1120]{1,0:T(8,128)(2,1)S(1)} %copy-done.9, bf16[2240,1120]{1,0:T(8,128)(2,1)} %key_weight.1), kind=kOutput, calls=%fused_computation.3 | convolution fusion | flops 642252800 | bytes 6451200 | tf_op jit(solution)/shard_map/dot_general | solution.py:72
  138.7 4.1 %convolution_add_fusion.1 = f32[128,2240]{0,1:T(8,128)S(1)} fusion(f32[128,2240]{0,1:T(8,128)S(1)} %fusion.1, bf16[128,1120]{1,0:T(8,128)(2,1)S(1)} %copy-done.10, bf16[2240,1120]{1,0:T(8,128)(2,1)} %weight.1), kind=kOutput, calls=%fused_computation.1 | convolution fusion | flops 642539520 | bytes 7598080 | tf_op jit(solution)/shard_map/dot_general | solution.py:72
  142.8 2.0 %collective-permute-start.17 = (f32[72,256]{1,0:T(8,128)S(1)}, f32[72,256]{1,0:T(8,128)S(1)}, u32[]{:S(2)}, u32[]{:S(2)}) collective-permute-start(f32[72,256]{1,0:T(8,128)S(1)} %copy-done.14), channel_id=1, source_target_pairs={{0,1},{1,16},{16,17},{17,0},{2,3},{3,18},{18,19},{19,2},{4,5},{5,2... | collective-permute-start | bytes 221192 | tf_op jit(solution)/shard_map/ppermute | solution.py:327
  144.8 2.7 %collective-permute-start.18 = (f32[72,256]{1,0:T(8,128)S(1)}, f32[72,256]{1,0:T(8,128)S(1)}, u32[]{:S(2)}, u32[]{:S(2)}) collective-permute-start(f32[72,256]{1,0:T(8,128)S(1)} %copy-done.13), channel_id=1, source_target_pairs={{0,16},{1,17},{16,0},{17,1},{2,18},{3,19},{18,2},{19,3},{4,20},{5,... | collective-permute-start | bytes 221192 | tf_op jit(solution)/shard_map/ppermute | solution.py:327
  149.0 2.4 %fusion = bf16[128,2240]{0,1:T(8,128)(2,1)} fusion(f32[128,2240]{0,1:T(8,128)S(1)} %convolution_add_fusion.1, bf16[128,1120]{1,0:T(8,128)(2,1)S(1)} %copy-done.8, bf16[2240,1120]{1,0:T(8,128)(2,1)S(1)} %bitcast.16), kind=kOutput, calls=%fused_computation.2 | convolution fusion | flops 642826240 | bytes 7024640 | tf_op jit(solution)/shard_map/dot_general | solution.py:72
  151.4 2.1 %copy.10 = bf16[128,2240]{1,0:T(8,128)(2,1)} copy(bf16[128,2240]{0,1:T(8,128)(2,1)} %fusion) | data formatting | bytes 1146880 | tf_op jit(solution)/shard_map/convert_element_type | solution.py:509
  153.5 18.4 %collective-permute-done.17.first = f32[72,256]{1,0:T(8,128)S(1)} collective-permute-done((f32[72,256]{1,0:T(8,128)S(1)}, f32[72,256]{1,0:T(8,128)S(1)}, u32[]{:S(2)}, u32[]{:S(2)}) %collective-permute-start.17) | collective-permute-done | bytes 73760 | tf_op jit(solution)/shard_map/ppermute | solution.py:327
  171.8 4.5 %all-to-all-done.4.key_value = f32[16,72,640]{2,1,0:T(8,128)S(1)} async-done(((f32[16,72,640]{2,1,0:T(8,128)}), f32[16,72,640]{2,1,0:T(8,128)S(1)}, u32[]{:S(2)}, u32[]{:S(2)}) %all-to-all-start.4) | async-done | bytes 2949152 | tf_op jit(solution)/shard_map/all_to_all | solution.py:323
  (70 shorter events, 23.9 us)
Async XLA Ops:
  10.7 10.0 %collective-permute-start.1 = (f32[1120,128]{1,0:T(8,128)}, f32[1120,128]{1,0:T(8,128)S(1)}, u32[]{:S(2)}, u32[]{:S(2)}) collective-permute-start(f32[1120,128]{1,0:T(8,128)} %get-tuple-element.59), channel_id=1, source_target_pairs={{0,8},{8,0},{1,9},{9,1},{2,10},{10,2},{3,11},{11,3},{4,12},{12,4},... | collective-permute-start | bytes 1720328 | tf_op jit(solution)/shard_map/ppermute | solution.py:335
  10.7 22.8 %all-to-all-start = ((f32[32,45,112]{2,1,0:T(8,128)}), f32[32,45,112]{2,1,0:T(8,128)S(1)}, u32[]{:S(2)}, u32[]{:S(2)}) async-start(f32[32,45,112]{2,1,0:T(8,128)} %get-tuple-element.55), calls=%async_computation | async-start | bytes 1572864 | tf_op jit(solution)/shard_map/all_to_all | solution.py:323
  19.0 14.5 %copy-start.2 = (bf16[1,16,8,1120]{3,2,1,0:T(8,128)(2,1)S(1)}, bf16[1,16,8,1120]{3,2,1,0:T(8,128)(2,1)}, u32[]{:S(2)}) copy-start(bf16[1,16,8,1120]{3,2,1,0:T(8,128)(2,1)} %param.9) | copy-start | bytes 860164
  19.0 19.6 %copy-start.11 = (f32[1120,128]{1,0:T(8,128)S(1)}, f32[1120,128]{1,0:T(8,128)}, u32[]{:S(2)}) copy-start(f32[1120,128]{1,0:T(8,128)} %get-tuple-element.64.refs_0_) | copy-start | bytes 1720324
  19.0 17.9 %collective-permute-start = (f32[1120,128]{1,0:T(8,128)}, f32[1120,128]{1,0:T(8,128)S(1)}, u32[]{:S(2)}, u32[]{:S(2)}) collective-permute-start(f32[1120,128]{1,0:T(8,128)} %get-tuple-element.64.refs_0_), channel_id=1, source_target_pairs={{0,32},{32,64},{64,96},{96,0},{1,33},{33,65},{65,97},{97,1},{2,34}... | collective-permute-start | bytes 1720328 | tf_op jit(solution)/shard_map/ppermute | solution.py:327
  20.7 16.3 %collective-permute-start.2 = (f32[1120,128]{1,0:T(8,128)S(1)}, f32[1120,128]{1,0:T(8,128)}, u32[]{:S(2)}, u32[]{:S(2)}) collective-permute-start(f32[1120,128]{1,0:T(8,128)S(1)} %collective-permute-done.1.refs_4_), channel_id=1, source_target_pairs={{0,96},{32,0},{64,32},{96,64},{1,97},{33,1},{65,33},{97,65},{2,98}... | collective-permute-start | bytes 1720328 | tf_op jit(solution)/shard_map/ppermute | solution.py:327
  34.5 29.3 %copy-start.1 = (bf16[10,128,112]{2,1,0:T(8,128)(2,1)S(1)}, bf16[10,128,112]{2,1,0:T(8,128)(2,1)}, u32[]{:S(2)}) copy-start(bf16[10,128,112]{2,1,0:T(8,128)(2,1)} %query.1.refs_1_) | copy-start | bytes 860164
  37.0 26.8 %copy-start.6 = (f32[10,112]{1,0:T(8,128)S(1)}, f32[10,112]{1,0:T(8,128)}, u32[]{:S(2)}) copy-start(f32[10,112]{1,0:T(8,128)} %get-tuple-element.62.refs_3_.total) | copy-start | bytes 13444
  37.0 14.1 %collective-permute-start.3 = (f32[1120,128]{1,0:T(8,128)S(1)}, f32[1120,128]{1,0:T(8,128)}, u32[]{:S(2)}, u32[]{:S(2)}) collective-permute-start(f32[1120,128]{1,0:T(8,128)S(1)} %collective-permute-done.1.refs_4_), channel_id=1, source_target_pairs={{0,32},{32,64},{64,96},{96,0},{1,33},{33,65},{65,97},{97,1},{2,34}... | collective-permute-start | bytes 1720328 | tf_op jit(solution)/shard_map/ppermute | solution.py:327
  38.6 13.7 %collective-permute-start.5 = (f32[1120,128]{1,0:T(8,128)S(1)}, f32[1120,128]{1,0:T(8,128)}, u32[]{:S(2)}, u32[]{:S(2)}) collective-permute-start(f32[1120,128]{1,0:T(8,128)S(1)} %copy-done.11), channel_id=1, source_target_pairs={{0,96},{32,0},{64,32},{96,64},{1,97},{33,1},{65,33},{97,65},{2,98}... | collective-permute-start | bytes 1720328 | tf_op jit(solution)/shard_map/ppermute | solution.py:327
  39.1 24.7 %all-to-all-start.1 = ((f32[32,70,112]{2,1,0:T(8,128)}), f32[32,70,112]{2,1,0:T(8,128)S(1)}, u32[]{:S(2)}, u32[]{:S(2)}) async-start(f32[32,70,112]{2,1,0:T(8,128)} %get-tuple-element.60), calls=%async_computation.1 | async-start | bytes 2359296 | tf_op jit(solution)/shard_map/all_to_all | solution.py:323
  51.1 12.7 %collective-permute-start.4 = (f32[1120,128]{1,0:T(8,128)}, f32[1120,128]{1,0:T(8,128)}, u32[]{:S(2)}, u32[]{:S(2)}) collective-permute-start(f32[1120,128]{1,0:T(8,128)} %collective-permute-done.3.refs_5_), channel_id=1, source_target_pairs={{0,8},{8,0},{1,9},{9,1},{2,10},{10,2},{3,11},{11,3},{4,12},{12,4},... | collective-permute-start | bytes 1720328 | tf_op jit(solution)/shard_map/ppermute | solution.py:335
  52.4 11.4 %collective-permute-start.6 = (f32[1120,128]{1,0:T(8,128)}, f32[1120,128]{1,0:T(8,128)}, u32[]{:S(2)}, u32[]{:S(2)}) collective-permute-start(f32[1120,128]{1,0:T(8,128)} %collective-permute-done.5.refs_3_), channel_id=1, source_target_pairs={{0,8},{8,0},{1,9},{9,1},{2,10},{10,2},{3,11},{11,3},{4,12},{12,4},... | collective-permute-start | bytes 1720328 | tf_op jit(solution)/shard_map/ppermute | solution.py:335
  52.4 15.5 %collective-permute-start.7 = (f32[1120,128]{1,0:T(8,128)S(1)}, f32[1120,128]{1,0:T(8,128)}, u32[]{:S(2)}, u32[]{:S(2)}) collective-permute-start(f32[1120,128]{1,0:T(8,128)S(1)} %collective-permute-done.refs_1_), channel_id=1, source_target_pairs={{0,32},{32,64},{64,96},{96,0},{1,33},{33,65},{65,97},{97,1},{2,34}... | collective-permute-start | bytes 1720328 | tf_op jit(solution)/shard_map/ppermute | solution.py:327
  53.7 15.4 %collective-permute-start.8 = (f32[1120,128]{1,0:T(8,128)}, f32[1120,128]{1,0:T(8,128)}, u32[]{:S(2)}, u32[]{:S(2)}) collective-permute-start(f32[1120,128]{1,0:T(8,128)} %collective-permute-done.2.refs_7_), channel_id=1, source_target_pairs={{0,96},{32,0},{64,32},{96,64},{1,97},{33,1},{65,33},{97,65},{2,98}... | collective-permute-start | bytes 1720328 | tf_op jit(solution)/shard_map/ppermute | solution.py:327
  69.1 21.3 %all-to-all-start.2 = ((f32[32,45,112]{2,1,0:T(8,128)}), f32[32,45,112]{2,1,0:T(8,128)S(1)}, u32[]{:S(2)}, u32[]{:S(2)}) async-start(f32[32,45,112]{2,1,0:T(8,128)} %get-tuple-element.70), calls=%async_computation.2 | async-start | bytes 1572864 | tf_op jit(solution)/shard_map/all_to_all | solution.py:323
  78.1 8.7 %collective-permute-start.10 = (f32[128,256]{1,0:T(8,128)}, f32[128,256]{1,0:T(8,128)S(1)}, u32[]{:S(2)}, u32[]{:S(2)}) collective-permute-start(f32[128,256]{1,0:T(8,128)} %get-tuple-element.77), channel_id=1, source_target_pairs={{0,64},{32,96},{64,0},{96,32},{1,65},{33,97},{65,1},{97,33},{2,66}... | collective-permute-start | bytes 393224 | tf_op jit(solution)/shard_map/ppermute | solution.py:327
  80.8 7.5 %collective-permute-start.11 = (f32[128,256]{1,0:T(8,128)}, f32[128,256]{1,0:T(8,128)S(1)}, u32[]{:S(2)}, u32[]{:S(2)}) collective-permute-start(f32[128,256]{1,0:T(8,128)} %get-tuple-element.78), channel_id=1, source_target_pairs={{0,96},{32,0},{64,32},{96,64},{1,97},{33,1},{65,33},{97,65},{2,98}... | collective-permute-start | bytes 393224 | tf_op jit(solution)/shard_map/ppermute | solution.py:327
  81.9 6.7 %collective-permute-start.9 = (f32[128,256]{1,0:T(8,128)}, f32[128,256]{1,0:T(8,128)S(1)}, u32[]{:S(2)}, u32[]{:S(2)}) collective-permute-start(f32[128,256]{1,0:T(8,128)} %get-tuple-element.76), channel_id=1, source_target_pairs={{0,32},{32,64},{64,96},{96,0},{1,33},{33,65},{65,97},{97,1},{2,34}... | collective-permute-start | bytes 393224 | tf_op jit(solution)/shard_map/ppermute | solution.py:327
  92.7 27.4 %all-to-all-start.3 = ((f32[4,128,640]{2,1,0:T(8,128)}), f32[4,128,640]{2,1,0:T(8,128)S(1)}, u32[]{:S(2)}, u32[]{:S(2)}) async-start(f32[4,128,640]{2,1,0:T(8,128)} %get-tuple-element.86.refs_4_), calls=%async_computation.3 | async-start | bytes 2621440 | tf_op jit(solution)/shard_map/all_to_all | solution.py:323
  97.5 1.9 %collective-permute-start.12 = (f32[512,256]{1,0:T(8,128)S(1)}, f32[512,256]{1,0:T(8,128)S(1)}, u32[]{:S(2)}, u32[]{:S(2)}) collective-permute-start(f32[512,256]{1,0:T(8,128)S(1)} %copy-done.7), channel_id=1, source_target_pairs={{0,8},{8,0},{1,9},{9,1},{2,10},{10,2},{3,11},{11,3},{4,12},{12,4},... | collective-permute-start | bytes 1572872 | tf_op jit(solution)/shard_map/ppermute | solution.py:335
  102.8 11.6 %collective-permute-start.13 = (f32[4,72,256]{2,1,0:T(8,128)}, f32[4,72,256]{2,1,0:T(8,128)S(1)}, u32[]{:S(2)}, u32[]{:S(2)}) collective-permute-start(f32[4,72,256]{2,1,0:T(8,128)} %get-tuple-element.89), channel_id=1, source_target_pairs={{0,4},{2,6},{4,0},{6,2},{1,5},{3,7},{5,1},{7,3},{8,12},{10,14},{12... | collective-permute-start | bytes 884744 | tf_op jit(solution)/shard_map/ppermute | solution.py:327
  105.9 13.9 %collective-permute-start.14 = (f32[4,72,256]{2,1,0:T(8,128)}, f32[4,72,256]{2,1,0:T(8,128)S(1)}, u32[]{:S(2)}, u32[]{:S(2)}) collective-permute-start(f32[4,72,256]{2,1,0:T(8,128)} %get-tuple-element.90), channel_id=1, source_target_pairs={{0,2},{2,4},{4,6},{6,0},{1,3},{3,5},{5,7},{7,1},{8,10},{10,12},{12... | collective-permute-start | bytes 884744 | tf_op jit(solution)/shard_map/ppermute | solution.py:327
  106.5 13.6 %collective-permute-start.15 = (f32[4,72,256]{2,1,0:T(8,128)}, f32[4,72,256]{2,1,0:T(8,128)S(1)}, u32[]{:S(2)}, u32[]{:S(2)}) collective-permute-start(f32[4,72,256]{2,1,0:T(8,128)} %get-tuple-element.91), channel_id=1, source_target_pairs={{0,6},{2,0},{4,2},{6,4},{1,7},{3,1},{5,3},{7,5},{8,14},{10,8},{12,... | collective-permute-start | bytes 884744 | tf_op jit(solution)/shard_map/ppermute | solution.py:327
  120.1 3.0 %collective-permute-start.16 = (f32[4,128,640]{2,1,0:T(8,128)S(1)}, f32[4,128,640]{2,1,0:T(8,128)S(1)}, u32[]{:S(2)}, u32[]{:S(2)}) collective-permute-start(f32[4,128,640]{2,1,0:T(8,128)S(1)} %all-to-all-done.3.refs_2_), channel_id=1, source_target_pairs={{0,8},{8,0},{1,9},{9,1},{2,10},{10,2},{3,11},{11,3},{4,12},{12,4},... | collective-permute-start | bytes 3932168 | tf_op jit(solution)/shard_map/ppermute | solution.py:335
  127.8 48.6 %all-to-all-start.4 = ((f32[16,72,640]{2,1,0:T(8,128)}), f32[16,72,640]{2,1,0:T(8,128)S(1)}, u32[]{:S(2)}, u32[]{:S(2)}) async-start(f32[16,72,640]{2,1,0:T(8,128)} %key_value_product.1), calls=%async_computation.4 | async-start | bytes 5898240 | tf_op jit(solution)/shard_map/all_to_all | solution.py:323
  134.4 14.5 %slice-start = ((s8[5160960]{0:T(1024)(128)(4,1)}), s8[4194304]{0:T(1024)(128)(4,1)S(1)}, s32[]{:S(2)}) async-start(s8[5160960]{0:T(1024)(128)(4,1)} %bitcast.15), calls=%async_computation.5 | async-start | bytes 8388608
  138.7 10.3 %slice-start.1 = ((s8[5160960]{0:T(1024)(128)(4,1)}), s8[966656]{0:T(1024)(128)(4,1)S(1)}, s32[]{:S(2)}) async-start(s8[5160960]{0:T(1024)(128)(4,1)} %bitcast.15), calls=%async_computation.6 | async-start | bytes 1933312
  138.7 10.3 %copy-start.8 = (bf16[128,1120]{1,0:T(8,128)(2,1)S(1)}, bf16[128,1120]{1,0:T(8,128)(2,1)}, u32[]{:S(2)}) copy-start(bf16[128,1120]{1,0:T(8,128)(2,1)} %get-tuple-element.84) | copy-start | bytes 860164
  142.8 29.0 %collective-permute-start.17 = (f32[72,256]{1,0:T(8,128)S(1)}, f32[72,256]{1,0:T(8,128)S(1)}, u32[]{:S(2)}, u32[]{:S(2)}) collective-permute-start(f32[72,256]{1,0:T(8,128)S(1)} %copy-done.14), channel_id=1, source_target_pairs={{0,1},{1,16},{16,17},{17,0},{2,3},{3,18},{18,19},{19,2},{4,5},{5,2... | collective-permute-start | bytes 221192 | tf_op jit(solution)/shard_map/ppermute | solution.py:327
  144.8 27.0 %collective-permute-start.18 = (f32[72,256]{1,0:T(8,128)S(1)}, f32[72,256]{1,0:T(8,128)S(1)}, u32[]{:S(2)}, u32[]{:S(2)}) collective-permute-start(f32[72,256]{1,0:T(8,128)S(1)} %copy-done.13), channel_id=1, source_target_pairs={{0,16},{1,17},{16,0},{17,1},{2,18},{3,19},{18,2},{19,3},{4,20},{5,... | collective-permute-start | bytes 221192 | tf_op jit(solution)/shard_map/ppermute | solution.py:327
  147.5 24.3 %collective-permute-start.19 = (f32[72,256]{1,0:T(8,128)S(1)}, f32[72,256]{1,0:T(8,128)S(1)}, u32[]{:S(2)}, u32[]{:S(2)}) collective-permute-start(f32[72,256]{1,0:T(8,128)S(1)} %copy-done.12), channel_id=1, source_target_pairs={{0,17},{1,0},{16,1},{17,16},{2,19},{3,2},{18,3},{19,18},{4,21},{5,... | collective-permute-start | bytes 221192 | tf_op jit(solution)/shard_map/ppermute | solution.py:327
  (10 other events, 63.4 us)

commit v13 on v12

--- a/solution.py
+++ b/solution.py
@@ -371,12 +371,11 @@
     )(tokens, key_weight, value_weight)
     sent, later_tokens = lax.optimization_barrier((sent, tokens))
     half = shaped((D // 2, TOKENS))
-    top, bottom = call(
+    top, other = call(
         turn_kernel, "turn", [half, half], [IN_SMEM, BLOCK], [pltpu.VMEM((D, TOKENS), F32)]
     )(core, later_tokens)
-    bottom = swap_cores(bottom)
     left_top = shift(top, 1, "dp")
-    right_bottom = shift(bottom, 3, "dp")
+    right_other = shift(other, 3, "dp")
     got = exchange(sent, IMAGE)
     (query,) = call(
         query_kernel,
@@ -392,12 +391,12 @@
         [state],
         arrived=(0, 1, 2),
     )(got, query, upstream)
-    sent, left_top, right_bottom, later_top, later_bottom = lax.optimization_barrier(
-        (sent, left_top, right_bottom, top, bottom)
+    sent, left_top, right_other, later_top, later_other = lax.optimization_barrier(
+        (sent, left_top, right_other, top, other)
     )
     far_top = shift(left_top, 1, "dp")
-    far_bottom = shift(right_bottom, 3, "dp")
-    left_bottom = shift(later_bottom, 1, "dp")
+    far_other = shift(right_other, 3, "dp")
+    left_bottom = swap_cores(shift(later_other, 1, "dp"))
     right_top = shift(later_top, 3, "dp")
     got_state = exchange(sent, IMAGE)
     sent, grad_denom = call(
@@ -407,9 +406,12 @@
         [BLOCK] * 4 + [ANYWHERE] * 2,
         [state, totals],
         arrived=(0, 1, 2, 3, 4, 5),
-    )(got_state, query, upstream, total, swap_cores(left_bottom), swap_cores(right_top))
-    sent, far_top, far_bottom, left_bottom, right_top = lax.optimization_barrier(
-        (sent, far_top, far_bottom, left_bottom, right_top)
+    )(got_state, query, upstream, total, left_bottom, swap_cores(right_top))
+    sent, far_top, far_other, left_bottom, right_top = lax.optimization_barrier(
+        (sent, far_top, far_other, left_bottom, right_top)
+    )
+    bottom, right_bottom, far_bottom = (
+        swap_cores(rows) for rows in (later_other, right_other, far_other)
     )
     got = exchange(sent, IMAGE)
 
@@ -431,12 +433,12 @@
         arrived=tuple(range(1, 8)),
     )(top, left_top, far_top, right_top, bottom, left_bottom, far_bottom, right_bottom)
     (query_columns,) = call(
-        pack_kernel,
+        lambda *refs: pack_kernel(*refs[:RING], refs[-1]),
         "pack_query",
         [shaped((REPLICAS * TOKENS, EARLY))],
-        [BLOCK] * RING,
+        [BLOCK] * RING + [ANYWHERE],
         arrived=(1, 2, 3),
-    )(*query_columns)
+    )(*query_columns, rows)
     got, rows, query_columns = lax.optimization_barrier((got, rows, query_columns))
 
     grad_key, grad_value, sent = call(

time: 179 us -> 180 us (level)
  starting transfers between devices: 55.1 us -> 58.3 us
  waiting for transfers between devices: 66.3 us -> 64.2 us
    all_to_all x5, starting transfers between devices: 31.7 us -> 33.6 us  [exchange(): return lax.all_to_all(blocks, axes, 0, 0, tiled=True)]
  transfers between devices with their start and end apart: 25 -> 27, of which waited for: 15 -> 16; matrix products, arithmetic and copies ran while one was open for 7% -> 7% of each run, Pallas kernels for 13% -> 14%
where the time goes in v13:
time: 180 us; the launch traced here: 179 us
  waiting for transfers between devices  64.2 us (36%)
  starting transfers between devices  58.3 us (32%)
  Pallas kernels  41.9 us (23%)
  matrix products  10.7 us (6%)
  local copies, waits for them, and re-layouts  3.16 us (2%)
    pallas_call x13, Pallas kernels, with_placed(): return run(*placed)  41.9 us
    ppermute x15, waiting for transfers between devices, shift(): lax.ppermute(values, axis, [(i, (i + by) % RING) for i in range(RING)])  40 us
    all_to_all x5, starting transfers between devices, exchange(): return lax.all_to_all(blocks, axes, 0, 0, tiled=True)  33.6 us
    ppermute x15, starting transfers between devices, shift(): lax.ppermute(values, axis, [(i, (i + by) % RING) for i in range(RING)])  24.1 us
    all_to_all x5, waiting for transfers between devices, exchange(): return lax.all_to_all(blocks, axes, 0, 0, tiled=True)  21 us
    dot_general x3, matrix products, dot(): lax.dot_general(left, right, (((left_dim,), (right_dim,)), ((), ())), pre...  10.7 us
  transfers between devices with their start and end apart: 27, of which 16 were waited for; matrix products, arithmetic and copies ran while one was open for 7% of the time, Pallas kernels for 14%

profile of v13, /device:TPU:8, one launch (start us, length us, event | category | flops | bytes accessed | tf_op | source)
XLA Modules:
  0.0 179.1 jit_solution(10472414309056353042)
XLA Ops:
  0.6 7.7 %key_value.1 = (bf16[10,128,112]{2,1,0:T(8,128)(2,1)}, bf16[10,128,112]{2,1,0:T(8,128)(2,1)}, f32[32,45,112]{2,1,0:T(8,128)}) custom-call(bf16[128,2240]{1,0:T(8,128)(2,1)} %bitcast.17, bf16[2240,1120]{1,0:T(8,128)(2,1)} %key_weight.1, bf16[2240,1120]{1,0:T(8,128)(2,1)} %value_weight.1), custom_call_target="tpu_custom_call" | custom-call | tf_op jit(solution)/shard_map/key_value/pallas_call | solution.py:66
  8.4 8.2 %all-to-all-start = ((f32[32,45,112]{2,1,0:T(8,128)}), f32[32,45,112]{2,1,0:T(8,128)S(1)}, u32[]{:S(2)}, u32[]{:S(2)}) async-start(f32[32,45,112]{2,1,0:T(8,128)} %get-tuple-element.55), calls=%async_computation | async-start | bytes 1572864 | tf_op jit(solution)/shard_map/all_to_all | solution.py:323
  16.6 2.3 %turn.1 = (f32[1120,128]{1,0:T(8,128)}, f32[1120,128]{1,0:T(8,128)}) custom-call(s32[1]{0:T(128)} %bitcast.3.core, bf16[128,2240]{1,0:T(8,128)(2,1)} %bitcast.18), custom_call_target="tpu_custom_call" | custom-call | tf_op jit(solution)/shard_map/turn/pallas_call | solution.py:66
  20.9 4.4 %query.1.refs_1_ = bf16[10,128,112]{2,1,0:T(8,128)(2,1)} custom-call(bf16[128,2240]{1,0:T(8,128)(2,1)} %bitcast.19, bf16[2240,1120]{1,0:T(8,128)(2,1)} %weight.1), custom_call_target="tpu_custom_call" | custom-call | tf_op jit(solution)/shard_map/query/pallas_call | solution.py:66
  25.3 5.8 %all-to-all-done.refs_0_ = f32[32,45,112]{2,1,0:T(8,128)S(1)} async-done(((f32[32,45,112]{2,1,0:T(8,128)}), f32[32,45,112]{2,1,0:T(8,128)S(1)}, u32[]{:S(2)}, u32[]{:S(2)}) %all-to-all-start) | async-done | bytes 645152 | tf_op jit(solution)/shard_map/all_to_all | solution.py:323
  32.0 2.4 %numerator.1 = (f32[32,70,112]{2,1,0:T(8,128)}, bf16[10,128,112]{2,1,0:T(8,128)(2,1)}, f32[10,112]{1,0:T(8,128)}) custom-call(f32[32,45,112]{2,1,0:T(8,128)S(1)} %all-to-all-done.refs_0_, bf16[10,128,112]{2,1,0:T(8,128)(2,1)S(1)} %copy-done, bf16[128,1120]{1,0:T(8,128)(2,1)S(1)} %bitcast.13), custom_call_target="tpu_custom_call" | custom-call | tf_op jit(solution)/shard_map/numerator/pallas_call | solution.py:66
  37.6 7.3 %all-to-all-start.1 = ((f32[32,70,112]{2,1,0:T(8,128)}), f32[32,70,112]{2,1,0:T(8,128)S(1)}, u32[]{:S(2)}, u32[]{:S(2)}) async-start(f32[32,70,112]{2,1,0:T(8,128)} %get-tuple-element.60), calls=%async_computation.1 | async-start | bytes 2359296 | tf_op jit(solution)/shard_map/all_to_all | solution.py:323
  44.9 5.0 %collective-permute-done.2 = f32[1120,128]{1,0:T(8,128)} collective-permute-done((f32[1120,128]{1,0:T(8,128)}, f32[1120,128]{1,0:T(8,128)}, u32[]{:S(2)}, u32[]{:S(2)}) %collective-permute-start.2) | collective-permute-done | bytes 573472 | tf_op jit(solution)/shard_map/ppermute | solution.py:327
  53.0 10.7 %all-to-all-done.1.refs_0_.got = f32[32,70,112]{2,1,0:T(8,128)S(1)} async-done(((f32[32,70,112]{2,1,0:T(8,128)}), f32[32,70,112]{2,1,0:T(8,128)S(1)}, u32[]{:S(2)}, u32[]{:S(2)}) %all-to-all-start.1) | async-done | bytes 1003552 | tf_op jit(solution)/shard_map/all_to_all | solution.py:323
  63.7 2.6 %total_grad.1 = (f32[32,45,112]{2,1,0:T(8,128)}, f32[128,10]{1,0:T(8,128)}) custom-call(f32[32,70,112]{2,1,0:T(8,128)S(1)} %all-to-all-done.1.refs_0_.got, bf16[10,128,112]{2,1,0:T(8,128)(2,1)S(1)} %copy-done.1, bf16[128,1120]{1,0:T(8,128)(2,1)S(1)} %bitcast.14, f32[10,112]{1,0:T(8,128)S(1)} %copy-done.6, ...), custom_call_target="tpu_custom_call" | custom-call | tf_op jit(solution)/shard_map/total_grad/pallas_call | solution.py:66
  68.0 7.1 %all-to-all-start.2 = ((f32[32,45,112]{2,1,0:T(8,128)}), f32[32,45,112]{2,1,0:T(8,128)S(1)}, u32[]{:S(2)}, u32[]{:S(2)}) async-start(f32[32,45,112]{2,1,0:T(8,128)} %get-tuple-element.70), calls=%async_computation.2 | async-start | bytes 1572864 | tf_op jit(solution)/shard_map/all_to_all | solution.py:323
  75.8 3.0 %query_grad.1 = (bf16[128,1120]{1,0:T(8,128)(2,1)}, f32[128,256]{1,0:T(8,128)}, f32[128,256]{1,0:T(8,128)}, f32[128,256]{1,0:T(8,128)}, f32[128,256]{1,0:T(8,128)}, /*index=5*/f32[4,128,24]{2,1,0:T(8,128)}) custom-call(s32[1]{0:T(128)} %bitcast.place.refs_0_, f32[32,70,112]{2,1,0:T(8,128)S(1)} %all-to-all-done.1.refs_0_.got, ...), custom_call_target="tpu_custom_call" | custom-call | tf_op jit(solution)/shard_map/query_grad/pallas_call | solution.py:66
  81.5 2.6 %collective-permute-start.13 = (f32[128,256]{1,0:T(8,128)}, f32[128,256]{1,0:T(8,128)S(1)}, u32[]{:S(2)}, u32[]{:S(2)}) collective-permute-start(f32[128,256]{1,0:T(8,128)} %get-tuple-element.78), channel_id=1, source_target_pairs={{0,96},{32,0},{64,32},{96,64},{1,97},{33,1},{65,33},{97,65},{2,98}... | collective-permute-start | bytes 393224 | tf_op jit(solution)/shard_map/ppermute | solution.py:327
  84.1 3.9 %join.1.refs_4_.refs_1_ = bf16[1120,1024]{1,0:T(8,128)(2,1)} custom-call(f32[1120,128]{1,0:T(8,128)} %get-tuple-element.64.refs_0_, f32[1120,128]{1,0:T(8,128)S(1)} %collective-permute-done.refs_1_, f32[1120,128]{1,0:T(8,128)} %collective-permute-done.6.refs_2_, f32[1120,128]{1,0:T(8,128)} %collective-permute-done.4.refs_3_, ...), custom_call_target="tpu_custom_call" | custom-call | tf_op jit(solution)/shard_map/join/pallas_call | solution.py:66
  91.6 2.3 %key_value_grad.1 = (bf16[128,1120]{1,0:T(8,128)(2,1)}, bf16[128,1120]{1,0:T(8,128)(2,1)}, f32[4,128,640]{2,1,0:T(8,128)}) custom-call(f32[32,45,112]{2,1,0:T(8,128)S(1)} %all-to-all-done.2.got, bf16[10,128,112]{2,1,0:T(8,128)(2,1)S(1)} %copy-done.3, bf16[10,128,112]{2,1,0:T(8,128)(2,1)S(1)} %copy-done.4, f32[4,128,24]{2,1,0:T(8,128)S(1)} %copy-done.5), custom_call_target="tpu_custom_call" | custom-call | tf_op jit(solution)/shard_map/key_value_grad/pallas_call | solution.py:66
  93.9 4.4 %all-to-all-start.3 = ((f32[4,128,640]{2,1,0:T(8,128)}), f32[4,128,640]{2,1,0:T(8,128)S(1)}, u32[]{:S(2)}, u32[]{:S(2)}) async-start(f32[4,128,640]{2,1,0:T(8,128)} %get-tuple-element.86.refs_4_), calls=%async_computation.3 | async-start | bytes 2621440 | tf_op jit(solution)/shard_map/all_to_all | solution.py:323
  98.4 1.9 %collective-permute-done.14.refs_3_ = f32[512,256]{1,0:T(8,128)S(1)} collective-permute-done((f32[512,256]{1,0:T(8,128)S(1)}, f32[512,256]{1,0:T(8,128)S(1)}, u32[]{:S(2)}, u32[]{:S(2)}) %collective-permute-start.14) | collective-permute-done | bytes 524320 | tf_op jit(solution)/shard_map/ppermute | solution.py:335
  100.3 3.3 %query_product.1 = (f32[4,72,256]{2,1,0:T(8,128)}, f32[4,72,256]{2,1,0:T(8,128)}, f32[4,72,256]{2,1,0:T(8,128)}, f32[4,72,256]{2,1,0:T(8,128)}) custom-call(s32[1]{0:T(128)} %bitcast.5.refs_0_, bf16[1120,1024]{1,0:T(8,128)(2,1)} %join.1.refs_4_.refs_1_, f32[512,256]{1,0:T(8,128)} %pack_query.1.refs_2_, f32[512,256]{1,0:T(8,128)S(1)} %collective-permute-done.14.refs_3_, ...), custom_call_target="tpu_custom_call" | custom-call | tf_op jit(solution)/shard_map/query_product/pallas_call | solution.py:66
  103.6 3.3 %collective-permute-start.15 = (f32[4,72,256]{2,1,0:T(8,128)}, f32[4,72,256]{2,1,0:T(8,128)S(1)}, u32[]{:S(2)}, u32[]{:S(2)}) collective-permute-start(f32[4,72,256]{2,1,0:T(8,128)} %get-tuple-element.89), channel_id=1, source_target_pairs={{0,4},{2,6},{4,0},{6,2},{1,5},{3,7},{5,1},{7,3},{8,12},{10,14},{12... | collective-permute-start | bytes 884744 | tf_op jit(solution)/shard_map/ppermute | solution.py:327
  107.5 2.7 %collective-permute-start.17 = (f32[4,72,256]{2,1,0:T(8,128)}, f32[4,72,256]{2,1,0:T(8,128)S(1)}, u32[]{:S(2)}, u32[]{:S(2)}) collective-permute-start(f32[4,72,256]{2,1,0:T(8,128)} %get-tuple-element.91), channel_id=1, source_target_pairs={{0,6},{2,0},{4,2},{6,4},{1,7},{3,1},{5,3},{7,5},{8,14},{10,8},{12,... | collective-permute-start | bytes 884744 | tf_op jit(solution)/shard_map/ppermute | solution.py:327
  110.2 5.1 %collective-permute-done.15.first = f32[4,72,256]{2,1,0:T(8,128)S(1)} collective-permute-done((f32[4,72,256]{2,1,0:T(8,128)}, f32[4,72,256]{2,1,0:T(8,128)S(1)}, u32[]{:S(2)}, u32[]{:S(2)}) %collective-permute-start.15) | collective-permute-done | bytes 294944 | tf_op jit(solution)/shard_map/ppermute | solution.py:327
  115.2 5.5 %collective-permute-done.16.second = f32[4,72,256]{2,1,0:T(8,128)S(1)} collective-permute-done((f32[4,72,256]{2,1,0:T(8,128)}, f32[4,72,256]{2,1,0:T(8,128)S(1)}, u32[]{:S(2)}, u32[]{:S(2)}) %collective-permute-start.16) | collective-permute-done | bytes 294944 | tf_op jit(solution)/shard_map/ppermute | solution.py:327
  124.1 4.7 %key_value_product.1 = f32[16,72,640]{2,1,0:T(8,128)} custom-call(s32[1]{0:T(128)} %bitcast.place.refs_0_, bf16[1120,1024]{1,0:T(8,128)(2,1)} %join.1.refs_4_.refs_1_, f32[4,128,640]{2,1,0:T(8,128)S(1)} %all-to-all-done.3.refs_2_, f32[4,128,640]{2,1,0:T(8,128)S(1)} %collective-permute-done.18.refs_3_, f32[72,256]{1,0:T(8,128)} %get-tuple-element.97.refs_4_.own), custom_call_target="tpu_custom_call" | custom-call | tf_op jit(solution)/shard_map/key_value_product/pallas_call | solution.py:66
  128.8 6.6 %all-to-all-start.4 = ((f32[16,72,640]{2,1,0:T(8,128)}), f32[16,72,640]{2,1,0:T(8,128)S(1)}, u32[]{:S(2)}, u32[]{:S(2)}) async-start(f32[16,72,640]{2,1,0:T(8,128)} %key_value_product.1), calls=%async_computation.4 | async-start | bytes 5898240 | tf_op jit(solution)/shard_map/all_to_all | solution.py:323
  135.4 4.2 %fusion.1 = f32[128,2240]{0,1:T(8,128)S(1)} fusion(bf16[128,1120]{1,0:T(8,128)(2,1)S(1)} %copy-done.9, bf16[2240,1120]{1,0:T(8,128)(2,1)} %key_weight.1), kind=kOutput, calls=%fused_computation.3 | convolution fusion | flops 642252800 | bytes 6451200 | tf_op jit(solution)/shard_map/dot_general | solution.py:72
  139.7 4.1 %convolution_add_fusion.1 = f32[128,2240]{0,1:T(8,128)S(1)} fusion(f32[128,2240]{0,1:T(8,128)S(1)} %fusion.1, bf16[128,1120]{1,0:T(8,128)(2,1)S(1)} %copy-done.10, bf16[2240,1120]{1,0:T(8,128)(2,1)} %weight.1), kind=kOutput, calls=%fused_computation.1 | convolution fusion | flops 642539520 | bytes 7598080 | tf_op jit(solution)/shard_map/dot_general | solution.py:72
  143.8 2.0 %collective-permute-start.19 = (f32[72,256]{1,0:T(8,128)S(1)}, f32[72,256]{1,0:T(8,128)S(1)}, u32[]{:S(2)}, u32[]{:S(2)}) collective-permute-start(f32[72,256]{1,0:T(8,128)S(1)} %copy-done.14), channel_id=1, source_target_pairs={{0,1},{1,16},{16,17},{17,0},{2,3},{3,18},{18,19},{19,2},{4,5},{5,2... | collective-permute-start | bytes 221192 | tf_op jit(solution)/shard_map/ppermute | solution.py:327
  145.8 2.7 %collective-permute-start.20 = (f32[72,256]{1,0:T(8,128)S(1)}, f32[72,256]{1,0:T(8,128)S(1)}, u32[]{:S(2)}, u32[]{:S(2)}) collective-permute-start(f32[72,256]{1,0:T(8,128)S(1)} %copy-done.13), channel_id=1, source_target_pairs={{0,16},{1,17},{16,0},{17,1},{2,18},{3,19},{18,2},{19,3},{4,20},{5,... | collective-permute-start | bytes 221192 | tf_op jit(solution)/shard_map/ppermute | solution.py:327
  149.9 2.4 %fusion = bf16[128,2240]{0,1:T(8,128)(2,1)} fusion(f32[128,2240]{0,1:T(8,128)S(1)} %convolution_add_fusion.1, bf16[128,1120]{1,0:T(8,128)(2,1)S(1)} %copy-done.8, bf16[2240,1120]{1,0:T(8,128)(2,1)S(1)} %bitcast.16), kind=kOutput, calls=%fused_computation.2 | convolution fusion | flops 642826240 | bytes 7024640 | tf_op jit(solution)/shard_map/dot_general | solution.py:72
  152.3 2.1 %copy.10 = bf16[128,2240]{1,0:T(8,128)(2,1)} copy(bf16[128,2240]{0,1:T(8,128)(2,1)} %fusion) | data formatting | bytes 1146880 | tf_op jit(solution)/shard_map/convert_element_type | solution.py:511
  154.5 18.3 %collective-permute-done.19.first = f32[72,256]{1,0:T(8,128)S(1)} collective-permute-done((f32[72,256]{1,0:T(8,128)S(1)}, f32[72,256]{1,0:T(8,128)S(1)}, u32[]{:S(2)}, u32[]{:S(2)}) %collective-permute-start.19) | collective-permute-done | bytes 73760 | tf_op jit(solution)/shard_map/ppermute | solution.py:327
  172.8 4.6 %all-to-all-done.4.key_value = f32[16,72,640]{2,1,0:T(8,128)S(1)} async-done(((f32[16,72,640]{2,1,0:T(8,128)}), f32[16,72,640]{2,1,0:T(8,128)S(1)}, u32[]{:S(2)}, u32[]{:S(2)}) %all-to-all-start.4) | async-done | bytes 2949152 | tf_op jit(solution)/shard_map/all_to_all | solution.py:323
  (74 shorter events, 25.1 us)
Async XLA Ops:
  8.4 22.7 %all-to-all-start = ((f32[32,45,112]{2,1,0:T(8,128)}), f32[32,45,112]{2,1,0:T(8,128)S(1)}, u32[]{:S(2)}, u32[]{:S(2)}) async-start(f32[32,45,112]{2,1,0:T(8,128)} %get-tuple-element.55), calls=%async_computation | async-start | bytes 1572864 | tf_op jit(solution)/shard_map/all_to_all | solution.py:323
  18.9 15.6 %collective-permute-start = (f32[1120,128]{1,0:T(8,128)}, f32[1120,128]{1,0:T(8,128)S(1)}, u32[]{:S(2)}, u32[]{:S(2)}) collective-permute-start(f32[1120,128]{1,0:T(8,128)} %get-tuple-element.64.refs_0_), channel_id=1, source_target_pairs={{0,32},{32,64},{64,96},{96,0},{1,33},{33,65},{65,97},{97,1},{2,34}... | collective-permute-start | bytes 1720328 | tf_op jit(solution)/shard_map/ppermute | solution.py:327
  20.5 10.6 %copy-start.2 = (bf16[1,16,8,1120]{3,2,1,0:T(8,128)(2,1)S(1)}, bf16[1,16,8,1120]{3,2,1,0:T(8,128)(2,1)}, u32[]{:S(2)}) copy-start(bf16[1,16,8,1120]{3,2,1,0:T(8,128)(2,1)} %param.9) | copy-start | bytes 860164
  20.5 15.1 %collective-permute-start.1 = (f32[1120,128]{1,0:T(8,128)}, f32[1120,128]{1,0:T(8,128)S(1)}, u32[]{:S(2)}, u32[]{:S(2)}) collective-permute-start(f32[1120,128]{1,0:T(8,128)} %get-tuple-element.63), channel_id=1, source_target_pairs={{0,96},{32,0},{64,32},{96,64},{1,97},{33,1},{65,33},{97,65},{2,98}... | collective-permute-start | bytes 1720328 | tf_op jit(solution)/shard_map/ppermute | solution.py:327
  32.0 31.6 %copy-start.1 = (bf16[10,128,112]{2,1,0:T(8,128)(2,1)S(1)}, bf16[10,128,112]{2,1,0:T(8,128)(2,1)}, u32[]{:S(2)}) copy-start(bf16[10,128,112]{2,1,0:T(8,128)(2,1)} %query.1.refs_1_) | copy-start | bytes 860164
  34.5 29.2 %copy-start.6 = (f32[10,112]{1,0:T(8,128)S(1)}, f32[10,112]{1,0:T(8,128)}, u32[]{:S(2)}) copy-start(f32[10,112]{1,0:T(8,128)} %get-tuple-element.62.refs_3_.total) | copy-start | bytes 13444
  35.6 14.3 %collective-permute-start.2 = (f32[1120,128]{1,0:T(8,128)}, f32[1120,128]{1,0:T(8,128)}, u32[]{:S(2)}, u32[]{:S(2)}) collective-permute-start(f32[1120,128]{1,0:T(8,128)} %get-tuple-element.63), channel_id=1, source_target_pairs={{0,32},{32,64},{64,96},{96,0},{1,33},{33,65},{65,97},{97,1},{2,34}... | collective-permute-start | bytes 1720328 | tf_op jit(solution)/shard_map/ppermute | solution.py:327
  36.9 14.1 %collective-permute-start.4 = (f32[1120,128]{1,0:T(8,128)}, f32[1120,128]{1,0:T(8,128)}, u32[]{:S(2)}, u32[]{:S(2)}) collective-permute-start(f32[1120,128]{1,0:T(8,128)} %get-tuple-element.64.refs_0_), channel_id=1, source_target_pairs={{0,96},{32,0},{64,32},{96,64},{1,97},{33,1},{65,33},{97,65},{2,98}... | collective-permute-start | bytes 1720328 | tf_op jit(solution)/shard_map/ppermute | solution.py:327
  37.6 26.1 %all-to-all-start.1 = ((f32[32,70,112]{2,1,0:T(8,128)}), f32[32,70,112]{2,1,0:T(8,128)S(1)}, u32[]{:S(2)}, u32[]{:S(2)}) async-start(f32[32,70,112]{2,1,0:T(8,128)} %get-tuple-element.60), calls=%async_computation.1 | async-start | bytes 2359296 | tf_op jit(solution)/shard_map/all_to_all | solution.py:323
  49.9 13.7 %collective-permute-start.3 = (f32[1120,128]{1,0:T(8,128)}, f32[1120,128]{1,0:T(8,128)S(1)}, u32[]{:S(2)}, u32[]{:S(2)}) collective-permute-start(f32[1120,128]{1,0:T(8,128)} %collective-permute-done.2), channel_id=1, source_target_pairs={{0,8},{8,0},{1,9},{9,1},{2,10},{10,2},{3,11},{11,3},{4,12},{12,4},... | collective-permute-start | bytes 1720328 | tf_op jit(solution)/shard_map/ppermute | solution.py:335
  50.9 12.7 %collective-permute-start.5 = (f32[1120,128]{1,0:T(8,128)}, f32[1120,128]{1,0:T(8,128)}, u32[]{:S(2)}, u32[]{:S(2)}) collective-permute-start(f32[1120,128]{1,0:T(8,128)} %collective-permute-done.4.refs_3_), channel_id=1, source_target_pairs={{0,8},{8,0},{1,9},{9,1},{2,10},{10,2},{3,11},{11,3},{4,12},{12,4},... | collective-permute-start | bytes 1720328 | tf_op jit(solution)/shard_map/ppermute | solution.py:335
  50.9 15.5 %collective-permute-start.6 = (f32[1120,128]{1,0:T(8,128)S(1)}, f32[1120,128]{1,0:T(8,128)}, u32[]{:S(2)}, u32[]{:S(2)}) collective-permute-start(f32[1120,128]{1,0:T(8,128)S(1)} %collective-permute-done.refs_1_), channel_id=1, source_target_pairs={{0,32},{32,64},{64,96},{96,0},{1,33},{33,65},{65,97},{97,1},{2,34}... | collective-permute-start | bytes 1720328 | tf_op jit(solution)/shard_map/ppermute | solution.py:327
  52.5 15.5 %collective-permute-start.7 = (f32[1120,128]{1,0:T(8,128)}, f32[1120,128]{1,0:T(8,128)}, u32[]{:S(2)}, u32[]{:S(2)}) collective-permute-start(f32[1120,128]{1,0:T(8,128)} %copy-done.11), channel_id=1, source_target_pairs={{0,96},{32,0},{64,32},{96,64},{1,97},{33,1},{65,33},{97,65},{2,98}... | collective-permute-start | bytes 1720328 | tf_op jit(solution)/shard_map/ppermute | solution.py:327
  52.9 28.5 %collective-permute-start.10 = (f32[1120,128]{1,0:T(8,128)}, f32[1120,128]{1,0:T(8,128)}, u32[]{:S(2)}, u32[]{:S(2)}) collective-permute-start(f32[1120,128]{1,0:T(8,128)} %copy-done.11), channel_id=1, source_target_pairs={{0,8},{8,0},{1,9},{9,1},{2,10},{10,2},{3,11},{11,3},{4,12},{12,4},... | collective-permute-start | bytes 1720328 | tf_op jit(solution)/shard_map/ppermute | solution.py:335
  68.0 23.6 %all-to-all-start.2 = ((f32[32,45,112]{2,1,0:T(8,128)}), f32[32,45,112]{2,1,0:T(8,128)S(1)}, u32[]{:S(2)}, u32[]{:S(2)}) async-start(f32[32,45,112]{2,1,0:T(8,128)} %get-tuple-element.70), calls=%async_computation.2 | async-start | bytes 1572864 | tf_op jit(solution)/shard_map/all_to_all | solution.py:323
  75.1 8.9 %collective-permute-start.8 = (f32[1120,128]{1,0:T(8,128)}, f32[1120,128]{1,0:T(8,128)}, u32[]{:S(2)}, u32[]{:S(2)}) collective-permute-start(f32[1120,128]{1,0:T(8,128)} %get-tuple-element.63), channel_id=1, source_target_pairs={{0,8},{8,0},{1,9},{9,1},{2,10},{10,2},{3,11},{11,3},{4,12},{12,4},... | collective-permute-start | bytes 1720328 | tf_op jit(solution)/shard_map/ppermute | solution.py:335
  75.5 8.6 %collective-permute-start.9 = (f32[1120,128]{1,0:T(8,128)}, f32[1120,128]{1,0:T(8,128)}, u32[]{:S(2)}, u32[]{:S(2)}) collective-permute-start(f32[1120,128]{1,0:T(8,128)} %collective-permute-done.7), channel_id=1, source_target_pairs={{0,8},{8,0},{1,9},{9,1},{2,10},{10,2},{3,11},{11,3},{4,12},{12,4},... | collective-permute-start | bytes 1720328 | tf_op jit(solution)/shard_map/ppermute | solution.py:335
  78.7 9.3 %collective-permute-start.11 = (f32[128,256]{1,0:T(8,128)}, f32[128,256]{1,0:T(8,128)S(1)}, u32[]{:S(2)}, u32[]{:S(2)}) collective-permute-start(f32[128,256]{1,0:T(8,128)} %get-tuple-element.76), channel_id=1, source_target_pairs={{0,32},{32,64},{64,96},{96,0},{1,33},{33,65},{65,97},{97,1},{2,34}... | collective-permute-start | bytes 393224 | tf_op jit(solution)/shard_map/ppermute | solution.py:327
  80.5 8.1 %collective-permute-start.12 = (f32[128,256]{1,0:T(8,128)}, f32[128,256]{1,0:T(8,128)S(1)}, u32[]{:S(2)}, u32[]{:S(2)}) collective-permute-start(f32[128,256]{1,0:T(8,128)} %get-tuple-element.77), channel_id=1, source_target_pairs={{0,64},{32,96},{64,0},{96,32},{1,65},{33,97},{65,1},{97,33},{2,66}... | collective-permute-start | bytes 393224 | tf_op jit(solution)/shard_map/ppermute | solution.py:327
  81.5 8.4 %collective-permute-start.13 = (f32[128,256]{1,0:T(8,128)}, f32[128,256]{1,0:T(8,128)S(1)}, u32[]{:S(2)}, u32[]{:S(2)}) collective-permute-start(f32[128,256]{1,0:T(8,128)} %get-tuple-element.78), channel_id=1, source_target_pairs={{0,96},{32,0},{64,32},{96,64},{1,97},{33,1},{65,33},{97,65},{2,98}... | collective-permute-start | bytes 393224 | tf_op jit(solution)/shard_map/ppermute | solution.py:327
  93.9 27.2 %all-to-all-start.3 = ((f32[4,128,640]{2,1,0:T(8,128)}), f32[4,128,640]{2,1,0:T(8,128)S(1)}, u32[]{:S(2)}, u32[]{:S(2)}) async-start(f32[4,128,640]{2,1,0:T(8,128)} %get-tuple-element.86.refs_4_), calls=%async_computation.3 | async-start | bytes 2621440 | tf_op jit(solution)/shard_map/all_to_all | solution.py:323
  98.4 1.9 %collective-permute-start.14 = (f32[512,256]{1,0:T(8,128)S(1)}, f32[512,256]{1,0:T(8,128)S(1)}, u32[]{:S(2)}, u32[]{:S(2)}) collective-permute-start(f32[512,256]{1,0:T(8,128)S(1)} %copy-done.7), channel_id=1, source_target_pairs={{0,8},{8,0},{1,9},{9,1},{2,10},{10,2},{3,11},{11,3},{4,12},{12,4},... | collective-permute-start | bytes 1572872 | tf_op jit(solution)/shard_map/ppermute | solution.py:335
  103.6 11.6 %collective-permute-start.15 = (f32[4,72,256]{2,1,0:T(8,128)}, f32[4,72,256]{2,1,0:T(8,128)S(1)}, u32[]{:S(2)}, u32[]{:S(2)}) collective-permute-start(f32[4,72,256]{2,1,0:T(8,128)} %get-tuple-element.89), channel_id=1, source_target_pairs={{0,4},{2,6},{4,0},{6,2},{1,5},{3,7},{5,1},{7,3},{8,12},{10,14},{12... | collective-permute-start | bytes 884744 | tf_op jit(solution)/shard_map/ppermute | solution.py:327
  106.9 13.8 %collective-permute-start.16 = (f32[4,72,256]{2,1,0:T(8,128)}, f32[4,72,256]{2,1,0:T(8,128)S(1)}, u32[]{:S(2)}, u32[]{:S(2)}) collective-permute-start(f32[4,72,256]{2,1,0:T(8,128)} %get-tuple-element.90), channel_id=1, source_target_pairs={{0,2},{2,4},{4,6},{6,0},{1,3},{3,5},{5,7},{7,1},{8,10},{10,12},{12... | collective-permute-start | bytes 884744 | tf_op jit(solution)/shard_map/ppermute | solution.py:327
  107.5 13.6 %collective-permute-start.17 = (f32[4,72,256]{2,1,0:T(8,128)}, f32[4,72,256]{2,1,0:T(8,128)S(1)}, u32[]{:S(2)}, u32[]{:S(2)}) collective-permute-start(f32[4,72,256]{2,1,0:T(8,128)} %get-tuple-element.91), channel_id=1, source_target_pairs={{0,6},{2,0},{4,2},{6,4},{1,7},{3,1},{5,3},{7,5},{8,14},{10,8},{12,... | collective-permute-start | bytes 884744 | tf_op jit(solution)/shard_map/ppermute | solution.py:327
  121.1 3.0 %collective-permute-start.18 = (f32[4,128,640]{2,1,0:T(8,128)S(1)}, f32[4,128,640]{2,1,0:T(8,128)S(1)}, u32[]{:S(2)}, u32[]{:S(2)}) collective-permute-start(f32[4,128,640]{2,1,0:T(8,128)S(1)} %all-to-all-done.3.refs_2_), channel_id=1, source_target_pairs={{0,8},{8,0},{1,9},{9,1},{2,10},{10,2},{3,11},{11,3},{4,12},{12,4},... | collective-permute-start | bytes 3932168 | tf_op jit(solution)/shard_map/ppermute | solution.py:335
  128.8 48.5 %all-to-all-start.4 = ((f32[16,72,640]{2,1,0:T(8,128)}), f32[16,72,640]{2,1,0:T(8,128)S(1)}, u32[]{:S(2)}, u32[]{:S(2)}) async-start(f32[16,72,640]{2,1,0:T(8,128)} %key_value_product.1), calls=%async_computation.4 | async-start | bytes 5898240 | tf_op jit(solution)/shard_map/all_to_all | solution.py:323
  135.4 14.5 %slice-start = ((s8[5160960]{0:T(1024)(128)(4,1)}), s8[4194304]{0:T(1024)(128)(4,1)S(1)}, s32[]{:S(2)}) async-start(s8[5160960]{0:T(1024)(128)(4,1)} %bitcast.15), calls=%async_computation.5 | async-start | bytes 8388608
  139.6 10.3 %slice-start.1 = ((s8[5160960]{0:T(1024)(128)(4,1)}), s8[966656]{0:T(1024)(128)(4,1)S(1)}, s32[]{:S(2)}) async-start(s8[5160960]{0:T(1024)(128)(4,1)} %bitcast.15), calls=%async_computation.6 | async-start | bytes 1933312
  143.8 29.0 %collective-permute-start.19 = (f32[72,256]{1,0:T(8,128)S(1)}, f32[72,256]{1,0:T(8,128)S(1)}, u32[]{:S(2)}, u32[]{:S(2)}) collective-permute-start(f32[72,256]{1,0:T(8,128)S(1)} %copy-done.14), channel_id=1, source_target_pairs={{0,1},{1,16},{16,17},{17,0},{2,3},{3,18},{18,19},{19,2},{4,5},{5,2... | collective-permute-start | bytes 221192 | tf_op jit(solution)/shard_map/ppermute | solution.py:327
  145.8 27.0 %collective-permute-start.20 = (f32[72,256]{1,0:T(8,128)S(1)}, f32[72,256]{1,0:T(8,128)S(1)}, u32[]{:S(2)}, u32[]{:S(2)}) collective-permute-start(f32[72,256]{1,0:T(8,128)S(1)} %copy-done.13), channel_id=1, source_target_pairs={{0,16},{1,17},{16,0},{17,1},{2,18},{3,19},{18,2},{19,3},{4,20},{5,... | collective-permute-start | bytes 221192 | tf_op jit(solution)/shard_map/ppermute | solution.py:327
  148.5 24.3 %collective-permute-start.21 = (f32[72,256]{1,0:T(8,128)S(1)}, f32[72,256]{1,0:T(8,128)S(1)}, u32[]{:S(2)}, u32[]{:S(2)}) collective-permute-start(f32[72,256]{1,0:T(8,128)S(1)} %copy-done.12), channel_id=1, source_target_pairs={{0,17},{1,0},{16,1},{17,16},{2,19},{3,2},{18,3},{19,18},{4,21},{5,... | collective-permute-start | bytes 221192 | tf_op jit(solution)/shard_map/ppermute | solution.py:327
  (12 other events, 60.8 us)

commit v14 on v12

--- a/solution.py
+++ b/solution.py
@@ -155,13 +155,16 @@
     return 1.0 / (jnp.sum(positive * total, axis=1, keepdims=True) + EPSILON)
 
 
-def numerator_kernel(loss_scale, got, query, upstream, sent, numer, total, state):
+def numerator_kernel(loss_scale, got, query_rows, upstream, sent, numer, total, state, query, arrived):
+    copy = pltpu.make_async_copy(query_rows, query, arrived)
+    copy.start()
     sums = got[0]
     for tile in range(1, TILES):
         sums = sums + got[tile]
     state_part = sums[:PART]
     totals = sums[PART : PART + HEADS]
     total[...] = totals
+    copy.wait()
     for index in range(HEADS):
         part = slice(index * HD, (index + 1) * HD)
         positive = relu(query[index])
@@ -381,16 +384,16 @@
     (query,) = call(
         query_kernel,
         "query",
-        [heads],
+        [pltpu.HBM((HEADS, TOKENS, HD), BF16)],
         [BLOCK, BLOCK],
     )(tokens, query_weight)
     sent, numer, total = call(
         lambda *refs: numerator_kernel(loss_scale, *refs),
         "numerator",
         [shaped((TILES, 2 * PART, HD)), heads, shaped((HEADS, HD))],
-        [BLOCK] * 3,
-        [state],
-        arrived=(0, 1, 2),
+        [BLOCK, IN_HBM, BLOCK],
+        [state, pltpu.VMEM((HEADS, TOKENS, HD), BF16), pltpu.SemaphoreType.DMA],
+        arrived=(0, 2),
     )(got, query, upstream)
     sent, left_top, right_bottom, later_top, later_bottom = lax.optimization_barrier(
         (sent, left_top, right_bottom, top, bottom)

time: 179 us -> 179 us (level)
  transfers between devices with their start and end apart: 25 -> 25, of which waited for: 15 -> 15; matrix products, arithmetic and copies ran while one was open for 7% -> 7% of each run, Pallas kernels for 13% -> 14%
where the time goes in v14:
time: 179 us; the launch traced here: 178 us
  waiting for transfers between devices  66.5 us (37%)
  starting transfers between devices  54.9 us (31%)
  Pallas kernels  43 us (24%)
  matrix products  10.7 us (6%)
  local copies, waits for them, and re-layouts  2.2 us (1%)
    pallas_call x13, Pallas kernels, with_placed(): return run(*placed)  43 us
    ppermute x15, waiting for transfers between devices, shift(): lax.ppermute(values, axis, [(i, (i + by) % RING) for i in range(RING)])  41.4 us
    all_to_all x5, starting transfers between devices, exchange(): return lax.all_to_all(blocks, axes, 0, 0, tiled=True)  31.4 us
    ppermute x15, starting transfers between devices, shift(): lax.ppermute(values, axis, [(i, (i + by) % RING) for i in range(RING)])  23.5 us
    all_to_all x5, waiting for transfers between devices, exchange(): return lax.all_to_all(blocks, axes, 0, 0, tiled=True)  21.8 us
    dot_general x3, matrix products, dot(): lax.dot_general(left, right, (((left_dim,), (right_dim,)), ((), ())), pre...  10.7 us
  transfers between devices with their start and end apart: 25, of which 15 were waited for; matrix products, arithmetic and copies ran while one was open for 7% of the time, Pallas kernels for 14%

profile of v14, /device:TPU:8, one launch (start us, length us, event | category | flops | bytes accessed | tf_op | source)
XLA Modules:
  0.0 178.1 jit_solution(4505318959161281309)
XLA Ops:
  0.6 7.7 %key_value.1 = (bf16[10,128,112]{2,1,0:T(8,128)(2,1)}, bf16[10,128,112]{2,1,0:T(8,128)(2,1)}, f32[32,45,112]{2,1,0:T(8,128)}) custom-call(bf16[128,2240]{1,0:T(8,128)(2,1)} %bitcast.17, bf16[2240,1120]{1,0:T(8,128)(2,1)} %key_weight.1, bf16[2240,1120]{1,0:T(8,128)(2,1)} %value_weight.1), custom_call_target="tpu_custom_call" | custom-call | tf_op jit(solution)/shard_map/key_value/pallas_call | solution.py:66
  8.4 2.3 %turn.1 = (f32[1120,128]{1,0:T(8,128)}, f32[1120,128]{1,0:T(8,128)}) custom-call(s32[1]{0:T(128)} %bitcast.3.core, bf16[128,2240]{1,0:T(8,128)(2,1)} %bitcast.18), custom_call_target="tpu_custom_call" | custom-call | tf_op jit(solution)/shard_map/turn/pallas_call | solution.py:66
  10.7 8.3 %all-to-all-start = ((f32[32,45,112]{2,1,0:T(8,128)}), f32[32,45,112]{2,1,0:T(8,128)S(1)}, u32[]{:S(2)}, u32[]{:S(2)}) async-start(f32[32,45,112]{2,1,0:T(8,128)} %get-tuple-element.55), calls=%async_computation | async-start | bytes 1572864 | tf_op jit(solution)/shard_map/all_to_all | solution.py:326
  21.1 4.4 %query.1.refs_1_ = bf16[10,128,112]{2,1,0:T(8,128)(2,1)} custom-call(bf16[128,2240]{1,0:T(8,128)(2,1)} %bitcast.19, bf16[2240,1120]{1,0:T(8,128)(2,1)} %weight.1), custom_call_target="tpu_custom_call" | custom-call | tf_op jit(solution)/shard_map/query/pallas_call | solution.py:66
  25.5 8.0 %all-to-all-done.refs_0_ = f32[32,45,112]{2,1,0:T(8,128)S(1)} async-done(((f32[32,45,112]{2,1,0:T(8,128)}), f32[32,45,112]{2,1,0:T(8,128)S(1)}, u32[]{:S(2)}, u32[]{:S(2)}) %all-to-all-start) | async-done | bytes 645152 | tf_op jit(solution)/shard_map/all_to_all | solution.py:326
  33.5 3.5 %numerator.1 = (f32[32,70,112]{2,1,0:T(8,128)}, bf16[10,128,112]{2,1,0:T(8,128)(2,1)}, f32[10,112]{1,0:T(8,128)}) custom-call(f32[32,45,112]{2,1,0:T(8,128)S(1)} %all-to-all-done.refs_0_, bf16[10,128,112]{2,1,0:T(8,128)(2,1)} %query.1.refs_1_, bf16[128,1120]{1,0:T(8,128)(2,1)S(1)} %bitcast.13), custom_call_target="tpu_custom_call" | custom-call | tf_op jit(solution)/shard_map/numerator/pallas_call | solution.py:66
  39.2 5.8 %all-to-all-start.1 = ((f32[32,70,112]{2,1,0:T(8,128)}), f32[32,70,112]{2,1,0:T(8,128)S(1)}, u32[]{:S(2)}, u32[]{:S(2)}) async-start(f32[32,70,112]{2,1,0:T(8,128)} %get-tuple-element.60), calls=%async_computation.1 | async-start | bytes 2359296 | tf_op jit(solution)/shard_map/all_to_all | solution.py:326
  45.0 6.2 %collective-permute-done.3.refs_5_ = f32[1120,128]{1,0:T(8,128)} collective-permute-done((f32[1120,128]{1,0:T(8,128)S(1)}, f32[1120,128]{1,0:T(8,128)}, u32[]{:S(2)}, u32[]{:S(2)}) %collective-permute-start.3) | collective-permute-done | bytes 573472 | tf_op jit(solution)/shard_map/ppermute | solution.py:330
  54.5 9.2 %all-to-all-done.1.refs_0_.got = f32[32,70,112]{2,1,0:T(8,128)S(1)} async-done(((f32[32,70,112]{2,1,0:T(8,128)}), f32[32,70,112]{2,1,0:T(8,128)S(1)}, u32[]{:S(2)}, u32[]{:S(2)}) %all-to-all-start.1) | async-done | bytes 1003552 | tf_op jit(solution)/shard_map/all_to_all | solution.py:326
  63.8 2.6 %total_grad.1 = (f32[32,45,112]{2,1,0:T(8,128)}, f32[128,10]{1,0:T(8,128)}) custom-call(f32[32,70,112]{2,1,0:T(8,128)S(1)} %all-to-all-done.1.refs_0_.got, bf16[10,128,112]{2,1,0:T(8,128)(2,1)S(1)} %copy-done, bf16[128,1120]{1,0:T(8,128)(2,1)S(1)} %bitcast.14, f32[10,112]{1,0:T(8,128)S(1)} %copy-done.5, f32[1120,128]{1,0:T(8,128)} %collective-permute-done.4.refs_4_, ...), custom_call_target="tpu_custom_call" | custom-call | tf_op jit(solution)/shard_map/total_grad/pallas_call | solution.py:66
  69.2 5.9 %all-to-all-start.2 = ((f32[32,45,112]{2,1,0:T(8,128)}), f32[32,45,112]{2,1,0:T(8,128)S(1)}, u32[]{:S(2)}, u32[]{:S(2)}) async-start(f32[32,45,112]{2,1,0:T(8,128)} %get-tuple-element.70), calls=%async_computation.2 | async-start | bytes 1572864 | tf_op jit(solution)/shard_map/all_to_all | solution.py:326
  75.1 3.0 %query_grad.1 = (bf16[128,1120]{1,0:T(8,128)(2,1)}, f32[128,256]{1,0:T(8,128)}, f32[128,256]{1,0:T(8,128)}, f32[128,256]{1,0:T(8,128)}, f32[128,256]{1,0:T(8,128)}, /*index=5*/f32[4,128,24]{2,1,0:T(8,128)}) custom-call(s32[1]{0:T(128)} %bitcast.place.refs_0_, f32[32,70,112]{2,1,0:T(8,128)S(1)} %all-to-all-done.1.refs_0_.got, ...), custom_call_target="tpu_custom_call" | custom-call | tf_op jit(solution)/shard_map/query_grad/pallas_call | solution.py:66
  78.1 2.7 %collective-permute-start.10 = (f32[128,256]{1,0:T(8,128)}, f32[128,256]{1,0:T(8,128)S(1)}, u32[]{:S(2)}, u32[]{:S(2)}) collective-permute-start(f32[128,256]{1,0:T(8,128)} %get-tuple-element.77), channel_id=1, source_target_pairs={{0,64},{32,96},{64,0},{96,32},{1,65},{33,97},{65,1},{97,33},{2,66}... | collective-permute-start | bytes 393224 | tf_op jit(solution)/shard_map/ppermute | solution.py:330
  82.8 4.0 %join.1.refs_1_ = bf16[1120,1024]{1,0:T(8,128)(2,1)} custom-call(f32[1120,128]{1,0:T(8,128)} %get-tuple-element.64.refs_0_, f32[1120,128]{1,0:T(8,128)S(1)} %collective-permute-done.refs_1_, f32[1120,128]{1,0:T(8,128)} %collective-permute-done.7.refs_2_, f32[1120,128]{1,0:T(8,128)} %collective-permute-done.5.refs_3_, ...), custom_call_target="tpu_custom_call" | custom-call | tf_op jit(solution)/shard_map/join/pallas_call | solution.py:66
  90.3 2.3 %key_value_grad.1 = (bf16[128,1120]{1,0:T(8,128)(2,1)}, bf16[128,1120]{1,0:T(8,128)(2,1)}, f32[4,128,640]{2,1,0:T(8,128)}) custom-call(f32[32,45,112]{2,1,0:T(8,128)S(1)} %all-to-all-done.2.got, bf16[10,128,112]{2,1,0:T(8,128)(2,1)S(1)} %copy-done.2, bf16[10,128,112]{2,1,0:T(8,128)(2,1)S(1)} %copy-done.3, f32[4,128,24]{2,1,0:T(8,128)S(1)} %copy-done.4), custom_call_target="tpu_custom_call" | custom-call | tf_op jit(solution)/shard_map/key_value_grad/pallas_call | solution.py:66
  92.6 4.8 %all-to-all-start.3 = ((f32[4,128,640]{2,1,0:T(8,128)}), f32[4,128,640]{2,1,0:T(8,128)S(1)}, u32[]{:S(2)}, u32[]{:S(2)}) async-start(f32[4,128,640]{2,1,0:T(8,128)} %get-tuple-element.86.refs_4_), calls=%async_computation.3 | async-start | bytes 2621440 | tf_op jit(solution)/shard_map/all_to_all | solution.py:326
  97.5 1.9 %collective-permute-done.12.refs_3_ = f32[512,256]{1,0:T(8,128)S(1)} collective-permute-done((f32[512,256]{1,0:T(8,128)S(1)}, f32[512,256]{1,0:T(8,128)S(1)}, u32[]{:S(2)}, u32[]{:S(2)}) %collective-permute-start.12) | collective-permute-done | bytes 524320 | tf_op jit(solution)/shard_map/ppermute | solution.py:338
  99.4 3.3 %query_product.1 = (f32[4,72,256]{2,1,0:T(8,128)}, f32[4,72,256]{2,1,0:T(8,128)}, f32[4,72,256]{2,1,0:T(8,128)}, f32[4,72,256]{2,1,0:T(8,128)}) custom-call(s32[1]{0:T(128)} %bitcast.5.refs_0_, bf16[1120,1024]{1,0:T(8,128)(2,1)} %join.1.refs_1_, f32[512,256]{1,0:T(8,128)} %pack_query.1.refs_2_, f32[512,256]{1,0:T(8,128)S(1)} %collective-permute-done.12.refs_3_, ...), custom_call_target="tpu_custom_call" | custom-call | tf_op jit(solution)/shard_map/query_product/pallas_call | solution.py:66
  102.7 3.2 %collective-permute-start.13 = (f32[4,72,256]{2,1,0:T(8,128)}, f32[4,72,256]{2,1,0:T(8,128)S(1)}, u32[]{:S(2)}, u32[]{:S(2)}) collective-permute-start(f32[4,72,256]{2,1,0:T(8,128)} %get-tuple-element.89), channel_id=1, source_target_pairs={{0,4},{2,6},{4,0},{6,2},{1,5},{3,7},{5,1},{7,3},{8,12},{10,14},{12... | collective-permute-start | bytes 884744 | tf_op jit(solution)/shard_map/ppermute | solution.py:330
  106.5 2.7 %collective-permute-start.15 = (f32[4,72,256]{2,1,0:T(8,128)}, f32[4,72,256]{2,1,0:T(8,128)S(1)}, u32[]{:S(2)}, u32[]{:S(2)}) collective-permute-start(f32[4,72,256]{2,1,0:T(8,128)} %get-tuple-element.91), channel_id=1, source_target_pairs={{0,6},{2,0},{4,2},{6,4},{1,7},{3,1},{5,3},{7,5},{8,14},{10,8},{12,... | collective-permute-start | bytes 884744 | tf_op jit(solution)/shard_map/ppermute | solution.py:330
  109.1 5.2 %collective-permute-done.13.first = f32[4,72,256]{2,1,0:T(8,128)S(1)} collective-permute-done((f32[4,72,256]{2,1,0:T(8,128)}, f32[4,72,256]{2,1,0:T(8,128)S(1)}, u32[]{:S(2)}, u32[]{:S(2)}) %collective-permute-start.13) | collective-permute-done | bytes 294944 | tf_op jit(solution)/shard_map/ppermute | solution.py:330
  114.4 5.5 %collective-permute-done.14.second = f32[4,72,256]{2,1,0:T(8,128)S(1)} collective-permute-done((f32[4,72,256]{2,1,0:T(8,128)}, f32[4,72,256]{2,1,0:T(8,128)S(1)}, u32[]{:S(2)}, u32[]{:S(2)}) %collective-permute-start.14) | collective-permute-done | bytes 294944 | tf_op jit(solution)/shard_map/ppermute | solution.py:330
  123.1 4.7 %key_value_product.1 = f32[16,72,640]{2,1,0:T(8,128)} custom-call(s32[1]{0:T(128)} %bitcast.place.refs_0_, bf16[1120,1024]{1,0:T(8,128)(2,1)} %join.1.refs_1_, f32[4,128,640]{2,1,0:T(8,128)S(1)} %all-to-all-done.3.refs_2_, f32[4,128,640]{2,1,0:T(8,128)S(1)} %collective-permute-done.16.refs_3_, f32[72,256]{1,0:T(8,128)} %get-tuple-element.97.refs_4_.own), custom_call_target="tpu_custom_call" | custom-call | tf_op jit(solution)/shard_map/key_value_product/pallas_call | solution.py:66
  127.8 6.6 %all-to-all-start.4 = ((f32[16,72,640]{2,1,0:T(8,128)}), f32[16,72,640]{2,1,0:T(8,128)S(1)}, u32[]{:S(2)}, u32[]{:S(2)}) async-start(f32[16,72,640]{2,1,0:T(8,128)} %key_value_product.1), calls=%async_computation.4 | async-start | bytes 5898240 | tf_op jit(solution)/shard_map/all_to_all | solution.py:326
  134.4 4.2 %fusion.1 = f32[128,2240]{0,1:T(8,128)S(1)} fusion(bf16[128,1120]{1,0:T(8,128)(2,1)S(1)} %copy-done.8, bf16[2240,1120]{1,0:T(8,128)(2,1)} %key_weight.1), kind=kOutput, calls=%fused_computation.3 | convolution fusion | flops 642252800 | bytes 6451200 | tf_op jit(solution)/shard_map/dot_general | solution.py:72
  138.7 4.1 %convolution_add_fusion.1 = f32[128,2240]{0,1:T(8,128)S(1)} fusion(f32[128,2240]{0,1:T(8,128)S(1)} %fusion.1, bf16[128,1120]{1,0:T(8,128)(2,1)S(1)} %copy-done.9, bf16[2240,1120]{1,0:T(8,128)(2,1)} %weight.1), kind=kOutput, calls=%fused_computation.1 | convolution fusion | flops 642539520 | bytes 7598080 | tf_op jit(solution)/shard_map/dot_general | solution.py:72
  142.8 2.0 %collective-permute-start.17 = (f32[72,256]{1,0:T(8,128)S(1)}, f32[72,256]{1,0:T(8,128)S(1)}, u32[]{:S(2)}, u32[]{:S(2)}) collective-permute-start(f32[72,256]{1,0:T(8,128)S(1)} %copy-done.13), channel_id=1, source_target_pairs={{0,1},{1,16},{16,17},{17,0},{2,3},{3,18},{18,19},{19,2},{4,5},{5,2... | collective-permute-start | bytes 221192 | tf_op jit(solution)/shard_map/ppermute | solution.py:330
  144.8 2.7 %collective-permute-start.18 = (f32[72,256]{1,0:T(8,128)S(1)}, f32[72,256]{1,0:T(8,128)S(1)}, u32[]{:S(2)}, u32[]{:S(2)}) collective-permute-start(f32[72,256]{1,0:T(8,128)S(1)} %copy-done.12), channel_id=1, source_target_pairs={{0,16},{1,17},{16,0},{17,1},{2,18},{3,19},{18,2},{19,3},{4,20},{5,... | collective-permute-start | bytes 221192 | tf_op jit(solution)/shard_map/ppermute | solution.py:330
  148.9 2.4 %fusion = bf16[128,2240]{0,1:T(8,128)(2,1)} fusion(f32[128,2240]{0,1:T(8,128)S(1)} %convolution_add_fusion.1, bf16[128,1120]{1,0:T(8,128)(2,1)S(1)} %copy-done.7, bf16[2240,1120]{1,0:T(8,128)(2,1)S(1)} %bitcast.16), kind=kOutput, calls=%fused_computation.2 | convolution fusion | flops 642826240 | bytes 7024640 | tf_op jit(solution)/shard_map/dot_general | solution.py:72
  151.3 2.1 %copy.10 = bf16[128,2240]{1,0:T(8,128)(2,1)} copy(bf16[128,2240]{0,1:T(8,128)(2,1)} %fusion) | data formatting | bytes 1146880 | tf_op jit(solution)/shard_map/convert_element_type | solution.py:512
  153.4 18.3 %collective-permute-done.17.first = f32[72,256]{1,0:T(8,128)S(1)} collective-permute-done((f32[72,256]{1,0:T(8,128)S(1)}, f32[72,256]{1,0:T(8,128)S(1)}, u32[]{:S(2)}, u32[]{:S(2)}) %collective-permute-start.17) | collective-permute-done | bytes 73760 | tf_op jit(solution)/shard_map/ppermute | solution.py:330
  171.8 4.6 %all-to-all-done.4.key_value = f32[16,72,640]{2,1,0:T(8,128)S(1)} async-done(((f32[16,72,640]{2,1,0:T(8,128)}), f32[16,72,640]{2,1,0:T(8,128)S(1)}, u32[]{:S(2)}, u32[]{:S(2)}) %all-to-all-start.4) | async-done | bytes 2949152 | tf_op jit(solution)/shard_map/all_to_all | solution.py:326
  (68 shorter events, 23.1 us)
Async XLA Ops:
  10.7 10.0 %collective-permute-start.1 = (f32[1120,128]{1,0:T(8,128)}, f32[1120,128]{1,0:T(8,128)S(1)}, u32[]{:S(2)}, u32[]{:S(2)}) collective-permute-start(f32[1120,128]{1,0:T(8,128)} %get-tuple-element.59), channel_id=1, source_target_pairs={{0,8},{8,0},{1,9},{9,1},{2,10},{10,2},{3,11},{11,3},{4,12},{12,4},... | collective-permute-start | bytes 1720328 | tf_op jit(solution)/shard_map/ppermute | solution.py:338
  10.7 22.8 %all-to-all-start = ((f32[32,45,112]{2,1,0:T(8,128)}), f32[32,45,112]{2,1,0:T(8,128)S(1)}, u32[]{:S(2)}, u32[]{:S(2)}) async-start(f32[32,45,112]{2,1,0:T(8,128)} %get-tuple-element.55), calls=%async_computation | async-start | bytes 1572864 | tf_op jit(solution)/shard_map/all_to_all | solution.py:326
  19.0 14.5 %copy-start.1 = (bf16[1,16,8,1120]{3,2,1,0:T(8,128)(2,1)S(1)}, bf16[1,16,8,1120]{3,2,1,0:T(8,128)(2,1)}, u32[]{:S(2)}) copy-start(bf16[1,16,8,1120]{3,2,1,0:T(8,128)(2,1)} %param.9) | copy-start | bytes 860164
  19.0 19.7 %copy-start.10 = (f32[1120,128]{1,0:T(8,128)S(1)}, f32[1120,128]{1,0:T(8,128)}, u32[]{:S(2)}) copy-start(f32[1120,128]{1,0:T(8,128)} %get-tuple-element.64.refs_0_) | copy-start | bytes 1720324
  19.0 18.1 %collective-permute-start = (f32[1120,128]{1,0:T(8,128)}, f32[1120,128]{1,0:T(8,128)S(1)}, u32[]{:S(2)}, u32[]{:S(2)}) collective-permute-start(f32[1120,128]{1,0:T(8,128)} %get-tuple-element.64.refs_0_), channel_id=1, source_target_pairs={{0,32},{32,64},{64,96},{96,0},{1,33},{33,65},{65,97},{97,1},{2,34}... | collective-permute-start | bytes 1720328 | tf_op jit(solution)/shard_map/ppermute | solution.py:330
  20.7 16.4 %collective-permute-start.2 = (f32[1120,128]{1,0:T(8,128)S(1)}, f32[1120,128]{1,0:T(8,128)}, u32[]{:S(2)}, u32[]{:S(2)}) collective-permute-start(f32[1120,128]{1,0:T(8,128)S(1)} %collective-permute-done.1.refs_4_), channel_id=1, source_target_pairs={{0,96},{32,0},{64,32},{96,64},{1,97},{33,1},{65,33},{97,65},{2,98}... | collective-permute-start | bytes 1720328 | tf_op jit(solution)/shard_map/ppermute | solution.py:330
  25.5 38.2 %copy-start = (bf16[10,128,112]{2,1,0:T(8,128)(2,1)S(1)}, bf16[10,128,112]{2,1,0:T(8,128)(2,1)}, u32[]{:S(2)}) copy-start(bf16[10,128,112]{2,1,0:T(8,128)(2,1)} %query.1.refs_1_) | copy-start | bytes 860164
  37.1 26.7 %copy-start.5 = (f32[10,112]{1,0:T(8,128)S(1)}, f32[10,112]{1,0:T(8,128)}, u32[]{:S(2)}) copy-start(f32[10,112]{1,0:T(8,128)} %get-tuple-element.62.refs_3_.total) | copy-start | bytes 13444
  37.1 14.1 %collective-permute-start.3 = (f32[1120,128]{1,0:T(8,128)S(1)}, f32[1120,128]{1,0:T(8,128)}, u32[]{:S(2)}, u32[]{:S(2)}) collective-permute-start(f32[1120,128]{1,0:T(8,128)S(1)} %collective-permute-done.1.refs_4_), channel_id=1, source_target_pairs={{0,32},{32,64},{64,96},{96,0},{1,33},{33,65},{65,97},{97,1},{2,34}... | collective-permute-start | bytes 1720328 | tf_op jit(solution)/shard_map/ppermute | solution.py:330
  38.8 13.7 %collective-permute-start.5 = (f32[1120,128]{1,0:T(8,128)S(1)}, f32[1120,128]{1,0:T(8,128)}, u32[]{:S(2)}, u32[]{:S(2)}) collective-permute-start(f32[1120,128]{1,0:T(8,128)S(1)} %copy-done.10), channel_id=1, source_target_pairs={{0,96},{32,0},{64,32},{96,64},{1,97},{33,1},{65,33},{97,65},{2,98}... | collective-permute-start | bytes 1720328 | tf_op jit(solution)/shard_map/ppermute | solution.py:330
  39.2 24.5 %all-to-all-start.1 = ((f32[32,70,112]{2,1,0:T(8,128)}), f32[32,70,112]{2,1,0:T(8,128)S(1)}, u32[]{:S(2)}, u32[]{:S(2)}) async-start(f32[32,70,112]{2,1,0:T(8,128)} %get-tuple-element.60), calls=%async_computation.1 | async-start | bytes 2359296 | tf_op jit(solution)/shard_map/all_to_all | solution.py:326
  51.2 12.6 %collective-permute-start.4 = (f32[1120,128]{1,0:T(8,128)}, f32[1120,128]{1,0:T(8,128)}, u32[]{:S(2)}, u32[]{:S(2)}) collective-permute-start(f32[1120,128]{1,0:T(8,128)} %collective-permute-done.3.refs_5_), channel_id=1, source_target_pairs={{0,8},{8,0},{1,9},{9,1},{2,10},{10,2},{3,11},{11,3},{4,12},{12,4},... | collective-permute-start | bytes 1720328 | tf_op jit(solution)/shard_map/ppermute | solution.py:338
  52.5 11.3 %collective-permute-start.6 = (f32[1120,128]{1,0:T(8,128)}, f32[1120,128]{1,0:T(8,128)}, u32[]{:S(2)}, u32[]{:S(2)}) collective-permute-start(f32[1120,128]{1,0:T(8,128)} %collective-permute-done.5.refs_3_), channel_id=1, source_target_pairs={{0,8},{8,0},{1,9},{9,1},{2,10},{10,2},{3,11},{11,3},{4,12},{12,4},... | collective-permute-start | bytes 1720328 | tf_op jit(solution)/shard_map/ppermute | solution.py:338
  52.5 15.5 %collective-permute-start.7 = (f32[1120,128]{1,0:T(8,128)S(1)}, f32[1120,128]{1,0:T(8,128)}, u32[]{:S(2)}, u32[]{:S(2)}) collective-permute-start(f32[1120,128]{1,0:T(8,128)S(1)} %collective-permute-done.refs_1_), channel_id=1, source_target_pairs={{0,32},{32,64},{64,96},{96,0},{1,33},{33,65},{65,97},{97,1},{2,34}... | collective-permute-start | bytes 1720328 | tf_op jit(solution)/shard_map/ppermute | solution.py:330
  53.8 15.4 %collective-permute-start.8 = (f32[1120,128]{1,0:T(8,128)}, f32[1120,128]{1,0:T(8,128)}, u32[]{:S(2)}, u32[]{:S(2)}) collective-permute-start(f32[1120,128]{1,0:T(8,128)} %collective-permute-done.2.refs_7_), channel_id=1, source_target_pairs={{0,96},{32,0},{64,32},{96,64},{1,97},{33,1},{65,33},{97,65},{2,98}... | collective-permute-start | bytes 1720328 | tf_op jit(solution)/shard_map/ppermute | solution.py:330
  69.2 21.1 %all-to-all-start.2 = ((f32[32,45,112]{2,1,0:T(8,128)}), f32[32,45,112]{2,1,0:T(8,128)S(1)}, u32[]{:S(2)}, u32[]{:S(2)}) async-start(f32[32,45,112]{2,1,0:T(8,128)} %get-tuple-element.70), calls=%async_computation.2 | async-start | bytes 1572864 | tf_op jit(solution)/shard_map/all_to_all | solution.py:326
  78.1 8.7 %collective-permute-start.10 = (f32[128,256]{1,0:T(8,128)}, f32[128,256]{1,0:T(8,128)S(1)}, u32[]{:S(2)}, u32[]{:S(2)}) collective-permute-start(f32[128,256]{1,0:T(8,128)} %get-tuple-element.77), channel_id=1, source_target_pairs={{0,64},{32,96},{64,0},{96,32},{1,65},{33,97},{65,1},{97,33},{2,66}... | collective-permute-start | bytes 393224 | tf_op jit(solution)/shard_map/ppermute | solution.py:330
  80.8 7.5 %collective-permute-start.11 = (f32[128,256]{1,0:T(8,128)}, f32[128,256]{1,0:T(8,128)S(1)}, u32[]{:S(2)}, u32[]{:S(2)}) collective-permute-start(f32[128,256]{1,0:T(8,128)} %get-tuple-element.78), channel_id=1, source_target_pairs={{0,96},{32,0},{64,32},{96,64},{1,97},{33,1},{65,33},{97,65},{2,98}... | collective-permute-start | bytes 393224 | tf_op jit(solution)/shard_map/ppermute | solution.py:330
  81.9 6.7 %collective-permute-start.9 = (f32[128,256]{1,0:T(8,128)}, f32[128,256]{1,0:T(8,128)S(1)}, u32[]{:S(2)}, u32[]{:S(2)}) collective-permute-start(f32[128,256]{1,0:T(8,128)} %get-tuple-element.76), channel_id=1, source_target_pairs={{0,32},{32,64},{64,96},{96,0},{1,33},{33,65},{65,97},{97,1},{2,34}... | collective-permute-start | bytes 393224 | tf_op jit(solution)/shard_map/ppermute | solution.py:330
  92.6 27.4 %all-to-all-start.3 = ((f32[4,128,640]{2,1,0:T(8,128)}), f32[4,128,640]{2,1,0:T(8,128)S(1)}, u32[]{:S(2)}, u32[]{:S(2)}) async-start(f32[4,128,640]{2,1,0:T(8,128)} %get-tuple-element.86.refs_4_), calls=%async_computation.3 | async-start | bytes 2621440 | tf_op jit(solution)/shard_map/all_to_all | solution.py:326
  97.5 1.9 %collective-permute-start.12 = (f32[512,256]{1,0:T(8,128)S(1)}, f32[512,256]{1,0:T(8,128)S(1)}, u32[]{:S(2)}, u32[]{:S(2)}) collective-permute-start(f32[512,256]{1,0:T(8,128)S(1)} %copy-done.6), channel_id=1, source_target_pairs={{0,8},{8,0},{1,9},{9,1},{2,10},{10,2},{3,11},{11,3},{4,12},{12,4},... | collective-permute-start | bytes 1572872 | tf_op jit(solution)/shard_map/ppermute | solution.py:338
  102.7 11.6 %collective-permute-start.13 = (f32[4,72,256]{2,1,0:T(8,128)}, f32[4,72,256]{2,1,0:T(8,128)S(1)}, u32[]{:S(2)}, u32[]{:S(2)}) collective-permute-start(f32[4,72,256]{2,1,0:T(8,128)} %get-tuple-element.89), channel_id=1, source_target_pairs={{0,4},{2,6},{4,0},{6,2},{1,5},{3,7},{5,1},{7,3},{8,12},{10,14},{12... | collective-permute-start | bytes 884744 | tf_op jit(solution)/shard_map/ppermute | solution.py:330
  105.9 13.9 %collective-permute-start.14 = (f32[4,72,256]{2,1,0:T(8,128)}, f32[4,72,256]{2,1,0:T(8,128)S(1)}, u32[]{:S(2)}, u32[]{:S(2)}) collective-permute-start(f32[4,72,256]{2,1,0:T(8,128)} %get-tuple-element.90), channel_id=1, source_target_pairs={{0,2},{2,4},{4,6},{6,0},{1,3},{3,5},{5,7},{7,1},{8,10},{10,12},{12... | collective-permute-start | bytes 884744 | tf_op jit(solution)/shard_map/ppermute | solution.py:330
  106.5 13.6 %collective-permute-start.15 = (f32[4,72,256]{2,1,0:T(8,128)}, f32[4,72,256]{2,1,0:T(8,128)S(1)}, u32[]{:S(2)}, u32[]{:S(2)}) collective-permute-start(f32[4,72,256]{2,1,0:T(8,128)} %get-tuple-element.91), channel_id=1, source_target_pairs={{0,6},{2,0},{4,2},{6,4},{1,7},{3,1},{5,3},{7,5},{8,14},{10,8},{12,... | collective-permute-start | bytes 884744 | tf_op jit(solution)/shard_map/ppermute | solution.py:330
  120.1 3.0 %collective-permute-start.16 = (f32[4,128,640]{2,1,0:T(8,128)S(1)}, f32[4,128,640]{2,1,0:T(8,128)S(1)}, u32[]{:S(2)}, u32[]{:S(2)}) collective-permute-start(f32[4,128,640]{2,1,0:T(8,128)S(1)} %all-to-all-done.3.refs_2_), channel_id=1, source_target_pairs={{0,8},{8,0},{1,9},{9,1},{2,10},{10,2},{3,11},{11,3},{4,12},{12,4},... | collective-permute-start | bytes 3932168 | tf_op jit(solution)/shard_map/ppermute | solution.py:338
  127.8 48.6 %all-to-all-start.4 = ((f32[16,72,640]{2,1,0:T(8,128)}), f32[16,72,640]{2,1,0:T(8,128)S(1)}, u32[]{:S(2)}, u32[]{:S(2)}) async-start(f32[16,72,640]{2,1,0:T(8,128)} %key_value_product.1), calls=%async_computation.4 | async-start | bytes 5898240 | tf_op jit(solution)/shard_map/all_to_all | solution.py:326
  134.4 14.5 %slice-start = ((s8[5160960]{0:T(1024)(128)(4,1)}), s8[4194304]{0:T(1024)(128)(4,1)S(1)}, s32[]{:S(2)}) async-start(s8[5160960]{0:T(1024)(128)(4,1)} %bitcast.15), calls=%async_computation.5 | async-start | bytes 8388608
  138.6 10.3 %slice-start.1 = ((s8[5160960]{0:T(1024)(128)(4,1)}), s8[966656]{0:T(1024)(128)(4,1)S(1)}, s32[]{:S(2)}) async-start(s8[5160960]{0:T(1024)(128)(4,1)} %bitcast.15), calls=%async_computation.6 | async-start | bytes 1933312
  138.6 10.3 %copy-start.7 = (bf16[128,1120]{1,0:T(8,128)(2,1)S(1)}, bf16[128,1120]{1,0:T(8,128)(2,1)}, u32[]{:S(2)}) copy-start(bf16[128,1120]{1,0:T(8,128)(2,1)} %get-tuple-element.84) | copy-start | bytes 860164
  142.8 29.0 %collective-permute-start.17 = (f32[72,256]{1,0:T(8,128)S(1)}, f32[72,256]{1,0:T(8,128)S(1)}, u32[]{:S(2)}, u32[]{:S(2)}) collective-permute-start(f32[72,256]{1,0:T(8,128)S(1)} %copy-done.13), channel_id=1, source_target_pairs={{0,1},{1,16},{16,17},{17,0},{2,3},{3,18},{18,19},{19,2},{4,5},{5,2... | collective-permute-start | bytes 221192 | tf_op jit(solution)/shard_map/ppermute | solution.py:330
  144.8 27.0 %collective-permute-start.18 = (f32[72,256]{1,0:T(8,128)S(1)}, f32[72,256]{1,0:T(8,128)S(1)}, u32[]{:S(2)}, u32[]{:S(2)}) collective-permute-start(f32[72,256]{1,0:T(8,128)S(1)} %copy-done.12), channel_id=1, source_target_pairs={{0,16},{1,17},{16,0},{17,1},{2,18},{3,19},{18,2},{19,3},{4,20},{5,... | collective-permute-start | bytes 221192 | tf_op jit(solution)/shard_map/ppermute | solution.py:330
  147.5 24.3 %collective-permute-start.19 = (f32[72,256]{1,0:T(8,128)S(1)}, f32[72,256]{1,0:T(8,128)S(1)}, u32[]{:S(2)}, u32[]{:S(2)}) collective-permute-start(f32[72,256]{1,0:T(8,128)S(1)} %copy-done.11), channel_id=1, source_target_pairs={{0,17},{1,0},{16,1},{17,16},{2,19},{3,2},{18,3},{19,18},{4,21},{5,... | collective-permute-start | bytes 221192 | tf_op jit(solution)/shard_map/ppermute | solution.py:330
  (9 other events, 62.4 us)

commit v15 on v14

--- a/solution.py
+++ b/solution.py
@@ -31,6 +31,7 @@
 IMAGE = ("zh", "core", "x", "zl")
 PLANE = ("zh", "x", "zl")
 CHUNKS = [(0, 1152), (1152, D - 1152)]
+WHOLE = [(0, D)]
 
 F32 = jnp.float32
 BF16 = jnp.bfloat16
@@ -84,9 +85,9 @@
     return jnp.maximum(values, jnp.zeros_like(values))
 
 
-def weight_copies(weight, buffer, semaphores, first):
+def weight_copies(weight, buffer, semaphores, first, chunks):
     copies = []
-    for index, (start, size) in enumerate(CHUNKS):
+    for index, (start, size) in enumerate(chunks):
         copies.append(
             pltpu.make_async_copy(
                 weight.at[pl.ds(start, size)],
@@ -97,9 +98,9 @@
     return copies
 
 
-def project(tokens, buffer, copies):
+def project(tokens, buffer, copies, chunks):
     total = None
-    for (start, size), copy in zip(CHUNKS, copies):
+    for (start, size), copy in zip(chunks, copies):
         copy.wait()
         term = dot(tokens[:, start : start + size], buffer[start : start + size, :], 1, 0)
         total = term if total is None else total + term
@@ -123,13 +124,13 @@
 def key_value_kernel(
     tokens, key_weight, value_weight, key, value, sent, key_buffer, value_buffer, state, total, semaphores
 ):
-    value_copies = weight_copies(value_weight, value_buffer, semaphores, 0)
-    key_copies = weight_copies(key_weight, key_buffer, semaphores, len(CHUNKS))
+    value_copies = weight_copies(value_weight, value_buffer, semaphores, 0, CHUNKS)
+    key_copies = weight_copies(key_weight, key_buffer, semaphores, len(CHUNKS), WHOLE)
     for copy in value_copies + key_copies:
         copy.start()
     rows = tokens[...]
-    value_rows = project(rows, value_buffer, value_copies)
-    key_rows = project(rows, key_buffer, key_copies)
+    value_rows = project(rows, value_buffer, value_copies, CHUNKS)
+    key_rows = project(rows, key_buffer, key_copies, WHOLE)
     for index in range(HEADS):
         part = slice(index * HD, (index + 1) * HD)
         key_head = key_rows[:, part]
@@ -369,7 +370,7 @@
         "key_value",
         [heads, heads, shaped((TILES, PART + HEADS, HD))],
         [BLOCK, IN_HBM, IN_HBM],
-        [weight, weight, state, totals, pltpu.SemaphoreType.DMA((2 * len(CHUNKS),))],
+        [weight, weight, state, totals, pltpu.SemaphoreType.DMA((len(CHUNKS) + 1,))],
         vmem=20,
     )(tokens, key_weight, value_weight)
     sent, later_tokens = lax.optimization_barrier((sent, tokens))

time: 179 us -> 179 us (level)
  no operation moved by 1% of the time
where the time goes in v15:
time: 179 us; the launch traced here: 178 us
  waiting for transfers between devices  66.5 us (37%)
  starting transfers between devices  54.9 us (31%)
  Pallas kernels  42.8 us (24%)
  matrix products  10.7 us (6%)
  local copies, waits for them, and re-layouts  2.2 us (1%)
    pallas_call x13, Pallas kernels, with_placed(): return run(*placed)  42.8 us
    ppermute x15, waiting for transfers between devices, shift(): lax.ppermute(values, axis, [(i, (i + by) % RING) for i in range(RING)])  41.4 us
    all_to_all x5, starting transfers between devices, exchange(): return lax.all_to_all(blocks, axes, 0, 0, tiled=True)  31.4 us
    ppermute x15, starting transfers between devices, shift(): lax.ppermute(values, axis, [(i, (i + by) % RING) for i in range(RING)])  23.5 us
    all_to_all x5, waiting for transfers between devices, exchange(): return lax.all_to_all(blocks, axes, 0, 0, tiled=True)  21.8 us
    dot_general x3, matrix products, dot(): lax.dot_general(left, right, (((left_dim,), (right_dim,)), ((), ())), pre...  10.7 us
  transfers between devices with their start and end apart: 25, of which 15 were waited for; matrix products, arithmetic and copies ran while one was open for 7% of the time, Pallas kernels for 14%

profile of v15, /device:TPU:8, one launch (start us, length us, event | category | flops | bytes accessed | tf_op | source)
XLA Modules:
  0.0 177.9 jit_solution(10675632399975697342)
XLA Ops:
  0.6 7.5 %key_value.1 = (bf16[10,128,112]{2,1,0:T(8,128)(2,1)}, bf16[10,128,112]{2,1,0:T(8,128)(2,1)}, f32[32,45,112]{2,1,0:T(8,128)}) custom-call(bf16[128,2240]{1,0:T(8,128)(2,1)} %bitcast.17, bf16[2240,1120]{1,0:T(8,128)(2,1)} %key_weight.1, bf16[2240,1120]{1,0:T(8,128)(2,1)} %value_weight.1), custom_call_target="tpu_custom_call" | custom-call | tf_op jit(solution)/shard_map/key_value/pallas_call | solution.py:67
  8.2 2.3 %turn.1 = (f32[1120,128]{1,0:T(8,128)}, f32[1120,128]{1,0:T(8,128)}) custom-call(s32[1]{0:T(128)} %bitcast.3.core, bf16[128,2240]{1,0:T(8,128)(2,1)} %bitcast.18), custom_call_target="tpu_custom_call" | custom-call | tf_op jit(solution)/shard_map/turn/pallas_call | solution.py:67
  10.5 8.3 %all-to-all-start = ((f32[32,45,112]{2,1,0:T(8,128)}), f32[32,45,112]{2,1,0:T(8,128)S(1)}, u32[]{:S(2)}, u32[]{:S(2)}) async-start(f32[32,45,112]{2,1,0:T(8,128)} %get-tuple-element.55), calls=%async_computation | async-start | bytes 1572864 | tf_op jit(solution)/shard_map/all_to_all | solution.py:327
  20.9 4.4 %query.1.refs_1_ = bf16[10,128,112]{2,1,0:T(8,128)(2,1)} custom-call(bf16[128,2240]{1,0:T(8,128)(2,1)} %bitcast.19, bf16[2240,1120]{1,0:T(8,128)(2,1)} %weight.1), custom_call_target="tpu_custom_call" | custom-call | tf_op jit(solution)/shard_map/query/pallas_call | solution.py:67
  25.3 8.0 %all-to-all-done.refs_0_ = f32[32,45,112]{2,1,0:T(8,128)S(1)} async-done(((f32[32,45,112]{2,1,0:T(8,128)}), f32[32,45,112]{2,1,0:T(8,128)S(1)}, u32[]{:S(2)}, u32[]{:S(2)}) %all-to-all-start) | async-done | bytes 645152 | tf_op jit(solution)/shard_map/all_to_all | solution.py:327
  33.3 3.5 %numerator.1 = (f32[32,70,112]{2,1,0:T(8,128)}, bf16[10,128,112]{2,1,0:T(8,128)(2,1)}, f32[10,112]{1,0:T(8,128)}) custom-call(f32[32,45,112]{2,1,0:T(8,128)S(1)} %all-to-all-done.refs_0_, bf16[10,128,112]{2,1,0:T(8,128)(2,1)} %query.1.refs_1_, bf16[128,1120]{1,0:T(8,128)(2,1)S(1)} %bitcast.13), custom_call_target="tpu_custom_call" | custom-call | tf_op jit(solution)/shard_map/numerator/pallas_call | solution.py:67
  39.0 5.7 %all-to-all-start.1 = ((f32[32,70,112]{2,1,0:T(8,128)}), f32[32,70,112]{2,1,0:T(8,128)S(1)}, u32[]{:S(2)}, u32[]{:S(2)}) async-start(f32[32,70,112]{2,1,0:T(8,128)} %get-tuple-element.60), calls=%async_computation.1 | async-start | bytes 2359296 | tf_op jit(solution)/shard_map/all_to_all | solution.py:327
  44.8 6.2 %collective-permute-done.3.refs_5_ = f32[1120,128]{1,0:T(8,128)} collective-permute-done((f32[1120,128]{1,0:T(8,128)S(1)}, f32[1120,128]{1,0:T(8,128)}, u32[]{:S(2)}, u32[]{:S(2)}) %collective-permute-start.3) | collective-permute-done | bytes 573472 | tf_op jit(solution)/shard_map/ppermute | solution.py:331
  54.3 9.2 %all-to-all-done.1.refs_0_.got = f32[32,70,112]{2,1,0:T(8,128)S(1)} async-done(((f32[32,70,112]{2,1,0:T(8,128)}), f32[32,70,112]{2,1,0:T(8,128)S(1)}, u32[]{:S(2)}, u32[]{:S(2)}) %all-to-all-start.1) | async-done | bytes 1003552 | tf_op jit(solution)/shard_map/all_to_all | solution.py:327
  63.6 2.6 %total_grad.1 = (f32[32,45,112]{2,1,0:T(8,128)}, f32[128,10]{1,0:T(8,128)}) custom-call(f32[32,70,112]{2,1,0:T(8,128)S(1)} %all-to-all-done.1.refs_0_.got, bf16[10,128,112]{2,1,0:T(8,128)(2,1)S(1)} %copy-done, bf16[128,1120]{1,0:T(8,128)(2,1)S(1)} %bitcast.14, f32[10,112]{1,0:T(8,128)S(1)} %copy-done.5, f32[1120,128]{1,0:T(8,128)} %collective-permute-done.4.refs_4_, ...), custom_call_target="tpu_custom_call" | custom-call | tf_op jit(solution)/shard_map/total_grad/pallas_call | solution.py:67
  69.0 5.9 %all-to-all-start.2 = ((f32[32,45,112]{2,1,0:T(8,128)}), f32[32,45,112]{2,1,0:T(8,128)S(1)}, u32[]{:S(2)}, u32[]{:S(2)}) async-start(f32[32,45,112]{2,1,0:T(8,128)} %get-tuple-element.70), calls=%async_computation.2 | async-start | bytes 1572864 | tf_op jit(solution)/shard_map/all_to_all | solution.py:327
  75.0 3.0 %query_grad.1 = (bf16[128,1120]{1,0:T(8,128)(2,1)}, f32[128,256]{1,0:T(8,128)}, f32[128,256]{1,0:T(8,128)}, f32[128,256]{1,0:T(8,128)}, f32[128,256]{1,0:T(8,128)}, /*index=5*/f32[4,128,24]{2,1,0:T(8,128)}) custom-call(s32[1]{0:T(128)} %bitcast.place.refs_0_, f32[32,70,112]{2,1,0:T(8,128)S(1)} %all-to-all-done.1.refs_0_.got, ...), custom_call_target="tpu_custom_call" | custom-call | tf_op jit(solution)/shard_map/query_grad/pallas_call | solution.py:67
  77.9 2.7 %collective-permute-start.10 = (f32[128,256]{1,0:T(8,128)}, f32[128,256]{1,0:T(8,128)S(1)}, u32[]{:S(2)}, u32[]{:S(2)}) collective-permute-start(f32[128,256]{1,0:T(8,128)} %get-tuple-element.77), channel_id=1, source_target_pairs={{0,64},{32,96},{64,0},{96,32},{1,65},{33,97},{65,1},{97,33},{2,66}... | collective-permute-start | bytes 393224 | tf_op jit(solution)/shard_map/ppermute | solution.py:331
  82.6 4.0 %join.1.refs_1_ = bf16[1120,1024]{1,0:T(8,128)(2,1)} custom-call(f32[1120,128]{1,0:T(8,128)} %get-tuple-element.64.refs_0_, f32[1120,128]{1,0:T(8,128)S(1)} %collective-permute-done.refs_1_, f32[1120,128]{1,0:T(8,128)} %collective-permute-done.7.refs_2_, f32[1120,128]{1,0:T(8,128)} %collective-permute-done.5.refs_3_, ...), custom_call_target="tpu_custom_call" | custom-call | tf_op jit(solution)/shard_map/join/pallas_call | solution.py:67
  90.2 2.3 %key_value_grad.1 = (bf16[128,1120]{1,0:T(8,128)(2,1)}, bf16[128,1120]{1,0:T(8,128)(2,1)}, f32[4,128,640]{2,1,0:T(8,128)}) custom-call(f32[32,45,112]{2,1,0:T(8,128)S(1)} %all-to-all-done.2.got, bf16[10,128,112]{2,1,0:T(8,128)(2,1)S(1)} %copy-done.2, bf16[10,128,112]{2,1,0:T(8,128)(2,1)S(1)} %copy-done.3, f32[4,128,24]{2,1,0:T(8,128)S(1)} %copy-done.4), custom_call_target="tpu_custom_call" | custom-call | tf_op jit(solution)/shard_map/key_value_grad/pallas_call | solution.py:67
  92.5 4.8 %all-to-all-start.3 = ((f32[4,128,640]{2,1,0:T(8,128)}), f32[4,128,640]{2,1,0:T(8,128)S(1)}, u32[]{:S(2)}, u32[]{:S(2)}) async-start(f32[4,128,640]{2,1,0:T(8,128)} %get-tuple-element.86.refs_4_), calls=%async_computation.3 | async-start | bytes 2621440 | tf_op jit(solution)/shard_map/all_to_all | solution.py:327
  97.3 1.9 %collective-permute-done.12.refs_3_ = f32[512,256]{1,0:T(8,128)S(1)} collective-permute-done((f32[512,256]{1,0:T(8,128)S(1)}, f32[512,256]{1,0:T(8,128)S(1)}, u32[]{:S(2)}, u32[]{:S(2)}) %collective-permute-start.12) | collective-permute-done | bytes 524320 | tf_op jit(solution)/shard_map/ppermute | solution.py:339
  99.2 3.3 %query_product.1 = (f32[4,72,256]{2,1,0:T(8,128)}, f32[4,72,256]{2,1,0:T(8,128)}, f32[4,72,256]{2,1,0:T(8,128)}, f32[4,72,256]{2,1,0:T(8,128)}) custom-call(s32[1]{0:T(128)} %bitcast.5.refs_0_, bf16[1120,1024]{1,0:T(8,128)(2,1)} %join.1.refs_1_, f32[512,256]{1,0:T(8,128)} %pack_query.1.refs_2_, f32[512,256]{1,0:T(8,128)S(1)} %collective-permute-done.12.refs_3_, ...), custom_call_target="tpu_custom_call" | custom-call | tf_op jit(solution)/shard_map/query_product/pallas_call | solution.py:67
  102.6 3.2 %collective-permute-start.13 = (f32[4,72,256]{2,1,0:T(8,128)}, f32[4,72,256]{2,1,0:T(8,128)S(1)}, u32[]{:S(2)}, u32[]{:S(2)}) collective-permute-start(f32[4,72,256]{2,1,0:T(8,128)} %get-tuple-element.89), channel_id=1, source_target_pairs={{0,4},{2,6},{4,0},{6,2},{1,5},{3,7},{5,1},{7,3},{8,12},{10,14},{12... | collective-permute-start | bytes 884744 | tf_op jit(solution)/shard_map/ppermute | solution.py:331
  106.3 2.7 %collective-permute-start.15 = (f32[4,72,256]{2,1,0:T(8,128)}, f32[4,72,256]{2,1,0:T(8,128)S(1)}, u32[]{:S(2)}, u32[]{:S(2)}) collective-permute-start(f32[4,72,256]{2,1,0:T(8,128)} %get-tuple-element.91), channel_id=1, source_target_pairs={{0,6},{2,0},{4,2},{6,4},{1,7},{3,1},{5,3},{7,5},{8,14},{10,8},{12,... | collective-permute-start | bytes 884744 | tf_op jit(solution)/shard_map/ppermute | solution.py:331
  109.0 5.2 %collective-permute-done.13.first = f32[4,72,256]{2,1,0:T(8,128)S(1)} collective-permute-done((f32[4,72,256]{2,1,0:T(8,128)}, f32[4,72,256]{2,1,0:T(8,128)S(1)}, u32[]{:S(2)}, u32[]{:S(2)}) %collective-permute-start.13) | collective-permute-done | bytes 294944 | tf_op jit(solution)/shard_map/ppermute | solution.py:331
  114.2 5.5 %collective-permute-done.14.second = f32[4,72,256]{2,1,0:T(8,128)S(1)} collective-permute-done((f32[4,72,256]{2,1,0:T(8,128)}, f32[4,72,256]{2,1,0:T(8,128)S(1)}, u32[]{:S(2)}, u32[]{:S(2)}) %collective-permute-start.14) | collective-permute-done | bytes 294944 | tf_op jit(solution)/shard_map/ppermute | solution.py:331
  122.9 4.7 %key_value_product.1 = f32[16,72,640]{2,1,0:T(8,128)} custom-call(s32[1]{0:T(128)} %bitcast.place.refs_0_, bf16[1120,1024]{1,0:T(8,128)(2,1)} %join.1.refs_1_, f32[4,128,640]{2,1,0:T(8,128)S(1)} %all-to-all-done.3.refs_2_, f32[4,128,640]{2,1,0:T(8,128)S(1)} %collective-permute-done.16.refs_3_, f32[72,256]{1,0:T(8,128)} %get-tuple-element.97.refs_4_.own), custom_call_target="tpu_custom_call" | custom-call | tf_op jit(solution)/shard_map/key_value_product/pallas_call | solution.py:67
  127.6 6.6 %all-to-all-start.4 = ((f32[16,72,640]{2,1,0:T(8,128)}), f32[16,72,640]{2,1,0:T(8,128)S(1)}, u32[]{:S(2)}, u32[]{:S(2)}) async-start(f32[16,72,640]{2,1,0:T(8,128)} %key_value_product.1), calls=%async_computation.4 | async-start | bytes 5898240 | tf_op jit(solution)/shard_map/all_to_all | solution.py:327
  134.2 4.2 %fusion.1 = f32[128,2240]{0,1:T(8,128)S(1)} fusion(bf16[128,1120]{1,0:T(8,128)(2,1)S(1)} %copy-done.8, bf16[2240,1120]{1,0:T(8,128)(2,1)} %key_weight.1), kind=kOutput, calls=%fused_computation.3 | convolution fusion | flops 642252800 | bytes 6451200 | tf_op jit(solution)/shard_map/dot_general | solution.py:73
  138.5 4.1 %convolution_add_fusion.1 = f32[128,2240]{0,1:T(8,128)S(1)} fusion(f32[128,2240]{0,1:T(8,128)S(1)} %fusion.1, bf16[128,1120]{1,0:T(8,128)(2,1)S(1)} %copy-done.9, bf16[2240,1120]{1,0:T(8,128)(2,1)} %weight.1), kind=kOutput, calls=%fused_computation.1 | convolution fusion | flops 642539520 | bytes 7598080 | tf_op jit(solution)/shard_map/dot_general | solution.py:73
  142.6 2.0 %collective-permute-start.17 = (f32[72,256]{1,0:T(8,128)S(1)}, f32[72,256]{1,0:T(8,128)S(1)}, u32[]{:S(2)}, u32[]{:S(2)}) collective-permute-start(f32[72,256]{1,0:T(8,128)S(1)} %copy-done.13), channel_id=1, source_target_pairs={{0,1},{1,16},{16,17},{17,0},{2,3},{3,18},{18,19},{19,2},{4,5},{5,2... | collective-permute-start | bytes 221192 | tf_op jit(solution)/shard_map/ppermute | solution.py:331
  144.6 2.7 %collective-permute-start.18 = (f32[72,256]{1,0:T(8,128)S(1)}, f32[72,256]{1,0:T(8,128)S(1)}, u32[]{:S(2)}, u32[]{:S(2)}) collective-permute-start(f32[72,256]{1,0:T(8,128)S(1)} %copy-done.12), channel_id=1, source_target_pairs={{0,16},{1,17},{16,0},{17,1},{2,18},{3,19},{18,2},{19,3},{4,20},{5,... | collective-permute-start | bytes 221192 | tf_op jit(solution)/shard_map/ppermute | solution.py:331
  148.8 2.4 %fusion = bf16[128,2240]{0,1:T(8,128)(2,1)} fusion(f32[128,2240]{0,1:T(8,128)S(1)} %convolution_add_fusion.1, bf16[128,1120]{1,0:T(8,128)(2,1)S(1)} %copy-done.7, bf16[2240,1120]{1,0:T(8,128)(2,1)S(1)} %bitcast.16), kind=kOutput, calls=%fused_computation.2 | convolution fusion | flops 642826240 | bytes 7024640 | tf_op jit(solution)/shard_map/dot_general | solution.py:73
  151.1 2.1 %copy.10 = bf16[128,2240]{1,0:T(8,128)(2,1)} copy(bf16[128,2240]{0,1:T(8,128)(2,1)} %fusion) | data formatting | bytes 1146880 | tf_op jit(solution)/shard_map/convert_element_type | solution.py:513
  153.3 18.3 %collective-permute-done.17.first = f32[72,256]{1,0:T(8,128)S(1)} collective-permute-done((f32[72,256]{1,0:T(8,128)S(1)}, f32[72,256]{1,0:T(8,128)S(1)}, u32[]{:S(2)}, u32[]{:S(2)}) %collective-permute-start.17) | collective-permute-done | bytes 73760 | tf_op jit(solution)/shard_map/ppermute | solution.py:331
  171.6 4.6 %all-to-all-done.4.key_value = f32[16,72,640]{2,1,0:T(8,128)S(1)} async-done(((f32[16,72,640]{2,1,0:T(8,128)}), f32[16,72,640]{2,1,0:T(8,128)S(1)}, u32[]{:S(2)}, u32[]{:S(2)}) %all-to-all-start.4) | async-done | bytes 2949152 | tf_op jit(solution)/shard_map/all_to_all | solution.py:327
  (68 shorter events, 23.1 us)
Async XLA Ops:
  10.5 10.0 %collective-permute-start.1 = (f32[1120,128]{1,0:T(8,128)}, f32[1120,128]{1,0:T(8,128)S(1)}, u32[]{:S(2)}, u32[]{:S(2)}) collective-permute-start(f32[1120,128]{1,0:T(8,128)} %get-tuple-element.59), channel_id=1, source_target_pairs={{0,8},{8,0},{1,9},{9,1},{2,10},{10,2},{3,11},{11,3},{4,12},{12,4},... | collective-permute-start | bytes 1720328 | tf_op jit(solution)/shard_map/ppermute | solution.py:339
  10.5 22.8 %all-to-all-start = ((f32[32,45,112]{2,1,0:T(8,128)}), f32[32,45,112]{2,1,0:T(8,128)S(1)}, u32[]{:S(2)}, u32[]{:S(2)}) async-start(f32[32,45,112]{2,1,0:T(8,128)} %get-tuple-element.55), calls=%async_computation | async-start | bytes 1572864 | tf_op jit(solution)/shard_map/all_to_all | solution.py:327
  18.8 14.5 %copy-start.1 = (bf16[1,16,8,1120]{3,2,1,0:T(8,128)(2,1)S(1)}, bf16[1,16,8,1120]{3,2,1,0:T(8,128)(2,1)}, u32[]{:S(2)}) copy-start(bf16[1,16,8,1120]{3,2,1,0:T(8,128)(2,1)} %param.9) | copy-start | bytes 860164
  18.8 19.7 %copy-start.10 = (f32[1120,128]{1,0:T(8,128)S(1)}, f32[1120,128]{1,0:T(8,128)}, u32[]{:S(2)}) copy-start(f32[1120,128]{1,0:T(8,128)} %get-tuple-element.64.refs_0_) | copy-start | bytes 1720324
  18.8 18.1 %collective-permute-start = (f32[1120,128]{1,0:T(8,128)}, f32[1120,128]{1,0:T(8,128)S(1)}, u32[]{:S(2)}, u32[]{:S(2)}) collective-permute-start(f32[1120,128]{1,0:T(8,128)} %get-tuple-element.64.refs_0_), channel_id=1, source_target_pairs={{0,32},{32,64},{64,96},{96,0},{1,33},{33,65},{65,97},{97,1},{2,34}... | collective-permute-start | bytes 1720328 | tf_op jit(solution)/shard_map/ppermute | solution.py:331
  20.5 16.4 %collective-permute-start.2 = (f32[1120,128]{1,0:T(8,128)S(1)}, f32[1120,128]{1,0:T(8,128)}, u32[]{:S(2)}, u32[]{:S(2)}) collective-permute-start(f32[1120,128]{1,0:T(8,128)S(1)} %collective-permute-done.1.refs_4_), channel_id=1, source_target_pairs={{0,96},{32,0},{64,32},{96,64},{1,97},{33,1},{65,33},{97,65},{2,98}... | collective-permute-start | bytes 1720328 | tf_op jit(solution)/shard_map/ppermute | solution.py:331
  25.3 38.2 %copy-start = (bf16[10,128,112]{2,1,0:T(8,128)(2,1)S(1)}, bf16[10,128,112]{2,1,0:T(8,128)(2,1)}, u32[]{:S(2)}) copy-start(bf16[10,128,112]{2,1,0:T(8,128)(2,1)} %query.1.refs_1_) | copy-start | bytes 860164
  36.9 26.7 %copy-start.5 = (f32[10,112]{1,0:T(8,128)S(1)}, f32[10,112]{1,0:T(8,128)}, u32[]{:S(2)}) copy-start(f32[10,112]{1,0:T(8,128)} %get-tuple-element.62.refs_3_.total) | copy-start | bytes 13444
  36.9 14.1 %collective-permute-start.3 = (f32[1120,128]{1,0:T(8,128)S(1)}, f32[1120,128]{1,0:T(8,128)}, u32[]{:S(2)}, u32[]{:S(2)}) collective-permute-start(f32[1120,128]{1,0:T(8,128)S(1)} %collective-permute-done.1.refs_4_), channel_id=1, source_target_pairs={{0,32},{32,64},{64,96},{96,0},{1,33},{33,65},{65,97},{97,1},{2,34}... | collective-permute-start | bytes 1720328 | tf_op jit(solution)/shard_map/ppermute | solution.py:331
  38.6 13.7 %collective-permute-start.5 = (f32[1120,128]{1,0:T(8,128)S(1)}, f32[1120,128]{1,0:T(8,128)}, u32[]{:S(2)}, u32[]{:S(2)}) collective-permute-start(f32[1120,128]{1,0:T(8,128)S(1)} %copy-done.10), channel_id=1, source_target_pairs={{0,96},{32,0},{64,32},{96,64},{1,97},{33,1},{65,33},{97,65},{2,98}... | collective-permute-start | bytes 1720328 | tf_op jit(solution)/shard_map/ppermute | solution.py:331
  39.0 24.5 %all-to-all-start.1 = ((f32[32,70,112]{2,1,0:T(8,128)}), f32[32,70,112]{2,1,0:T(8,128)S(1)}, u32[]{:S(2)}, u32[]{:S(2)}) async-start(f32[32,70,112]{2,1,0:T(8,128)} %get-tuple-element.60), calls=%async_computation.1 | async-start | bytes 2359296 | tf_op jit(solution)/shard_map/all_to_all | solution.py:327
  51.0 12.6 %collective-permute-start.4 = (f32[1120,128]{1,0:T(8,128)}, f32[1120,128]{1,0:T(8,128)}, u32[]{:S(2)}, u32[]{:S(2)}) collective-permute-start(f32[1120,128]{1,0:T(8,128)} %collective-permute-done.3.refs_5_), channel_id=1, source_target_pairs={{0,8},{8,0},{1,9},{9,1},{2,10},{10,2},{3,11},{11,3},{4,12},{12,4},... | collective-permute-start | bytes 1720328 | tf_op jit(solution)/shard_map/ppermute | solution.py:339
  52.3 11.3 %collective-permute-start.6 = (f32[1120,128]{1,0:T(8,128)}, f32[1120,128]{1,0:T(8,128)}, u32[]{:S(2)}, u32[]{:S(2)}) collective-permute-start(f32[1120,128]{1,0:T(8,128)} %collective-permute-done.5.refs_3_), channel_id=1, source_target_pairs={{0,8},{8,0},{1,9},{9,1},{2,10},{10,2},{3,11},{11,3},{4,12},{12,4},... | collective-permute-start | bytes 1720328 | tf_op jit(solution)/shard_map/ppermute | solution.py:339
  52.3 15.5 %collective-permute-start.7 = (f32[1120,128]{1,0:T(8,128)S(1)}, f32[1120,128]{1,0:T(8,128)}, u32[]{:S(2)}, u32[]{:S(2)}) collective-permute-start(f32[1120,128]{1,0:T(8,128)S(1)} %collective-permute-done.refs_1_), channel_id=1, source_target_pairs={{0,32},{32,64},{64,96},{96,0},{1,33},{33,65},{65,97},{97,1},{2,34}... | collective-permute-start | bytes 1720328 | tf_op jit(solution)/shard_map/ppermute | solution.py:331
  53.6 15.4 %collective-permute-start.8 = (f32[1120,128]{1,0:T(8,128)}, f32[1120,128]{1,0:T(8,128)}, u32[]{:S(2)}, u32[]{:S(2)}) collective-permute-start(f32[1120,128]{1,0:T(8,128)} %collective-permute-done.2.refs_7_), channel_id=1, source_target_pairs={{0,96},{32,0},{64,32},{96,64},{1,97},{33,1},{65,33},{97,65},{2,98}... | collective-permute-start | bytes 1720328 | tf_op jit(solution)/shard_map/ppermute | solution.py:331
  69.0 21.1 %all-to-all-start.2 = ((f32[32,45,112]{2,1,0:T(8,128)}), f32[32,45,112]{2,1,0:T(8,128)S(1)}, u32[]{:S(2)}, u32[]{:S(2)}) async-start(f32[32,45,112]{2,1,0:T(8,128)} %get-tuple-element.70), calls=%async_computation.2 | async-start | bytes 1572864 | tf_op jit(solution)/shard_map/all_to_all | solution.py:327
  77.9 8.7 %collective-permute-start.10 = (f32[128,256]{1,0:T(8,128)}, f32[128,256]{1,0:T(8,128)S(1)}, u32[]{:S(2)}, u32[]{:S(2)}) collective-permute-start(f32[128,256]{1,0:T(8,128)} %get-tuple-element.77), channel_id=1, source_target_pairs={{0,64},{32,96},{64,0},{96,32},{1,65},{33,97},{65,1},{97,33},{2,66}... | collective-permute-start | bytes 393224 | tf_op jit(solution)/shard_map/ppermute | solution.py:331
  80.6 7.5 %collective-permute-start.11 = (f32[128,256]{1,0:T(8,128)}, f32[128,256]{1,0:T(8,128)S(1)}, u32[]{:S(2)}, u32[]{:S(2)}) collective-permute-start(f32[128,256]{1,0:T(8,128)} %get-tuple-element.78), channel_id=1, source_target_pairs={{0,96},{32,0},{64,32},{96,64},{1,97},{33,1},{65,33},{97,65},{2,98}... | collective-permute-start | bytes 393224 | tf_op jit(solution)/shard_map/ppermute | solution.py:331
  81.7 6.7 %collective-permute-start.9 = (f32[128,256]{1,0:T(8,128)}, f32[128,256]{1,0:T(8,128)S(1)}, u32[]{:S(2)}, u32[]{:S(2)}) collective-permute-start(f32[128,256]{1,0:T(8,128)} %get-tuple-element.76), channel_id=1, source_target_pairs={{0,32},{32,64},{64,96},{96,0},{1,33},{33,65},{65,97},{97,1},{2,34}... | collective-permute-start | bytes 393224 | tf_op jit(solution)/shard_map/ppermute | solution.py:331
  92.5 27.4 %all-to-all-start.3 = ((f32[4,128,640]{2,1,0:T(8,128)}), f32[4,128,640]{2,1,0:T(8,128)S(1)}, u32[]{:S(2)}, u32[]{:S(2)}) async-start(f32[4,128,640]{2,1,0:T(8,128)} %get-tuple-element.86.refs_4_), calls=%async_computation.3 | async-start | bytes 2621440 | tf_op jit(solution)/shard_map/all_to_all | solution.py:327
  97.3 1.9 %collective-permute-start.12 = (f32[512,256]{1,0:T(8,128)S(1)}, f32[512,256]{1,0:T(8,128)S(1)}, u32[]{:S(2)}, u32[]{:S(2)}) collective-permute-start(f32[512,256]{1,0:T(8,128)S(1)} %copy-done.6), channel_id=1, source_target_pairs={{0,8},{8,0},{1,9},{9,1},{2,10},{10,2},{3,11},{11,3},{4,12},{12,4},... | collective-permute-start | bytes 1572872 | tf_op jit(solution)/shard_map/ppermute | solution.py:339
  102.6 11.6 %collective-permute-start.13 = (f32[4,72,256]{2,1,0:T(8,128)}, f32[4,72,256]{2,1,0:T(8,128)S(1)}, u32[]{:S(2)}, u32[]{:S(2)}) collective-permute-start(f32[4,72,256]{2,1,0:T(8,128)} %get-tuple-element.89), channel_id=1, source_target_pairs={{0,4},{2,6},{4,0},{6,2},{1,5},{3,7},{5,1},{7,3},{8,12},{10,14},{12... | collective-permute-start | bytes 884744 | tf_op jit(solution)/shard_map/ppermute | solution.py:331
  105.7 13.9 %collective-permute-start.14 = (f32[4,72,256]{2,1,0:T(8,128)}, f32[4,72,256]{2,1,0:T(8,128)S(1)}, u32[]{:S(2)}, u32[]{:S(2)}) collective-permute-start(f32[4,72,256]{2,1,0:T(8,128)} %get-tuple-element.90), channel_id=1, source_target_pairs={{0,2},{2,4},{4,6},{6,0},{1,3},{3,5},{5,7},{7,1},{8,10},{10,12},{12... | collective-permute-start | bytes 884744 | tf_op jit(solution)/shard_map/ppermute | solution.py:331
  106.3 13.6 %collective-permute-start.15 = (f32[4,72,256]{2,1,0:T(8,128)}, f32[4,72,256]{2,1,0:T(8,128)S(1)}, u32[]{:S(2)}, u32[]{:S(2)}) collective-permute-start(f32[4,72,256]{2,1,0:T(8,128)} %get-tuple-element.91), channel_id=1, source_target_pairs={{0,6},{2,0},{4,2},{6,4},{1,7},{3,1},{5,3},{7,5},{8,14},{10,8},{12,... | collective-permute-start | bytes 884744 | tf_op jit(solution)/shard_map/ppermute | solution.py:331
  119.9 3.0 %collective-permute-start.16 = (f32[4,128,640]{2,1,0:T(8,128)S(1)}, f32[4,128,640]{2,1,0:T(8,128)S(1)}, u32[]{:S(2)}, u32[]{:S(2)}) collective-permute-start(f32[4,128,640]{2,1,0:T(8,128)S(1)} %all-to-all-done.3.refs_2_), channel_id=1, source_target_pairs={{0,8},{8,0},{1,9},{9,1},{2,10},{10,2},{3,11},{11,3},{4,12},{12,4},... | collective-permute-start | bytes 3932168 | tf_op jit(solution)/shard_map/ppermute | solution.py:339
  127.6 48.6 %all-to-all-start.4 = ((f32[16,72,640]{2,1,0:T(8,128)}), f32[16,72,640]{2,1,0:T(8,128)S(1)}, u32[]{:S(2)}, u32[]{:S(2)}) async-start(f32[16,72,640]{2,1,0:T(8,128)} %key_value_product.1), calls=%async_computation.4 | async-start | bytes 5898240 | tf_op jit(solution)/shard_map/all_to_all | solution.py:327
  134.2 14.5 %slice-start = ((s8[5160960]{0:T(1024)(128)(4,1)}), s8[4194304]{0:T(1024)(128)(4,1)S(1)}, s32[]{:S(2)}) async-start(s8[5160960]{0:T(1024)(128)(4,1)} %bitcast.15), calls=%async_computation.5 | async-start | bytes 8388608
  138.5 10.3 %slice-start.1 = ((s8[5160960]{0:T(1024)(128)(4,1)}), s8[966656]{0:T(1024)(128)(4,1)S(1)}, s32[]{:S(2)}) async-start(s8[5160960]{0:T(1024)(128)(4,1)} %bitcast.15), calls=%async_computation.6 | async-start | bytes 1933312
  138.5 10.3 %copy-start.7 = (bf16[128,1120]{1,0:T(8,128)(2,1)S(1)}, bf16[128,1120]{1,0:T(8,128)(2,1)}, u32[]{:S(2)}) copy-start(bf16[128,1120]{1,0:T(8,128)(2,1)} %get-tuple-element.84) | copy-start | bytes 860164
  142.6 29.0 %collective-permute-start.17 = (f32[72,256]{1,0:T(8,128)S(1)}, f32[72,256]{1,0:T(8,128)S(1)}, u32[]{:S(2)}, u32[]{:S(2)}) collective-permute-start(f32[72,256]{1,0:T(8,128)S(1)} %copy-done.13), channel_id=1, source_target_pairs={{0,1},{1,16},{16,17},{17,0},{2,3},{3,18},{18,19},{19,2},{4,5},{5,2... | collective-permute-start | bytes 221192 | tf_op jit(solution)/shard_map/ppermute | solution.py:331
  144.6 27.0 %collective-permute-start.18 = (f32[72,256]{1,0:T(8,128)S(1)}, f32[72,256]{1,0:T(8,128)S(1)}, u32[]{:S(2)}, u32[]{:S(2)}) collective-permute-start(f32[72,256]{1,0:T(8,128)S(1)} %copy-done.12), channel_id=1, source_target_pairs={{0,16},{1,17},{16,0},{17,1},{2,18},{3,19},{18,2},{19,3},{4,20},{5,... | collective-permute-start | bytes 221192 | tf_op jit(solution)/shard_map/ppermute | solution.py:331
  147.3 24.3 %collective-permute-start.19 = (f32[72,256]{1,0:T(8,128)S(1)}, f32[72,256]{1,0:T(8,128)S(1)}, u32[]{:S(2)}, u32[]{:S(2)}) collective-permute-start(f32[72,256]{1,0:T(8,128)S(1)} %copy-done.11), channel_id=1, source_target_pairs={{0,17},{1,0},{16,1},{17,16},{2,19},{3,2},{18,3},{19,18},{4,21},{5,... | collective-permute-start | bytes 221192 | tf_op jit(solution)/shard_map/ppermute | solution.py:331
  (9 other events, 62.4 us)
